TPU v7x, 32 devices: a whole 2x2x4 slice. The times are simulated.
32 devices in a mesh: vocab: 8 (over y, x, core), blk: 4 (over z).
Axes of the slice: x: 2, y: 2, z: 4, core: 2. Of those that a mesh axis runs over, the one named last changes fastest.
Arguments:
- char_ids: int32 [16384, 50], P(('vocab', 'blk')), may hold values from 0 to 255, as said below
- char_table: bfloat16 [256, 16], replicated, may hold values from -5 to 5
- conv_weight: bfloat16 [112, 896], replicated, may hold values from -0.75 to 0.75
- proj_weight: bfloat16 [896, 1024], replicated, may hold values from -0.1875 to 0.1875
- gate_weight: bfloat16 [2, 1024, 1024], replicated, may hold values from -0.1875 to 0.1875
- trans_weight: bfloat16 [2, 1024, 1024], replicated, may hold values from -0.1875 to 0.1875
- gate_bias: float32 [2, 1024], replicated, may hold values from -4 to 4
- hidden: bfloat16 [2048, 1024], P(('vocab', 'blk')), may hold values from -48 to 48
- targets: int32 [2048], P(('vocab', 'blk')), may hold values from 0 to 16383
Outputs:
- row_loss: float32 [2048], P(('vocab', 'blk'))
- hidden_grad: bfloat16 [2048, 1024], P(('vocab', 'blk'))
Inputs may be any that keep to these rules, and one draw needn't show every extreme that they name: `char_ids`: each word has 2 to 50 characters with ids 1 and up, followed by the padding id 0.
All inputs are finite; a program needn't handle non-finite values.
Results may differ from a plain program's by a relative error of at most 0.014.
The roundings to bfloat16 on the way count: a program that leaves them out, or rounds other values in their place, can miss the bound.
Values may be sent and summed in bfloat16 or wider, within the bound.
No kernel may reach another device: no remote copies, remote signals or barrier semaphores. Data moves between devices by JAX's collectives and lax.ppermute only.
A program may use at most 128 MiB of HBM per device.

v0:
```python
import math

import jax
import jax.numpy as jnp
from jax import lax
from jax.sharding import PartitionSpec as P


def shifted(array, axis, by):
    count = lax.axis_size(axis)
    return lax.ppermute(array, axis, [(i, (i + by) % count) for i in range(count)])


def char_features(char_ids, char_table, conv_weight):
    num_words = char_ids.shape[0]
    length = char_ids.shape[1]
    symbols = char_table.shape[0]
    embed_dim = char_table.shape[1]
    widths = conv_weight.shape[0] // embed_dim
    filters = conv_weight.shape[1] // widths
    onehot = (char_ids[:, :, None] == jnp.arange(symbols, dtype=jnp.int32)[None, None, :]).astype(
        jnp.bfloat16
    )
    vectors = jnp.dot(
        onehot.reshape(num_words * length, symbols), char_table, preferred_element_type=jnp.float32
    )
    vectors = vectors.astype(jnp.bfloat16).reshape(num_words, length, embed_dim)
    padded = jnp.pad(vectors, ((0, 0), (0, widths - 1), (0, 0)))
    windows = jnp.concatenate(
        [padded[:, shift_at : shift_at + length, :] for shift_at in range(widths)], axis=2
    )
    offset = jnp.arange(widths * embed_dim) // embed_dim
    kernel = jnp.arange(widths * filters) // filters + 1
    masked = jnp.where(offset[:, None] < kernel[None, :], conv_weight, jnp.zeros_like(conv_weight))
    conv_out = jnp.dot(
        windows.reshape(num_words * length, widths * embed_dim),
        masked,
        preferred_element_type=jnp.float32,
    )
    conv_out = conv_out.reshape(num_words, length, widths * filters)
    position = jnp.arange(length)
    usable = position[:, None] <= length - kernel[None, :]
    pooled = jnp.max(jnp.where(usable[None, :, :], conv_out, -jnp.inf), axis=1)
    return jnp.tanh(pooled).astype(jnp.bfloat16)


def embed_words(
    char_ids, char_table, conv_weight, proj_weight, gate_weight, trans_weight, gate_bias
):
    features = char_features(char_ids, char_table, conv_weight)
    current = jnp.dot(features, proj_weight, preferred_element_type=jnp.float32).astype(
        jnp.bfloat16
    )
    for layer_idx in range(gate_weight.shape[0]):
        opened = jax.nn.sigmoid(
            jnp.dot(current, gate_weight[layer_idx], preferred_element_type=jnp.float32)
            + gate_bias[layer_idx]
        )
        carried = jax.nn.relu(
            jnp.dot(current, trans_weight[layer_idx], preferred_element_type=jnp.float32)
        )
        current = (opened * carried + (1.0 - opened) * current.astype(jnp.float32)).astype(
            jnp.bfloat16
        )
    return current


def embed_all(char_ids, char_table, conv_weight, proj_weight, gate_weight, trans_weight, gate_bias):
    num_total = char_ids.shape[0]
    block_size = math.gcd(num_total, 128)
    grouped = char_ids.reshape(num_total // block_size, block_size, char_ids.shape[1])

    def one_block(piece_ids):
        return embed_words(
            piece_ids, char_table, conv_weight, proj_weight, gate_weight, trans_weight, gate_bias
        )

    return lax.map(one_block, grouped).reshape(num_total, proj_weight.shape[1])


def pick_targets(word_panel, row_spot):
    count_words = word_panel.shape[0]
    inside = (row_spot >= 0) & (row_spot < count_words)
    picked = jnp.take(word_panel, jnp.clip(row_spot, 0, count_words - 1), axis=0).astype(
        jnp.float32
    )
    return jnp.where(inside[:, None], picked, jnp.zeros_like(picked))


def fold_panel(acc_state, row_block, row_spot, word_panel):
    run_max, run_total, weighted, target_vec = acc_state
    scores = lax.dot_general(
        row_block, word_panel, (((1,), (1,)), ((), ())), preferred_element_type=jnp.float32
    )
    new_max = jnp.maximum(run_max, jnp.max(scores, axis=1))
    rescale = jnp.exp(run_max - new_max)
    soft_weights = jnp.exp(scores - new_max[:, None]).astype(jnp.bfloat16)
    run_total = run_total * rescale + jnp.sum(soft_weights.astype(jnp.float32), axis=1)
    weighted = weighted * rescale[:, None] + jnp.dot(
        soft_weights, word_panel, preferred_element_type=jnp.float32
    )
    target_vec = target_vec + pick_targets(word_panel, row_spot)
    return (new_max, run_total, weighted, target_vec)


def finish_rows(hidden, run_max, run_total, weighted, target_vec):
    target_score = jnp.sum(hidden.astype(jnp.float32) * target_vec, axis=1)
    row_loss = run_max + jnp.log(run_total) - target_score
    hidden_grad = (weighted / run_total[:, None] - target_vec).astype(jnp.bfloat16)
    return (row_loss, hidden_grad)


def per_device(
    char_ids,
    char_table,
    conv_weight,
    proj_weight,
    gate_weight,
    trans_weight,
    gate_bias,
    hidden,
    targets,
):
    embeds = embed_all(
        char_ids, char_table, conv_weight, proj_weight, gate_weight, trans_weight, gate_bias
    )
    local_words = embeds.shape[0]
    my_rows = hidden.shape[0]
    model_dim = hidden.shape[1]
    blocks = lax.axis_size("blk")
    group_idx = lax.axis_index("blk")
    word_panel = lax.all_gather(embeds, "vocab", axis=0, tiled=True)
    group_hidden = lax.all_gather(hidden, "blk", axis=0, tiled=True)
    group_goal = lax.all_gather(targets, "blk", axis=0, tiled=True)
    owner_dev = group_goal // local_words
    in_group = owner_dev % blocks == group_idx
    spot_all = jnp.where(in_group, owner_dev // blocks * local_words + group_goal % local_words, -1)
    running = (
        jnp.full((my_rows,), -jnp.inf, jnp.float32),
        jnp.zeros((my_rows,), jnp.float32),
        jnp.zeros((my_rows, model_dim), jnp.float32),
        jnp.zeros((my_rows, model_dim), jnp.float32),
    )
    for step_idx in range(blocks):
        which_block = (group_idx - step_idx) % blocks
        row_block = lax.dynamic_slice_in_dim(group_hidden, which_block * my_rows, my_rows, 0)
        row_spot = lax.dynamic_slice_in_dim(spot_all, which_block * my_rows, my_rows, 0)
        running = fold_panel(running, row_block, row_spot, word_panel)
        running = shifted((running[0], running[1], running[2], running[3]), "blk", 1)
    run_max, run_total, weighted, target_vec = running
    return finish_rows(hidden, run_max, run_total, weighted, target_vec)


def solution(mesh):
    return jax.shard_map(
        per_device,
        mesh=mesh,
        in_specs=(
            P(("vocab", "blk"), None),
            P(),
            P(),
            P(),
            P(),
            P(),
            P(),
            P(("vocab", "blk"), None),
            P(("vocab", "blk")),
        ),
        out_specs=(P(("vocab", "blk")), P(("vocab", "blk"), None)),
        check_vma=False,
    )
```

profile of v0, /device:TPU:0, one launch (start us, length us, event | category | flops | bytes accessed | tf_op | source)
XLA Modules:
  0.0 273.5 jit_solution(3712595097836582395)
XLA Ops:
  8.3 100.8 %while.13 = (s32[]{:T(128)}, bf16[4,128,1024]{2,1,0:T(8,128)(2,1)}, s32[4,128,50]{2,1,0:T(8,128)S(1)}, bf16[256,16]{0,1:T(8,128)(2,1)}, bf16[112,896]{1,0:T(8,12...) while((s32[]{:T(128)}, bf16[4,128,1024]{2,1,0:T(8,128)(2,1)}, ...), condition=%wide.region_2.3_spmd, body=%wide.region_0.2_spmd.sunk | while | flops 2662044928 | bytes 67010176 | solution.py:78
  8.5 4.2 %convolution_convert_fusion.4 = bf16[6400,16]{0,1:T(8,128)(2,1)S(1)} fusion(bf16[256,16]{0,1:T(8,128)(2,1)} %get-tuple-element.308, s32[6400]{0:T(1024)S(1)} %eq.53), kind=kOutput, calls=%fused_computation.5.clone.1 | convolution fusion | flops 54169600 | bytes 238592 | tf_op jit(solution)/shard_map/while/body/eval_jaxpr/dot_general | solution.py:24
  24.2 4.8 %select_reduce_fusion.2 = f32[128,896]{1,0:T(8,128)S(1)} fusion(pred[50,896]{1,0:T(8,128)(4,1)S(1)} %iota_compare_fusion.6, bf16[128,50,112]{0,2,1:T(8,128)(2,1)} %constant_dynamic-update-slice_fusion.20, bf16[112,896]{1,0:T(8,128)(2,1)S(1)} %copy-done.9, s32[896]{0:T(1024)S(1)} %fusion.150, s32[112]{0:T(128)S(1)} %and_select_fusion.6), kind=kOutput, calls=%fused_computation.4.clone.1 | convolution fusion | flops 1296060416 | bytes 2141888 | tf_op jit(solution)/shard_map/while/body/eval_jaxpr/dot_general | solution.py:35
  33.7 4.2 %convolution_convert_fusion.4 = bf16[6400,16]{0,1:T(8,128)(2,1)S(1)} fusion(bf16[256,16]{0,1:T(8,128)(2,1)} %get-tuple-element.308, s32[6400]{0:T(1024)S(1)} %eq.53), kind=kOutput, calls=%fused_computation.5.clone.1 | convolution fusion | flops 54169600 | bytes 238592 | tf_op jit(solution)/shard_map/while/body/eval_jaxpr/dot_general | solution.py:24
  49.4 4.8 %select_reduce_fusion.2 = f32[128,896]{1,0:T(8,128)S(1)} fusion(pred[50,896]{1,0:T(8,128)(4,1)S(1)} %iota_compare_fusion.6, bf16[128,50,112]{0,2,1:T(8,128)(2,1)} %constant_dynamic-update-slice_fusion.20, bf16[112,896]{1,0:T(8,128)(2,1)S(1)} %copy-done.9, s32[896]{0:T(1024)S(1)} %fusion.150, s32[112]{0:T(128)S(1)} %and_select_fusion.6), kind=kOutput, calls=%fused_computation.4.clone.1 | convolution fusion | flops 1296060416 | bytes 2141888 | tf_op jit(solution)/shard_map/while/body/eval_jaxpr/dot_general | solution.py:35
  58.9 4.2 %convolution_convert_fusion.4 = bf16[6400,16]{0,1:T(8,128)(2,1)S(1)} fusion(bf16[256,16]{0,1:T(8,128)(2,1)} %get-tuple-element.308, s32[6400]{0:T(1024)S(1)} %eq.53), kind=kOutput, calls=%fused_computation.5.clone.1 | convolution fusion | flops 54169600 | bytes 238592 | tf_op jit(solution)/shard_map/while/body/eval_jaxpr/dot_general | solution.py:24
  74.6 4.8 %select_reduce_fusion.2 = f32[128,896]{1,0:T(8,128)S(1)} fusion(pred[50,896]{1,0:T(8,128)(4,1)S(1)} %iota_compare_fusion.6, bf16[128,50,112]{0,2,1:T(8,128)(2,1)} %constant_dynamic-update-slice_fusion.20, bf16[112,896]{1,0:T(8,128)(2,1)S(1)} %copy-done.9, s32[896]{0:T(1024)S(1)} %fusion.150, s32[112]{0:T(128)S(1)} %and_select_fusion.6), kind=kOutput, calls=%fused_computation.4.clone.1 | convolution fusion | flops 1296060416 | bytes 2141888 | tf_op jit(solution)/shard_map/while/body/eval_jaxpr/dot_general | solution.py:35
  84.1 4.2 %convolution_convert_fusion.4 = bf16[6400,16]{0,1:T(8,128)(2,1)S(1)} fusion(bf16[256,16]{0,1:T(8,128)(2,1)} %get-tuple-element.308, s32[6400]{0:T(1024)S(1)} %eq.53), kind=kOutput, calls=%fused_computation.5.clone.1 | convolution fusion | flops 54169600 | bytes 238592 | tf_op jit(solution)/shard_map/while/body/eval_jaxpr/dot_general | solution.py:24
  99.8 4.8 %select_reduce_fusion.2 = f32[128,896]{1,0:T(8,128)S(1)} fusion(pred[50,896]{1,0:T(8,128)(4,1)S(1)} %iota_compare_fusion.6, bf16[128,50,112]{0,2,1:T(8,128)(2,1)} %constant_dynamic-update-slice_fusion.20, bf16[112,896]{1,0:T(8,128)(2,1)S(1)} %copy-done.9, s32[896]{0:T(1024)S(1)} %fusion.150, s32[112]{0:T(128)S(1)} %and_select_fusion.6), kind=kOutput, calls=%fused_computation.4.clone.1 | convolution fusion | flops 1296060416 | bytes 2141888 | tf_op jit(solution)/shard_map/while/body/eval_jaxpr/dot_general | solution.py:35
  110.7 9.9 %all-reduce.1 = s32[256]{0:T(256)S(1)} all-reduce(s32[256]{0:T(256)S(1)} %dynamic-update-slice), channel_id=1, replica_groups=mesh['vocab'=8,'blk'=4] {'blk'}, use_global_device_ids=true, to_apply=%add.1 | all-reduce | flops 256 | bytes 2048
  121.3 15.9 %all_gather.9 = bf16[256,1024]{1,0:T(8,128)(2,1)S(1)} all-gather(bf16[64,1024]{1,0:T(8,128)(2,1)} %param.20), channel_id=1, replica_groups=mesh['vocab'=8,'blk'=4] {'blk'}, dimensions={0}, use_global_device_ids=true | all-gather | bytes 655360 | tf_op jit(solution)/shard_map/all_gather | solution.py:133
  137.3 29.1 %all-gather.2.cloned.1.call-done = bf16[4096,1024]{1,0:T(8,128)(2,1)} async-done(((bf16[512,1024]{1,0:T(8,128)(2,1)}), bf16[4096,1024]{1,0:T(8,128)(2,1)}) %all-gather.2.cloned.1.call-update) | async-done | bytes 8388624 | tf_op jit(solution)/shard_map/all_gather | solution.py:132
  166.3 5.3 %gather_fusion = bf16[64,1024]{1,0:T(8,128)(2,1)S(1)} fusion(bf16[4096,1024]{1,0:T(8,128)(2,1)} %all-gather.2.cloned.1.call-done, s32[1024]{0:T(1024)S(1)} %pad_clamp_fusion.3), kind=kCustom, calls=%fused_computation.clone | custom fusion | bytes 262400 | tf_op jit(solution)/shard_map/jit(_take)/gather | solution.py:84
  173.9 6.7 %fusion.101 = (f32[64]{0:T(128)S(1)}, f32[64,4096]{1,0:T(8,128)S(1)}) fusion(bf16[4096,1024]{1,0:T(8,128)(2,1)} %all-gather.2.cloned.1.call-done, bf16[256,1024]{1,0:T(8,128)(2,1)S(1)} %all_gather.9, s32[]{:T(128)S(6)} %select_n.128), kind=kOutput, calls=%fused_computation.147 | convolution fusion | flops 537132992 | bytes 9568516 | tf_op jit(solution)/shard_map/dot_general | solution.py:92
  187.1 3.3 %fusion.102 = (f32[64]{0:T(128)}, f32[64,4096]{1,0:T(8,128)S(1)}) fusion(bf16[4096,1024]{1,0:T(8,128)(2,1)S(1)} %copy-done, bf16[256,1024]{1,0:T(8,128)(2,1)S(1)} %all_gather.9, s32[]{:T(128)S(6)} %select_n.130), kind=kOutput, calls=%fused_computation.148 | convolution fusion | flops 537132992 | bytes 9568516 | tf_op jit(solution)/shard_map/dot_general | solution.py:92
  193.6 4.2 %fusion.104 = (f32[64]{0:T(128)}, f32[64,4096]{1,0:T(8,128)S(1)}) fusion(bf16[4096,1024]{1,0:T(8,128)(2,1)S(1)} %copy-done, bf16[256,1024]{1,0:T(8,128)(2,1)} %copy-done.2, s32[]{:T(128)S(6)} %select_n.134), kind=kOutput, calls=%fused_computation.150 | convolution fusion | flops 537132992 | bytes 9568516 | tf_op jit(solution)/shard_map/dot_general | solution.py:92
  197.8 5.3 %gather_fusion.1 = bf16[64,1024]{1,0:T(8,128)(2,1)S(1)} fusion(bf16[4096,1024]{1,0:T(8,128)(2,1)} %all-gather.2.cloned.1.call-done, s32[1024]{0:T(1024)S(1)} %pad_clamp_fusion.2), kind=kCustom, calls=%fused_computation.1.clone | custom fusion | bytes 262400 | tf_op jit(solution)/shard_map/jit(_take)/gather | solution.py:84
  203.0 5.3 %gather_fusion.2 = bf16[64,1024]{1,0:T(8,128)(2,1)S(1)} fusion(bf16[4096,1024]{1,0:T(8,128)(2,1)} %all-gather.2.cloned.1.call-done, s32[1024]{0:T(1024)S(1)} %pad_clamp_fusion.1), kind=kCustom, calls=%fused_computation.2.clone | custom fusion | bytes 262400 | tf_op jit(solution)/shard_map/jit(_take)/gather | solution.py:84
  208.3 5.3 %gather_fusion.3 = bf16[64,1024]{1,0:T(8,128)(2,1)S(1)} fusion(bf16[4096,1024]{1,0:T(8,128)(2,1)} %all-gather.2.cloned.1.call-done, s32[1024]{0:T(1024)S(1)} %pad_clamp_fusion), kind=kCustom, calls=%fused_computation.3.clone | custom fusion | bytes 262400 | tf_op jit(solution)/shard_map/jit(_take)/gather | solution.py:84
  227.5 5.2 %multiply_add_fusion.2 = f32[64,1024]{1,0:T(8,128)S(1)} fusion(f32[64,1024]{1,0:T(8,128)} %collective-permute-done.12, f32[64]{0:T(128)S(1)} %get-tuple-element.173, bf16[4096,1024]{1,0:T(8,128)(2,1)} %all-gather.2.cloned.1.call-done, f32[64,4096]{1,0:T(8,128)S(1)} %get-tuple-element.209, f32[64]{0:T(128)S(1)} %max.43), kind=kOutput, calls=%fused_computation.88 | convolution fusion | flops 537526272 | bytes 9961984 | tf_op jit(solution)/shard_map/dot_general | solution.py:99
  233.0 4.1 %collective-permute-done.9 = f32[64,1024]{1,0:T(8,128)S(1)} collective-permute-done((f32[64,1024]{1,0:T(8,128)S(1)}, f32[64,1024]{1,0:T(8,128)S(1)}, u32[]{:S(2)}, u32[]{:S(2)}) %collective-permute-start.9) | collective-permute-done | bytes 262176 | tf_op jit(solution)/shard_map/ppermute | solution.py:11
  237.3 6.5 %collective-permute-done.13 = f32[64,1024]{1,0:T(8,128)S(1)} collective-permute-done((f32[64,1024]{1,0:T(8,128)S(1)}, f32[64,1024]{1,0:T(8,128)S(1)}, u32[]{:S(2)}, u32[]{:S(2)}) %collective-permute-start.13) | collective-permute-done | bytes 262176 | tf_op jit(solution)/shard_map/ppermute | solution.py:11
  248.8 6.4 %collective-permute-done.14 = f32[64,1024]{1,0:T(8,128)S(1)} collective-permute-done((f32[64,1024]{1,0:T(8,128)S(1)}, f32[64,1024]{1,0:T(8,128)S(1)}, u32[]{:S(2)}, u32[]{:S(2)}) %collective-permute-start.14) | collective-permute-done | bytes 262176 | tf_op jit(solution)/shard_map/ppermute | solution.py:11
  259.7 5.6 %collective-permute-done.7 = f32[64]{0:T(128)S(1)} collective-permute-done((f32[64]{0:T(128)S(1)}, f32[64]{0:T(128)S(1)}, u32[]{:S(2)}, u32[]{:S(2)}) %collective-permute-start.7) | collective-permute-done | bytes 288 | tf_op jit(solution)/shard_map/ppermute | solution.py:11
  (233 shorter events, 104.1 us)
Async XLA Ops:
  7.2 159.2 %all-gather.2.cloned.1.call-start = ((), (), s32[]{:S(2)}) async-start(), calls=%async_computation | async-start | bytes 9437184 | tf_op jit(solution)/shard_map/all_gather | solution.py:132
  8.2 100.9 %copy-start.11 = (u32[32]{0:T(128)S(1)}, u32[32]{0:T(128)}, u32[]{:S(2)}) copy-start(u32[32]{0:T(128)} %constant.224) | copy-start | bytes 388
  8.3 102.2 %copy-start.10 = (s32[64]{0:T(128)S(1)}, s32[64]{0:T(128)}, u32[]{:S(2)}) copy-start(s32[64]{0:T(128)} %param.21) | copy-start | bytes 772
  137.3 53.1 %copy-start.2 = (bf16[256,1024]{1,0:T(8,128)(2,1)}, bf16[256,1024]{1,0:T(8,128)(2,1)S(1)}, u32[]{:S(2)}) copy-start(bf16[256,1024]{1,0:T(8,128)(2,1)S(1)} %all_gather.9) | copy-start | bytes 1572868
  172.4 10.7 %copy-start = (bf16[4096,1024]{1,0:T(8,128)(2,1)S(1)}, bf16[4096,1024]{1,0:T(8,128)(2,1)}, u32[]{:S(2)}) copy-start(bf16[4096,1024]{1,0:T(8,128)(2,1)} %all-gather.2.cloned.1.call-done) | copy-start | bytes 25165828
  172.4 53.7 %collective-permute-start.8 = (f32[64,1024]{1,0:T(8,128)}, f32[64,1024]{1,0:T(8,128)}, u32[]{:S(2)}, u32[]{:S(2)}) collective-permute-start(f32[64,1024]{1,0:T(8,128)} %convert_select_fusion), channel_id=1, source_target_pairs={{0,1},{1,2},{2,3},{3,0},{4,5},{5,6},{6,7},{7,4},{8,9},{9,10},{10,1... | collective-permute-start | bytes 786440 | tf_op jit(solution)/shard_map/ppermute | solution.py:11
  180.6 32.9 %collective-permute-start = (f32[64]{0:T(128)S(1)}, f32[64]{0:T(128)}, u32[]{:S(2)}, u32[]{:S(2)}) collective-permute-start(f32[64]{0:T(128)S(1)} %get-tuple-element.206), channel_id=1, source_target_pairs={{0,1},{1,2},{2,3},{3,0},{4,5},{5,6},{6,7},{7,4},{8,9},{9,10},{10,1... | collective-permute-start | bytes 776 | tf_op jit(solution)/shard_map/ppermute | solution.py:11
  185.5 41.9 %collective-permute-start.12 = (f32[64,1024]{1,0:T(8,128)}, f32[64,1024]{1,0:T(8,128)}, u32[]{:S(2)}, u32[]{:S(2)}) collective-permute-start(f32[64,1024]{1,0:T(8,128)} %convolution_add_fusion), channel_id=1, source_target_pairs={{0,1},{1,2},{2,3},{3,0},{4,5},{5,6},{6,7},{7,4},{8,9},{9,10},{10,1... | collective-permute-start | bytes 786440 | tf_op jit(solution)/shard_map/ppermute | solution.py:11
  187.0 29.4 %collective-permute-start.4 = (f32[64]{0:T(128)}, f32[64]{0:T(128)}, u32[]{:S(2)}, u32[]{:S(2)}) collective-permute-start(f32[64]{0:T(128)} %get-tuple-element.205), channel_id=1, source_target_pairs={{0,1},{1,2},{2,3},{3,0},{4,5},{5,6},{6,7},{7,4},{8,9},{9,10},{10,1... | collective-permute-start | bytes 776 | tf_op jit(solution)/shard_map/ppermute | solution.py:11
  214.2 5.3 %collective-permute-start.1 = (f32[64]{0:T(128)S(1)}, f32[64]{0:T(128)S(1)}, u32[]{:S(2)}, u32[]{:S(2)}) collective-permute-start(f32[64]{0:T(128)S(1)} %max.43), channel_id=1, source_target_pairs={{0,1},{1,2},{2,3},{3,0},{4,5},{5,6},{6,7},{7,4},{8,9},{9,10},{10,1... | collective-permute-start | bytes 776 | tf_op jit(solution)/shard_map/ppermute | solution.py:11
  217.0 5.3 %collective-permute-start.5 = (f32[64]{0:T(128)S(1)}, f32[64]{0:T(128)S(1)}, u32[]{:S(2)}, u32[]{:S(2)}) collective-permute-start(f32[64]{0:T(128)S(1)} %get-tuple-element.172), channel_id=1, source_target_pairs={{0,1},{1,2},{2,3},{3,0},{4,5},{5,6},{6,7},{7,4},{8,9},{9,10},{10,1... | collective-permute-start | bytes 776 | tf_op jit(solution)/shard_map/ppermute | solution.py:11
  220.2 5.3 %collective-permute-start.2 = (f32[64]{0:T(128)S(1)}, f32[64]{0:T(128)S(1)}, u32[]{:S(2)}, u32[]{:S(2)}) collective-permute-start(f32[64]{0:T(128)S(1)} %max.44), channel_id=1, source_target_pairs={{0,1},{1,2},{2,3},{3,0},{4,5},{5,6},{6,7},{7,4},{8,9},{9,10},{10,1... | collective-permute-start | bytes 776 | tf_op jit(solution)/shard_map/ppermute | solution.py:11
  220.6 23.1 %slice-start = ((s8[8388608]{0:T(1024)(128)(4,1)}), s8[4194304]{0:T(1024)(128)(4,1)S(1)}, s32[]{:S(2)}) async-start(s8[8388608]{0:T(1024)(128)(4,1)} %bitcast.111), calls=%async_computation.1 | async-start | bytes 8388608
  222.4 23.1 %collective-permute-start.6 = (f32[64]{0:T(128)S(1)}, f32[64]{0:T(128)S(1)}, u32[]{:S(2)}, u32[]{:S(2)}) collective-permute-start(f32[64]{0:T(128)S(1)} %get-tuple-element.170), channel_id=1, source_target_pairs={{0,1},{1,2},{2,3},{3,0},{4,5},{5,6},{6,7},{7,4},{8,9},{9,10},{10,1... | collective-permute-start | bytes 776 | tf_op jit(solution)/shard_map/ppermute | solution.py:11
  227.1 10.0 %collective-permute-start.9 = (f32[64,1024]{1,0:T(8,128)S(1)}, f32[64,1024]{1,0:T(8,128)S(1)}, u32[]{:S(2)}, u32[]{:S(2)}) collective-permute-start(f32[64,1024]{1,0:T(8,128)S(1)} %select_add_fusion.2), channel_id=1, source_target_pairs={{0,1},{1,2},{2,3},{3,0},{4,5},{5,6},{6,7},{7,4},{8,9},{9,10},{10,1... | collective-permute-start | bytes 786440 | tf_op jit(solution)/shard_map/ppermute | solution.py:11
  227.5 16.3 %slice-start.1 = ((s8[8388608]{0:T(1024)(128)(4,1)}), s8[4194304]{0:T(1024)(128)(4,1)S(1)}, s32[]{:S(2)}) async-start(s8[8388608]{0:T(1024)(128)(4,1)} %bitcast.111), calls=%async_computation.2 | async-start | bytes 8388608
  232.6 11.1 %collective-permute-start.13 = (f32[64,1024]{1,0:T(8,128)S(1)}, f32[64,1024]{1,0:T(8,128)S(1)}, u32[]{:S(2)}, u32[]{:S(2)}) collective-permute-start(f32[64,1024]{1,0:T(8,128)S(1)} %multiply_add_fusion.2), channel_id=1, source_target_pairs={{0,1},{1,2},{2,3},{3,0},{4,5},{5,6},{6,7},{7,4},{8,9},{9,10},{10,1... | collective-permute-start | bytes 786440 | tf_op jit(solution)/shard_map/ppermute | solution.py:11
  237.2 11.4 %collective-permute-start.10 = (f32[64,1024]{1,0:T(8,128)S(1)}, f32[64,1024]{1,0:T(8,128)S(1)}, u32[]{:S(2)}, u32[]{:S(2)}) collective-permute-start(f32[64,1024]{1,0:T(8,128)S(1)} %select_add_fusion.1), channel_id=1, source_target_pairs={{0,1},{1,2},{2,3},{3,0},{4,5},{5,6},{6,7},{7,4},{8,9},{9,10},{10,1... | collective-permute-start | bytes 786440 | tf_op jit(solution)/shard_map/ppermute | solution.py:11
  245.4 9.8 %collective-permute-start.14 = (f32[64,1024]{1,0:T(8,128)S(1)}, f32[64,1024]{1,0:T(8,128)S(1)}, u32[]{:S(2)}, u32[]{:S(2)}) collective-permute-start(f32[64,1024]{1,0:T(8,128)S(1)} %multiply_add_fusion.1), channel_id=1, source_target_pairs={{0,1},{1,2},{2,3},{3,0},{4,5},{5,6},{6,7},{7,4},{8,9},{9,10},{10,1... | collective-permute-start | bytes 786440 | tf_op jit(solution)/shard_map/ppermute | solution.py:11
  248.7 16.5 %collective-permute-start.11 = (f32[64,1024]{1,0:T(8,128)S(1)}, f32[64,1024]{1,0:T(8,128)S(1)}, u32[]{:S(2)}, u32[]{:S(2)}) collective-permute-start(f32[64,1024]{1,0:T(8,128)S(1)} %select_add_fusion), channel_id=1, source_target_pairs={{0,1},{1,2},{2,3},{3,0},{4,5},{5,6},{6,7},{7,4},{8,9},{9,10},{10,1... | collective-permute-start | bytes 786440 | tf_op jit(solution)/shard_map/ppermute | solution.py:11
  255.2 10.0 %copy-start.3 = (bf16[64,1024]{1,0:T(8,128)(2,1)S(1)}, bf16[64,1024]{1,0:T(8,128)(2,1)}, u32[]{:S(2)}) copy-start(bf16[64,1024]{1,0:T(8,128)(2,1)} %param.20) | copy-start | bytes 393220
  256.9 8.3 %collective-permute-start.15 = (f32[64,1024]{1,0:T(8,128)S(1)}, f32[64,1024]{1,0:T(8,128)S(1)}, u32[]{:S(2)}, u32[]{:S(2)}) collective-permute-start(f32[64,1024]{1,0:T(8,128)S(1)} %multiply_add_fusion), channel_id=1, source_target_pairs={{0,1},{1,2},{2,3},{3,0},{4,5},{5,6},{6,7},{7,4},{8,9},{9,10},{10,1... | collective-permute-start | bytes 786440 | tf_op jit(solution)/shard_map/ppermute | solution.py:11
  257.0 8.2 %collective-permute-start.7 = (f32[64]{0:T(128)S(1)}, f32[64]{0:T(128)S(1)}, u32[]{:S(2)}, u32[]{:S(2)}) collective-permute-start(f32[64]{0:T(128)S(1)} %get-tuple-element.168), channel_id=1, source_target_pairs={{0,1},{1,2},{2,3},{3,0},{4,5},{5,6},{6,7},{7,4},{8,9},{9,10},{10,1... | collective-permute-start | bytes 776 | tf_op jit(solution)/shard_map/ppermute | solution.py:11
  257.2 8.9 %collective-permute-start.3 = (f32[64]{0:T(128)S(1)}, f32[64]{0:T(128)S(1)}, u32[]{:S(2)}, u32[]{:S(2)}) collective-permute-start(f32[64]{0:T(128)S(1)} %max.45), channel_id=1, source_target_pairs={{0,1},{1,2},{2,3},{3,0},{4,5},{5,6},{6,7},{7,4},{8,9},{9,10},{10,1... | collective-permute-start | bytes 776 | tf_op jit(solution)/shard_map/ppermute | solution.py:11
  (22 other events, 119.4 us)
Sparse Core Ops, SparseCore 0:
  109.2 57.0 all-gather.1
where the time goes:
time: 274 us; the launch traced here: 273 us
  matrix products  77.2 us (28%)
  local copies, waits for them, and re-layouts  74.1 us (27%)
  waiting for transfers between devices  60.3 us (22%)
  blocking collectives  25.8 us (9%)
  between operations  15.1 us (6%)
  starting transfers between devices  11.7 us (4%)
  other arithmetic  8.73 us (3%)
    ppermute x16, waiting for transfers between devices, shifted(): lax.ppermute(array, axis, [(i, (i + by) % count) for i in range(count)])  31.2 us
    all_gather x1, waiting for transfers between devices, per_device(): word_panel = lax.all_gather(embeds, 'vocab', axis=0, tiled=True)  29.1 us
    while x64, local copies, waits for them, and re-layouts  22.6 us
    gather x4, local copies, waits for them, and re-layouts, pick_targets(): jnp.take(word_panel, jnp.clip(row_spot, 0, count_words - 1), axis=0)  21 us
    dot_general x4, matrix products, char_features(): jnp.dot(windows.reshape(num_words * length, widths * embed_dim), masked,...  19.3 us
    slice x28, local copies, waits for them, and re-layouts, char_features(): padded[:, shift_at:shift_at + length, :]  17.8 us
    dot_general x4, matrix products, fold_panel(): lax.dot_general(row_block, word_panel, (((1,), (1,)), ((), ())), preferre...  17.4 us
    dot_general x4, matrix products, char_features(): jnp.dot(onehot.reshape(num_words * length, symbols), char_table, preferre...  16.7 us
  transfers between devices with their start and end apart: 17, of which 9 were waited for; matrix products, arithmetic and copies ran while one was open for 19% of the time, Pallas kernels for 0%

commit v1 on v0

v1 whole, which is shorter than its diff:
```python
import functools
import jax
import jax.numpy as jnp
from jax import lax
from jax.experimental import pallas as pl
from jax.experimental.pallas import tpu as pltpu
from jax.sharding import PartitionSpec as P

bf16=jnp.bfloat16; f32=jnp.float32
LANES=128; SPAN=8

def prep_toeplitz(conv_ref, toep, ce, widths, filters):
    depth = toep.shape[0]
    for k in range(widths):
        rows = (k + 1) * ce
        piece = conv_ref[0:rows, k * filters:(k + 1) * filters]
        for o in range(SPAN):
            cols = slice((k * SPAN + o) * filters, (k * SPAN + o + 1) * filters)
            if o:
                toep[0:o * ce, cols] = jnp.zeros((o * ce, filters), bf16)
            toep[o * ce:o * ce + rows, cols] = piece
            rest = depth - o * ce - rows
            if rest:
                toep[o * ce + rows:depth, cols] = jnp.zeros((rest, filters), bf16)

def lookup(ids_ref, tab_ref, vec, words, length, ce):
    per = LANES // ce
    for t in range(words // LANES):
        for g in range(vec.shape[1] // LANES):
            parts = []
            for q in range(per):
                p = g * per + q
                if p >= length:
                    parts.append(jnp.zeros((ce, LANES), f32)); continue
                idx = jnp.broadcast_to(ids_ref[p:p + 1, t * LANES:(t + 1) * LANES], (8, LANES))
                low = jnp.bitwise_and(idx, LANES - 1)
                top = idx >= LANES
                for h in range(ce // 8):
                    a = jnp.take_along_axis(tab_ref[h * 8:h * 8 + 8, 0:LANES], low, axis=1)
                    b = jnp.take_along_axis(tab_ref[h * 8:h * 8 + 8, LANES:2 * LANES], low, axis=1)
                    parts.append(jnp.where(top, b, a))
            block = jnp.concatenate(parts, axis=0)
            vec[t * LANES:(t + 1) * LANES, g * LANES:(g + 1) * LANES] = block.T.astype(bf16)

def conv_pool(vec, toep, acc, length, widths, filters):
    words = vec.shape[0]
    def tile(b, k, o, lhs):
        cols = slice((k * SPAN + o) * filters, (k * SPAN + o + 2) * filters)
        return jnp.dot(lhs, toep[:, cols], preferred_element_type=f32)
    acc[...] = jnp.full(acc.shape, -jnp.inf, f32)
    least = (length - widths + 1) // SPAN
    def body(b, _):
        lhs = vec[:, pl.ds(pl.multiple_of(b * LANES, LANES), 2 * LANES)]
        for k in range(widths):
            best = acc[:, k * filters:(k + 1) * filters]
            for o in range(0, SPAN, 2):
                r = tile(b, k, o, lhs)
                best = jnp.maximum(best, jnp.maximum(r[:, :filters], r[:, filters:]))
            acc[:, k * filters:(k + 1) * filters] = best
        return 0
    lax.fori_loop(0, least, body, 0)
    for b in range(least, -(-length // SPAN)):
        lhs = vec[:, b * LANES:(b + 2) * LANES]
        for k in range(widths):
            usable = min(SPAN, length - k - b * SPAN)
            if usable <= 0: continue
            best = acc[:, k * filters:(k + 1) * filters]
            for o in range(0, usable, 2):
                r = tile(b, k, o, lhs)
                best = jnp.maximum(best, r[:, :filters])
                if o + 1 < usable:
                    best = jnp.maximum(best, r[:, filters:])
            acc[:, k * filters:(k + 1) * filters] = best

def cnn_kernel(ids_ref, tab_ref, conv_ref, bias_ref, proj_hbm, gate_hbm, trans_hbm, *rest,
               widths, filters, ce, length, layers, nt, outs):
    out_refs, scratch = rest[:outs], rest[outs:]
    vec, toep, acc, feat, proj, gate, trans, state, last, sems = scratch
    copies = [pltpu.make_async_copy(s, d, sems.at[i]) for i, (s, d) in enumerate(
        ((proj_hbm, proj), (gate_hbm, gate), (trans_hbm, trans)))]
    for c in copies:
        c.start()
    words = ids_ref.shape[1]
    prep_toeplitz(conv_ref, toep, ce, widths, filters)
    lookup(ids_ref, tab_ref, vec, words, length, ce)
    conv_pool(vec, toep, acc, length, widths, filters)
    for c in copies:
        c.wait()
    feat[...] = jnp.tanh(acc[...]).astype(bf16)
    model = last.shape[1]
    for n in range(0, model, nt):
        state[:, n:n + nt] = jnp.dot(feat[...], proj[:, n:n + nt], preferred_element_type=f32).astype(bf16)
    for l in range(layers):
        for n in range(0, model, nt):
            cur = state[...]
            g = jnp.dot(cur, gate[l, :, n:n + nt], preferred_element_type=f32) + bias_ref[l:l + 1, n:n + nt]
            t = jnp.dot(cur, trans[l, :, n:n + nt], preferred_element_type=f32)
            opened = jax.nn.sigmoid(g)
            carried = jnp.maximum(t, 0.0)
            new = (opened * carried + (1.0 - opened) * state[:, n:n + nt].astype(f32)).astype(bf16)
            if l + 1 < layers:
                last[:, n:n + nt] = new
            else:
                at = 0
                for ref in out_refs:
                    ref[:, n:n + nt] = new[at:at + ref.shape[0], :]
                    at += ref.shape[0]
        if l + 1 < layers:
            state[...] = last[...]


ANY = pl.BlockSpec(memory_space=pl.ANY)
VM = pl.BlockSpec(memory_space=pltpu.VMEM)


def params(limit_mib=56):
    return pltpu.CompilerParams(vmem_limit_bytes=limit_mib << 20)


def embed(ids_t, sizes, tab_t, conv_weight, proj_weight, gate_weight, trans_weight, gate_bias, nt=256):
    length, words = ids_t.shape
    ce = tab_t.shape[0]
    widths = conv_weight.shape[0] // ce
    filters = conv_weight.shape[1] // widths
    layers, model, _ = gate_weight.shape
    flops = 2 * words * (length * 256 * widths * filters + widths * filters * model + 2 * layers * model * model)
    return pl.pallas_call(
        functools.partial(cnn_kernel, widths=widths, filters=filters, ce=ce, length=length, layers=layers, nt=nt,
                          outs=len(sizes)),
        out_shape=[jax.ShapeDtypeStruct((s, model), bf16) for s in sizes],
        in_specs=[VM, VM, VM, VM, ANY, ANY, ANY],
        out_specs=[VM] * len(sizes),
        scratch_shapes=[
            pltpu.VMEM((words, (-(-length // SPAN) + 1) * LANES), bf16),
            pltpu.VMEM((2 * LANES, widths * SPAN * filters), bf16),
            pltpu.VMEM((words, widths * filters), f32),
            pltpu.VMEM((words, widths * filters), bf16),
            pltpu.VMEM(proj_weight.shape, bf16),
            pltpu.VMEM(gate_weight.shape, bf16),
            pltpu.VMEM(trans_weight.shape, bf16),
            pltpu.VMEM((words, model), bf16),
            pltpu.VMEM((words, model), bf16),
            pltpu.SemaphoreType.DMA((3,)),
        ],
        compiler_params=params(),
        cost_estimate=pl.CostEstimate(flops=flops, bytes_accessed=12 << 20, transcendentals=words * 4096),
        name="embed",
    )(ids_t, tab_t, conv_weight, gate_bias, proj_weight, gate_weight, trans_weight)


def pick_kernel(spot_ref, ids_ref, out_ref):
    words = ids_ref.shape[1]
    rows = spot_ref.shape[1]
    at = lax.broadcasted_iota(jnp.int32, (words, rows), 0)
    hot = jnp.where(at == spot_ref[...], 1.0, 0.0).astype(bf16)
    out_ref[...] = jnp.dot(ids_ref[...], hot, preferred_element_type=f32).astype(bf16)


def pick(spot, ids):
    return pl.pallas_call(
        pick_kernel,
        out_shape=jax.ShapeDtypeStruct((ids.shape[0], spot.shape[1]), bf16),
        in_specs=[VM, VM], out_specs=VM, compiler_params=params(),
        cost_estimate=pl.CostEstimate(flops=2 * 256 * ids.shape[1] * spot.shape[1], bytes_accessed=1 << 20,
                                      transcendentals=0),
        name="pick",
    )(spot, ids)


def by_row(line, i):
    return jnp.broadcast_to(line[i:i + 1, :], (LANES, LANES)).T


def as_line(column):
    return jnp.broadcast_to(column, (LANES, LANES)).T[0:1, :]


def part_of_softmax(rows_ref, words, score, prob, out):
    at = 0
    top = None
    for ref in words:
        n = ref.shape[0]
        piece = lax.dot_general(rows_ref[...], ref[...], (((1,), (1,)), ((), ())), preferred_element_type=f32)
        score[:, at:at + n] = piece
        best = jnp.max(piece, axis=1, keepdims=True)
        top = best if top is None else jnp.maximum(top, best)
        at += n
    at = 0
    total = None
    for ref in words:
        n = ref.shape[0]
        w = jnp.exp(score[:, at:at + n] - top).astype(bf16)
        prob[:, at:at + n] = w
        s = jnp.sum(w.astype(f32), axis=1, keepdims=True)
        total = s if total is None else total + s
        at += n
    model = out.shape[1]
    for n in range(0, model, 256):
        at = 0
        res = None
        for ref in words:
            size = ref.shape[0]
            d = jnp.dot(prob[:, at:at + size], ref[:, n:n + 256], preferred_element_type=f32)
            res = d if res is None else res + d
            at += size
        out[:, n:n + 256] = res
    return top, total


def first_kernel(*refs, nh, nw):
    hid, words = refs[:nh], refs[nh:nh + nw]
    out, top_ref, total_ref, rows, score, prob = refs[nh + nw:]
    at = 0
    for h in hid:
        rows[at:at + h.shape[0], :] = h[...]
        at += h.shape[0]
    top, total = part_of_softmax(rows, words, score, prob, out)
    top_ref[...] = jnp.broadcast_to(top, top_ref.shape)
    total_ref[...] = jnp.broadcast_to(total, total_ref.shape)


def fold_cost(rows, words, model):
    return pl.CostEstimate(flops=4 * rows * words * model, bytes_accessed=2 * (rows + words) * model,
                           transcendentals=rows * words)


def first_fold(hid, words):
    model = hid[0].shape[1]
    rows = sum(h.shape[0] for h in hid)
    count = sum(w.shape[0] for w in words)
    return pl.pallas_call(
        functools.partial(first_kernel, nh=len(hid), nw=len(words)),
        out_shape=[jax.ShapeDtypeStruct((rows, model), f32), jax.ShapeDtypeStruct((rows, LANES), f32),
                   jax.ShapeDtypeStruct((rows, LANES), f32)],
        in_specs=[VM] * (len(hid) + len(words)), out_specs=[VM] * 3,
        scratch_shapes=[pltpu.VMEM((rows, model), bf16), pltpu.VMEM((rows, count), f32),
                        pltpu.VMEM((rows, count), bf16)],
        compiler_params=params(), cost_estimate=fold_cost(rows, count, model), name="first_fold",
    )(*hid, *words)


def second_kernel(*refs, nh, nw):
    hid, words = refs[:nh], refs[nh:nh + nw]
    old, top_ref, total_ref, a_keep, a_send, b_keep, b_send, lse, rows, score, prob, new = refs[nh + nw:]
    at = 0
    for h in hid:
        rows[at:at + h.shape[0], :] = h[...]
        at += h.shape[0]
    top2, total2 = part_of_softmax(rows, words, score, prob, new)
    top1, total1 = top_ref[:, 0:1], total_ref[:, 0:1]
    top = jnp.maximum(top1, top2)
    s1, s2 = jnp.exp(top1 - top), jnp.exp(top2 - top)
    total = s1 * total1 + s2 * total2
    s1, s2 = s1 / total, s2 / total
    whole = top + jnp.log(total)
    count, model = new.shape
    half, quarter = model // 2, count // 4
    for i in range(count // LANES):
        part = slice(i * LANES, (i + 1) * LANES)
        lse[i:i + 1, :] = as_line(whole[part, :])
    for q in range(4):
        part = slice(q * quarter, (q + 1) * quarter)
        mix = s1[part, :] * old[part, :] + s2[part, :] * new[part, :]
        mix = mix.astype(bf16)
        a = a_keep if q < 2 else a_send
        a[(q % 2) * quarter:(q % 2 + 1) * quarter, :] = mix[:, :half]
        b = b_keep if q % 2 == 0 else b_send
        b[(q // 2) * quarter:(q // 2 + 1) * quarter, :] = mix[:, half:]


def second_fold(hid, words, state):
    model = hid[0].shape[1]
    rows = sum(h.shape[0] for h in hid)
    count = sum(w.shape[0] for w in words)
    side = jax.ShapeDtypeStruct((rows // 2, model // 2), bf16)
    return pl.pallas_call(
        functools.partial(second_kernel, nh=len(hid), nw=len(words)),
        out_shape=[side] * 4 + [jax.ShapeDtypeStruct((rows // LANES, LANES), f32)],
        in_specs=[VM] * (len(hid) + len(words) + 3), out_specs=[VM] * 5,
        scratch_shapes=[pltpu.VMEM((rows, model), bf16), pltpu.VMEM((rows, count), f32),
                        pltpu.VMEM((rows, count), bf16), pltpu.VMEM((rows, model), f32)],
        compiler_params=params(), cost_estimate=fold_cost(rows, count, model), name="second_fold",
    )(*hid, *words, *state)


def join(one, two):
    top = jnp.maximum(one, two)
    s1, s2 = jnp.exp(one - top), jnp.exp(two - top)
    total = s1 + s2
    return s1 / total, s2 / total, top + jnp.log(total)


def mix_rows(mine, other, s1, s2):
    parts = []
    for n in range(0, mine.shape[1], LANES):
        parts.append(s1 * mine[:, n:n + LANES].astype(f32) + s2 * other[:, n:n + LANES].astype(f32))
    return jnp.concatenate(parts, axis=1)


def merge_one_kernel(a_keep, a_got, b_keep, b_got, lse, a_lse, b_lse,
                     a_keep2, a_send2, b_keep2, b_send2, a_line, b_line):
    lines = lse.shape[0]
    per = lines // 4
    for keep, got, got_lse, outs, line, mine_q, their_q in (
            (a_keep, a_got, a_lse, (a_keep2, a_send2), a_line, (0, 1), (2, 3)),
            (b_keep, b_got, b_lse, (b_keep2, b_send2), b_line, (0, 2), (1, 3))):
        for j in range(2):
            for i in range(per):
                mi, ti = mine_q[j] * per + i, their_q[j] * per + i
                w1, w2, _ = join(by_row(lse, mi), by_row(got_lse, ti))
                row = slice((j * per + i) * LANES, (j * per + i + 1) * LANES)
                outs[j][i * LANES:(i + 1) * LANES, :] = mix_rows(keep[row, :], got[row, :], w1, w2).astype(bf16)
                line[j * per + i:j * per + i + 1, :] = join(lse[mi:mi + 1, :], got_lse[ti:ti + 1, :])[2]


def merge_one(a_keep, a_got, b_keep, b_got, lse, a_lse, b_lse):
    rows, half = a_keep.shape
    side = jax.ShapeDtypeStruct((rows // 2, half), bf16)
    line = jax.ShapeDtypeStruct((lse.shape[0] // 2, LANES), f32)
    return pl.pallas_call(
        merge_one_kernel, out_shape=[side] * 4 + [line] * 2,
        in_specs=[VM] * 7, out_specs=[VM] * 6, compiler_params=params(),
        cost_estimate=pl.CostEstimate(flops=4 * rows * half, bytes_accessed=12 * rows * half, transcendentals=0),
        name="merge_one",
    )(a_keep, a_got, b_keep, b_got, lse, a_lse, b_lse)


def merge_two_kernel(a_keep, a_got, b_keep, b_got, a_line, b_line, a_lse, b_lse, keep2, send2, lines):
    per = a_line.shape[0] // 2
    rows, half = a_keep.shape
    for c, (keep, got, line, got_line) in enumerate(
            ((a_keep, a_got, a_line, a_lse), (b_keep, b_got, b_line, b_lse))):
        for i in range(per):
            w1, w2, _ = join(by_row(line, i), by_row(got_line, per + i))
            row = slice(i * LANES, (i + 1) * LANES)
            out = mix_rows(keep[row, :], got[row, :], w1, w2).astype(bf16)
            cols = slice(c * half, (c + 1) * half)
            for at in range(0, LANES, LANES // 2):
                to = i * LANES + at
                ref = keep2 if to < rows // 2 else send2
                to = to if to < rows // 2 else to - rows // 2
                ref[to:to + LANES // 2, cols] = out[at:at + LANES // 2, :]
            lines[c * per + i:c * per + i + 1, :] = join(line[i:i + 1, :], got_line[per + i:per + i + 1, :])[2]


def merge_two(a_keep, a_got, b_keep, b_got, a_line, b_line, a_lse, b_lse):
    rows, half = a_keep.shape
    side = jax.ShapeDtypeStruct((rows // 2, 2 * half), bf16)
    return pl.pallas_call(
        merge_two_kernel, out_shape=[side] * 2 + [jax.ShapeDtypeStruct(a_line.shape, f32)],
        in_specs=[VM] * 8, out_specs=[VM] * 3, compiler_params=params(),
        cost_estimate=pl.CostEstimate(flops=8 * rows * half, bytes_accessed=12 * rows * half, transcendentals=0),
        name="merge_two",
    )(a_keep, a_got, b_keep, b_got, a_line, b_line, a_lse, b_lse)


def finish_kernel(keep, got, lines, got_lines, hid, target, loss, grad):
    rows, model = keep.shape
    for c in range(2):
        mine = lines[c:c + 1, :]
        other = pltpu.roll(got_lines[c:c + 1, :], LANES // 2, axis=1)
        w1, w2, whole = join(by_row(mine, 0), by_row(other, 0))
        cols = slice(c * model // 2, (c + 1) * model // 2)
        out = mix_rows(keep[:, cols], got[:, cols], w1[:rows], w2[:rows])
        grad[:, cols] = (out - target[:, cols].astype(f32)).astype(bf16)
        if c == 0:
            lse = whole[:rows, 0:1]
    aim = jnp.sum(hid[...].astype(f32) * target[...].astype(f32), axis=1, keepdims=True)
    column = jnp.concatenate([lse - aim, jnp.zeros((LANES - rows, 1), f32)], axis=0)
    loss[...] = as_line(column)


def finish(keep, got, lines, got_lines, hid, target):
    rows, model = keep.shape
    return pl.pallas_call(
        finish_kernel,
        out_shape=[jax.ShapeDtypeStruct((1, LANES), f32), jax.ShapeDtypeStruct((rows, model), bf16)],
        in_specs=[VM] * 6, out_specs=[VM] * 2, compiler_params=params(),
        cost_estimate=pl.CostEstimate(flops=8 * rows * model, bytes_accessed=12 * rows * model, transcendentals=0),
        name="finish",
    )(keep, got, lines, got_lines, hid, target)


def halve_kernel(keep, got, lines, got_lines, keep2, send2, lines2):
    rows, model = keep.shape
    per = lines.shape[0] // 2
    near = per // 2
    for c in range(2):
        cols = slice(c * model // 2, (c + 1) * model // 2)
        for i in range(near):
            mine, other = c * per + i, c * per + near + i
            w1, w2, _ = join(by_row(lines, mine), by_row(got_lines, other))
            row = slice(i * LANES, (i + 1) * LANES)
            out = mix_rows(keep[row, cols], got[row, cols], w1, w2).astype(bf16)
            for at in range(0, LANES, LANES // 2):
                to = i * LANES + at
                ref = keep2 if to < rows // 2 else send2
                to = to if to < rows // 2 else to - rows // 2
                ref[to:to + LANES // 2, cols] = out[at:at + LANES // 2, :]
            lines2[c * near + i:c * near + i + 1, :] = join(
                lines[mine:mine + 1, :], got_lines[other:other + 1, :])[2]


def halve(keep, got, lines, got_lines):
    rows, model = keep.shape
    side = jax.ShapeDtypeStruct((rows // 2, model), bf16)
    return pl.pallas_call(
        halve_kernel, out_shape=[side] * 2 + [jax.ShapeDtypeStruct((lines.shape[0] // 2, LANES), f32)],
        in_specs=[VM] * 4, out_specs=[VM] * 3, compiler_params=params(), name="halve",
    )(keep, got, lines, got_lines)


def per_device(char_ids, char_table, conv_weight, proj_weight, gate_weight, trans_weight, gate_bias, hidden, targets,
               *, vocab, blk):
    devices = vocab * blk
    axes = ("vocab", "blk")

    def swap(x, bits):
        return lax.ppermute(x, axes, [(i, i ^ bits) for i in range(devices)])

    core, near = blk, 1
    bit_a, bit_b = 2 * blk, 4 * blk
    rest = [1 << i for i in range(1, blk.bit_length() - 1)] + [
        blk << i for i in range(3, vocab.bit_length() - 1)]
    me = lax.axis_index("vocab") * blk + lax.axis_index("blk")
    local, length = char_ids.shape
    mine = hidden.shape[0]

    rows, goal = hidden, targets.reshape(1, mine)
    for bit in rest:
        rows, goal = (jnp.concatenate([rows, swap(rows, bit)], axis=0),
                      jnp.concatenate([goal, swap(goal, bit)], axis=1))
    hid = [rows] + [swap(rows, b) for b in (bit_b, bit_a, bit_a | bit_b)]
    goal = jnp.concatenate([goal] + [swap(goal, b) for b in (bit_b, bit_a, bit_a | bit_b)], axis=1)

    ids_t = char_ids.T
    some = ids_t.astype(bf16)
    some = jnp.concatenate([some, swap(some, core)], axis=1)
    some = jnp.concatenate([some, swap(some, near)], axis=1)
    apart = (goal // local) ^ me
    slot = jnp.where(apart == 0, 0, jnp.where(apart == core, 1, jnp.where(
        apart == near, 2, jnp.where(apart == (core | near), 3, -1))))
    spot = jnp.where(slot >= 0, slot * local + goal % local, -1)
    chars = pick(spot, some)
    for bit in [bit_a, bit_b] + rest[::-1]:
        n = chars.shape[1] // 2
        chars = chars[:, :n] + swap(chars[:, n:], bit)
    aim_ids = chars.astype(jnp.int32)
    pad = -mine % LANES
    aim_ids = jnp.pad(aim_ids, ((0, 0), (0, pad)))

    tab_t = char_table.T.astype(f32)
    weights = (tab_t, conv_weight, proj_weight, gate_weight, trans_weight, gate_bias)
    half = local // 2
    (e0,) = embed(ids_t[:, :half], (half,), *weights)
    e1, aim = embed(jnp.concatenate([ids_t[:, half:], aim_ids], axis=1), (half, mine), *weights)
    c0, c1 = swap(e0, core), swap(e1, core)
    z0, z1 = swap(e0, near), swap(e1, near)
    d0, d1 = swap(z0, core), swap(z1, core)

    state = first_fold(hid, [e0, c0, e1, c1])
    a_keep, a_send, b_keep, b_send, lse = second_fold(hid, [z0, d0, z1, d1], state)
    a_keep, a_send, b_keep, b_send, a_line, b_line = merge_one(
        a_keep, swap(a_send, bit_a), b_keep, swap(b_send, bit_b), lse, swap(lse, bit_a), swap(lse, bit_b))
    keep, send, lines = merge_two(
        a_keep, swap(a_send, bit_b), b_keep, swap(b_send, bit_a), a_line, b_line,
        swap(a_line, bit_b), swap(b_line, bit_a))
    for bit in rest[:0:-1]:
        keep, send, lines = halve(keep, swap(send, bit), lines, swap(lines, bit))
    loss, grad = finish(keep, swap(send, rest[0]), lines, swap(lines, rest[0]), hidden, aim)
    return loss[0, :mine], grad


def solution(mesh):
    words = P(("vocab", "blk"))
    return jax.shard_map(
        functools.partial(per_device, vocab=mesh.shape["vocab"], blk=mesh.shape["blk"]),
        mesh=mesh,
        in_specs=(P(("vocab", "blk"), None), P(), P(), P(), P(), P(), P(), P(("vocab", "blk"), None), words),
        out_specs=(words, P(("vocab", "blk"), None)),
        check_vma=False,
    )
```

time: 274 us -> 138 us (0.50)
  matrix products: 77.2 us -> 0 us
  local copies, waits for them, and re-layouts: 74.1 us -> 8.89 us
  Pallas kernels: 0 us -> 51 us
  blocking collectives: 25.8 us -> 0 us
  waiting for transfers between devices: 60.3 us -> 38.7 us
  starting transfers between devices: 11.7 us -> 32.9 us
  between operations: 15.1 us -> 0.84 us
  other arithmetic: 8.73 us -> 5.69 us
    dot_general x36 -> x0, matrix products: 77.2 us -> none  [the longest x4 19.3 us: char_features(): jnp.dot(windows.reshape(num_words * length, widths * embed_dim), masked,...]
    pallas_call x0 -> x8, Pallas kernels: none -> 51 us  [the longest x2 30.7 us: embed(): pl.pallas_call(functools.partial(cnn_kernel, widths=widths, filters=filte...]
    all_gather x1 -> x0, waiting for transfers between devices: 29.1 us -> none  [per_device(): word_panel = lax.all_gather(embeds, 'vocab', axis=0, tiled=True)]
    while x64 -> x0, local copies, waits for them, and re-layouts: 22.6 us -> none
    ppermute x16 -> x29, starting transfers between devices: 11.7 us -> 32.9 us  [swap(): return lax.ppermute(x, axes, [(i, i ^ bits) for i in range(devices)])]
    gather x4 -> x0, local copies, waits for them, and re-layouts: 21 us -> none  [pick_targets(): jnp.take(word_panel, jnp.clip(row_spot, 0, count_words - 1), axis=0)]
    all_gather x1 -> x0, blocking collectives: 15.9 us -> none  [per_device(): group_hidden = lax.all_gather(hidden, 'blk', axis=0, tiled=True)]
    slice x32 -> x4, local copies, waits for them, and re-layouts: 17.9 us -> 2.31 us  [the longest x1 1.48 us: per_device(): ids_t[:, half:]]
  transfers between devices with their start and end apart: 17 -> 29, of which waited for: 9 -> 15; matrix products, arithmetic and copies ran while one was open for 19% -> 6% of each run, Pallas kernels for 0% -> 28%
where the time goes in v1:
time: 138 us
  Pallas kernels  51 us (37%)
  waiting for transfers between devices  38.7 us (28%)
  starting transfers between devices  32.9 us (24%)
  local copies, waits for them, and re-layouts  8.89 us (6%)
  other arithmetic  5.69 us (4%)
    ppermute x29, waiting for transfers between devices, swap(): return lax.ppermute(x, axes, [(i, i ^ bits) for i in range(devices)])  38.7 us
    ppermute x29, starting transfers between devices, swap(): return lax.ppermute(x, axes, [(i, i ^ bits) for i in range(devices)])  32.9 us
    pallas_call x2, Pallas kernels, embed(): pl.pallas_call(functools.partial(cnn_kernel, widths=widths, filters=filte...  30.7 us
    pallas_call x1, Pallas kernels, second_fold(): pl.pallas_call(functools.partial(second_kernel, nh=len(hid), nw=len(words...  6.1 us
    pallas_call x1, Pallas kernels, first_fold(): pl.pallas_call(functools.partial(first_kernel, nh=len(hid), nw=len(words)...  5.77 us
    unnamed x45, local copies, waits for them, and re-layouts  4.73 us
  transfers between devices with their start and end apart: 29, of which 15 were waited for; matrix products, arithmetic and copies ran while one was open for 6% of the time, Pallas kernels for 28%

profile of v1, /device:TPU:0, one launch (start us, length us, event | category | flops | bytes accessed | tf_op | source)
XLA Modules:
  0.0 137.9 jit_solution(13464371115580568865)
XLA Ops:
  0.6 4.1 %collective-permute-start.6 = (s32[1,64]{1,0:T(1,128)}, s32[1,64]{1,0:T(1,128)S(1)}, u32[]{:S(2)}, u32[]{:S(2)}) collective-permute-start(s32[1,64]{1,0:T(1,128)} %bitcast.8), channel_id=1, source_target_pairs={{0,2},{1,3},{2,0},{3,1},{4,6},{5,7},{6,4},{7,5},{8,10},{9,11},{10,... | collective-permute-start | bytes 776 | tf_op jit(solution)/shard_map/ppermute | solution.py:419
  8.0 1.8 %collective-permute-start.7 = (s32[1,128]{1,0:T(1,128)S(1)}, s32[1,128]{1,0:T(1,128)S(1)}, u32[]{:S(2)}, u32[]{:S(2)}) collective-permute-start(s32[1,128]{1,0:T(1,128)S(1)} %pad_add_fusion.1), channel_id=1, source_target_pairs={{0,16},{1,17},{2,18},{3,19},{4,20},{5,21},{6,22},{7,23},{8,24},{9,... | collective-permute-start | bytes 1544 | tf_op jit(solution)/shard_map/ppermute | solution.py:419
  11.6 1.8 %collective-permute-done.8 = s32[1,128]{1,0:T(1,128)S(1)} collective-permute-done((s32[1,128]{1,0:T(1,128)S(1)}, s32[1,128]{1,0:T(1,128)S(1)}, u32[]{:S(2)}, u32[]{:S(2)}) %collective-permute-start.8) | collective-permute-done | bytes 544 | tf_op jit(solution)/shard_map/ppermute | solution.py:419
  13.4 2.4 %collective-permute-done.9 = s32[1,128]{1,0:T(1,128)S(1)} collective-permute-done((s32[1,128]{1,0:T(1,128)S(1)}, s32[1,128]{1,0:T(1,128)S(1)}, u32[]{:S(2)}, u32[]{:S(2)}) %collective-permute-start.9) | collective-permute-done | bytes 544 | tf_op jit(solution)/shard_map/ppermute | solution.py:419
  18.8 2.6 %collective-permute-done.11 = bf16[50,1024]{1,0:T(8,128)(2,1)S(1)} collective-permute-done((bf16[50,1024]{1,0:T(8,128)(2,1)S(1)}, bf16[50,1024]{1,0:T(8,128)(2,1)S(1)}, u32[]{:S(2)}, u32[]{:S(2)}) %collective-permute-start.11) | collective-permute-done | bytes 102432 | tf_op jit(solution)/shard_map/ppermute | solution.py:419
  22.1 2.0 %pick.1 = bf16[50,512]{1,0:T(8,128)(2,1)} custom-call(s32[1,512]{1,0:T(1,128)} %compare_select_fusion.spot_ref, bf16[50,2048]{1,0:T(8,128)(2,1)} %pad_maximum_fusion.ids_ref), custom_call_target="tpu_custom_call" | custom-call | flops 536870912 | bytes 1048576 | tf_op jit(solution)/shard_map/pick/pallas_call | solution.py:160
  26.7 2.0 %collective-permute-done.12 = bf16[50,256]{1,0:T(8,128)(2,1)S(1)} collective-permute-done((bf16[50,256]{1,0:T(8,128)(2,1)S(1)}, bf16[50,256]{1,0:T(8,128)(2,1)S(1)}, u32[]{:S(2)}, u32[]{:S(2)}) %collective-permute-start.12) | collective-permute-done | bytes 25632 | tf_op jit(solution)/shard_map/ppermute | solution.py:419
  30.0 12.9 %embed.2.refs_4_ = bf16[256,1024]{1,0:T(8,128)(2,1)} custom-call(s32[50,256]{1,0:T(8,128)} %get-tuple-element.45.ids_ref, f32[16,256]{1,0:T(8,128)} %convert_bitcast_fusion.tab_ref, bf16[112,896]{1,0:T(8,128)(2,1)} %conv_ref.3, f32[2,1024]{1,0:T(2,128)} %bias_ref.3, bf16[896,1024]{1,0:T(8,128)(2,1)} %proj_hbm.3, bf16[2,1024,1024]{2,1,0:T(8,128)(2,1)} %gate_hbm.3, ...), custom_call_target="tpu_custom_call" | custom-call | flops 8489271296 | bytes 12582912 | tf_op jit(solution)/shard_map/embed/pallas_call | solution.py:127
  44.7 2.6 %collective-permute-start.14 = (bf16[50,64]{1,0:T(8,128)(2,1)S(1)}, bf16[50,64]{1,0:T(8,128)(2,1)S(1)}, u32[]{:S(2)}, u32[]{:S(2)}) collective-permute-start(bf16[50,64]{1,0:T(8,128)(2,1)S(1)} %slice.43), channel_id=1, source_target_pairs={{0,2},{1,3},{2,0},{3,1},{4,6},{5,7},{6,4},{7,5},{8,10},{9,11},{10,... | collective-permute-start | bytes 19208 | tf_op jit(solution)/shard_map/ppermute | solution.py:419
  47.3 5.0 %collective-permute-done.14 = bf16[50,64]{1,0:T(8,128)(2,1)S(1)} collective-permute-done((bf16[50,64]{1,0:T(8,128)(2,1)S(1)}, bf16[50,64]{1,0:T(8,128)(2,1)S(1)}, u32[]{:S(2)}, u32[]{:S(2)}) %collective-permute-start.14) | collective-permute-done | bytes 6432 | tf_op jit(solution)/shard_map/ppermute | solution.py:419
  53.0 17.8 %embed.3 = (bf16[256,1024]{1,0:T(8,128)(2,1)}, bf16[64,1024]{1,0:T(8,128)(2,1)}) custom-call(s32[50,384]{1,0:T(8,128)} %pad_add_fusion.ids_ref, f32[16,256]{1,0:T(8,128)} %convert_bitcast_fusion.tab_ref, bf16[112,896]{1,0:T(8,128)(2,1)} %conv_ref.3, f32[2,1024]{1,0:T(2,128)} %bias_ref.3, bf16[896,1024]{1,0:T(8,128)(2,1)} %proj_hbm.3, ...), custom_call_target="tpu_custom_call" | custom-call | flops 12733906944 | bytes 12582912 | tf_op jit(solution)/shard_map/embed/pallas_call | solution.py:127
  70.8 3.6 %collective-permute-start.15 = (bf16[256,1024]{1,0:T(8,128)(2,1)}, bf16[256,1024]{1,0:T(8,128)(2,1)S(1)}, u32[]{:S(2)}, u32[]{:S(2)}) collective-permute-start(bf16[256,1024]{1,0:T(8,128)(2,1)} %get-tuple-element.23.refs_6_), channel_id=1, source_target_pairs={{0,1},{1,0},{2,3},{3,2},{4,5},{5,4},{6,7},{7,6},{8,9},{9,8},{10,11... | collective-permute-start | bytes 1572872 | tf_op jit(solution)/shard_map/ppermute | solution.py:419
  76.5 4.3 %collective-permute-done.1.refs_1_ = bf16[128,1024]{1,0:T(8,128)(2,1)S(1)} collective-permute-done((bf16[128,1024]{1,0:T(8,128)(2,1)S(1)}, bf16[128,1024]{1,0:T(8,128)(2,1)S(1)}, u32[]{:S(2)}, u32[]{:S(2)}) %collective-permute-start.1) | collective-permute-done | bytes 262176 | tf_op jit(solution)/shard_map/ppermute | solution.py:419
  83.3 8.0 %collective-permute-done.3.refs_3_ = bf16[128,1024]{1,0:T(8,128)(2,1)S(1)} collective-permute-done((bf16[128,1024]{1,0:T(8,128)(2,1)S(1)}, bf16[128,1024]{1,0:T(8,128)(2,1)S(1)}, u32[]{:S(2)}, u32[]{:S(2)}) %collective-permute-start.3) | collective-permute-done | bytes 262176 | tf_op jit(solution)/shard_map/ppermute | solution.py:419
  93.1 5.8 %first_fold.1 = (f32[512,1024]{1,0:T(8,128)}, f32[512,128]{1,0:T(8,128)}, f32[512,128]{1,0:T(8,128)}) custom-call(bf16[128,1024]{1,0:T(8,128)(2,1)} %copy-done.6, bf16[128,1024]{1,0:T(8,128)(2,1)} %copy-done.19, bf16[128,1024]{1,0:T(8,128)(2,1)} %copy-done.20, bf16[128,1024]{1,0:T(8,128)(2,1)} %copy-done.21, bf16[256,1024]{1,0:T(8,128)(2,1)} %embed.2.refs_4_, ...), custom_call_target="tpu_custom_call" | custom-call | flops 2147483648 | bytes 3145728 | tf_op jit(solution)/shard_map/first_fold/pallas_call | solution.py:231
  99.8 6.1 %second_fold.1 = (bf16[256,512]{1,0:T(8,128)(2,1)}, bf16[256,512]{1,0:T(8,128)(2,1)}, bf16[256,512]{1,0:T(8,128)(2,1)}, bf16[256,512]{1,0:T(8,128)(2,1)}, f32[4,128]{1,0:T(4,128)}) custom-call(bf16[128,1024]{1,0:T(8,128)(2,1)} %copy-done.6, bf16[128,1024]{1,0:T(8,128)(2,1)} %copy-done.19, bf16[128,1024]{1,0:T(8,128)(2,1)} %copy-done.20, ...), custom_call_target="tpu_custom_call" | custom-call | flops 2147483648 | bytes 3145728 | tf_op jit(solution)/shard_map/second_fold/pallas_call | solution.py:276
  110.0 3.4 %collective-permute-done.21.a_lse = f32[4,128]{1,0:T(4,128)S(1)} collective-permute-done((f32[4,128]{1,0:T(4,128)}, f32[4,128]{1,0:T(4,128)S(1)}, u32[]{:S(2)}, u32[]{:S(2)}) %collective-permute-start.21) | collective-permute-done | bytes 2080 | tf_op jit(solution)/shard_map/ppermute | solution.py:419
  114.9 2.3 %merge_one.1 = (bf16[128,512]{1,0:T(8,128)(2,1)}, bf16[128,512]{1,0:T(8,128)(2,1)}, bf16[128,512]{1,0:T(8,128)(2,1)}, bf16[128,512]{1,0:T(8,128)(2,1)}, f32[2,128]{1,0:T(2,128)}, /*index=5*/f32[2,128]{1,0:T(2,128)}) custom-call(bf16[256,512]{1,0:T(8,128)(2,1)} %get-tuple-element.27.a_keep, bf16[256,512]{1,0:T(8,128)(2,1)} %copy-done.1, ...), custom_call_target="tpu_custom_call" | custom-call | flops 524288 | bytes 1572864 | tf_op jit(solution)/shard_map/merge_one/pallas_call | solution.py:320
  117.2 1.7 %collective-permute-start.23 = (bf16[128,512]{1,0:T(8,128)(2,1)}, bf16[128,512]{1,0:T(8,128)(2,1)S(1)}, u32[]{:S(2)}, u32[]{:S(2)}) collective-permute-start(bf16[128,512]{1,0:T(8,128)(2,1)} %get-tuple-element.33), channel_id=1, source_target_pairs={{0,16},{1,17},{2,18},{3,19},{4,20},{5,21},{6,22},{7,23},{8,24},{9,... | collective-permute-start | bytes 393224 | tf_op jit(solution)/shard_map/ppermute | solution.py:419
  121.2 2.8 %collective-permute-done.25.a_lse = f32[2,128]{1,0:T(2,128)S(1)} collective-permute-done((f32[2,128]{1,0:T(2,128)}, f32[2,128]{1,0:T(2,128)S(1)}, u32[]{:S(2)}, u32[]{:S(2)}) %collective-permute-start.25) | collective-permute-done | bytes 1056 | tf_op jit(solution)/shard_map/ppermute | solution.py:419
  125.2 2.0 %merge_two.1 = (bf16[64,1024]{1,0:T(8,128)(2,1)}, bf16[64,1024]{1,0:T(8,128)(2,1)}, f32[2,128]{1,0:T(2,128)}) custom-call(bf16[128,512]{1,0:T(8,128)(2,1)} %get-tuple-element.32.a_keep, bf16[128,512]{1,0:T(8,128)(2,1)} %copy-done.3, bf16[128,512]{1,0:T(8,128)(2,1)} %get-tuple-element.34.b_keep, bf16[128,512]{1,0:T(8,128)(2,1)} %copy-done.4, ...), custom_call_target="tpu_custom_call" | custom-call | flops 524288 | bytes 786432 | tf_op jit(solution)/shard_map/merge_two/pallas_call | solution.py:349
  127.2 2.1 %collective-permute-start.27 = (bf16[64,1024]{1,0:T(8,128)(2,1)}, bf16[64,1024]{1,0:T(8,128)(2,1)S(1)}, u32[]{:S(2)}, u32[]{:S(2)}) collective-permute-start(bf16[64,1024]{1,0:T(8,128)(2,1)} %get-tuple-element.39), channel_id=1, source_target_pairs={{0,2},{1,3},{2,0},{3,1},{4,6},{5,7},{6,4},{7,5},{8,10},{9,11},{10,... | collective-permute-start | bytes 393224 | tf_op jit(solution)/shard_map/ppermute | solution.py:419
  130.1 4.0 %collective-permute-done.28.got_lines = f32[2,128]{1,0:T(2,128)S(1)} collective-permute-done((f32[2,128]{1,0:T(2,128)}, f32[2,128]{1,0:T(2,128)S(1)}, u32[]{:S(2)}, u32[]{:S(2)}) %collective-permute-start.28) | collective-permute-done | bytes 1056 | tf_op jit(solution)/shard_map/ppermute | solution.py:419
  134.7 2.1 %finish.1 = (f32[1,128]{1,0:T(1,128)}, bf16[64,1024]{1,0:T(8,128)(2,1)}) custom-call(bf16[64,1024]{1,0:T(8,128)(2,1)} %get-tuple-element.38.keep, bf16[64,1024]{1,0:T(8,128)(2,1)} %copy-done.5, f32[2,128]{1,0:T(2,128)} %get-tuple-element.40.lines, f32[2,128]{1,0:T(2,128)} %copy-done.11, bf16[64,1024]{1,0:T(8,128)(2,1)} %hid.1, ...), custom_call_target="tpu_custom_call" | custom-call | flops 524288 | bytes 786432 | tf_op jit(solution)/shard_map/finish/pallas_call | solution.py:375
  (105 shorter events, 33.7 us)
Async XLA Ops:
  0.6 6.7 %collective-permute-start.6 = (s32[1,64]{1,0:T(1,128)}, s32[1,64]{1,0:T(1,128)S(1)}, u32[]{:S(2)}, u32[]{:S(2)}) collective-permute-start(s32[1,64]{1,0:T(1,128)} %bitcast.8), channel_id=1, source_target_pairs={{0,2},{1,3},{2,0},{3,1},{4,6},{5,7},{6,4},{7,5},{8,10},{9,11},{10,... | collective-permute-start | bytes 776 | tf_op jit(solution)/shard_map/ppermute | solution.py:419
  5.6 10.9 %collective-permute-start.10 = (bf16[50,512]{1,0:T(8,128)(2,1)S(1)}, bf16[50,512]{1,0:T(8,128)(2,1)S(1)}, u32[]{:S(2)}, u32[]{:S(2)}) collective-permute-start(bf16[50,512]{1,0:T(8,128)(2,1)S(1)} %bitcast_convert_fusion), channel_id=1, source_target_pairs={{0,4},{1,5},{2,6},{3,7},{4,0},{5,1},{6,2},{7,3},{8,12},{9,13},{10,... | collective-permute-start | bytes 153608 | tf_op jit(solution)/shard_map/ppermute | solution.py:419
  5.7 68.7 %collective-permute-start = (bf16[64,1024]{1,0:T(8,128)(2,1)}, bf16[64,1024]{1,0:T(8,128)(2,1)S(1)}, u32[]{:S(2)}, u32[]{:S(2)}) collective-permute-start(bf16[64,1024]{1,0:T(8,128)(2,1)} %hid.1), channel_id=1, source_target_pairs={{0,2},{1,3},{2,0},{3,1},{4,6},{5,7},{6,4},{7,5},{8,10},{9,11},{10,... | collective-permute-start | bytes 393224 | tf_op jit(solution)/shard_map/ppermute | solution.py:419
  11.3 4.4 %collective-permute-start.9 = (s32[1,128]{1,0:T(1,128)S(1)}, s32[1,128]{1,0:T(1,128)S(1)}, u32[]{:S(2)}, u32[]{:S(2)}) collective-permute-start(s32[1,128]{1,0:T(1,128)S(1)} %pad_add_fusion.1), channel_id=1, source_target_pairs={{0,24},{1,25},{2,26},{3,27},{4,28},{5,29},{6,30},{7,31},{8,16},{9,... | collective-permute-start | bytes 1544 | tf_op jit(solution)/shard_map/ppermute | solution.py:419
  16.5 4.9 %collective-permute-start.11 = (bf16[50,1024]{1,0:T(8,128)(2,1)S(1)}, bf16[50,1024]{1,0:T(8,128)(2,1)S(1)}, u32[]{:S(2)}, u32[]{:S(2)}) collective-permute-start(bf16[50,1024]{1,0:T(8,128)(2,1)S(1)} %pad_maximum_fusion.1), channel_id=1, source_target_pairs={{0,1},{1,0},{2,3},{3,2},{4,5},{5,4},{6,7},{7,6},{8,9},{9,8},{10,11... | collective-permute-start | bytes 307208 | tf_op jit(solution)/shard_map/ppermute | solution.py:419
  29.5 15.1 %collective-permute-start.13 = (bf16[50,128]{1,0:T(8,128)(2,1)S(1)}, bf16[50,128]{1,0:T(8,128)(2,1)S(1)}, u32[]{:S(2)}, u32[]{:S(2)}) collective-permute-start(bf16[50,128]{1,0:T(8,128)(2,1)S(1)} %slice.41), channel_id=1, source_target_pairs={{0,16},{1,17},{2,18},{3,19},{4,20},{5,21},{6,22},{7,23},{8,24},{9,... | collective-permute-start | bytes 38408 | tf_op jit(solution)/shard_map/ppermute | solution.py:419
  42.9 37.9 %collective-permute-start.4 = (bf16[256,1024]{1,0:T(8,128)(2,1)}, bf16[256,1024]{1,0:T(8,128)(2,1)S(1)}, u32[]{:S(2)}, u32[]{:S(2)}) collective-permute-start(bf16[256,1024]{1,0:T(8,128)(2,1)} %embed.2.refs_4_), channel_id=1, source_target_pairs={{0,1},{1,0},{2,3},{3,2},{4,5},{5,4},{6,7},{7,6},{8,9},{9,8},{10,11... | collective-permute-start | bytes 1572872 | tf_op jit(solution)/shard_map/ppermute | solution.py:419
  44.7 7.7 %collective-permute-start.14 = (bf16[50,64]{1,0:T(8,128)(2,1)S(1)}, bf16[50,64]{1,0:T(8,128)(2,1)S(1)}, u32[]{:S(2)}, u32[]{:S(2)}) collective-permute-start(bf16[50,64]{1,0:T(8,128)(2,1)S(1)} %slice.43), channel_id=1, source_target_pairs={{0,2},{1,3},{2,0},{3,1},{4,6},{5,7},{6,4},{7,5},{8,10},{9,11},{10,... | collective-permute-start | bytes 19208 | tf_op jit(solution)/shard_map/ppermute | solution.py:419
  70.8 10.9 %collective-permute-start.15 = (bf16[256,1024]{1,0:T(8,128)(2,1)}, bf16[256,1024]{1,0:T(8,128)(2,1)S(1)}, u32[]{:S(2)}, u32[]{:S(2)}) collective-permute-start(bf16[256,1024]{1,0:T(8,128)(2,1)} %get-tuple-element.23.refs_6_), channel_id=1, source_target_pairs={{0,1},{1,0},{2,3},{3,2},{4,5},{5,4},{6,7},{7,6},{8,9},{9,8},{10,11... | collective-permute-start | bytes 1572872 | tf_op jit(solution)/shard_map/ppermute | solution.py:419
  74.4 6.4 %collective-permute-start.1 = (bf16[128,1024]{1,0:T(8,128)(2,1)S(1)}, bf16[128,1024]{1,0:T(8,128)(2,1)S(1)}, u32[]{:S(2)}, u32[]{:S(2)}) collective-permute-start(bf16[128,1024]{1,0:T(8,128)(2,1)S(1)} %constant_dynamic-update-slice_fusion.refs_0_), channel_id=1, source_target_pairs={{0,16},{1,17},{2,18},{3,19},{4,20},{5,21},{6,22},{7,23},{8,24},{9,... | collective-permute-start | bytes 786440 | tf_op jit(solution)/shard_map/ppermute | solution.py:419
  76.0 6.4 %collective-permute-start.2 = (bf16[128,1024]{1,0:T(8,128)(2,1)S(1)}, bf16[128,1024]{1,0:T(8,128)(2,1)S(1)}, u32[]{:S(2)}, u32[]{:S(2)}) collective-permute-start(bf16[128,1024]{1,0:T(8,128)(2,1)S(1)} %constant_dynamic-update-slice_fusion.refs_0_), channel_id=1, source_target_pairs={{0,8},{1,9},{2,10},{3,11},{4,12},{5,13},{6,14},{7,15},{8,0},{9,1},... | collective-permute-start | bytes 786440 | tf_op jit(solution)/shard_map/ppermute | solution.py:419
  76.5 14.9 %collective-permute-start.17 = (bf16[256,1024]{1,0:T(8,128)(2,1)S(1)}, bf16[256,1024]{1,0:T(8,128)(2,1)S(1)}, u32[]{:S(2)}, u32[]{:S(2)}) collective-permute-start(bf16[256,1024]{1,0:T(8,128)(2,1)S(1)} %copy-done.13), channel_id=1, source_target_pairs={{0,4},{1,5},{2,6},{3,7},{4,0},{5,1},{6,2},{7,3},{8,12},{9,13},{10,... | collective-permute-start | bytes 1572872 | tf_op jit(solution)/shard_map/ppermute | solution.py:419
  80.8 10.5 %collective-permute-start.18 = (bf16[256,1024]{1,0:T(8,128)(2,1)}, bf16[256,1024]{1,0:T(8,128)(2,1)S(1)}, u32[]{:S(2)}, u32[]{:S(2)}) collective-permute-start(bf16[256,1024]{1,0:T(8,128)(2,1)} %get-tuple-element.23.refs_6_), channel_id=1, source_target_pairs={{0,4},{1,5},{2,6},{3,7},{4,0},{5,1},{6,2},{7,3},{8,12},{9,13},{10,... | collective-permute-start | bytes 1572872 | tf_op jit(solution)/shard_map/ppermute | solution.py:419
  80.9 18.0 %collective-permute-start.5 = (bf16[256,1024]{1,0:T(8,128)(2,1)S(1)}, bf16[256,1024]{1,0:T(8,128)(2,1)S(1)}, u32[]{:S(2)}, u32[]{:S(2)}) collective-permute-start(bf16[256,1024]{1,0:T(8,128)(2,1)S(1)} %collective-permute-done.4.refs_4_), channel_id=1, source_target_pairs={{0,4},{1,5},{2,6},{3,7},{4,0},{5,1},{6,2},{7,3},{8,12},{9,13},{10,... | collective-permute-start | bytes 1572872 | tf_op jit(solution)/shard_map/ppermute | solution.py:419
  81.8 17.1 %collective-permute-start.16 = (bf16[256,1024]{1,0:T(8,128)(2,1)S(1)}, bf16[256,1024]{1,0:T(8,128)(2,1)S(1)}, u32[]{:S(2)}, u32[]{:S(2)}) collective-permute-start(bf16[256,1024]{1,0:T(8,128)(2,1)S(1)} %collective-permute-done.15.refs_6_), channel_id=1, source_target_pairs={{0,4},{1,5},{2,6},{3,7},{4,0},{5,1},{6,2},{7,3},{8,12},{9,13},{10,... | collective-permute-start | bytes 1572872 | tf_op jit(solution)/shard_map/ppermute | solution.py:419
  82.4 9.0 %collective-permute-start.3 = (bf16[128,1024]{1,0:T(8,128)(2,1)S(1)}, bf16[128,1024]{1,0:T(8,128)(2,1)S(1)}, u32[]{:S(2)}, u32[]{:S(2)}) collective-permute-start(bf16[128,1024]{1,0:T(8,128)(2,1)S(1)} %constant_dynamic-update-slice_fusion.refs_0_), channel_id=1, source_target_pairs={{0,24},{1,25},{2,26},{3,27},{4,28},{5,29},{6,30},{7,31},{8,16},{9,... | collective-permute-start | bytes 786440 | tf_op jit(solution)/shard_map/ppermute | solution.py:419
  105.9 8.2 %collective-permute-start.19 = (bf16[256,512]{1,0:T(8,128)(2,1)}, bf16[256,512]{1,0:T(8,128)(2,1)S(1)}, u32[]{:S(2)}, u32[]{:S(2)}) collective-permute-start(bf16[256,512]{1,0:T(8,128)(2,1)} %get-tuple-element.28), channel_id=1, source_target_pairs={{0,8},{1,9},{2,10},{3,11},{4,12},{5,13},{6,14},{7,15},{8,0},{9,1},... | collective-permute-start | bytes 786440 | tf_op jit(solution)/shard_map/ppermute | solution.py:419
  106.6 7.5 %collective-permute-start.20 = (bf16[256,512]{1,0:T(8,128)(2,1)}, bf16[256,512]{1,0:T(8,128)(2,1)S(1)}, u32[]{:S(2)}, u32[]{:S(2)}) collective-permute-start(bf16[256,512]{1,0:T(8,128)(2,1)} %get-tuple-element.30), channel_id=1, source_target_pairs={{0,16},{1,17},{2,18},{3,19},{4,20},{5,21},{6,22},{7,23},{8,24},{9,... | collective-permute-start | bytes 786440 | tf_op jit(solution)/shard_map/ppermute | solution.py:419
  108.0 5.4 %collective-permute-start.21 = (f32[4,128]{1,0:T(4,128)}, f32[4,128]{1,0:T(4,128)S(1)}, u32[]{:S(2)}, u32[]{:S(2)}) collective-permute-start(f32[4,128]{1,0:T(4,128)} %get-tuple-element.31.lse), channel_id=1, source_target_pairs={{0,8},{1,9},{2,10},{3,11},{4,12},{5,13},{6,14},{7,15},{8,0},{9,1},... | collective-permute-start | bytes 6152 | tf_op jit(solution)/shard_map/ppermute | solution.py:419
  109.5 4.6 %collective-permute-start.22 = (f32[4,128]{1,0:T(4,128)}, f32[4,128]{1,0:T(4,128)S(1)}, u32[]{:S(2)}, u32[]{:S(2)}) collective-permute-start(f32[4,128]{1,0:T(4,128)} %get-tuple-element.31.lse), channel_id=1, source_target_pairs={{0,16},{1,17},{2,18},{3,19},{4,20},{5,21},{6,22},{7,23},{8,24},{9,... | collective-permute-start | bytes 6152 | tf_op jit(solution)/shard_map/ppermute | solution.py:419
  117.2 7.3 %collective-permute-start.23 = (bf16[128,512]{1,0:T(8,128)(2,1)}, bf16[128,512]{1,0:T(8,128)(2,1)S(1)}, u32[]{:S(2)}, u32[]{:S(2)}) collective-permute-start(bf16[128,512]{1,0:T(8,128)(2,1)} %get-tuple-element.33), channel_id=1, source_target_pairs={{0,16},{1,17},{2,18},{3,19},{4,20},{5,21},{6,22},{7,23},{8,24},{9,... | collective-permute-start | bytes 393224 | tf_op jit(solution)/shard_map/ppermute | solution.py:419
  118.9 5.6 %collective-permute-start.24 = (bf16[128,512]{1,0:T(8,128)(2,1)}, bf16[128,512]{1,0:T(8,128)(2,1)S(1)}, u32[]{:S(2)}, u32[]{:S(2)}) collective-permute-start(bf16[128,512]{1,0:T(8,128)(2,1)} %get-tuple-element.35), channel_id=1, source_target_pairs={{0,8},{1,9},{2,10},{3,11},{4,12},{5,13},{6,14},{7,15},{8,0},{9,1},... | collective-permute-start | bytes 393224 | tf_op jit(solution)/shard_map/ppermute | solution.py:419
  127.2 6.9 %collective-permute-start.27 = (bf16[64,1024]{1,0:T(8,128)(2,1)}, bf16[64,1024]{1,0:T(8,128)(2,1)S(1)}, u32[]{:S(2)}, u32[]{:S(2)}) collective-permute-start(bf16[64,1024]{1,0:T(8,128)(2,1)} %get-tuple-element.39), channel_id=1, source_target_pairs={{0,2},{1,3},{2,0},{3,1},{4,6},{5,7},{6,4},{7,5},{8,10},{9,11},{10,... | collective-permute-start | bytes 393224 | tf_op jit(solution)/shard_map/ppermute | solution.py:419
  129.3 4.8 %collective-permute-start.28 = (f32[2,128]{1,0:T(2,128)}, f32[2,128]{1,0:T(2,128)S(1)}, u32[]{:S(2)}, u32[]{:S(2)}) collective-permute-start(f32[2,128]{1,0:T(2,128)} %get-tuple-element.40.lines), channel_id=1, source_target_pairs={{0,2},{1,3},{2,0},{3,1},{4,6},{5,7},{6,4},{7,5},{8,10},{9,11},{10,... | collective-permute-start | bytes 3080 | tf_op jit(solution)/shard_map/ppermute | solution.py:419
  (27 other events, 141.5 us)

commit v2 on v1

--- a/solution.py
+++ b/solution.py
@@ -7,7 +7,8 @@
 from jax.sharding import PartitionSpec as P
 
 bf16=jnp.bfloat16; f32=jnp.float32
-LANES=128; SPAN=8
+LANES = 128
+SPAN = 8
 
 def prep_toeplitz(conv_ref, toep, ce, widths, filters):
     depth = toep.shape[0]
@@ -23,24 +24,30 @@
             if rest:
                 toep[o * ce + rows:depth, cols] = jnp.zeros((rest, filters), bf16)
 
-def lookup(ids_ref, tab_ref, vec, words, length, ce):
+def lookup(ids_ref, start, words, tab_ref, vec, turn, length, ce):
     per = LANES // ce
-    for t in range(words // LANES):
+    for at in range(0, words, LANES):
+        count = min(LANES, words - at)
+        turn[...] = jnp.zeros(turn.shape, f32)
+        turn[0:count, 0:length] = ids_ref[start + at:start + at + count, 0:length].astype(f32)
+        ids = turn[...].T.astype(jnp.int32)
         for g in range(vec.shape[1] // LANES):
             parts = []
             for q in range(per):
                 p = g * per + q
                 if p >= length:
-                    parts.append(jnp.zeros((ce, LANES), f32)); continue
-                idx = jnp.broadcast_to(ids_ref[p:p + 1, t * LANES:(t + 1) * LANES], (8, LANES))
+                    parts.append(jnp.zeros((ce, LANES), f32))
+                    continue
+                idx = jnp.broadcast_to(ids[p:p + 1, :], (8, LANES))
                 low = jnp.bitwise_and(idx, LANES - 1)
                 top = idx >= LANES
                 for h in range(ce // 8):
-                    a = jnp.take_along_axis(tab_ref[h * 8:h * 8 + 8, 0:LANES], low, axis=1)
-                    b = jnp.take_along_axis(tab_ref[h * 8:h * 8 + 8, LANES:2 * LANES], low, axis=1)
-                    parts.append(jnp.where(top, b, a))
+                    one = jnp.take_along_axis(tab_ref[h * 8:h * 8 + 8, 0:LANES], low, axis=1)
+                    two = jnp.take_along_axis(tab_ref[h * 8:h * 8 + 8, LANES:2 * LANES], low, axis=1)
+                    parts.append(jnp.where(top, two, one))
             block = jnp.concatenate(parts, axis=0)
-            vec[t * LANES:(t + 1) * LANES, g * LANES:(g + 1) * LANES] = block.T.astype(bf16)
+            vec[at:at + count, g * LANES:(g + 1) * LANES] = block.T[0:count].astype(bf16)
+
 
 def conv_pool(vec, toep, acc, length, widths, filters):
     words = vec.shape[0]
@@ -73,16 +80,15 @@
             acc[:, k * filters:(k + 1) * filters] = best
 
 def cnn_kernel(ids_ref, tab_ref, conv_ref, bias_ref, proj_hbm, gate_hbm, trans_hbm, *rest,
-               widths, filters, ce, length, layers, nt, outs):
-    out_refs, scratch = rest[:outs], rest[outs:]
-    vec, toep, acc, feat, proj, gate, trans, state, last, sems = scratch
+               widths, filters, ce, length, layers, nt, start):
+    out_ref, vec, toep, acc, feat, proj, gate, trans, state, last, turn, sems = rest
     copies = [pltpu.make_async_copy(s, d, sems.at[i]) for i, (s, d) in enumerate(
         ((proj_hbm, proj), (gate_hbm, gate), (trans_hbm, trans)))]
     for c in copies:
         c.start()
-    words = ids_ref.shape[1]
+    words = out_ref.shape[0]
     prep_toeplitz(conv_ref, toep, ce, widths, filters)
-    lookup(ids_ref, tab_ref, vec, words, length, ce)
+    lookup(ids_ref, start, words, tab_ref, vec, turn, length, ce)
     conv_pool(vec, toep, acc, length, widths, filters)
     for c in copies:
         c.wait()
@@ -101,10 +107,7 @@
             if l + 1 < layers:
                 last[:, n:n + nt] = new
             else:
-                at = 0
-                for ref in out_refs:
-                    ref[:, n:n + nt] = new[at:at + ref.shape[0], :]
-                    at += ref.shape[0]
+                out_ref[:, n:n + nt] = new
         if l + 1 < layers:
             state[...] = last[...]
 
@@ -117,8 +120,7 @@
     return pltpu.CompilerParams(vmem_limit_bytes=limit_mib << 20)
 
 
-def embed(ids_t, sizes, tab_t, conv_weight, proj_weight, gate_weight, trans_weight, gate_bias, nt=256):
-    length, words = ids_t.shape
+def embed(ids, length, start, words, tab_t, conv_weight, proj_weight, gate_weight, trans_weight, gate_bias, nt=256):
     ce = tab_t.shape[0]
     widths = conv_weight.shape[0] // ce
     filters = conv_weight.shape[1] // widths
@@ -126,10 +128,10 @@
     flops = 2 * words * (length * 256 * widths * filters + widths * filters * model + 2 * layers * model * model)
     return pl.pallas_call(
         functools.partial(cnn_kernel, widths=widths, filters=filters, ce=ce, length=length, layers=layers, nt=nt,
-                          outs=len(sizes)),
-        out_shape=[jax.ShapeDtypeStruct((s, model), bf16) for s in sizes],
+                          start=start),
+        out_shape=jax.ShapeDtypeStruct((words, model), bf16),
         in_specs=[VM, VM, VM, VM, ANY, ANY, ANY],
-        out_specs=[VM] * len(sizes),
+        out_specs=VM,
         scratch_shapes=[
             pltpu.VMEM((words, (-(-length // SPAN) + 1) * LANES), bf16),
             pltpu.VMEM((2 * LANES, widths * SPAN * filters), bf16),
@@ -140,31 +142,53 @@
             pltpu.VMEM(trans_weight.shape, bf16),
             pltpu.VMEM((words, model), bf16),
             pltpu.VMEM((words, model), bf16),
+            pltpu.VMEM((LANES, LANES), f32),
             pltpu.SemaphoreType.DMA((3,)),
         ],
         compiler_params=params(),
         cost_estimate=pl.CostEstimate(flops=flops, bytes_accessed=12 << 20, transcendentals=words * 4096),
         name="embed",
-    )(ids_t, tab_t, conv_weight, gate_bias, proj_weight, gate_weight, trans_weight)
-
-
-def pick_kernel(spot_ref, ids_ref, out_ref):
-    words = ids_ref.shape[1]
-    rows = spot_ref.shape[1]
-    at = lax.broadcasted_iota(jnp.int32, (words, rows), 0)
-    hot = jnp.where(at == spot_ref[...], 1.0, 0.0).astype(bf16)
-    out_ref[...] = jnp.dot(ids_ref[...], hot, preferred_element_type=f32).astype(bf16)
-
-
-def pick(spot, ids):
-    return pl.pallas_call(
-        pick_kernel,
-        out_shape=jax.ShapeDtypeStruct((ids.shape[0], spot.shape[1]), bf16),
-        in_specs=[VM, VM], out_specs=VM, compiler_params=params(),
-        cost_estimate=pl.CostEstimate(flops=2 * 256 * ids.shape[1] * spot.shape[1], bytes_accessed=1 << 20,
+    )(ids, tab_t, conv_weight, gate_bias, proj_weight, gate_weight, trans_weight)
+
+
+def pick_kernel(me_ref, *refs, nh, order, local):
+    hid, ids = refs[:nh], refs[nh:nh + len(order)]
+    keep, send = refs[nh + len(order):]
+    model = hid[0].shape[1] - LANES
+    at = 0
+    for h in hid:
+        rows = h.shape[0]
+        code = h[:, model:model + LANES].astype(f32).astype(jnp.int32)
+        goal = code[:, 0:1] * 256 + code[:, 1:2]
+        owner = lax.div(goal, local)
+        apart = jnp.bitwise_xor(owner, me_ref[0])
+        place = goal - owner * local
+        lane = lax.broadcasted_iota(jnp.int32, (rows, local), 1)
+        out = None
+        for ref, bits in zip(ids, order):
+            spot = jnp.where(apart == bits, place, -1)
+            hot = jnp.where(lane == spot, 1.0, 0.0).astype(bf16)
+            d = lax.dot_general(hot, ref[...], (((1,), (1,)), ((), ())), preferred_element_type=f32)
+            out = d if out is None else out + d
+        ref = keep if at < keep.shape[0] else send
+        to = at if at < keep.shape[0] else at - keep.shape[0]
+        ref[to:to + rows, 0:out.shape[1]] = out.astype(bf16)
+        at += rows
+
+
+def pick(me, hid, ids, order):
+    rows = sum(h.shape[0] for h in hid)
+    chars, local = ids[0].shape
+    side = jax.ShapeDtypeStruct((rows // 2, chars), bf16)
+    return pl.pallas_call(
+        functools.partial(pick_kernel, nh=len(hid), order=order, local=local),
+        out_shape=[side] * 2,
+        in_specs=[pl.BlockSpec(memory_space=pltpu.SMEM)] + [VM] * (len(hid) + len(ids)), out_specs=[VM] * 2,
+        compiler_params=params(),
+        cost_estimate=pl.CostEstimate(flops=2 * 256 * rows * local * len(ids), bytes_accessed=2 << 20,
                                       transcendentals=0),
         name="pick",
-    )(spot, ids)
+    )(me, *hid, *ids)
 
 
 def by_row(line, i):
@@ -212,7 +236,7 @@
     out, top_ref, total_ref, rows, score, prob = refs[nh + nw:]
     at = 0
     for h in hid:
-        rows[at:at + h.shape[0], :] = h[...]
+        rows[at:at + h.shape[0], :] = h[:, 0:rows.shape[1]]
         at += h.shape[0]
     top, total = part_of_softmax(rows, words, score, prob, out)
     top_ref[...] = jnp.broadcast_to(top, top_ref.shape)
@@ -225,7 +249,7 @@
 
 
 def first_fold(hid, words):
-    model = hid[0].shape[1]
+    model = words[0].shape[1]
     rows = sum(h.shape[0] for h in hid)
     count = sum(w.shape[0] for w in words)
     return pl.pallas_call(
@@ -244,7 +268,7 @@
     old, top_ref, total_ref, a_keep, a_send, b_keep, b_send, lse, rows, score, prob, new = refs[nh + nw:]
     at = 0
     for h in hid:
-        rows[at:at + h.shape[0], :] = h[...]
+        rows[at:at + h.shape[0], :] = h[:, 0:rows.shape[1]]
         at += h.shape[0]
     top2, total2 = part_of_softmax(rows, words, score, prob, new)
     top1, total1 = top_ref[:, 0:1], total_ref[:, 0:1]
@@ -269,7 +293,7 @@
 
 
 def second_fold(hid, words, state):
-    model = hid[0].shape[1]
+    model = words[0].shape[1]
     rows = sum(h.shape[0] for h in hid)
     count = sum(w.shape[0] for w in words)
     side = jax.ShapeDtypeStruct((rows // 2, model // 2), bf16)
@@ -426,40 +450,44 @@
     local, length = char_ids.shape
     mine = hidden.shape[0]
 
-    rows, goal = hidden, targets.reshape(1, mine)
+    goal = targets.reshape(mine, 1)
+    code = jnp.concatenate([goal // 256, goal % 256], axis=1).astype(bf16)
+    rows = jnp.concatenate([hidden, code, jnp.zeros((mine, LANES - 2), bf16)], axis=1)
     for bit in rest:
-        rows, goal = (jnp.concatenate([rows, swap(rows, bit)], axis=0),
-                      jnp.concatenate([goal, swap(goal, bit)], axis=1))
-    hid = [rows] + [swap(rows, b) for b in (bit_b, bit_a, bit_a | bit_b)]
-    goal = jnp.concatenate([goal] + [swap(goal, b) for b in (bit_b, bit_a, bit_a | bit_b)], axis=1)
-
-    ids_t = char_ids.T
-    some = ids_t.astype(bf16)
-    some = jnp.concatenate([some, swap(some, core)], axis=1)
-    some = jnp.concatenate([some, swap(some, near)], axis=1)
-    apart = (goal // local) ^ me
-    slot = jnp.where(apart == 0, 0, jnp.where(apart == core, 1, jnp.where(
-        apart == near, 2, jnp.where(apart == (core | near), 3, -1))))
-    spot = jnp.where(slot >= 0, slot * local + goal % local, -1)
-    chars = pick(spot, some)
-    for bit in [bit_a, bit_b] + rest[::-1]:
-        n = chars.shape[1] // 2
-        chars = chars[:, :n] + swap(chars[:, n:], bit)
-    aim_ids = chars.astype(jnp.int32)
-    pad = -mine % LANES
-    aim_ids = jnp.pad(aim_ids, ((0, 0), (0, pad)))
+        rows = jnp.concatenate([rows, swap(rows, bit)], axis=0)
+
+    ids_own = char_ids.T.astype(bf16)
+    ids_core, ids_near = swap(ids_own, core), swap(ids_own, near)
 
     tab_t = char_table.T.astype(f32)
     weights = (tab_t, conv_weight, proj_weight, gate_weight, trans_weight, gate_bias)
-    half = local // 2
-    (e0,) = embed(ids_t[:, :half], (half,), *weights)
-    e1, aim = embed(jnp.concatenate([ids_t[:, half:], aim_ids], axis=1), (half, mine), *weights)
-    c0, c1 = swap(e0, core), swap(e1, core)
-    z0, z1 = swap(e0, near), swap(e1, near)
-    d0, d1 = swap(z0, core), swap(z1, core)
-
-    state = first_fold(hid, [e0, c0, e1, c1])
-    a_keep, a_send, b_keep, b_send, lse = second_fold(hid, [z0, d0, z1, d1], state)
+    sizes = (192, 192, 128) if local == 512 else (local // 2, local // 4, local // 4)
+    pieces, start, ids = [], 0, char_ids
+    hid = None
+    for i, size in enumerate(sizes):
+        pieces.append(embed(ids, length, start, size, *weights))
+        start += size
+        if i == 0:
+            rows, ids_core, ids_near, ids, _ = lax.optimization_barrier((rows, ids_core, ids_near, ids, pieces[0]))
+            hid = [rows] + [swap(rows, b) for b in (bit_b, bit_a, bit_a | bit_b)]
+            ids_far = swap(ids_near, core)
+        elif i == 1:
+            *hid, ids_far, ids = lax.optimization_barrier((*hid, ids_far, ids))
+    cores = [swap(e, core) for e in pieces]
+    nears = [swap(e, near) for e in pieces]
+    fars = [swap(e, core) for e in nears]
+
+    late = 1 if 4 * hid[0].shape[0] <= local else len(nears)
+    state = first_fold(hid, pieces + cores + nears[:-late] + fars[:-late])
+    me = me.astype(jnp.int32).reshape(1)
+    chars, away = pick(me, hid, [ids_own, ids_core, ids_near, ids_far], (0, core, near, core | near))
+    chars = chars + swap(away, bit_a)
+    for bit in [bit_b] + rest[::-1]:
+        n = chars.shape[0] // 2
+        chars = chars[:n] + swap(chars[n:], bit)
+    aim = embed(chars, length, 0, mine, *weights)
+
+    a_keep, a_send, b_keep, b_send, lse = second_fold(hid, nears[-late:] + fars[-late:], state)
     a_keep, a_send, b_keep, b_send, a_line, b_line = merge_one(
         a_keep, swap(a_send, bit_a), b_keep, swap(b_send, bit_b), lse, swap(lse, bit_a), swap(lse, bit_b))
     keep, send, lines = merge_two(

time: 138 us -> 137 us (level)
  Pallas kernels: 51 us -> 66.2 us
  waiting for transfers between devices: 38.7 us -> 29.1 us
  starting transfers between devices: 32.9 us -> 26.9 us
  other arithmetic: 5.69 us -> 3.52 us
    pallas_call x2 -> x4, Pallas kernels: 30.7 us -> 41.2 us  [embed(): pl.pallas_call(functools.partial(cnn_kernel, widths=widths, filters=filte...]
    ppermute x29, waiting for transfers between devices: 38.7 us -> 29.1 us  [swap(): return lax.ppermute(x, axes, [(i, i ^ bits) for i in range(devices)])]
    ppermute x29, starting transfers between devices: 32.9 us -> 26.9 us  [swap(): return lax.ppermute(x, axes, [(i, i ^ bits) for i in range(devices)])]
    pallas_call x1, Pallas kernels: 5.77 us -> 11 us  [first_fold(): pl.pallas_call(functools.partial(first_kernel, nh=len(hid), nw=len(words)...]
    slice x4 -> x2, local copies, waits for them, and re-layouts: 2.31 us -> 0.01 us  [per_device(): chars = chars[:n] + swap(chars[n:], bit)]
    concatenate x4 -> x1, other arithmetic: 2.08 us -> 0.02 us  [per_device(): rows = jnp.concatenate([rows, swap(rows, bit)], axis=0)]
    optimization_barrier x0 -> x2, local copies, waits for them, and re-layouts: none -> 1.72 us  [the longest x1 0.86 us: per_device(): *hid, ids_far, ids = lax.optimization_barrier((*hid, ids_far, ids))]
    unnamed x45 -> x57, local copies, waits for them, and re-layouts: 4.73 us -> 5.35 us
  transfers between devices with their start and end apart: 29 -> 29, of which waited for: 15 -> 9; matrix products, arithmetic and copies ran while one was open for 6% -> 5% of each run, Pallas kernels for 28% -> 46%
where the time goes in v2:
time: 137 us; the launch traced here: 136 us
  Pallas kernels  66.2 us (48%)
  waiting for transfers between devices  29.1 us (21%)
  starting transfers between devices  26.9 us (20%)
  local copies, waits for them, and re-layouts  9.5 us (7%)
  other arithmetic  3.52 us (3%)
    pallas_call x4, Pallas kernels, embed(): pl.pallas_call(functools.partial(cnn_kernel, widths=widths, filters=filte...  41.2 us
    ppermute x29, waiting for transfers between devices, swap(): return lax.ppermute(x, axes, [(i, i ^ bits) for i in range(devices)])  29.1 us
    ppermute x29, starting transfers between devices, swap(): return lax.ppermute(x, axes, [(i, i ^ bits) for i in range(devices)])  26.9 us
    pallas_call x1, Pallas kernels, first_fold(): pl.pallas_call(functools.partial(first_kernel, nh=len(hid), nw=len(words)...  11 us
    unnamed x57, local copies, waits for them, and re-layouts  5.35 us
    pallas_call x1, Pallas kernels, second_fold(): pl.pallas_call(functools.partial(second_kernel, nh=len(hid), nw=len(words...  4.79 us
    pallas_call x1, Pallas kernels, pick(): pl.pallas_call(functools.partial(pick_kernel, nh=len(hid), order=order, l...  2.85 us
  transfers between devices with their start and end apart: 29, of which 9 were waited for; matrix products, arithmetic and copies ran while one was open for 5% of the time, Pallas kernels for 46%

profile of v2, /device:TPU:0, one launch (start us, length us, event | category | flops | bytes accessed | tf_op | source)
XLA Modules:
  0.0 136.2 jit_solution(3682073385593860020)
XLA Ops:
  2.1 2.6 %collective-permute-start.2 = (bf16[50,512]{1,0:T(8,128)(2,1)S(1)}, bf16[50,512]{1,0:T(8,128)(2,1)S(1)}, u32[]{:S(2)}, u32[]{:S(2)}) collective-permute-start(bf16[50,512]{1,0:T(8,128)(2,1)S(1)} %convert_bitcast_fusion.refs_4_), channel_id=1, source_target_pairs={{0,1},{1,0},{2,3},{3,2},{4,5},{5,4},{6,7},{7,6},{8,9},{9,8},{10,11... | collective-permute-start | bytes 153608 | tf_op jit(solution)/shard_map/ppermute | solution.py:443
  6.6 2.7 %collective-permute-start = (bf16[64,1152]{1,0:T(8,128)(2,1)S(1)}, bf16[64,1152]{1,0:T(8,128)(2,1)S(1)}, u32[]{:S(2)}, u32[]{:S(2)}) collective-permute-start(bf16[64,1152]{1,0:T(8,128)(2,1)S(1)} %concatenate.9), channel_id=1, source_target_pairs={{0,2},{1,3},{2,0},{3,1},{4,6},{5,7},{6,4},{7,5},{8,10},{9,11},{10,... | collective-permute-start | bytes 442376 | tf_op jit(solution)/shard_map/ppermute | solution.py:443
  9.3 1.8 %copy.13.ids_ref = s32[512,50]{1,0:T(8,128)} copy(s32[512,50]{0,1:T(8,128)} %param.9) | data formatting | bytes 204800 | tf_op args[0]
  12.3 11.3 %embed.4.refs_4_ = bf16[192,1024]{1,0:T(8,128)(2,1)} custom-call(s32[512,50]{1,0:T(8,128)} %copy.13.ids_ref, f32[16,256]{1,0:T(8,128)} %convert_bitcast_fusion.1.tab_ref, bf16[112,896]{1,0:T(8,128)(2,1)} %conv_ref.7, f32[2,1024]{1,0:T(2,128)} %bias_ref.7, bf16[896,1024]{1,0:T(8,128)(2,1)} %proj_hbm.7, bf16[2,1024,1024]{2,1,0:T(8,128)(2,1)} %gate_hbm.7, ...), custom_call_target="tpu_custom_call" | custom-call | flops 6366953472 | bytes 12582912 | tf_op jit(solution)/shard_map/embed/pallas_call | solution.py:129
  25.1 11.3 %embed.6.refs_5_ = bf16[192,1024]{1,0:T(8,128)(2,1)} custom-call(s32[512,50]{1,0:T(8,128)} %copy.15.ids_ref, f32[16,256]{1,0:T(8,128)} %convert_bitcast_fusion.1.tab_ref, bf16[112,896]{1,0:T(8,128)(2,1)} %conv_ref.7, f32[2,1024]{1,0:T(2,128)} %bias_ref.7, bf16[896,1024]{1,0:T(8,128)(2,1)} %proj_hbm.7, bf16[2,1024,1024]{2,1,0:T(8,128)(2,1)} %gate_hbm.7, ...), custom_call_target="tpu_custom_call" | custom-call | flops 6366953472 | bytes 12582912 | tf_op jit(solution)/shard_map/embed/pallas_call | solution.py:129
  36.5 1.6 %collective-permute-start.13 = (bf16[192,1024]{1,0:T(8,128)(2,1)}, bf16[192,1024]{1,0:T(8,128)(2,1)S(1)}, u32[]{:S(2)}, u32[]{:S(2)}) collective-permute-start(bf16[192,1024]{1,0:T(8,128)(2,1)} %embed.6.refs_5_), channel_id=1, source_target_pairs={{0,1},{1,0},{2,3},{3,2},{4,5},{5,4},{6,7},{7,6},{8,9},{9,8},{10,11... | collective-permute-start | bytes 1179656 | tf_op jit(solution)/shard_map/ppermute | solution.py:443
  38.1 1.5 %collective-permute-start.3 = (bf16[128,1152]{1,0:T(8,128)(2,1)S(1)}, bf16[128,1152]{1,0:T(8,128)(2,1)S(1)}, u32[]{:S(2)}, u32[]{:S(2)}) collective-permute-start(bf16[128,1152]{1,0:T(8,128)(2,1)S(1)} %pad_maximum_fusion.refs_0_), channel_id=1, source_target_pairs={{0,16},{1,17},{2,18},{3,19},{4,20},{5,21},{6,22},{7,23},{8,24},{9,... | collective-permute-start | bytes 884744 | tf_op jit(solution)/shard_map/ppermute | solution.py:443
  41.9 5.6 %collective-permute-done.3.refs_1_ = bf16[128,1152]{1,0:T(8,128)(2,1)S(1)} collective-permute-done((bf16[128,1152]{1,0:T(8,128)(2,1)S(1)}, bf16[128,1152]{1,0:T(8,128)(2,1)S(1)}, u32[]{:S(2)}, u32[]{:S(2)}) %collective-permute-start.3) | collective-permute-done | bytes 294944 | tf_op jit(solution)/shard_map/ppermute | solution.py:443
  47.5 1.9 %collective-permute-done.4.refs_2_ = bf16[128,1152]{1,0:T(8,128)(2,1)S(1)} collective-permute-done((bf16[128,1152]{1,0:T(8,128)(2,1)S(1)}, bf16[128,1152]{1,0:T(8,128)(2,1)S(1)}, u32[]{:S(2)}, u32[]{:S(2)}) %collective-permute-start.4) | collective-permute-done | bytes 294944 | tf_op jit(solution)/shard_map/ppermute | solution.py:443
  49.5 5.5 %collective-permute-done.5.refs_3_ = bf16[128,1152]{1,0:T(8,128)(2,1)S(1)} collective-permute-done((bf16[128,1152]{1,0:T(8,128)(2,1)S(1)}, bf16[128,1152]{1,0:T(8,128)(2,1)S(1)}, u32[]{:S(2)}, u32[]{:S(2)}) %collective-permute-start.5) | collective-permute-done | bytes 294944 | tf_op jit(solution)/shard_map/ppermute | solution.py:443
  55.9 9.2 %embed.5.refs_6_ = bf16[128,1024]{1,0:T(8,128)(2,1)} custom-call(s32[512,50]{1,0:T(8,128)} %copy.14.ids_ref, f32[16,256]{1,0:T(8,128)} %convert_bitcast_fusion.1.tab_ref, bf16[112,896]{1,0:T(8,128)(2,1)} %conv_ref.7, f32[2,1024]{1,0:T(2,128)} %bias_ref.7, bf16[896,1024]{1,0:T(8,128)(2,1)} %proj_hbm.7, bf16[2,1024,1024]{2,1,0:T(8,128)(2,1)} %gate_hbm.7, ...), custom_call_target="tpu_custom_call" | custom-call | flops 4244635648 | bytes 12582912 | tf_op jit(solution)/shard_map/embed/pallas_call | solution.py:129
  65.8 2.8 %pick.1 = (bf16[256,50]{1,0:T(8,128)(2,1)}, bf16[256,50]{1,0:T(8,128)(2,1)}) custom-call(s32[1]{0:T(128)} %bitcast.4.me_ref, bf16[128,1152]{1,0:T(8,128)(2,1)} %copy-done.1, bf16[128,1152]{1,0:T(8,128)(2,1)} %copy-done.2, bf16[128,1152]{1,0:T(8,128)(2,1)} %copy-done.3, bf16[128,1152]{1,0:T(8,128)(2,1)} %copy-done.4, bf16[50,512]{1,0:T(8,128)(2,1)} %copy-done.13, ...), custom_call_target="tpu_custom_call" | custom-call | flops 536870912 | bytes 2097152 | tf_op jit(solution)/shard_map/pick/pallas_call | solution.py:183
  68.6 1.6 %collective-permute-start.26 = (bf16[256,50]{1,0:T(8,128)(2,1)}, bf16[256,50]{1,0:T(8,128)(2,1)S(1)}, u32[]{:S(2)}, u32[]{:S(2)}) collective-permute-start(bf16[256,50]{1,0:T(8,128)(2,1)} %get-tuple-element.61), channel_id=1, source_target_pairs={{0,8},{1,9},{2,10},{3,11},{4,12},{5,13},{6,14},{7,15},{8,0},{9,1},... | collective-permute-start | bytes 76808 | tf_op jit(solution)/shard_map/ppermute | solution.py:443
  70.2 3.8 %collective-permute-done.7.refs_4_ = bf16[128,1024]{1,0:T(8,128)(2,1)S(1)} collective-permute-done((bf16[128,1024]{1,0:T(8,128)(2,1)}, bf16[128,1024]{1,0:T(8,128)(2,1)S(1)}, u32[]{:S(2)}, u32[]{:S(2)}) %collective-permute-start.7) | collective-permute-done | bytes 262176 | tf_op jit(solution)/shard_map/ppermute | solution.py:443
  74.8 11.0 %first_fold.1 = (f32[512,1024]{1,0:T(8,128)}, f32[512,128]{1,0:T(8,128)}, f32[512,128]{1,0:T(8,128)}) custom-call(bf16[128,1152]{1,0:T(8,128)(2,1)} %copy-done.1, bf16[128,1152]{1,0:T(8,128)(2,1)} %copy-done.2, bf16[128,1152]{1,0:T(8,128)(2,1)} %copy-done.3, bf16[128,1152]{1,0:T(8,128)(2,1)} %copy-done.4, bf16[192,1024]{1,0:T(8,128)(2,1)} %embed.4.refs_4_, ...), custom_call_target="tpu_custom_call" | custom-call | flops 3758096384 | bytes 4718592 | tf_op jit(solution)/shard_map/first_fold/pallas_call | solution.py:255
  86.5 4.8 %second_fold.1 = (bf16[256,512]{1,0:T(8,128)(2,1)}, bf16[256,512]{1,0:T(8,128)(2,1)}, bf16[256,512]{1,0:T(8,128)(2,1)}, bf16[256,512]{1,0:T(8,128)(2,1)}, f32[4,128]{1,0:T(4,128)}) custom-call(bf16[128,1152]{1,0:T(8,128)(2,1)} %copy-done.1, bf16[128,1152]{1,0:T(8,128)(2,1)} %copy-done.2, bf16[128,1152]{1,0:T(8,128)(2,1)} %copy-done.3, ...), custom_call_target="tpu_custom_call" | custom-call | flops 536870912 | bytes 1572864 | tf_op jit(solution)/shard_map/second_fold/pallas_call | solution.py:300
  94.9 7.2 %collective-permute-done.27 = bf16[128,50]{1,0:T(8,128)(2,1)S(1)} collective-permute-done((bf16[128,50]{1,0:T(8,128)(2,1)S(1)}, bf16[128,50]{1,0:T(8,128)(2,1)S(1)}, u32[]{:S(2)}, u32[]{:S(2)}) %collective-permute-start.27) | collective-permute-done | bytes 12832 | tf_op jit(solution)/shard_map/ppermute | solution.py:443
  104.5 1.8 %collective-permute-done.18.a_lse = f32[4,128]{1,0:T(4,128)S(1)} collective-permute-done((f32[4,128]{1,0:T(4,128)}, f32[4,128]{1,0:T(4,128)S(1)}, u32[]{:S(2)}, u32[]{:S(2)}) %collective-permute-start.18) | collective-permute-done | bytes 2080 | tf_op jit(solution)/shard_map/ppermute | solution.py:443
  107.6 2.3 %merge_one.1 = (bf16[128,512]{1,0:T(8,128)(2,1)}, bf16[128,512]{1,0:T(8,128)(2,1)}, bf16[128,512]{1,0:T(8,128)(2,1)}, bf16[128,512]{1,0:T(8,128)(2,1)}, f32[2,128]{1,0:T(2,128)}, /*index=5*/f32[2,128]{1,0:T(2,128)}) custom-call(bf16[256,512]{1,0:T(8,128)(2,1)} %get-tuple-element.44.a_keep, bf16[256,512]{1,0:T(8,128)(2,1)} %copy-done.7, ...), custom_call_target="tpu_custom_call" | custom-call | flops 524288 | bytes 1572864 | tf_op jit(solution)/shard_map/merge_one/pallas_call | solution.py:344
  114.6 2.1 %collective-permute-done.22.a_lse = f32[2,128]{1,0:T(2,128)S(1)} collective-permute-done((f32[2,128]{1,0:T(2,128)}, f32[2,128]{1,0:T(2,128)S(1)}, u32[]{:S(2)}, u32[]{:S(2)}) %collective-permute-start.22) | collective-permute-done | bytes 1056 | tf_op jit(solution)/shard_map/ppermute | solution.py:443
  117.9 2.0 %merge_two.1 = (bf16[64,1024]{1,0:T(8,128)(2,1)}, bf16[64,1024]{1,0:T(8,128)(2,1)}, f32[2,128]{1,0:T(2,128)}) custom-call(bf16[128,512]{1,0:T(8,128)(2,1)} %get-tuple-element.49.a_keep, bf16[128,512]{1,0:T(8,128)(2,1)} %copy-done.9, bf16[128,512]{1,0:T(8,128)(2,1)} %get-tuple-element.51.b_keep, bf16[128,512]{1,0:T(8,128)(2,1)} %copy-done.10, ...), custom_call_target="tpu_custom_call" | custom-call | flops 524288 | bytes 786432 | tf_op jit(solution)/shard_map/merge_two/pallas_call | solution.py:373
  120.0 2.6 %collective-permute-start.24 = (bf16[64,1024]{1,0:T(8,128)(2,1)}, bf16[64,1024]{1,0:T(8,128)(2,1)S(1)}, u32[]{:S(2)}, u32[]{:S(2)}) collective-permute-start(bf16[64,1024]{1,0:T(8,128)(2,1)} %get-tuple-element.56), channel_id=1, source_target_pairs={{0,2},{1,3},{2,0},{3,1},{4,6},{5,7},{6,4},{7,5},{8,10},{9,11},{10,... | collective-permute-start | bytes 393224 | tf_op jit(solution)/shard_map/ppermute | solution.py:443
  122.9 9.4 %embed.7.target = bf16[64,1024]{1,0:T(8,128)(2,1)} custom-call(bf16[64,50]{1,0:T(8,128)(2,1)} %slice_add_fusion.1.ids_ref, f32[16,256]{1,0:T(8,128)} %convert_bitcast_fusion.1.tab_ref, bf16[112,896]{1,0:T(8,128)(2,1)} %conv_ref.7, f32[2,1024]{1,0:T(2,128)} %bias_ref.7, bf16[896,1024]{1,0:T(8,128)(2,1)} %proj_hbm.7, bf16[2,1024,1024]{2,1,0:T(8,128)(2,1)} %gate_hbm.7, ...), custom_call_target="tpu_custom_call" | custom-call | flops 2122317824 | bytes 12582912 | tf_op jit(solution)/shard_map/embed/pallas_call | solution.py:129
  133.0 2.1 %finish.1 = (f32[1,128]{1,0:T(1,128)}, bf16[64,1024]{1,0:T(8,128)(2,1)}) custom-call(bf16[64,1024]{1,0:T(8,128)(2,1)} %get-tuple-element.55.keep, bf16[64,1024]{1,0:T(8,128)(2,1)} %copy-done.11, f32[2,128]{1,0:T(2,128)} %get-tuple-element.57.lines, f32[2,128]{1,0:T(2,128)} %copy-done.18, bf16[64,1024]{1,0:T(8,128)(2,1)} %hid.1, bf16[64,1024]{1,0:T(8,128)(2,1)} %embed.7.target), custom_call_target="tpu_custom_call" | custom-call | flops 524288 | bytes 786432 | tf_op jit(solution)/shard_map/finish/pallas_call | solution.py:399
  (117 shorter events, 26.7 us)
Async XLA Ops:
  1.6 22.7 %collective-permute-start.1 = (bf16[50,512]{1,0:T(8,128)(2,1)S(1)}, bf16[50,512]{1,0:T(8,128)(2,1)S(1)}, u32[]{:S(2)}, u32[]{:S(2)}) collective-permute-start(bf16[50,512]{1,0:T(8,128)(2,1)S(1)} %convert_bitcast_fusion.refs_4_), channel_id=1, source_target_pairs={{0,4},{1,5},{2,6},{3,7},{4,0},{5,1},{6,2},{7,3},{8,12},{9,13},{10,... | collective-permute-start | bytes 153608 | tf_op jit(solution)/shard_map/ppermute | solution.py:443
  2.1 22.2 %collective-permute-start.2 = (bf16[50,512]{1,0:T(8,128)(2,1)S(1)}, bf16[50,512]{1,0:T(8,128)(2,1)S(1)}, u32[]{:S(2)}, u32[]{:S(2)}) collective-permute-start(bf16[50,512]{1,0:T(8,128)(2,1)S(1)} %convert_bitcast_fusion.refs_4_), channel_id=1, source_target_pairs={{0,1},{1,0},{2,3},{3,2},{4,5},{5,4},{6,7},{7,6},{8,9},{9,8},{10,11... | collective-permute-start | bytes 153608 | tf_op jit(solution)/shard_map/ppermute | solution.py:443
  6.6 17.6 %collective-permute-start = (bf16[64,1152]{1,0:T(8,128)(2,1)S(1)}, bf16[64,1152]{1,0:T(8,128)(2,1)S(1)}, u32[]{:S(2)}, u32[]{:S(2)}) collective-permute-start(bf16[64,1152]{1,0:T(8,128)(2,1)S(1)} %concatenate.9), channel_id=1, source_target_pairs={{0,2},{1,3},{2,0},{3,1},{4,6},{5,7},{6,4},{7,5},{8,10},{9,11},{10,... | collective-permute-start | bytes 442376 | tf_op jit(solution)/shard_map/ppermute | solution.py:443
  23.7 18.2 %collective-permute-start.12 = (bf16[192,1024]{1,0:T(8,128)(2,1)}, bf16[192,1024]{1,0:T(8,128)(2,1)S(1)}, u32[]{:S(2)}, u32[]{:S(2)}) collective-permute-start(bf16[192,1024]{1,0:T(8,128)(2,1)} %embed.4.refs_4_), channel_id=1, source_target_pairs={{0,1},{1,0},{2,3},{3,2},{4,5},{5,4},{6,7},{7,6},{8,9},{9,8},{10,11... | collective-permute-start | bytes 1179656 | tf_op jit(solution)/shard_map/ppermute | solution.py:443
  36.5 19.4 %collective-permute-start.13 = (bf16[192,1024]{1,0:T(8,128)(2,1)}, bf16[192,1024]{1,0:T(8,128)(2,1)S(1)}, u32[]{:S(2)}, u32[]{:S(2)}) collective-permute-start(bf16[192,1024]{1,0:T(8,128)(2,1)} %embed.6.refs_5_), channel_id=1, source_target_pairs={{0,1},{1,0},{2,3},{3,2},{4,5},{5,4},{6,7},{7,6},{8,9},{9,8},{10,11... | collective-permute-start | bytes 1179656 | tf_op jit(solution)/shard_map/ppermute | solution.py:443
  38.1 9.4 %collective-permute-start.3 = (bf16[128,1152]{1,0:T(8,128)(2,1)S(1)}, bf16[128,1152]{1,0:T(8,128)(2,1)S(1)}, u32[]{:S(2)}, u32[]{:S(2)}) collective-permute-start(bf16[128,1152]{1,0:T(8,128)(2,1)S(1)} %pad_maximum_fusion.refs_0_), channel_id=1, source_target_pairs={{0,16},{1,17},{2,18},{3,19},{4,20},{5,21},{6,22},{7,23},{8,24},{9,... | collective-permute-start | bytes 884744 | tf_op jit(solution)/shard_map/ppermute | solution.py:443
  39.7 9.8 %collective-permute-start.4 = (bf16[128,1152]{1,0:T(8,128)(2,1)S(1)}, bf16[128,1152]{1,0:T(8,128)(2,1)S(1)}, u32[]{:S(2)}, u32[]{:S(2)}) collective-permute-start(bf16[128,1152]{1,0:T(8,128)(2,1)S(1)} %pad_maximum_fusion.refs_0_), channel_id=1, source_target_pairs={{0,8},{1,9},{2,10},{3,11},{4,12},{5,13},{6,14},{7,15},{8,0},{9,1},... | collective-permute-start | bytes 884744 | tf_op jit(solution)/shard_map/ppermute | solution.py:443
  41.1 13.9 %collective-permute-start.5 = (bf16[128,1152]{1,0:T(8,128)(2,1)S(1)}, bf16[128,1152]{1,0:T(8,128)(2,1)S(1)}, u32[]{:S(2)}, u32[]{:S(2)}) collective-permute-start(bf16[128,1152]{1,0:T(8,128)(2,1)S(1)} %pad_maximum_fusion.refs_0_), channel_id=1, source_target_pairs={{0,24},{1,25},{2,26},{3,27},{4,28},{5,29},{6,30},{7,31},{8,16},{9,... | collective-permute-start | bytes 884744 | tf_op jit(solution)/shard_map/ppermute | solution.py:443
  41.8 23.9 %collective-permute-start.9 = (bf16[192,1024]{1,0:T(8,128)(2,1)S(1)}, bf16[192,1024]{1,0:T(8,128)(2,1)S(1)}, u32[]{:S(2)}, u32[]{:S(2)}) collective-permute-start(bf16[192,1024]{1,0:T(8,128)(2,1)S(1)} %copy-done.19), channel_id=1, source_target_pairs={{0,4},{1,5},{2,6},{3,7},{4,0},{5,1},{6,2},{7,3},{8,12},{9,13},{10,... | collective-permute-start | bytes 1179656 | tf_op jit(solution)/shard_map/ppermute | solution.py:443
  47.5 21.1 %collective-permute-start.10 = (bf16[192,1024]{1,0:T(8,128)(2,1)}, bf16[192,1024]{1,0:T(8,128)(2,1)S(1)}, u32[]{:S(2)}, u32[]{:S(2)}) collective-permute-start(bf16[192,1024]{1,0:T(8,128)(2,1)} %embed.6.refs_5_), channel_id=1, source_target_pairs={{0,4},{1,5},{2,6},{3,7},{4,0},{5,1},{6,2},{7,3},{8,12},{9,13},{10,... | collective-permute-start | bytes 1179656 | tf_op jit(solution)/shard_map/ppermute | solution.py:443
  49.5 24.5 %collective-permute-start.14 = (bf16[192,1024]{1,0:T(8,128)(2,1)S(1)}, bf16[192,1024]{1,0:T(8,128)(2,1)}, u32[]{:S(2)}, u32[]{:S(2)}) collective-permute-start(bf16[192,1024]{1,0:T(8,128)(2,1)S(1)} %collective-permute-done.12.refs_10_), channel_id=1, source_target_pairs={{0,4},{1,5},{2,6},{3,7},{4,0},{5,1},{6,2},{7,3},{8,12},{9,13},{10,... | collective-permute-start | bytes 1179656 | tf_op jit(solution)/shard_map/ppermute | solution.py:443
  55.9 18.1 %collective-permute-start.15 = (bf16[192,1024]{1,0:T(8,128)(2,1)S(1)}, bf16[192,1024]{1,0:T(8,128)(2,1)}, u32[]{:S(2)}, u32[]{:S(2)}) collective-permute-start(bf16[192,1024]{1,0:T(8,128)(2,1)S(1)} %collective-permute-done.13.refs_11_), channel_id=1, source_target_pairs={{0,4},{1,5},{2,6},{3,7},{4,0},{5,1},{6,2},{7,3},{8,12},{9,13},{10,... | collective-permute-start | bytes 1179656 | tf_op jit(solution)/shard_map/ppermute | solution.py:443
  65.2 8.8 %collective-permute-start.7 = (bf16[128,1024]{1,0:T(8,128)(2,1)}, bf16[128,1024]{1,0:T(8,128)(2,1)S(1)}, u32[]{:S(2)}, u32[]{:S(2)}) collective-permute-start(bf16[128,1024]{1,0:T(8,128)(2,1)} %embed.5.refs_6_), channel_id=1, source_target_pairs={{0,1},{1,0},{2,3},{3,2},{4,5},{5,4},{6,7},{7,6},{8,9},{9,8},{10,11... | collective-permute-start | bytes 786440 | tf_op jit(solution)/shard_map/ppermute | solution.py:443
  65.7 8.3 %collective-permute-start.11 = (bf16[128,1024]{1,0:T(8,128)(2,1)}, bf16[128,1024]{1,0:T(8,128)(2,1)S(1)}, u32[]{:S(2)}, u32[]{:S(2)}) collective-permute-start(bf16[128,1024]{1,0:T(8,128)(2,1)} %embed.5.refs_6_), channel_id=1, source_target_pairs={{0,4},{1,5},{2,6},{3,7},{4,0},{5,1},{6,2},{7,3},{8,12},{9,13},{10,... | collective-permute-start | bytes 786440 | tf_op jit(solution)/shard_map/ppermute | solution.py:443
  68.6 25.7 %collective-permute-start.26 = (bf16[256,50]{1,0:T(8,128)(2,1)}, bf16[256,50]{1,0:T(8,128)(2,1)S(1)}, u32[]{:S(2)}, u32[]{:S(2)}) collective-permute-start(bf16[256,50]{1,0:T(8,128)(2,1)} %get-tuple-element.61), channel_id=1, source_target_pairs={{0,8},{1,9},{2,10},{3,11},{4,12},{5,13},{6,14},{7,15},{8,0},{9,1},... | collective-permute-start | bytes 76808 | tf_op jit(solution)/shard_map/ppermute | solution.py:443
  74.0 11.8 %collective-permute-start.8 = (bf16[128,1024]{1,0:T(8,128)(2,1)S(1)}, bf16[128,1024]{1,0:T(8,128)(2,1)S(1)}, u32[]{:S(2)}, u32[]{:S(2)}) collective-permute-start(bf16[128,1024]{1,0:T(8,128)(2,1)S(1)} %collective-permute-done.7.refs_4_), channel_id=1, source_target_pairs={{0,4},{1,5},{2,6},{3,7},{4,0},{5,1},{6,2},{7,3},{8,12},{9,13},{10,... | collective-permute-start | bytes 786440 | tf_op jit(solution)/shard_map/ppermute | solution.py:443
  91.3 15.6 %collective-permute-start.16 = (bf16[256,512]{1,0:T(8,128)(2,1)}, bf16[256,512]{1,0:T(8,128)(2,1)S(1)}, u32[]{:S(2)}, u32[]{:S(2)}) collective-permute-start(bf16[256,512]{1,0:T(8,128)(2,1)} %get-tuple-element.45), channel_id=1, source_target_pairs={{0,8},{1,9},{2,10},{3,11},{4,12},{5,13},{6,14},{7,15},{8,0},{9,1},... | collective-permute-start | bytes 786440 | tf_op jit(solution)/shard_map/ppermute | solution.py:443
  92.8 14.1 %collective-permute-start.17 = (bf16[256,512]{1,0:T(8,128)(2,1)}, bf16[256,512]{1,0:T(8,128)(2,1)S(1)}, u32[]{:S(2)}, u32[]{:S(2)}) collective-permute-start(bf16[256,512]{1,0:T(8,128)(2,1)} %get-tuple-element.47), channel_id=1, source_target_pairs={{0,16},{1,17},{2,18},{3,19},{4,20},{5,21},{6,22},{7,23},{8,24},{9,... | collective-permute-start | bytes 786440 | tf_op jit(solution)/shard_map/ppermute | solution.py:443
  94.3 7.7 %collective-permute-start.27 = (bf16[128,50]{1,0:T(8,128)(2,1)S(1)}, bf16[128,50]{1,0:T(8,128)(2,1)S(1)}, u32[]{:S(2)}, u32[]{:S(2)}) collective-permute-start(bf16[128,50]{1,0:T(8,128)(2,1)S(1)} %slice.21), channel_id=1, source_target_pairs={{0,16},{1,17},{2,18},{3,19},{4,20},{5,21},{6,22},{7,23},{8,24},{9,... | collective-permute-start | bytes 38408 | tf_op jit(solution)/shard_map/ppermute | solution.py:443
  102.1 11.9 %collective-permute-start.28 = (bf16[64,50]{1,0:T(8,128)(2,1)S(1)}, bf16[64,50]{1,0:T(8,128)(2,1)S(1)}, u32[]{:S(2)}, u32[]{:S(2)}) collective-permute-start(bf16[64,50]{1,0:T(8,128)(2,1)S(1)} %slice.23), channel_id=1, source_target_pairs={{0,2},{1,3},{2,0},{3,1},{4,6},{5,7},{6,4},{7,5},{8,10},{9,11},{10,... | collective-permute-start | bytes 19208 | tf_op jit(solution)/shard_map/ppermute | solution.py:443
  109.9 7.3 %collective-permute-start.20 = (bf16[128,512]{1,0:T(8,128)(2,1)}, bf16[128,512]{1,0:T(8,128)(2,1)S(1)}, u32[]{:S(2)}, u32[]{:S(2)}) collective-permute-start(bf16[128,512]{1,0:T(8,128)(2,1)} %get-tuple-element.50), channel_id=1, source_target_pairs={{0,16},{1,17},{2,18},{3,19},{4,20},{5,21},{6,22},{7,23},{8,24},{9,... | collective-permute-start | bytes 393224 | tf_op jit(solution)/shard_map/ppermute | solution.py:443
  111.4 5.8 %collective-permute-start.21 = (bf16[128,512]{1,0:T(8,128)(2,1)}, bf16[128,512]{1,0:T(8,128)(2,1)S(1)}, u32[]{:S(2)}, u32[]{:S(2)}) collective-permute-start(bf16[128,512]{1,0:T(8,128)(2,1)} %get-tuple-element.52), channel_id=1, source_target_pairs={{0,8},{1,9},{2,10},{3,11},{4,12},{5,13},{6,14},{7,15},{8,0},{9,1},... | collective-permute-start | bytes 393224 | tf_op jit(solution)/shard_map/ppermute | solution.py:443
  120.0 12.3 %collective-permute-start.24 = (bf16[64,1024]{1,0:T(8,128)(2,1)}, bf16[64,1024]{1,0:T(8,128)(2,1)S(1)}, u32[]{:S(2)}, u32[]{:S(2)}) collective-permute-start(bf16[64,1024]{1,0:T(8,128)(2,1)} %get-tuple-element.56), channel_id=1, source_target_pairs={{0,2},{1,3},{2,0},{3,1},{4,6},{5,7},{6,4},{7,5},{8,10},{9,11},{10,... | collective-permute-start | bytes 393224 | tf_op jit(solution)/shard_map/ppermute | solution.py:443
  122.5 9.7 %collective-permute-start.25 = (f32[2,128]{1,0:T(2,128)}, f32[2,128]{1,0:T(2,128)S(1)}, u32[]{:S(2)}, u32[]{:S(2)}) collective-permute-start(f32[2,128]{1,0:T(2,128)} %get-tuple-element.57.lines), channel_id=1, source_target_pairs={{0,2},{1,3},{2,0},{3,1},{4,6},{5,7},{6,4},{7,5},{8,10},{9,11},{10,... | collective-permute-start | bytes 3080 | tf_op jit(solution)/shard_map/ppermute | solution.py:443
  (33 other events, 253.7 us)

commit v3 on v2

v3 whole, which is shorter than its diff:
```python
import functools
import jax
import jax.numpy as jnp
from jax import lax
from jax.experimental import pallas as pl
from jax.experimental.pallas import tpu as pltpu
from jax.sharding import PartitionSpec as P

bf16=jnp.bfloat16; f32=jnp.float32
LANES = 128
SPAN = 8

def prep_toeplitz(conv_ref, toep, ce, widths, filters):
    depth = toep.shape[0]
    for k in range(widths):
        rows = (k + 1) * ce
        piece = conv_ref[0:rows, k * filters:(k + 1) * filters]
        for o in range(SPAN):
            cols = slice((k * SPAN + o) * filters, (k * SPAN + o + 1) * filters)
            if o:
                toep[0:o * ce, cols] = jnp.zeros((o * ce, filters), bf16)
            toep[o * ce:o * ce + rows, cols] = piece
            rest = depth - o * ce - rows
            if rest:
                toep[o * ce + rows:depth, cols] = jnp.zeros((rest, filters), bf16)

def lookup(ids_ref, start, words, tab_ref, vec, turn, length, ce):
    per = LANES // ce
    for at in range(0, words, LANES):
        count = min(LANES, words - at)
        turn[...] = jnp.zeros(turn.shape, f32)
        turn[0:count, 0:length] = ids_ref[start + at:start + at + count, 0:length].astype(f32)
        ids = turn[...].T.astype(jnp.int32)
        for g in range(vec.shape[1] // LANES):
            parts = []
            for q in range(per):
                p = g * per + q
                if p >= length:
                    parts.append(jnp.zeros((ce, LANES), f32))
                    continue
                idx = jnp.broadcast_to(ids[p:p + 1, :], (8, LANES))
                low = jnp.bitwise_and(idx, LANES - 1)
                top = idx >= LANES
                for h in range(ce // 8):
                    one = jnp.take_along_axis(tab_ref[h * 8:h * 8 + 8, 0:LANES], low, axis=1)
                    two = jnp.take_along_axis(tab_ref[h * 8:h * 8 + 8, LANES:2 * LANES], low, axis=1)
                    parts.append(jnp.where(top, two, one))
            block = jnp.concatenate(parts, axis=0)
            vec[at:at + count, g * LANES:(g + 1) * LANES] = block.T[0:count].astype(bf16)


def conv_pool(vec, toep, acc, length, widths, filters):
    words = vec.shape[0]
    def tile(b, k, o, lhs):
        cols = slice((k * SPAN + o) * filters, (k * SPAN + o + 2) * filters)
        return jnp.dot(lhs, toep[:, cols], preferred_element_type=f32)
    acc[...] = jnp.full(acc.shape, -jnp.inf, f32)
    least = (length - widths + 1) // SPAN
    def body(b, _):
        lhs = vec[:, pl.ds(pl.multiple_of(b * LANES, LANES), 2 * LANES)]
        for k in range(widths):
            best = acc[:, k * filters:(k + 1) * filters]
            for o in range(0, SPAN, 2):
                r = tile(b, k, o, lhs)
                best = jnp.maximum(best, jnp.maximum(r[:, :filters], r[:, filters:]))
            acc[:, k * filters:(k + 1) * filters] = best
        return 0
    lax.fori_loop(0, least, body, 0)
    for b in range(least, -(-length // SPAN)):
        lhs = vec[:, b * LANES:(b + 2) * LANES]
        for k in range(widths):
            usable = min(SPAN, length - k - b * SPAN)
            if usable <= 0: continue
            best = acc[:, k * filters:(k + 1) * filters]
            for o in range(0, usable, 2):
                r = tile(b, k, o, lhs)
                best = jnp.maximum(best, r[:, :filters])
                if o + 1 < usable:
                    best = jnp.maximum(best, r[:, filters:])
            acc[:, k * filters:(k + 1) * filters] = best

def cnn_kernel(ids_ref, tab_ref, conv_ref, bias_ref, proj_hbm, gate_hbm, trans_hbm, *rest,
               widths, filters, ce, length, layers, nt, start):
    out_ref, vec, toep, acc, feat, proj, gate, trans, state, last, turn, sems = rest
    copies = [pltpu.make_async_copy(s, d, sems.at[i]) for i, (s, d) in enumerate(
        ((proj_hbm, proj), (gate_hbm, gate), (trans_hbm, trans)))]
    for c in copies:
        c.start()
    words = out_ref.shape[0]
    prep_toeplitz(conv_ref, toep, ce, widths, filters)
    lookup(ids_ref, start, words, tab_ref, vec, turn, length, ce)
    conv_pool(vec, toep, acc, length, widths, filters)
    for c in copies:
        c.wait()
    feat[...] = jnp.tanh(acc[...]).astype(bf16)
    model = last.shape[1]
    for n in range(0, model, nt):
        state[:, n:n + nt] = jnp.dot(feat[...], proj[:, n:n + nt], preferred_element_type=f32).astype(bf16)
    for l in range(layers):
        for n in range(0, model, nt):
            cur = state[...]
            g = jnp.dot(cur, gate[l, :, n:n + nt], preferred_element_type=f32) + bias_ref[l:l + 1, n:n + nt]
            t = jnp.dot(cur, trans[l, :, n:n + nt], preferred_element_type=f32)
            opened = jax.nn.sigmoid(g)
            carried = jnp.maximum(t, 0.0)
            new = (opened * carried + (1.0 - opened) * state[:, n:n + nt].astype(f32)).astype(bf16)
            if l + 1 < layers:
                last[:, n:n + nt] = new
            else:
                out_ref[:, n:n + nt] = new
        if l + 1 < layers:
            state[...] = last[...]


ANY = pl.BlockSpec(memory_space=pl.ANY)
VM = pl.BlockSpec(memory_space=pltpu.VMEM)


def params(limit_mib=56):
    return pltpu.CompilerParams(vmem_limit_bytes=limit_mib << 20)


def embed(ids, length, start, words, tab_t, conv_weight, proj_weight, gate_weight, trans_weight, gate_bias, nt=256):
    ce = tab_t.shape[0]
    widths = conv_weight.shape[0] // ce
    filters = conv_weight.shape[1] // widths
    layers, model, _ = gate_weight.shape
    flops = 2 * words * (length * 256 * widths * filters + widths * filters * model + 2 * layers * model * model)
    return pl.pallas_call(
        functools.partial(cnn_kernel, widths=widths, filters=filters, ce=ce, length=length, layers=layers, nt=nt,
                          start=start),
        out_shape=jax.ShapeDtypeStruct((words, model), bf16),
        in_specs=[VM, VM, VM, VM, ANY, ANY, ANY],
        out_specs=VM,
        scratch_shapes=[
            pltpu.VMEM((words, (-(-length // SPAN) + 1) * LANES), bf16),
            pltpu.VMEM((2 * LANES, widths * SPAN * filters), bf16),
            pltpu.VMEM((words, widths * filters), f32),
            pltpu.VMEM((words, widths * filters), bf16),
            pltpu.VMEM(proj_weight.shape, bf16),
            pltpu.VMEM(gate_weight.shape, bf16),
            pltpu.VMEM(trans_weight.shape, bf16),
            pltpu.VMEM((words, model), bf16),
            pltpu.VMEM((words, model), bf16),
            pltpu.VMEM((LANES, LANES), f32),
            pltpu.SemaphoreType.DMA((3,)),
        ],
        compiler_params=params(),
        cost_estimate=pl.CostEstimate(flops=flops, bytes_accessed=12 << 20, transcendentals=words * 4096),
        name="embed",
    )(ids, tab_t, conv_weight, gate_bias, proj_weight, gate_weight, trans_weight)


def as_line(column):
    return jnp.broadcast_to(column, (LANES, LANES)).T[0:1, :]


def to_lines(column, out, at):
    for i in range(column.shape[0] // LANES):
        out[at + i:at + i + 1, :] = as_line(column[i * LANES:(i + 1) * LANES, :])


def aims(me_ref, hid, local):
    model = hid[0].shape[1] - LANES
    apart, place = [], []
    for h in hid:
        code = h[:, model:model + LANES].astype(f32).astype(jnp.int32)
        goal = code[:, 0:1] * 256 + code[:, 1:2]
        owner = lax.div(goal, local)
        apart.append(jnp.bitwise_xor(owner, me_ref[0]))
        place.append(goal - owner * local)
    return jnp.concatenate(apart, axis=0), jnp.concatenate(place, axis=0)


def spots(apart, place, meta):
    bits, start = meta
    return jnp.where(apart == bits, place - start, -1)


def scores_of(rows, words, metas, apart, place, score, prob):
    at, top, aim = 0, None, None
    for ref, meta in zip(words, metas):
        n = ref.shape[0]
        piece = lax.dot_general(rows[...], ref[...], (((1,), (1,)), ((), ())), preferred_element_type=f32)
        score[:, at:at + n] = piece
        lane = lax.broadcasted_iota(jnp.int32, piece.shape, 1)
        hit = jnp.sum(jnp.where(lane == spots(apart, place, meta), piece, 0.0), axis=1, keepdims=True)
        best = jnp.max(piece, axis=1, keepdims=True)
        top = best if top is None else jnp.maximum(top, best)
        aim = hit if aim is None else aim + hit
        at += n
    at, total = 0, None
    for ref in words:
        n = ref.shape[0]
        w = jnp.exp(score[:, at:at + n] - top).astype(bf16)
        prob[:, at:at + n] = w
        part = jnp.sum(w.astype(f32), axis=1, keepdims=True)
        total = part if total is None else total + part
        at += n
    return top, total, aim


def sums_of(words, metas, apart, place, prob, hot, out, target, before=None):
    at = 0
    for ref, meta in zip(words, metas):
        n = ref.shape[0]
        lane = lax.broadcasted_iota(jnp.int32, (prob.shape[0], n), 1)
        hot[:, at:at + n] = jnp.where(lane == spots(apart, place, meta), 1.0, 0.0).astype(bf16)
        at += n
    model = out.shape[1]
    for n in range(0, model, 256):
        at, res, aim = 0, None, None
        for ref in words:
            size = ref.shape[0]
            block = ref[:, n:n + 256]
            one = jnp.dot(prob[:, at:at + size], block, preferred_element_type=f32)
            two = jnp.dot(hot[:, at:at + size], block, preferred_element_type=f32)
            res = one if res is None else res + one
            aim = two if aim is None else aim + two
            at += size
        out[:, n:n + 256] = res
        if before is not None:
            aim = aim + before[:, n:n + 256].astype(f32)
        target[:, n:n + 256] = aim.astype(bf16)


def load_rows(hid, rows):
    at = 0
    for h in hid:
        rows[at:at + h.shape[0], :] = h[:, 0:rows.shape[1]]
        at += h.shape[0]


def first_kernel(me_ref, *refs, nh, metas, local):
    hid, words = refs[:nh], refs[nh:nh + len(metas)]
    out, target, stats, rows, score, prob, hot = refs[nh + len(metas):]
    load_rows(hid, rows)
    apart, place = aims(me_ref, hid, local)
    top, total, aim = scores_of(rows, words, metas, apart, place, score, prob)
    stats[:, 0:LANES] = jnp.broadcast_to(top, (top.shape[0], LANES))
    stats[:, LANES:2 * LANES] = jnp.broadcast_to(total, (top.shape[0], LANES))
    stats[:, 2 * LANES:3 * LANES] = jnp.broadcast_to(aim, (top.shape[0], LANES))
    sums_of(words, metas, apart, place, prob, hot, out, target)


def cost(flops, size, trans=0):
    return pl.CostEstimate(flops=flops, bytes_accessed=size, transcendentals=trans)


SM = pl.BlockSpec(memory_space=pltpu.SMEM)


def first_fold(me, hid, words, metas, local):
    model = words[0].shape[1]
    rows = sum(h.shape[0] for h in hid)
    count = sum(w.shape[0] for w in words)
    return pl.pallas_call(
        functools.partial(first_kernel, nh=len(hid), metas=metas, local=local),
        out_shape=[jax.ShapeDtypeStruct((rows, model), f32), jax.ShapeDtypeStruct((rows, model), bf16),
                   jax.ShapeDtypeStruct((rows, 3 * LANES), f32)],
        in_specs=[SM] + [VM] * (len(hid) + len(words)), out_specs=[VM] * 3,
        scratch_shapes=[pltpu.VMEM((rows, model), bf16), pltpu.VMEM((rows, count), f32),
                        pltpu.VMEM((rows, count), bf16), pltpu.VMEM((rows, count), bf16)],
        compiler_params=params(), cost_estimate=cost(6 * rows * count * model, 2 * (rows + count) * model),
        name="first_fold",
    )(me, *hid, *words)


def score_kernel(me_ref, *refs, nh, metas, local):
    hid, words = refs[:nh], refs[nh:nh + len(metas)]
    stats, prob, tops, lines, rows, score = refs[nh + len(metas):]
    load_rows(hid, rows)
    apart, place = aims(me_ref, hid, local)
    top2, total2, aim2 = scores_of(rows, words, metas, apart, place, score, prob)
    top1, total1 = stats[:, 0:1], stats[:, LANES:LANES + 1]
    top = jnp.maximum(top1, top2)
    total = jnp.exp(top1 - top) * total1 + jnp.exp(top2 - top) * total2
    tops[...] = jnp.broadcast_to(top2, tops.shape)
    to_lines(top + jnp.log(total), lines, 0)
    to_lines(stats[:, 2 * LANES:2 * LANES + 1] + aim2, lines, lines.shape[0] // 2)


def last_scores(me, hid, words, metas, local, stats):
    model = words[0].shape[1]
    rows = sum(h.shape[0] for h in hid)
    count = sum(w.shape[0] for w in words)
    return pl.pallas_call(
        functools.partial(score_kernel, nh=len(hid), metas=metas, local=local),
        out_shape=[jax.ShapeDtypeStruct((rows, count), bf16), jax.ShapeDtypeStruct((rows, LANES), f32),
                   jax.ShapeDtypeStruct((2 * rows // LANES, LANES), f32)],
        in_specs=[SM] + [VM] * (len(hid) + len(words) + 1), out_specs=[VM] * 3,
        scratch_shapes=[pltpu.VMEM((rows, model), bf16), pltpu.VMEM((rows, count), f32)],
        compiler_params=params(), cost_estimate=cost(2 * rows * count * model, 2 * (rows + count) * model),
        name="last_scores",
    )(me, *hid, *words, stats)


def sum_kernel(me_ref, *refs, nh, metas, local):
    hid, words = refs[:nh], refs[nh:nh + len(metas)]
    prob, before, out, target, hot = refs[nh + len(metas):]
    apart, place = aims(me_ref, hid, local)
    sums_of(words, metas, apart, place, prob, hot, out, target, before)


def last_sums(me, hid, words, metas, local, prob, before):
    rows, model = before.shape
    count = prob.shape[1]
    return pl.pallas_call(
        functools.partial(sum_kernel, nh=len(hid), metas=metas, local=local),
        out_shape=[jax.ShapeDtypeStruct((rows, model), f32), jax.ShapeDtypeStruct((rows, model), bf16)],
        in_specs=[SM] + [VM] * (len(hid) + len(words) + 2), out_specs=[VM] * 2,
        scratch_shapes=[pltpu.VMEM((rows, count), bf16)],
        compiler_params=params(), cost_estimate=cost(4 * rows * count * model, 2 * (rows + count) * model),
        name="last_sums",
    )(me, *hid, *words, prob, before)


def combine_kernel(*refs, flips):
    nl = len(flips)
    lines = refs[:nl]

    def value(j, i, kind):
        over, halves = flips[j]
        v = lines[j][kind * per + (i ^ over):kind * per + (i ^ over) + 1, :]
        return pltpu.roll(v, LANES // 2, axis=1) if halves else v

    one, two, target, stats, tops, a_keep, a_send, b_keep, b_send, loss = refs[nl:]
    per = lines[0].shape[0] // 2
    count, model = one.shape
    half, quarter = model // 2, count // 4
    for i in range(per):
        each = [value(j, i, 0) for j in range(nl)]
        top = each[0]
        for v in each[1:]:
            top = jnp.maximum(top, v)
        total = sum(jnp.exp(v - top) for v in each)
        aim = sum(value(j, i, 1) for j in range(nl))
        whole = top + jnp.log(total)
        if i == 0:
            loss[...] = whole - aim
        whole = jnp.broadcast_to(whole, (LANES, LANES)).T
        part = slice(i * LANES, (i + 1) * LANES)
        c1 = jnp.exp(stats[part, 0:LANES] - whole)
        c2 = jnp.exp(tops[part, :] - whole)
        q = i * LANES // quarter
        at = i * LANES - q * quarter
        a, b = (a_keep, a_send)[q // 2], (b_keep, b_send)[q % 2]
        a_at, b_at = (q % 2) * quarter + at, (q // 2) * quarter + at
        for n in range(0, model, LANES):
            cols = slice(n, n + LANES)
            mix = (c1 * one[part, cols] + c2 * two[part, cols] - target[part, cols].astype(f32)).astype(bf16)
            if n < half:
                a[a_at:a_at + LANES, cols] = mix
            else:
                b[b_at:b_at + LANES, n - half:n - half + LANES] = mix


def combine(lines, flips, one, two, target, stats, tops):
    rows, model = one.shape
    side = jax.ShapeDtypeStruct((rows // 2, model // 2), bf16)
    return pl.pallas_call(
        functools.partial(combine_kernel, flips=flips),
        out_shape=[side] * 4 + [jax.ShapeDtypeStruct((1, LANES), f32)],
        in_specs=[VM] * (len(lines) + 5), out_specs=[VM] * 5,
        compiler_params=params(), cost_estimate=cost(8 * rows * model, 12 * rows * model), name="combine",
    )(*lines, one, two, target, stats, tops)


def plus(a, b):
    return (a.astype(f32) + b.astype(f32)).astype(bf16)


def add_kernel(*refs):
    n = len(refs) // 4
    for i in range(n):
        keep, got = refs[2 * i:2 * i + 2]
        first, second = refs[2 * n + 2 * i:2 * n + 2 * i + 2]
        rows = first.shape[0]
        first[...] = plus(keep[0:rows, :], got[0:rows, :])
        second[...] = plus(keep[rows:2 * rows, :], got[rows:2 * rows, :])


def add_halves(*pairs):
    outs = [jax.ShapeDtypeStruct((p.shape[0] // 2, p.shape[1]), bf16) for p in pairs]
    return pl.pallas_call(
        add_kernel, out_shape=outs, in_specs=[VM] * len(pairs), out_specs=[VM] * len(pairs),
        compiler_params=params(), cost_estimate=cost(pairs[0].size, 8 * pairs[0].size), name="add_halves",
    )(*pairs)


def add_across_kernel(a_keep, a_got, b_keep, b_got, first, second):
    rows, half = first.shape[0], a_keep.shape[1]
    for c, (keep, got) in enumerate(((a_keep, a_got), (b_keep, b_got))):
        cols = slice(c * half, (c + 1) * half)
        first[:, cols] = plus(keep[0:rows, :], got[0:rows, :])
        second[:, cols] = plus(keep[rows:2 * rows, :], got[rows:2 * rows, :])


def add_across(a_keep, a_got, b_keep, b_got):
    rows, half = a_keep.shape
    return pl.pallas_call(
        add_across_kernel, out_shape=[jax.ShapeDtypeStruct((rows // 2, 2 * half), bf16)] * 2,
        in_specs=[VM] * 4, out_specs=[VM] * 2,
        compiler_params=params(), cost_estimate=cost(2 * rows * half, 12 * rows * half), name="add_across",
    )(a_keep, a_got, b_keep, b_got)


def per_device(char_ids, char_table, conv_weight, proj_weight, gate_weight, trans_weight, gate_bias, hidden, targets,
               *, vocab, blk):
    devices = vocab * blk
    axes = ("vocab", "blk")

    def swap(x, bits):
        return lax.ppermute(x, axes, [(i, i ^ bits) for i in range(devices)])

    core, near = blk, 1
    bit_a, bit_b = 2 * blk, 4 * blk
    rest = [1 << i for i in range(1, blk.bit_length() - 1)] + [
        blk << i for i in range(3, vocab.bit_length() - 1)]
    me = lax.axis_index("vocab") * blk + lax.axis_index("blk")
    local, length = char_ids.shape
    mine = hidden.shape[0]

    goal = targets.reshape(mine, 1)
    code = jnp.concatenate([goal // 256, goal % 256], axis=1).astype(bf16)
    rows = jnp.concatenate([hidden, code, jnp.zeros((mine, LANES - 2), bf16)], axis=1)
    for bit in rest:
        rows = jnp.concatenate([rows, swap(rows, bit)], axis=0)

    tab_t = char_table.T.astype(f32)
    weights = (tab_t, conv_weight, proj_weight, gate_weight, trans_weight, gate_bias)
    sizes = (local // 2, local // 2)
    pieces, marks, start = [], [], 0
    for i, size in enumerate(sizes):
        pieces.append(embed(char_ids, length, start, size, *weights))
        marks.append(start)
        start += size
    hid = [rows] + [swap(rows, b) for b in (bit_b, bit_a, bit_a | bit_b)]
    cores = [swap(e, core) for e in pieces]
    nears = [swap(e, near) for e in pieces]
    fars = [swap(e, core) for e in nears]

    me = me.astype(jnp.int32).reshape(1)
    meta = [tuple((bits, m) for m in marks) for bits in (0, core, near, core | near)]
    late = 1 if 4 * hid[0].shape[0] <= local else len(nears)
    one, target, stats = first_fold(
        me, hid, pieces + cores + nears[:-late] + fars[:-late],
        meta[0] + meta[1] + meta[2][:-late] + meta[3][:-late], local)
    words, metas = nears[-late:] + fars[-late:], meta[2][-late:] + meta[3][-late:]
    prob, tops, line = last_scores(me, hid, words, metas, local, stats)
    bits = [bit_a, bit_b] + rest
    others = [sum(b for j, b in enumerate(bits) if k >> j & 1) for k in range(1, 1 << len(bits))]
    order = rest + [bit_b, bit_a]
    flips = tuple((sum(1 << (j - 1) for j, b in enumerate(order) if j and o & b), bool(o & rest[0])) for o in others)
    lines = [swap(line, o) for o in others]
    two, target = last_sums(me, hid, words, metas, local, prob, target)
    a_keep, a_send, b_keep, b_send, loss = combine([line] + lines, ((0, False),) + flips, one, two, target, stats, tops)
    a_keep, a_send, b_keep, b_send = add_halves(a_keep, swap(a_send, bit_a), b_keep, swap(b_send, bit_b))
    keep, send = add_across(a_keep, swap(a_send, bit_b), b_keep, swap(b_send, bit_a))
    for bit in rest[:0:-1]:
        keep, send = add_halves(keep, swap(send, bit))
    grad = plus(keep, swap(send, rest[0]))
    return loss[0, :mine], grad


def solution(mesh):
    words = P(("vocab", "blk"))
    return jax.shard_map(
        functools.partial(per_device, vocab=mesh.shape["vocab"], blk=mesh.shape["blk"]),
        mesh=mesh,
        in_specs=(P(("vocab", "blk"), None), P(), P(), P(), P(), P(), P(), P(("vocab", "blk"), None), words),
        out_specs=(words, P(("vocab", "blk"), None)),
        check_vma=False,
    )
```

time: 137 us -> 120 us (0.88)
  Pallas kernels: 66.2 us -> 54 us
  local copies, waits for them, and re-layouts: 9.5 us -> 7.58 us
  starting transfers between devices: 26.9 us -> 25.2 us
    pallas_call x4 -> x2, Pallas kernels: 41.2 us -> 26.8 us  [embed(): pl.pallas_call(functools.partial(cnn_kernel, widths=widths, filters=filte...]
    pallas_call x6, Pallas kernels: 25 us -> 27.1 us  [the longest x1 9.6 us: first_fold(): pl.pallas_call(functools.partial(first_kernel, nh=len(hid), metas=metas,...]
    optimization_barrier x2 -> x0, local copies, waits for them, and re-layouts: 1.72 us -> none  [the longest x1 0.86 us: per_device(): *hid, ids_far, ids = lax.optimization_barrier((*hid, ids_far, ids))]
    ppermute x29 -> x22, starting transfers between devices: 26.9 us -> 25.2 us  [swap(): return lax.ppermute(x, axes, [(i, i ^ bits) for i in range(devices)])]
    ppermute x29 -> x22, waiting for transfers between devices: 29.1 us -> 28.2 us  [swap(): return lax.ppermute(x, axes, [(i, i ^ bits) for i in range(devices)])]
    unnamed x57 -> x39, local copies, waits for them, and re-layouts: 5.35 us -> 5.22 us
  transfers between devices with their start and end apart: 29 -> 22, of which waited for: 9 -> 8; matrix products, arithmetic and copies ran while one was open for 5% -> 4% of each run, Pallas kernels for 46% -> 35%
where the time goes in v3:
time: 120 us; the launch traced here: 119 us
  Pallas kernels  54 us (45%)
  waiting for transfers between devices  28.2 us (24%)
  starting transfers between devices  25.2 us (21%)
  local copies, waits for them, and re-layouts  7.58 us (6%)
  other arithmetic  3.59 us (3%)
    ppermute x22, waiting for transfers between devices, swap(): return lax.ppermute(x, axes, [(i, i ^ bits) for i in range(devices)])  28.2 us
    pallas_call x2, Pallas kernels, embed(): pl.pallas_call(functools.partial(cnn_kernel, widths=widths, filters=filte...  26.8 us
    ppermute x22, starting transfers between devices, swap(): return lax.ppermute(x, axes, [(i, i ^ bits) for i in range(devices)])  25.2 us
    pallas_call x1, Pallas kernels, first_fold(): pl.pallas_call(functools.partial(first_kernel, nh=len(hid), metas=metas,...  9.6 us
    unnamed x39, local copies, waits for them, and re-layouts  5.22 us
    pallas_call x1, Pallas kernels, last_sums(): pl.pallas_call(functools.partial(sum_kernel, nh=len(hid), metas=metas, lo...  5.04 us
    pallas_call x1, Pallas kernels, last_scores(): pl.pallas_call(functools.partial(score_kernel, nh=len(hid), metas=metas,...  4.36 us
    pallas_call x1, Pallas kernels, combine(): pl.pallas_call(functools.partial(combine_kernel, flips=flips), out_shape=...  4.31 us
  transfers between devices with their start and end apart: 22, of which 8 were waited for; matrix products, arithmetic and copies ran while one was open for 4% of the time, Pallas kernels for 35%

profile of v3, /device:TPU:0, one launch (start us, length us, event | category | flops | bytes accessed | tf_op | source)
XLA Modules:
  0.0 119.4 jit_solution(11486279733830712854)
XLA Ops:
  2.5 4.1 %collective-permute-start = (bf16[64,1152]{1,0:T(8,128)(2,1)S(1)}, bf16[64,1152]{1,0:T(8,128)(2,1)S(1)}, u32[]{:S(2)}, u32[]{:S(2)}) collective-permute-start(bf16[64,1152]{1,0:T(8,128)(2,1)S(1)} %concatenate.9), channel_id=1, source_target_pairs={{0,2},{1,3},{2,0},{3,1},{4,6},{5,7},{6,4},{7,5},{8,10},{9,11},{10,... | collective-permute-start | bytes 442376 | tf_op jit(solution)/shard_map/ppermute | solution.py:414
  7.9 1.7 %copy.13.ids_ref = s32[512,50]{1,0:T(8,128)} copy(s32[512,50]{0,1:T(8,128)} %param.9) | data formatting | bytes 204800 | tf_op args[0]
  9.7 13.3 %embed.3.refs_4_ = bf16[256,1024]{1,0:T(8,128)(2,1)} custom-call(s32[512,50]{1,0:T(8,128)} %copy.13.ids_ref, f32[16,256]{1,0:T(8,128)} %convert_bitcast_fusion.tab_ref, bf16[112,896]{1,0:T(8,128)(2,1)} %conv_ref.3, f32[2,1024]{1,0:T(2,128)} %bias_ref.3, bf16[896,1024]{1,0:T(8,128)(2,1)} %proj_hbm.3, bf16[2,1024,1024]{2,1,0:T(8,128)(2,1)} %gate_hbm.3, ...), custom_call_target="tpu_custom_call" | custom-call | flops 8489271296 | bytes 12582912 | tf_op jit(solution)/shard_map/embed/pallas_call | solution.py:129
  23.0 1.6 %collective-permute-start.8 = (bf16[256,1024]{1,0:T(8,128)(2,1)}, bf16[256,1024]{1,0:T(8,128)(2,1)S(1)}, u32[]{:S(2)}, u32[]{:S(2)}) collective-permute-start(bf16[256,1024]{1,0:T(8,128)(2,1)} %embed.3.refs_4_), channel_id=1, source_target_pairs={{0,1},{1,0},{2,3},{3,2},{4,5},{5,4},{6,7},{7,6},{8,9},{9,8},{10,11... | collective-permute-start | bytes 1572872 | tf_op jit(solution)/shard_map/ppermute | solution.py:414
  24.7 2.5 %collective-permute-start.3 = (bf16[128,1152]{1,0:T(8,128)(2,1)S(1)}, bf16[128,1152]{1,0:T(8,128)(2,1)S(1)}, u32[]{:S(2)}, u32[]{:S(2)}) collective-permute-start(bf16[128,1152]{1,0:T(8,128)(2,1)S(1)} %pad_maximum_fusion.refs_0_), channel_id=1, source_target_pairs={{0,24},{1,25},{2,26},{3,27},{4,28},{5,29},{6,30},{7,31},{8,16},{9,... | collective-permute-start | bytes 884744 | tf_op jit(solution)/shard_map/ppermute | solution.py:414
  27.2 13.5 %embed.2.refs_5_ = bf16[256,1024]{1,0:T(8,128)(2,1)} custom-call(s32[512,50]{1,0:T(8,128)} %copy.13.ids_ref, f32[16,256]{1,0:T(8,128)} %convert_bitcast_fusion.tab_ref, bf16[112,896]{1,0:T(8,128)(2,1)} %conv_ref.3, f32[2,1024]{1,0:T(2,128)} %bias_ref.3, bf16[896,1024]{1,0:T(8,128)(2,1)} %proj_hbm.3, bf16[2,1024,1024]{2,1,0:T(8,128)(2,1)} %gate_hbm.3, ...), custom_call_target="tpu_custom_call" | custom-call | flops 8489271296 | bytes 12582912 | tf_op jit(solution)/shard_map/embed/pallas_call | solution.py:129
  42.5 6.4 %collective-permute-done.2.refs_2_ = bf16[128,1152]{1,0:T(8,128)(2,1)S(1)} collective-permute-done((bf16[128,1152]{1,0:T(8,128)(2,1)S(1)}, bf16[128,1152]{1,0:T(8,128)(2,1)S(1)}, u32[]{:S(2)}, u32[]{:S(2)}) %collective-permute-start.2) | collective-permute-done | bytes 294944 | tf_op jit(solution)/shard_map/ppermute | solution.py:414
  49.4 4.4 %collective-permute-done.4.refs_4_ = bf16[256,1024]{1,0:T(8,128)(2,1)S(1)} collective-permute-done((bf16[256,1024]{1,0:T(8,128)(2,1)}, bf16[256,1024]{1,0:T(8,128)(2,1)S(1)}, u32[]{:S(2)}, u32[]{:S(2)}) %collective-permute-start.4) | collective-permute-done | bytes 524320 | tf_op jit(solution)/shard_map/ppermute | solution.py:414
  53.8 1.8 %collective-permute-done.1.refs_1_ = bf16[128,1152]{1,0:T(8,128)(2,1)S(1)} collective-permute-done((bf16[128,1152]{1,0:T(8,128)(2,1)S(1)}, bf16[128,1152]{1,0:T(8,128)(2,1)S(1)}, u32[]{:S(2)}, u32[]{:S(2)}) %collective-permute-start.1) | collective-permute-done | bytes 294944 | tf_op jit(solution)/shard_map/ppermute | solution.py:414
  56.3 9.6 %first_fold.1 = (f32[512,1024]{1,0:T(8,128)}, bf16[512,1024]{1,0:T(8,128)(2,1)}, f32[512,384]{1,0:T(8,128)}) custom-call(s32[1]{0:T(128)} %bitcast.me_ref, bf16[128,1152]{1,0:T(8,128)(2,1)} %copy-done, bf16[128,1152]{1,0:T(8,128)(2,1)} %copy-done.5, bf16[128,1152]{1,0:T(8,128)(2,1)} %copy-done.4, bf16[128,1152]{1,0:T(8,128)(2,1)} %copy-done.3, ...), custom_call_target="tpu_custom_call" | custom-call | flops 4831838208 | bytes 4194304 | tf_op jit(solution)/shard_map/first_fold/pallas_call | solution.py:257
  66.8 4.4 %last_scores.1 = (bf16[512,512]{1,0:T(8,128)(2,1)}, f32[512,128]{1,0:T(8,128)}, f32[8,128]{1,0:T(8,128)}) custom-call(s32[1]{0:T(128)} %bitcast.me_ref, bf16[128,1152]{1,0:T(8,128)(2,1)} %copy-done, bf16[128,1152]{1,0:T(8,128)(2,1)} %copy-done.5, bf16[128,1152]{1,0:T(8,128)(2,1)} %copy-done.4, bf16[128,1152]{1,0:T(8,128)(2,1)} %copy-done.3, ...), custom_call_target="tpu_custom_call" | custom-call | flops 536870912 | bytes 2097152 | tf_op jit(solution)/shard_map/last_scores/pallas_call | solution.py:287
  71.6 3.3 %collective-permute-start.15 = (f32[8,128]{1,0:T(8,128)}, f32[8,128]{1,0:T(8,128)S(1)}, u32[]{:S(2)}, u32[]{:S(2)}) collective-permute-start(f32[8,128]{1,0:T(8,128)} %get-tuple-element.22.refs_0_), channel_id=1, source_target_pairs={{0,18},{1,19},{2,16},{3,17},{4,22},{5,23},{6,20},{7,21},{8,26},{9,... | collective-permute-start | bytes 12296 | tf_op jit(solution)/shard_map/ppermute | solution.py:414
  76.2 2.6 %collective-permute-start.13 = (f32[8,128]{1,0:T(8,128)}, f32[8,128]{1,0:T(8,128)S(1)}, u32[]{:S(2)}, u32[]{:S(2)}) collective-permute-start(f32[8,128]{1,0:T(8,128)} %get-tuple-element.22.refs_0_), channel_id=1, source_target_pairs={{0,2},{1,3},{2,0},{3,1},{4,6},{5,7},{6,4},{7,5},{8,10},{9,11},{10,... | collective-permute-start | bytes 12296 | tf_op jit(solution)/shard_map/ppermute | solution.py:414
  79.2 1.5 %collective-permute-start.11 = (f32[8,128]{1,0:T(8,128)}, f32[8,128]{1,0:T(8,128)S(1)}, u32[]{:S(2)}, u32[]{:S(2)}) collective-permute-start(f32[8,128]{1,0:T(8,128)} %get-tuple-element.22.refs_0_), channel_id=1, source_target_pairs={{0,16},{1,17},{2,18},{3,19},{4,20},{5,21},{6,22},{7,23},{8,24},{9,... | collective-permute-start | bytes 12296 | tf_op jit(solution)/shard_map/ppermute | solution.py:414
  80.8 1.5 %collective-permute-start.10 = (f32[8,128]{1,0:T(8,128)}, f32[8,128]{1,0:T(8,128)S(1)}, u32[]{:S(2)}, u32[]{:S(2)}) collective-permute-start(f32[8,128]{1,0:T(8,128)} %get-tuple-element.22.refs_0_), channel_id=1, source_target_pairs={{0,8},{1,9},{2,10},{3,11},{4,12},{5,13},{6,14},{7,15},{8,0},{9,1},... | collective-permute-start | bytes 12296 | tf_op jit(solution)/shard_map/ppermute | solution.py:414
  82.3 5.0 %last_sums.1 = (f32[512,1024]{1,0:T(8,128)}, bf16[512,1024]{1,0:T(8,128)(2,1)}) custom-call(s32[1]{0:T(128)} %bitcast.me_ref, bf16[128,1152]{1,0:T(8,128)(2,1)} %copy-done, bf16[128,1152]{1,0:T(8,128)(2,1)} %copy-done.5, bf16[128,1152]{1,0:T(8,128)(2,1)} %copy-done.4, bf16[128,1152]{1,0:T(8,128)(2,1)} %copy-done.3, bf16[256,1024]{1,0:T(8,128)(2,1)} %copy-done.1, ...), custom_call_target="tpu_custom_call" | custom-call | flops 1073741824 | bytes 2097152 | tf_op jit(solution)/shard_map/last_sums/pallas_call | solution.py:308
  88.0 4.3 %combine.1 = (bf16[256,512]{1,0:T(8,128)(2,1)}, bf16[256,512]{1,0:T(8,128)(2,1)}, bf16[256,512]{1,0:T(8,128)(2,1)}, bf16[256,512]{1,0:T(8,128)(2,1)}, f32[1,128]{1,0:T(1,128)}) custom-call(f32[8,128]{1,0:T(8,128)} %get-tuple-element.22.refs_0_, f32[8,128]{1,0:T(8,128)} %copy-done.16, f32[8,128]{1,0:T(8,128)} %copy-done.15, f32[8,128]{1,0:T(8,128)} %copy-done.14, ...), custom_call_target="tpu_custom_call" | custom-call | flops 4194304 | bytes 6291456 | tf_op jit(solution)/shard_map/combine/pallas_call | solution.py:361
  93.3 5.5 %collective-permute-done.17.refs_1_ = bf16[256,512]{1,0:T(8,128)(2,1)S(1)} collective-permute-done((bf16[256,512]{1,0:T(8,128)(2,1)}, bf16[256,512]{1,0:T(8,128)(2,1)S(1)}, u32[]{:S(2)}, u32[]{:S(2)}) %collective-permute-start.17) | collective-permute-done | bytes 262176 | tf_op jit(solution)/shard_map/ppermute | solution.py:414
  100.1 2.0 %add_halves.1 = (bf16[128,512]{1,0:T(8,128)(2,1)}, bf16[128,512]{1,0:T(8,128)(2,1)}, bf16[128,512]{1,0:T(8,128)(2,1)}, bf16[128,512]{1,0:T(8,128)(2,1)}) custom-call(bf16[256,512]{1,0:T(8,128)(2,1)} %get-tuple-element.30.refs_0_, bf16[256,512]{1,0:T(8,128)(2,1)} %copy-done.6, bf16[256,512]{1,0:T(8,128)(2,1)} %get-tuple-element.32.refs_2_, ...), custom_call_target="tpu_custom_call" | custom-call | flops 131072 | bytes 1048576 | tf_op jit(solution)/shard_map/add_halves/pallas_call | solution.py:385
  102.6 1.5 %collective-permute-start.20 = (bf16[128,512]{1,0:T(8,128)(2,1)}, bf16[128,512]{1,0:T(8,128)(2,1)S(1)}, u32[]{:S(2)}, u32[]{:S(2)}) collective-permute-start(bf16[128,512]{1,0:T(8,128)(2,1)} %get-tuple-element.37), channel_id=1, source_target_pairs={{0,8},{1,9},{2,10},{3,11},{4,12},{5,13},{6,14},{7,15},{8,0},{9,1},... | collective-permute-start | bytes 393224 | tf_op jit(solution)/shard_map/ppermute | solution.py:414
  104.1 3.2 %collective-permute-done.19.a_got = bf16[128,512]{1,0:T(8,128)(2,1)S(1)} collective-permute-done((bf16[128,512]{1,0:T(8,128)(2,1)}, bf16[128,512]{1,0:T(8,128)(2,1)S(1)}, u32[]{:S(2)}, u32[]{:S(2)}) %collective-permute-start.19) | collective-permute-done | bytes 131104 | tf_op jit(solution)/shard_map/ppermute | solution.py:414
  108.5 1.8 %add_across.1 = (bf16[64,1024]{1,0:T(8,128)(2,1)}, bf16[64,1024]{1,0:T(8,128)(2,1)}) custom-call(bf16[128,512]{1,0:T(8,128)(2,1)} %get-tuple-element.34.a_keep, bf16[128,512]{1,0:T(8,128)(2,1)} %copy-done.8, bf16[128,512]{1,0:T(8,128)(2,1)} %get-tuple-element.36.b_keep, bf16[128,512]{1,0:T(8,128)(2,1)} %copy-done.9), custom_call_target="tpu_custom_call" | custom-call | flops 131072 | bytes 786432 | tf_op jit(solution)/shard_map/add_across/pallas_call | solution.py:401
  112.0 5.8 %collective-permute-done.21 = bf16[64,1024]{1,0:T(8,128)(2,1)S(1)} collective-permute-done((bf16[64,1024]{1,0:T(8,128)(2,1)}, bf16[64,1024]{1,0:T(8,128)(2,1)S(1)}, u32[]{:S(2)}, u32[]{:S(2)}) %collective-permute-start.21) | collective-permute-done | bytes 131104 | tf_op jit(solution)/shard_map/ppermute | solution.py:414
  117.8 1.6 %add_convert_fusion = bf16[64,1024]{1,0:T(8,128)(2,1)} fusion(bf16[64,1024]{1,0:T(8,128)(2,1)S(1)} %collective-permute-done.21, bf16[64,1024]{1,0:T(8,128)(2,1)} %get-tuple-element.38), kind=kLoop, calls=%fused_computation.1 | loop fusion | flops 262144 | bytes 393216 | tf_op jit(solution)/shard_map/convert_element_type | solution.py:370
  (76 shorter events, 15.5 us)
Async XLA Ops:
  2.5 22.1 %collective-permute-start = (bf16[64,1152]{1,0:T(8,128)(2,1)S(1)}, bf16[64,1152]{1,0:T(8,128)(2,1)S(1)}, u32[]{:S(2)}, u32[]{:S(2)}) collective-permute-start(bf16[64,1152]{1,0:T(8,128)(2,1)S(1)} %concatenate.9), channel_id=1, source_target_pairs={{0,2},{1,3},{2,0},{3,1},{4,6},{5,7},{6,4},{7,5},{8,10},{9,11},{10,... | collective-permute-start | bytes 442376 | tf_op jit(solution)/shard_map/ppermute | solution.py:414
  23.0 19.3 %collective-permute-start.8 = (bf16[256,1024]{1,0:T(8,128)(2,1)}, bf16[256,1024]{1,0:T(8,128)(2,1)S(1)}, u32[]{:S(2)}, u32[]{:S(2)}) collective-permute-start(bf16[256,1024]{1,0:T(8,128)(2,1)} %embed.3.refs_4_), channel_id=1, source_target_pairs={{0,1},{1,0},{2,3},{3,2},{4,5},{5,4},{6,7},{7,6},{8,9},{9,8},{10,11... | collective-permute-start | bytes 1572872 | tf_op jit(solution)/shard_map/ppermute | solution.py:414
  24.7 24.2 %copy-start = (bf16[128,1152]{1,0:T(8,128)(2,1)}, bf16[128,1152]{1,0:T(8,128)(2,1)S(1)}, u32[]{:S(2)}) copy-start(bf16[128,1152]{1,0:T(8,128)(2,1)S(1)} %pad_maximum_fusion.refs_0_) | copy-start | bytes 884740
  24.7 17.1 %copy-start.17 = (bf16[256,1024]{1,0:T(8,128)(2,1)S(1)}, bf16[256,1024]{1,0:T(8,128)(2,1)}, u32[]{:S(2)}) copy-start(bf16[256,1024]{1,0:T(8,128)(2,1)} %embed.3.refs_4_) | copy-start | bytes 1572868
  24.7 17.1 %collective-permute-start.3 = (bf16[128,1152]{1,0:T(8,128)(2,1)S(1)}, bf16[128,1152]{1,0:T(8,128)(2,1)S(1)}, u32[]{:S(2)}, u32[]{:S(2)}) collective-permute-start(bf16[128,1152]{1,0:T(8,128)(2,1)S(1)} %pad_maximum_fusion.refs_0_), channel_id=1, source_target_pairs={{0,24},{1,25},{2,26},{3,27},{4,28},{5,29},{6,30},{7,31},{8,16},{9,... | collective-permute-start | bytes 884744 | tf_op jit(solution)/shard_map/ppermute | solution.py:414
  40.7 13.1 %collective-permute-start.4 = (bf16[256,1024]{1,0:T(8,128)(2,1)}, bf16[256,1024]{1,0:T(8,128)(2,1)S(1)}, u32[]{:S(2)}, u32[]{:S(2)}) collective-permute-start(bf16[256,1024]{1,0:T(8,128)(2,1)} %embed.2.refs_5_), channel_id=1, source_target_pairs={{0,1},{1,0},{2,3},{3,2},{4,5},{5,4},{6,7},{7,6},{8,9},{9,8},{10,11... | collective-permute-start | bytes 1572872 | tf_op jit(solution)/shard_map/ppermute | solution.py:414
  41.2 7.6 %collective-permute-start.2 = (bf16[128,1152]{1,0:T(8,128)(2,1)S(1)}, bf16[128,1152]{1,0:T(8,128)(2,1)S(1)}, u32[]{:S(2)}, u32[]{:S(2)}) collective-permute-start(bf16[128,1152]{1,0:T(8,128)(2,1)S(1)} %pad_maximum_fusion.refs_0_), channel_id=1, source_target_pairs={{0,8},{1,9},{2,10},{3,11},{4,12},{5,13},{6,14},{7,15},{8,0},{9,1},... | collective-permute-start | bytes 884744 | tf_op jit(solution)/shard_map/ppermute | solution.py:414
  41.8 13.8 %collective-permute-start.7 = (bf16[256,1024]{1,0:T(8,128)(2,1)}, bf16[256,1024]{1,0:T(8,128)(2,1)}, u32[]{:S(2)}, u32[]{:S(2)}) collective-permute-start(bf16[256,1024]{1,0:T(8,128)(2,1)} %embed.2.refs_5_), channel_id=1, source_target_pairs={{0,4},{1,5},{2,6},{3,7},{4,0},{5,1},{6,2},{7,3},{8,12},{9,13},{10,... | collective-permute-start | bytes 1572872 | tf_op jit(solution)/shard_map/ppermute | solution.py:414
  41.8 13.8 %collective-permute-start.6 = (bf16[256,1024]{1,0:T(8,128)(2,1)S(1)}, bf16[256,1024]{1,0:T(8,128)(2,1)}, u32[]{:S(2)}, u32[]{:S(2)}) collective-permute-start(bf16[256,1024]{1,0:T(8,128)(2,1)S(1)} %copy-done.17), channel_id=1, source_target_pairs={{0,4},{1,5},{2,6},{3,7},{4,0},{5,1},{6,2},{7,3},{8,12},{9,13},{10,... | collective-permute-start | bytes 1572872 | tf_op jit(solution)/shard_map/ppermute | solution.py:414
  42.4 13.2 %collective-permute-start.9 = (bf16[256,1024]{1,0:T(8,128)(2,1)S(1)}, bf16[256,1024]{1,0:T(8,128)(2,1)}, u32[]{:S(2)}, u32[]{:S(2)}) collective-permute-start(bf16[256,1024]{1,0:T(8,128)(2,1)S(1)} %collective-permute-done.8.refs_8_), channel_id=1, source_target_pairs={{0,4},{1,5},{2,6},{3,7},{4,0},{5,1},{6,2},{7,3},{8,12},{9,13},{10,... | collective-permute-start | bytes 1572872 | tf_op jit(solution)/shard_map/ppermute | solution.py:414
  48.9 6.7 %collective-permute-start.1 = (bf16[128,1152]{1,0:T(8,128)(2,1)S(1)}, bf16[128,1152]{1,0:T(8,128)(2,1)S(1)}, u32[]{:S(2)}, u32[]{:S(2)}) collective-permute-start(bf16[128,1152]{1,0:T(8,128)(2,1)S(1)} %pad_maximum_fusion.refs_0_), channel_id=1, source_target_pairs={{0,16},{1,17},{2,18},{3,19},{4,20},{5,21},{6,22},{7,23},{8,24},{9,... | collective-permute-start | bytes 884744 | tf_op jit(solution)/shard_map/ppermute | solution.py:414
  53.8 12.1 %collective-permute-start.5 = (bf16[256,1024]{1,0:T(8,128)(2,1)S(1)}, bf16[256,1024]{1,0:T(8,128)(2,1)S(1)}, u32[]{:S(2)}, u32[]{:S(2)}) collective-permute-start(bf16[256,1024]{1,0:T(8,128)(2,1)S(1)} %collective-permute-done.4.refs_4_), channel_id=1, source_target_pairs={{0,4},{1,5},{2,6},{3,7},{4,0},{5,1},{6,2},{7,3},{8,12},{9,13},{10,... | collective-permute-start | bytes 1572872 | tf_op jit(solution)/shard_map/ppermute | solution.py:414
  71.1 8.1 %collective-permute-start.16 = (f32[8,128]{1,0:T(8,128)}, f32[8,128]{1,0:T(8,128)S(1)}, u32[]{:S(2)}, u32[]{:S(2)}) collective-permute-start(f32[8,128]{1,0:T(8,128)} %get-tuple-element.22.refs_0_), channel_id=1, source_target_pairs={{0,26},{1,27},{2,24},{3,25},{4,30},{5,31},{6,28},{7,29},{8,18},{9,... | collective-permute-start | bytes 12296 | tf_op jit(solution)/shard_map/ppermute | solution.py:414
  71.6 9.2 %collective-permute-start.15 = (f32[8,128]{1,0:T(8,128)}, f32[8,128]{1,0:T(8,128)S(1)}, u32[]{:S(2)}, u32[]{:S(2)}) collective-permute-start(f32[8,128]{1,0:T(8,128)} %get-tuple-element.22.refs_0_), channel_id=1, source_target_pairs={{0,18},{1,19},{2,16},{3,17},{4,22},{5,23},{6,20},{7,21},{8,26},{9,... | collective-permute-start | bytes 12296 | tf_op jit(solution)/shard_map/ppermute | solution.py:414
  74.9 12.4 %collective-permute-start.14 = (f32[8,128]{1,0:T(8,128)}, f32[8,128]{1,0:T(8,128)S(1)}, u32[]{:S(2)}, u32[]{:S(2)}) collective-permute-start(f32[8,128]{1,0:T(8,128)} %get-tuple-element.22.refs_0_), channel_id=1, source_target_pairs={{0,10},{1,11},{2,8},{3,9},{4,14},{5,15},{6,12},{7,13},{8,2},{9,3},... | collective-permute-start | bytes 12296 | tf_op jit(solution)/shard_map/ppermute | solution.py:414
  76.2 11.1 %collective-permute-start.13 = (f32[8,128]{1,0:T(8,128)}, f32[8,128]{1,0:T(8,128)S(1)}, u32[]{:S(2)}, u32[]{:S(2)}) collective-permute-start(f32[8,128]{1,0:T(8,128)} %get-tuple-element.22.refs_0_), channel_id=1, source_target_pairs={{0,2},{1,3},{2,0},{3,1},{4,6},{5,7},{6,4},{7,5},{8,10},{9,11},{10,... | collective-permute-start | bytes 12296 | tf_op jit(solution)/shard_map/ppermute | solution.py:414
  78.8 8.6 %collective-permute-start.12 = (f32[8,128]{1,0:T(8,128)}, f32[8,128]{1,0:T(8,128)S(1)}, u32[]{:S(2)}, u32[]{:S(2)}) collective-permute-start(f32[8,128]{1,0:T(8,128)} %get-tuple-element.22.refs_0_), channel_id=1, source_target_pairs={{0,24},{1,25},{2,26},{3,27},{4,28},{5,29},{6,30},{7,31},{8,16},{9,... | collective-permute-start | bytes 12296 | tf_op jit(solution)/shard_map/ppermute | solution.py:414
  79.2 8.1 %collective-permute-start.11 = (f32[8,128]{1,0:T(8,128)}, f32[8,128]{1,0:T(8,128)S(1)}, u32[]{:S(2)}, u32[]{:S(2)}) collective-permute-start(f32[8,128]{1,0:T(8,128)} %get-tuple-element.22.refs_0_), channel_id=1, source_target_pairs={{0,16},{1,17},{2,18},{3,19},{4,20},{5,21},{6,22},{7,23},{8,24},{9,... | collective-permute-start | bytes 12296 | tf_op jit(solution)/shard_map/ppermute | solution.py:414
  80.8 6.6 %collective-permute-start.10 = (f32[8,128]{1,0:T(8,128)}, f32[8,128]{1,0:T(8,128)S(1)}, u32[]{:S(2)}, u32[]{:S(2)}) collective-permute-start(f32[8,128]{1,0:T(8,128)} %get-tuple-element.22.refs_0_), channel_id=1, source_target_pairs={{0,8},{1,9},{2,10},{3,11},{4,12},{5,13},{6,14},{7,15},{8,0},{9,1},... | collective-permute-start | bytes 12296 | tf_op jit(solution)/shard_map/ppermute | solution.py:414
  92.3 6.6 %collective-permute-start.17 = (bf16[256,512]{1,0:T(8,128)(2,1)}, bf16[256,512]{1,0:T(8,128)(2,1)S(1)}, u32[]{:S(2)}, u32[]{:S(2)}) collective-permute-start(bf16[256,512]{1,0:T(8,128)(2,1)} %get-tuple-element.31), channel_id=1, source_target_pairs={{0,8},{1,9},{2,10},{3,11},{4,12},{5,13},{6,14},{7,15},{8,0},{9,1},... | collective-permute-start | bytes 786440 | tf_op jit(solution)/shard_map/ppermute | solution.py:414
  92.8 6.6 %collective-permute-start.18 = (bf16[256,512]{1,0:T(8,128)(2,1)}, bf16[256,512]{1,0:T(8,128)(2,1)S(1)}, u32[]{:S(2)}, u32[]{:S(2)}) collective-permute-start(bf16[256,512]{1,0:T(8,128)(2,1)} %get-tuple-element.33), channel_id=1, source_target_pairs={{0,16},{1,17},{2,18},{3,19},{4,20},{5,21},{6,22},{7,23},{8,24},{9,... | collective-permute-start | bytes 786440 | tf_op jit(solution)/shard_map/ppermute | solution.py:414
  102.1 5.2 %collective-permute-start.19 = (bf16[128,512]{1,0:T(8,128)(2,1)}, bf16[128,512]{1,0:T(8,128)(2,1)S(1)}, u32[]{:S(2)}, u32[]{:S(2)}) collective-permute-start(bf16[128,512]{1,0:T(8,128)(2,1)} %get-tuple-element.35), channel_id=1, source_target_pairs={{0,16},{1,17},{2,18},{3,19},{4,20},{5,21},{6,22},{7,23},{8,24},{9,... | collective-permute-start | bytes 393224 | tf_op jit(solution)/shard_map/ppermute | solution.py:414
  102.6 5.2 %collective-permute-start.20 = (bf16[128,512]{1,0:T(8,128)(2,1)}, bf16[128,512]{1,0:T(8,128)(2,1)S(1)}, u32[]{:S(2)}, u32[]{:S(2)}) collective-permute-start(bf16[128,512]{1,0:T(8,128)(2,1)} %get-tuple-element.37), channel_id=1, source_target_pairs={{0,8},{1,9},{2,10},{3,11},{4,12},{5,13},{6,14},{7,15},{8,0},{9,1},... | collective-permute-start | bytes 393224 | tf_op jit(solution)/shard_map/ppermute | solution.py:414
  110.3 7.5 %collective-permute-start.21 = (bf16[64,1024]{1,0:T(8,128)(2,1)}, bf16[64,1024]{1,0:T(8,128)(2,1)S(1)}, u32[]{:S(2)}, u32[]{:S(2)}) collective-permute-start(bf16[64,1024]{1,0:T(8,128)(2,1)} %get-tuple-element.39), channel_id=1, source_target_pairs={{0,2},{1,3},{2,0},{3,1},{4,6},{5,7},{6,4},{7,5},{8,10},{9,11},{10,... | collective-permute-start | bytes 393224 | tf_op jit(solution)/shard_map/ppermute | solution.py:414
  (17 other events, 68.0 us)

commit v4 on v3

--- a/solution.py
+++ b/solution.py
@@ -9,6 +9,7 @@
 bf16=jnp.bfloat16; f32=jnp.float32
 LANES = 128
 SPAN = 8
+
 
 def prep_toeplitz(conv_ref, toep, ce, widths, filters):
     depth = toep.shape[0]
@@ -24,13 +25,11 @@
             if rest:
                 toep[o * ce + rows:depth, cols] = jnp.zeros((rest, filters), bf16)
 
-def lookup(ids_ref, start, words, tab_ref, vec, turn, length, ce):
+def lookup(ids_ref, start, words, tab_ref, vec, length, ce):
     per = LANES // ce
+    low_tab = tab_ref[:, 0:LANES].astype(f32)
+    top_tab = tab_ref[:, LANES:2 * LANES].astype(f32)
     for at in range(0, words, LANES):
-        count = min(LANES, words - at)
-        turn[...] = jnp.zeros(turn.shape, f32)
-        turn[0:count, 0:length] = ids_ref[start + at:start + at + count, 0:length].astype(f32)
-        ids = turn[...].T.astype(jnp.int32)
         for g in range(vec.shape[1] // LANES):
             parts = []
             for q in range(per):
@@ -38,15 +37,15 @@
                 if p >= length:
                     parts.append(jnp.zeros((ce, LANES), f32))
                     continue
-                idx = jnp.broadcast_to(ids[p:p + 1, :], (8, LANES))
+                idx = jnp.broadcast_to(ids_ref[p:p + 1, start + at:start + at + LANES], (8, LANES))
                 low = jnp.bitwise_and(idx, LANES - 1)
                 top = idx >= LANES
-                for h in range(ce // 8):
-                    one = jnp.take_along_axis(tab_ref[h * 8:h * 8 + 8, 0:LANES], low, axis=1)
-                    two = jnp.take_along_axis(tab_ref[h * 8:h * 8 + 8, LANES:2 * LANES], low, axis=1)
+                for h in range(0, ce, 8):
+                    one = jnp.take_along_axis(low_tab[h:h + 8], low, axis=1)
+                    two = jnp.take_along_axis(top_tab[h:h + 8], low, axis=1)
                     parts.append(jnp.where(top, two, one))
             block = jnp.concatenate(parts, axis=0)
-            vec[at:at + count, g * LANES:(g + 1) * LANES] = block.T[0:count].astype(bf16)
+            vec[at:at + LANES, g * LANES:(g + 1) * LANES] = block.T.astype(bf16)
 
 
 def conv_pool(vec, toep, acc, length, widths, filters):
@@ -81,14 +80,14 @@
 
 def cnn_kernel(ids_ref, tab_ref, conv_ref, bias_ref, proj_hbm, gate_hbm, trans_hbm, *rest,
                widths, filters, ce, length, layers, nt, start):
-    out_ref, vec, toep, acc, feat, proj, gate, trans, state, last, turn, sems = rest
+    out_ref, vec, toep, acc, feat, proj, gate, trans, state, last, sems = rest
     copies = [pltpu.make_async_copy(s, d, sems.at[i]) for i, (s, d) in enumerate(
         ((proj_hbm, proj), (gate_hbm, gate), (trans_hbm, trans)))]
     for c in copies:
         c.start()
     words = out_ref.shape[0]
     prep_toeplitz(conv_ref, toep, ce, widths, filters)
-    lookup(ids_ref, start, words, tab_ref, vec, turn, length, ce)
+    lookup(ids_ref, start, words, tab_ref, vec, length, ce)
     conv_pool(vec, toep, acc, length, widths, filters)
     for c in copies:
         c.wait()
@@ -142,7 +141,6 @@
             pltpu.VMEM(trans_weight.shape, bf16),
             pltpu.VMEM((words, model), bf16),
             pltpu.VMEM((words, model), bf16),
-            pltpu.VMEM((LANES, LANES), f32),
             pltpu.SemaphoreType.DMA((3,)),
         ],
         compiler_params=params(),
@@ -177,17 +175,14 @@
     return jnp.where(apart == bits, place - start, -1)
 
 
-def scores_of(rows, words, metas, apart, place, score, prob):
-    at, top, aim = 0, None, None
-    for ref, meta in zip(words, metas):
+def scores_of(rows, words, score, prob):
+    at, top = 0, None
+    for ref in words:
         n = ref.shape[0]
         piece = lax.dot_general(rows[...], ref[...], (((1,), (1,)), ((), ())), preferred_element_type=f32)
         score[:, at:at + n] = piece
-        lane = lax.broadcasted_iota(jnp.int32, piece.shape, 1)
-        hit = jnp.sum(jnp.where(lane == spots(apart, place, meta), piece, 0.0), axis=1, keepdims=True)
         best = jnp.max(piece, axis=1, keepdims=True)
         top = best if top is None else jnp.maximum(top, best)
-        aim = hit if aim is None else aim + hit
         at += n
     at, total = 0, None
     for ref in words:
@@ -197,31 +192,26 @@
         part = jnp.sum(w.astype(f32), axis=1, keepdims=True)
         total = part if total is None else total + part
         at += n
-    return top, total, aim
-
-
-def sums_of(words, metas, apart, place, prob, hot, out, target, before=None):
+    return top, total
+
+
+def hot_words(words, metas, apart, place, hot):
     at = 0
     for ref, meta in zip(words, metas):
         n = ref.shape[0]
-        lane = lax.broadcasted_iota(jnp.int32, (prob.shape[0], n), 1)
+        lane = lax.broadcasted_iota(jnp.int32, (hot.shape[0], n), 1)
         hot[:, at:at + n] = jnp.where(lane == spots(apart, place, meta), 1.0, 0.0).astype(bf16)
         at += n
-    model = out.shape[1]
-    for n in range(0, model, 256):
-        at, res, aim = 0, None, None
-        for ref in words:
-            size = ref.shape[0]
-            block = ref[:, n:n + 256]
-            one = jnp.dot(prob[:, at:at + size], block, preferred_element_type=f32)
-            two = jnp.dot(hot[:, at:at + size], block, preferred_element_type=f32)
-            res = one if res is None else res + one
-            aim = two if aim is None else aim + two
-            at += size
-        out[:, n:n + 256] = res
-        if before is not None:
-            aim = aim + before[:, n:n + 256].astype(f32)
-        target[:, n:n + 256] = aim.astype(bf16)
+
+
+def product(left, words, n, size):
+    at, res = 0, None
+    for ref in words:
+        count = ref.shape[0]
+        d = jnp.dot(left[:, at:at + count], ref[:, n:n + size], preferred_element_type=f32)
+        res = d if res is None else res + d
+        at += count
+    return res
 
 
 def load_rows(hid, rows):
@@ -235,12 +225,13 @@
     hid, words = refs[:nh], refs[nh:nh + len(metas)]
     out, target, stats, rows, score, prob, hot = refs[nh + len(metas):]
     load_rows(hid, rows)
-    apart, place = aims(me_ref, hid, local)
-    top, total, aim = scores_of(rows, words, metas, apart, place, score, prob)
+    top, total = scores_of(rows, words, score, prob)
     stats[:, 0:LANES] = jnp.broadcast_to(top, (top.shape[0], LANES))
     stats[:, LANES:2 * LANES] = jnp.broadcast_to(total, (top.shape[0], LANES))
-    stats[:, 2 * LANES:3 * LANES] = jnp.broadcast_to(aim, (top.shape[0], LANES))
-    sums_of(words, metas, apart, place, prob, hot, out, target)
+    hot_words(words, metas, *aims(me_ref, hid, local), hot)
+    for n in range(0, out.shape[1], 256):
+        out[:, n:n + 256] = product(prob, words, n, 256)
+        target[:, n:n + 256] = product(hot, words, n, 256).astype(bf16)
 
 
 def cost(flops, size, trans=0):
@@ -257,7 +248,7 @@
     return pl.pallas_call(
         functools.partial(first_kernel, nh=len(hid), metas=metas, local=local),
         out_shape=[jax.ShapeDtypeStruct((rows, model), f32), jax.ShapeDtypeStruct((rows, model), bf16),
-                   jax.ShapeDtypeStruct((rows, 3 * LANES), f32)],
+                   jax.ShapeDtypeStruct((rows, 2 * LANES), f32)],
         in_specs=[SM] + [VM] * (len(hid) + len(words)), out_specs=[VM] * 3,
         scratch_shapes=[pltpu.VMEM((rows, model), bf16), pltpu.VMEM((rows, count), f32),
                         pltpu.VMEM((rows, count), bf16), pltpu.VMEM((rows, count), bf16)],
@@ -266,104 +257,108 @@
     )(me, *hid, *words)
 
 
-def score_kernel(me_ref, *refs, nh, metas, local):
+def last_kernel(me_ref, *refs, nh, metas, group, local):
     hid, words = refs[:nh], refs[nh:nh + len(metas)]
-    stats, prob, tops, lines, rows, score = refs[nh + len(metas):]
+    own, one, before, stats, value, target, facts, lines, rows, score, prob, hot = refs[nh + len(metas):]
     load_rows(hid, rows)
+    count, model = one.shape
     apart, place = aims(me_ref, hid, local)
-    top2, total2, aim2 = scores_of(rows, words, metas, apart, place, score, prob)
+    top2, total2 = scores_of(rows, words, score, prob)
+    hot_words(words, metas, apart, place, hot)
     top1, total1 = stats[:, 0:1], stats[:, LANES:LANES + 1]
     top = jnp.maximum(top1, top2)
-    total = jnp.exp(top1 - top) * total1 + jnp.exp(top2 - top) * total2
-    tops[...] = jnp.broadcast_to(top2, tops.shape)
-    to_lines(top + jnp.log(total), lines, 0)
-    to_lines(stats[:, 2 * LANES:2 * LANES + 1] + aim2, lines, lines.shape[0] // 2)
-
-
-def last_scores(me, hid, words, metas, local, stats):
-    model = words[0].shape[1]
-    rows = sum(h.shape[0] for h in hid)
+    s1, s2 = jnp.exp(top1 - top), jnp.exp(top2 - top)
+    total = s1 * total1 + s2 * total2
+    s1, s2 = s1 / total, s2 / total
+    whole = top + jnp.log(total)
+    centre = jnp.sum(own[0:LANES, :].astype(f32), axis=0, keepdims=True) * (1.0 / LANES)
+    aim = None
+    for n in range(0, model, 256):
+        cols = slice(n, n + 256)
+        mix = s1 * one[:, cols] + s2 * product(prob, words, n, 256)
+        value[:, cols] = (mix - centre[:, cols]).astype(bf16)
+        goal = product(hot, words, n, 256) + before[:, cols].astype(f32)
+        target[:, cols] = goal.astype(bf16)
+        part = jnp.sum(goal * rows[:, cols].astype(f32), axis=1, keepdims=True)
+        aim = part if aim is None else aim + part
+    inside = sum(jnp.where(apart == bits, 1.0, 0.0) for bits in group)
+    facts[:, 0:LANES] = jnp.broadcast_to(whole, (count, LANES))
+    facts[:, LANES:2 * LANES] = jnp.broadcast_to(inside, (count, LANES))
+    per = count // LANES
+    to_lines(whole, lines, 0)
+    to_lines(aim, lines, per)
+    for n in range(model // LANES):
+        lines[2 * per + n:2 * per + n + 1, :] = centre[:, n * LANES:(n + 1) * LANES]
+
+
+def last_fold(me, hid, words, metas, group, local, own, one, before, stats):
+    rows, model = one.shape
     count = sum(w.shape[0] for w in words)
     return pl.pallas_call(
-        functools.partial(score_kernel, nh=len(hid), metas=metas, local=local),
-        out_shape=[jax.ShapeDtypeStruct((rows, count), bf16), jax.ShapeDtypeStruct((rows, LANES), f32),
-                   jax.ShapeDtypeStruct((2 * rows // LANES, LANES), f32)],
-        in_specs=[SM] + [VM] * (len(hid) + len(words) + 1), out_specs=[VM] * 3,
-        scratch_shapes=[pltpu.VMEM((rows, model), bf16), pltpu.VMEM((rows, count), f32)],
-        compiler_params=params(), cost_estimate=cost(2 * rows * count * model, 2 * (rows + count) * model),
-        name="last_scores",
-    )(me, *hid, *words, stats)
-
-
-def sum_kernel(me_ref, *refs, nh, metas, local):
-    hid, words = refs[:nh], refs[nh:nh + len(metas)]
-    prob, before, out, target, hot = refs[nh + len(metas):]
-    apart, place = aims(me_ref, hid, local)
-    sums_of(words, metas, apart, place, prob, hot, out, target, before)
-
-
-def last_sums(me, hid, words, metas, local, prob, before):
-    rows, model = before.shape
-    count = prob.shape[1]
-    return pl.pallas_call(
-        functools.partial(sum_kernel, nh=len(hid), metas=metas, local=local),
-        out_shape=[jax.ShapeDtypeStruct((rows, model), f32), jax.ShapeDtypeStruct((rows, model), bf16)],
-        in_specs=[SM] + [VM] * (len(hid) + len(words) + 2), out_specs=[VM] * 2,
-        scratch_shapes=[pltpu.VMEM((rows, count), bf16)],
-        compiler_params=params(), cost_estimate=cost(4 * rows * count * model, 2 * (rows + count) * model),
-        name="last_sums",
-    )(me, *hid, *words, prob, before)
+        functools.partial(last_kernel, nh=len(hid), metas=metas, group=group, local=local),
+        out_shape=[jax.ShapeDtypeStruct((rows, model), bf16)] * 2 + [
+            jax.ShapeDtypeStruct((rows, 2 * LANES), f32),
+            jax.ShapeDtypeStruct((2 * rows // LANES + model // LANES, LANES), f32)],
+        in_specs=[SM] + [VM] * (len(hid) + len(words) + 4), out_specs=[VM] * 4,
+        scratch_shapes=[pltpu.VMEM((rows, model), bf16), pltpu.VMEM((rows, count), f32),
+                        pltpu.VMEM((rows, count), bf16), pltpu.VMEM((rows, count), bf16)],
+        compiler_params=params(), cost_estimate=cost(6 * rows * count * model, 2 * (rows + count) * model),
+        name="last_fold",
+    )(me, *hid, *words, own, one, before, stats)
 
 
 def combine_kernel(*refs, flips):
     nl = len(flips)
     lines = refs[:nl]
-
-    def value(j, i, kind):
+    value, target, facts, a_keep, a_send, b_keep, b_send, loss = refs[nl:]
+    count, model = value.shape
+    per = count // LANES
+    half, quarter = model // 2, count // 4
+
+    def line(j, i, kind):
         over, halves = flips[j]
         v = lines[j][kind * per + (i ^ over):kind * per + (i ^ over) + 1, :]
         return pltpu.roll(v, LANES // 2, axis=1) if halves else v
 
-    one, two, target, stats, tops, a_keep, a_send, b_keep, b_send, loss = refs[nl:]
-    per = lines[0].shape[0] // 2
-    count, model = one.shape
-    half, quarter = model // 2, count // 4
+    mus, shifts = [], []
+    for n in range(model // LANES):
+        row = slice(2 * per + n, 2 * per + n + 1)
+        mu = sum(ref[row, :] for ref in lines) * (1.0 / nl)
+        mus.append(jnp.broadcast_to(mu, (LANES, LANES)))
+        shifts.append(jnp.broadcast_to(lines[0][row, :] - mu, (LANES, LANES)))
     for i in range(per):
-        each = [value(j, i, 0) for j in range(nl)]
-        top = each[0]
-        for v in each[1:]:
-            top = jnp.maximum(top, v)
-        total = sum(jnp.exp(v - top) for v in each)
-        aim = sum(value(j, i, 1) for j in range(nl))
-        whole = top + jnp.log(total)
+        each = [line(j, i, 0) for j in range(nl)]
+        top = functools.reduce(jnp.maximum, each)
+        whole = top + jnp.log(sum(jnp.exp(v - top) for v in each))
         if i == 0:
-            loss[...] = whole - aim
+            loss[...] = whole - sum(line(j, i, 1) for j in range(nl))
         whole = jnp.broadcast_to(whole, (LANES, LANES)).T
         part = slice(i * LANES, (i + 1) * LANES)
-        c1 = jnp.exp(stats[part, 0:LANES] - whole)
-        c2 = jnp.exp(tops[part, :] - whole)
+        weight = jnp.exp(facts[part, 0:LANES] - whole)
+        inside = facts[part, LANES:2 * LANES]
         q = i * LANES // quarter
         at = i * LANES - q * quarter
         a, b = (a_keep, a_send)[q // 2], (b_keep, b_send)[q % 2]
         a_at, b_at = (q % 2) * quarter + at, (q // 2) * quarter + at
-        for n in range(0, model, LANES):
-            cols = slice(n, n + LANES)
-            mix = (c1 * one[part, cols] + c2 * two[part, cols] - target[part, cols].astype(f32)).astype(bf16)
-            if n < half:
+        for n in range(model // LANES):
+            cols = slice(n * LANES, (n + 1) * LANES)
+            mix = weight * (value[part, cols].astype(f32) + shifts[n])
+            mix = (mix - (target[part, cols].astype(f32) - inside * mus[n])).astype(bf16)
+            if n * LANES < half:
                 a[a_at:a_at + LANES, cols] = mix
             else:
-                b[b_at:b_at + LANES, n - half:n - half + LANES] = mix
-
-
-def combine(lines, flips, one, two, target, stats, tops):
-    rows, model = one.shape
+                b[b_at:b_at + LANES, n * LANES - half:(n + 1) * LANES - half] = mix
+
+
+def combine(lines, flips, value, target, facts):
+    rows, model = value.shape
     side = jax.ShapeDtypeStruct((rows // 2, model // 2), bf16)
     return pl.pallas_call(
         functools.partial(combine_kernel, flips=flips),
         out_shape=[side] * 4 + [jax.ShapeDtypeStruct((1, LANES), f32)],
-        in_specs=[VM] * (len(lines) + 5), out_specs=[VM] * 5,
-        compiler_params=params(), cost_estimate=cost(8 * rows * model, 12 * rows * model), name="combine",
-    )(*lines, one, two, target, stats, tops)
+        in_specs=[VM] * (len(lines) + 3), out_specs=[VM] * 5,
+        compiler_params=params(), cost_estimate=cost(8 * rows * model, 8 * rows * model), name="combine",
+    )(*lines, value, target, facts)
 
 
 def plus(a, b):
@@ -421,21 +416,23 @@
     local, length = char_ids.shape
     mine = hidden.shape[0]
 
-    goal = targets.reshape(mine, 1)
-    code = jnp.concatenate([goal // 256, goal % 256], axis=1).astype(bf16)
-    rows = jnp.concatenate([hidden, code, jnp.zeros((mine, LANES - 2), bf16)], axis=1)
+    rows, goal = hidden, targets.reshape(1, mine)
     for bit in rest:
         rows = jnp.concatenate([rows, swap(rows, bit)], axis=0)
-
-    tab_t = char_table.T.astype(f32)
-    weights = (tab_t, conv_weight, proj_weight, gate_weight, trans_weight, gate_bias)
-    sizes = (local // 2, local // 2)
-    pieces, marks, start = [], [], 0
-    for i, size in enumerate(sizes):
-        pieces.append(embed(char_ids, length, start, size, *weights))
-        marks.append(start)
-        start += size
+        goal = jnp.concatenate([goal, swap(goal, bit)], axis=1)
+    goal = goal.reshape(-1, 1)
+    code = jnp.concatenate([goal // 256, goal % 256], axis=1).astype(bf16)
+    rows = jnp.concatenate([rows, jnp.pad(code, ((0, 0), (0, LANES - 2)))], axis=1)
+
+    weights = (char_table.T, conv_weight, proj_weight, gate_weight, trans_weight, gate_bias)
+    size = local // 2
+    marks = (0, size)
+    ids = char_ids.T
+    e0 = embed(ids, length, 0, size, *weights)
     hid = [rows] + [swap(rows, b) for b in (bit_b, bit_a, bit_a | bit_b)]
+    e1 = embed(ids, length, size, size, *weights)
+    held, *hid = lax.optimization_barrier((e1, *hid))
+    pieces = [e0, held]
     cores = [swap(e, core) for e in pieces]
     nears = [swap(e, near) for e in pieces]
     fars = [swap(e, core) for e in nears]
@@ -447,14 +444,14 @@
         me, hid, pieces + cores + nears[:-late] + fars[:-late],
         meta[0] + meta[1] + meta[2][:-late] + meta[3][:-late], local)
     words, metas = nears[-late:] + fars[-late:], meta[2][-late:] + meta[3][-late:]
-    prob, tops, line = last_scores(me, hid, words, metas, local, stats)
+    value, target, facts, line = last_fold(
+        me, hid, words, metas, (0, core, near, core | near), local, e0, one, target, stats)
     bits = [bit_a, bit_b] + rest
     others = [sum(b for j, b in enumerate(bits) if k >> j & 1) for k in range(1, 1 << len(bits))]
     order = rest + [bit_b, bit_a]
     flips = tuple((sum(1 << (j - 1) for j, b in enumerate(order) if j and o & b), bool(o & rest[0])) for o in others)
     lines = [swap(line, o) for o in others]
-    two, target = last_sums(me, hid, words, metas, local, prob, target)
-    a_keep, a_send, b_keep, b_send, loss = combine([line] + lines, ((0, False),) + flips, one, two, target, stats, tops)
+    a_keep, a_send, b_keep, b_send, loss = combine([line] + lines, ((0, False),) + flips, value, target, facts)
     a_keep, a_send, b_keep, b_send = add_halves(a_keep, swap(a_send, bit_a), b_keep, swap(b_send, bit_b))
     keep, send = add_across(a_keep, swap(a_send, bit_b), b_keep, swap(b_send, bit_a))
     for bit in rest[:0:-1]:

time: 120 us -> 113 us (0.942)
  Pallas kernels: 54 us -> 49 us
  starting transfers between devices: 25.2 us -> 29.2 us
  local copies, waits for them, and re-layouts: 7.58 us -> 4.8 us
  other arithmetic: 3.59 us -> 1.72 us
    ppermute x22 -> x23, starting transfers between devices: 25.2 us -> 29.2 us  [swap(): return lax.ppermute(x, axes, [(i, i ^ bits) for i in range(devices)])]
    pallas_call x2 -> x1, Pallas kernels: 9.4 us -> 6.36 us  [last_fold(): pl.pallas_call(functools.partial(last_kernel, nh=len(hid), metas=metas, g...]
    unnamed x39 -> x44, local copies, waits for them, and re-layouts: 5.22 us -> 3.57 us
    convert_element_type x1 -> x0, other arithmetic: 1.3 us -> none  [per_device(): tab_t = char_table.T.astype(f32)]
    ppermute x22 -> x23, waiting for transfers between devices: 28.2 us -> 27.5 us  [swap(): return lax.ppermute(x, axes, [(i, i ^ bits) for i in range(devices)])]
  transfers between devices with their start and end apart: 22 -> 23, of which waited for: 8 -> 10; matrix products, arithmetic and copies ran while one was open for 4% -> 1% of each run, Pallas kernels for 35% -> 31%
where the time goes in v4:
time: 113 us
  Pallas kernels  49 us (43%)
  starting transfers between devices  29.2 us (26%)
  waiting for transfers between devices  27.5 us (24%)
  local copies, waits for them, and re-layouts  4.8 us (4%)
  other arithmetic  1.72 us (2%)
    ppermute x23, starting transfers between devices, swap(): return lax.ppermute(x, axes, [(i, i ^ bits) for i in range(devices)])  29.2 us
    ppermute x23, waiting for transfers between devices, swap(): return lax.ppermute(x, axes, [(i, i ^ bits) for i in range(devices)])  27.5 us
    pallas_call x2, Pallas kernels, embed(): pl.pallas_call(functools.partial(cnn_kernel, widths=widths, filters=filte...  26 us
    pallas_call x1, Pallas kernels, first_fold(): pl.pallas_call(functools.partial(first_kernel, nh=len(hid), metas=metas,...  9.32 us
    pallas_call x1, Pallas kernels, last_fold(): pl.pallas_call(functools.partial(last_kernel, nh=len(hid), metas=metas, g...  6.36 us
    unnamed x44, local copies, waits for them, and re-layouts  3.57 us
    pallas_call x1, Pallas kernels, combine(): pl.pallas_call(functools.partial(combine_kernel, flips=flips), out_shape=...  3.42 us
  transfers between devices with their start and end apart: 23, of which 10 were waited for; matrix products, arithmetic and copies ran while one was open for 1% of the time, Pallas kernels for 31%

profile of v4, /device:TPU:0, one launch (start us, length us, event | category | flops | bytes accessed | tf_op | source)
XLA Modules:
  0.0 113.1 jit_solution(9287419454144657310)
XLA Ops:
  0.6 4.1 %collective-permute-start.1 = (s32[1,64]{1,0:T(1,128)}, s32[1,64]{1,0:T(1,128)S(1)}, u32[]{:S(2)}, u32[]{:S(2)}) collective-permute-start(s32[1,64]{1,0:T(1,128)} %bitcast.13), channel_id=1, source_target_pairs={{0,2},{1,3},{2,0},{3,1},{4,6},{5,7},{6,4},{7,5},{8,10},{9,11},{10,... | collective-permute-start | bytes 776 | tf_op jit(solution)/shard_map/ppermute | solution.py:409
  4.8 12.9 %embed.3.refs_4_.refs_6_ = bf16[256,1024]{1,0:T(8,128)(2,1)} custom-call(s32[50,512]{1,0:T(8,128)} %bitcast.15, bf16[16,256]{1,0:T(8,128)(2,1)} %bitcast.17, bf16[112,896]{1,0:T(8,128)(2,1)} %conv_ref.3, f32[2,1024]{1,0:T(2,128)} %bias_ref.3, bf16[896,1024]{1,0:T(8,128)(2,1)} %proj_hbm.3, bf16[2,1024,1024]{2,1,0:T(8,128)(2,1)} %gate_hbm.3, ...), custom_call_target="tpu_custom_call" | custom-call | flops 8489271296 | bytes 12582912 | tf_op jit(solution)/shard_map/embed/pallas_call | solution.py:128
  17.8 1.9 %collective-permute-start.9 = (bf16[256,1024]{1,0:T(8,128)(2,1)}, bf16[256,1024]{1,0:T(8,128)(2,1)S(1)}, u32[]{:S(2)}, u32[]{:S(2)}) collective-permute-start(bf16[256,1024]{1,0:T(8,128)(2,1)} %embed.3.refs_4_.refs_6_), channel_id=1, source_target_pairs={{0,1},{1,0},{2,3},{3,2},{4,5},{5,4},{6,7},{7,6},{8,9},{9,8},{10,11... | collective-permute-start | bytes 1572872 | tf_op jit(solution)/shard_map/ppermute | solution.py:409
  20.0 2.5 %collective-permute-start.4 = (bf16[128,1152]{1,0:T(8,128)(2,1)S(1)}, bf16[128,1152]{1,0:T(8,128)(2,1)S(1)}, u32[]{:S(2)}, u32[]{:S(2)}) collective-permute-start(bf16[128,1152]{1,0:T(8,128)(2,1)S(1)} %fusion.1.refs_0_), channel_id=1, source_target_pairs={{0,24},{1,25},{2,26},{3,27},{4,28},{5,29},{6,30},{7,31},{8,16},{9,... | collective-permute-start | bytes 884744 | tf_op jit(solution)/shard_map/ppermute | solution.py:409
  23.5 13.1 %embed.2.refs_5_ = bf16[256,1024]{1,0:T(8,128)(2,1)} custom-call(s32[50,512]{1,0:T(8,128)} %bitcast.16, bf16[16,256]{1,0:T(8,128)(2,1)} %bitcast.18, bf16[112,896]{1,0:T(8,128)(2,1)} %conv_ref.3, f32[2,1024]{1,0:T(2,128)} %bias_ref.3, bf16[896,1024]{1,0:T(8,128)(2,1)} %proj_hbm.3, bf16[2,1024,1024]{2,1,0:T(8,128)(2,1)} %gate_hbm.3, ...), custom_call_target="tpu_custom_call" | custom-call | flops 8489271296 | bytes 12582912 | tf_op jit(solution)/shard_map/embed/pallas_call | solution.py:128
  37.6 11.7 %collective-permute-done.5.refs_4_ = bf16[256,1024]{1,0:T(8,128)(2,1)S(1)} collective-permute-done((bf16[256,1024]{1,0:T(8,128)(2,1)}, bf16[256,1024]{1,0:T(8,128)(2,1)S(1)}, u32[]{:S(2)}, u32[]{:S(2)}) %collective-permute-start.5) | collective-permute-done | bytes 524320 | tf_op jit(solution)/shard_map/ppermute | solution.py:409
  50.1 9.3 %first_fold.1 = (f32[512,1024]{1,0:T(8,128)}, bf16[512,1024]{1,0:T(8,128)(2,1)}, f32[512,256]{1,0:T(8,128)}) custom-call(s32[1]{0:T(128)} %bitcast.me_ref, bf16[128,1152]{1,0:T(8,128)(2,1)} %copy-done, bf16[128,1152]{1,0:T(8,128)(2,1)} %copy-done.6, bf16[128,1152]{1,0:T(8,128)(2,1)} %copy-done.5, bf16[128,1152]{1,0:T(8,128)(2,1)} %copy-done.4, ...), custom_call_target="tpu_custom_call" | custom-call | flops 4831838208 | bytes 4194304 | tf_op jit(solution)/shard_map/first_fold/pallas_call | solution.py:248
  60.3 6.4 %last_fold.1 = (bf16[512,1024]{1,0:T(8,128)(2,1)}, bf16[512,1024]{1,0:T(8,128)(2,1)}, f32[512,256]{1,0:T(8,128)}, f32[16,128]{1,0:T(8,128)}) custom-call(s32[1]{0:T(128)} %bitcast.me_ref, bf16[128,1152]{1,0:T(8,128)(2,1)} %copy-done, bf16[128,1152]{1,0:T(8,128)(2,1)} %copy-done.6, bf16[128,1152]{1,0:T(8,128)(2,1)} %copy-done.5, bf16[128,1152]{1,0:T(8,128)(2,1)} %copy-done.4, ...), custom_call_target="tpu_custom_call" | custom-call | flops 1610612736 | bytes 2097152 | tf_op jit(solution)/shard_map/last_fold/pallas_call | solution.py:297
  66.6 4.5 %collective-permute-start.17 = (f32[16,128]{1,0:T(8,128)}, f32[16,128]{1,0:T(8,128)S(1)}, u32[]{:S(2)}, u32[]{:S(2)}) collective-permute-start(f32[16,128]{1,0:T(8,128)} %get-tuple-element.33.refs_0_), channel_id=1, source_target_pairs={{0,26},{1,27},{2,24},{3,25},{4,30},{5,31},{6,28},{7,29},{8,18},{9,... | collective-permute-start | bytes 24584 | tf_op jit(solution)/shard_map/ppermute | solution.py:409
  71.4 2.5 %collective-permute-start.15 = (f32[16,128]{1,0:T(8,128)}, f32[16,128]{1,0:T(8,128)S(1)}, u32[]{:S(2)}, u32[]{:S(2)}) collective-permute-start(f32[16,128]{1,0:T(8,128)} %get-tuple-element.33.refs_0_), channel_id=1, source_target_pairs={{0,10},{1,11},{2,8},{3,9},{4,14},{5,15},{6,12},{7,13},{8,2},{9,3},... | collective-permute-start | bytes 24584 | tf_op jit(solution)/shard_map/ppermute | solution.py:409
  74.3 2.5 %collective-permute-start.13 = (f32[16,128]{1,0:T(8,128)}, f32[16,128]{1,0:T(8,128)S(1)}, u32[]{:S(2)}, u32[]{:S(2)}) collective-permute-start(f32[16,128]{1,0:T(8,128)} %get-tuple-element.33.refs_0_), channel_id=1, source_target_pairs={{0,24},{1,25},{2,26},{3,27},{4,28},{5,29},{6,30},{7,31},{8,16},{9,... | collective-permute-start | bytes 24584 | tf_op jit(solution)/shard_map/ppermute | solution.py:409
  79.0 1.6 %collective-permute-done.12.refs_2_ = f32[16,128]{1,0:T(8,128)S(1)} collective-permute-done((f32[16,128]{1,0:T(8,128)}, f32[16,128]{1,0:T(8,128)S(1)}, u32[]{:S(2)}, u32[]{:S(2)}) %collective-permute-start.12) | collective-permute-done | bytes 8224 | tf_op jit(solution)/shard_map/ppermute | solution.py:409
  81.7 3.4 %combine.1 = (bf16[256,512]{1,0:T(8,128)(2,1)}, bf16[256,512]{1,0:T(8,128)(2,1)}, bf16[256,512]{1,0:T(8,128)(2,1)}, bf16[256,512]{1,0:T(8,128)(2,1)}, f32[1,128]{1,0:T(1,128)}) custom-call(f32[16,128]{1,0:T(8,128)} %get-tuple-element.33.refs_0_, f32[16,128]{1,0:T(8,128)} %copy-done.18, f32[16,128]{1,0:T(8,128)} %copy-done.17, f32[16,128]{1,0:T(8,128)} %copy-done.16, ...), custom_call_target="tpu_custom_call" | custom-call | flops 4194304 | bytes 4194304 | tf_op jit(solution)/shard_map/combine/pallas_call | solution.py:356
  85.7 1.5 %collective-permute-start.19 = (bf16[256,512]{1,0:T(8,128)(2,1)}, bf16[256,512]{1,0:T(8,128)(2,1)S(1)}, u32[]{:S(2)}, u32[]{:S(2)}) collective-permute-start(bf16[256,512]{1,0:T(8,128)(2,1)} %get-tuple-element.41), channel_id=1, source_target_pairs={{0,16},{1,17},{2,18},{3,19},{4,20},{5,21},{6,22},{7,23},{8,24},{9,... | collective-permute-start | bytes 786440 | tf_op jit(solution)/shard_map/ppermute | solution.py:409
  87.2 4.5 %collective-permute-done.18.refs_1_ = bf16[256,512]{1,0:T(8,128)(2,1)S(1)} collective-permute-done((bf16[256,512]{1,0:T(8,128)(2,1)}, bf16[256,512]{1,0:T(8,128)(2,1)S(1)}, u32[]{:S(2)}, u32[]{:S(2)}) %collective-permute-start.18) | collective-permute-done | bytes 262176 | tf_op jit(solution)/shard_map/ppermute | solution.py:409
  92.9 2.0 %add_halves.1 = (bf16[128,512]{1,0:T(8,128)(2,1)}, bf16[128,512]{1,0:T(8,128)(2,1)}, bf16[128,512]{1,0:T(8,128)(2,1)}, bf16[128,512]{1,0:T(8,128)(2,1)}) custom-call(bf16[256,512]{1,0:T(8,128)(2,1)} %get-tuple-element.38.refs_0_, bf16[256,512]{1,0:T(8,128)(2,1)} %copy-done.7, bf16[256,512]{1,0:T(8,128)(2,1)} %get-tuple-element.40.refs_2_, ...), custom_call_target="tpu_custom_call" | custom-call | flops 131072 | bytes 1048576 | tf_op jit(solution)/shard_map/add_halves/pallas_call | solution.py:380
  94.9 1.5 %collective-permute-start.20 = (bf16[128,512]{1,0:T(8,128)(2,1)}, bf16[128,512]{1,0:T(8,128)(2,1)S(1)}, u32[]{:S(2)}, u32[]{:S(2)}) collective-permute-start(bf16[128,512]{1,0:T(8,128)(2,1)} %get-tuple-element.43), channel_id=1, source_target_pairs={{0,16},{1,17},{2,18},{3,19},{4,20},{5,21},{6,22},{7,23},{8,24},{9,... | collective-permute-start | bytes 393224 | tf_op jit(solution)/shard_map/ppermute | solution.py:409
  96.5 1.5 %collective-permute-start.21 = (bf16[128,512]{1,0:T(8,128)(2,1)}, bf16[128,512]{1,0:T(8,128)(2,1)S(1)}, u32[]{:S(2)}, u32[]{:S(2)}) collective-permute-start(bf16[128,512]{1,0:T(8,128)(2,1)} %get-tuple-element.45), channel_id=1, source_target_pairs={{0,8},{1,9},{2,10},{3,11},{4,12},{5,13},{6,14},{7,15},{8,0},{9,1},... | collective-permute-start | bytes 393224 | tf_op jit(solution)/shard_map/ppermute | solution.py:409
  97.9 2.2 %collective-permute-done.20.a_got = bf16[128,512]{1,0:T(8,128)(2,1)S(1)} collective-permute-done((bf16[128,512]{1,0:T(8,128)(2,1)}, bf16[128,512]{1,0:T(8,128)(2,1)S(1)}, u32[]{:S(2)}, u32[]{:S(2)}) %collective-permute-start.20) | collective-permute-done | bytes 131104 | tf_op jit(solution)/shard_map/ppermute | solution.py:409
  100.1 1.5 %collective-permute-done.21.b_got = bf16[128,512]{1,0:T(8,128)(2,1)S(1)} collective-permute-done((bf16[128,512]{1,0:T(8,128)(2,1)}, bf16[128,512]{1,0:T(8,128)(2,1)S(1)}, u32[]{:S(2)}, u32[]{:S(2)}) %collective-permute-start.21) | collective-permute-done | bytes 131104 | tf_op jit(solution)/shard_map/ppermute | solution.py:409
  102.3 1.8 %add_across.1 = (bf16[64,1024]{1,0:T(8,128)(2,1)}, bf16[64,1024]{1,0:T(8,128)(2,1)}) custom-call(bf16[128,512]{1,0:T(8,128)(2,1)} %get-tuple-element.42.a_keep, bf16[128,512]{1,0:T(8,128)(2,1)} %copy-done.10, bf16[128,512]{1,0:T(8,128)(2,1)} %get-tuple-element.44.b_keep, bf16[128,512]{1,0:T(8,128)(2,1)} %copy-done.11), custom_call_target="tpu_custom_call" | custom-call | flops 131072 | bytes 786432 | tf_op jit(solution)/shard_map/add_across/pallas_call | solution.py:396
  104.1 2.6 %collective-permute-start.22 = (bf16[64,1024]{1,0:T(8,128)(2,1)}, bf16[64,1024]{1,0:T(8,128)(2,1)S(1)}, u32[]{:S(2)}, u32[]{:S(2)}) collective-permute-start(bf16[64,1024]{1,0:T(8,128)(2,1)} %get-tuple-element.47), channel_id=1, source_target_pairs={{0,2},{1,3},{2,0},{3,1},{4,6},{5,7},{6,4},{7,5},{8,10},{9,11},{10,... | collective-permute-start | bytes 393224 | tf_op jit(solution)/shard_map/ppermute | solution.py:409
  107.8 3.7 %collective-permute-done.22 = bf16[64,1024]{1,0:T(8,128)(2,1)S(1)} collective-permute-done((bf16[64,1024]{1,0:T(8,128)(2,1)}, bf16[64,1024]{1,0:T(8,128)(2,1)S(1)}, u32[]{:S(2)}, u32[]{:S(2)}) %collective-permute-start.22) | collective-permute-done | bytes 131104 | tf_op jit(solution)/shard_map/ppermute | solution.py:409
  111.5 1.6 %add_convert_fusion = bf16[64,1024]{1,0:T(8,128)(2,1)} fusion(bf16[64,1024]{1,0:T(8,128)(2,1)S(1)} %collective-permute-done.22, bf16[64,1024]{1,0:T(8,128)(2,1)} %get-tuple-element.46), kind=kLoop, calls=%fused_computation.3 | loop fusion | flops 262144 | bytes 393216 | tf_op jit(solution)/shard_map/convert_element_type | solution.py:365
  (80 shorter events, 11.4 us)
Async XLA Ops:
  0.6 19.0 %collective-permute-start.1 = (s32[1,64]{1,0:T(1,128)}, s32[1,64]{1,0:T(1,128)S(1)}, u32[]{:S(2)}, u32[]{:S(2)}) collective-permute-start(s32[1,64]{1,0:T(1,128)} %bitcast.13), channel_id=1, source_target_pairs={{0,2},{1,3},{2,0},{3,1},{4,6},{5,7},{6,4},{7,5},{8,10},{9,11},{10,... | collective-permute-start | bytes 776 | tf_op jit(solution)/shard_map/ppermute | solution.py:409
  4.7 15.2 %collective-permute-start = (bf16[64,1024]{1,0:T(8,128)(2,1)}, bf16[64,1024]{1,0:T(8,128)(2,1)S(1)}, u32[]{:S(2)}, u32[]{:S(2)}) collective-permute-start(bf16[64,1024]{1,0:T(8,128)(2,1)} %param.16), channel_id=1, source_target_pairs={{0,2},{1,3},{2,0},{3,1},{4,6},{5,7},{6,4},{7,5},{8,10},{9,11},{10,... | collective-permute-start | bytes 393224 | tf_op jit(solution)/shard_map/ppermute | solution.py:409
  17.8 19.7 %collective-permute-start.9 = (bf16[256,1024]{1,0:T(8,128)(2,1)}, bf16[256,1024]{1,0:T(8,128)(2,1)S(1)}, u32[]{:S(2)}, u32[]{:S(2)}) collective-permute-start(bf16[256,1024]{1,0:T(8,128)(2,1)} %embed.3.refs_4_.refs_6_), channel_id=1, source_target_pairs={{0,1},{1,0},{2,3},{3,2},{4,5},{5,4},{6,7},{7,6},{8,9},{9,8},{10,11... | collective-permute-start | bytes 1572872 | tf_op jit(solution)/shard_map/ppermute | solution.py:409
  20.0 17.0 %copy-start.1 = (bf16[256,1024]{1,0:T(8,128)(2,1)S(1)}, bf16[256,1024]{1,0:T(8,128)(2,1)}, u32[]{:S(2)}) copy-start(bf16[256,1024]{1,0:T(8,128)(2,1)} %embed.3.refs_4_.refs_6_) | copy-start | bytes 1572868
  20.0 16.7 %collective-permute-start.4 = (bf16[128,1152]{1,0:T(8,128)(2,1)S(1)}, bf16[128,1152]{1,0:T(8,128)(2,1)S(1)}, u32[]{:S(2)}, u32[]{:S(2)}) collective-permute-start(bf16[128,1152]{1,0:T(8,128)(2,1)S(1)} %fusion.1.refs_0_), channel_id=1, source_target_pairs={{0,24},{1,25},{2,26},{3,27},{4,28},{5,29},{6,30},{7,31},{8,16},{9,... | collective-permute-start | bytes 884744 | tf_op jit(solution)/shard_map/ppermute | solution.py:409
  22.5 14.2 %collective-permute-start.3 = (bf16[128,1152]{1,0:T(8,128)(2,1)S(1)}, bf16[128,1152]{1,0:T(8,128)(2,1)S(1)}, u32[]{:S(2)}, u32[]{:S(2)}) collective-permute-start(bf16[128,1152]{1,0:T(8,128)(2,1)S(1)} %fusion.1.refs_0_), channel_id=1, source_target_pairs={{0,8},{1,9},{2,10},{3,11},{4,12},{5,13},{6,14},{7,15},{8,0},{9,1},... | collective-permute-start | bytes 884744 | tf_op jit(solution)/shard_map/ppermute | solution.py:409
  23.0 13.7 %collective-permute-start.2 = (bf16[128,1152]{1,0:T(8,128)(2,1)S(1)}, bf16[128,1152]{1,0:T(8,128)(2,1)S(1)}, u32[]{:S(2)}, u32[]{:S(2)}) collective-permute-start(bf16[128,1152]{1,0:T(8,128)(2,1)S(1)} %fusion.1.refs_0_), channel_id=1, source_target_pairs={{0,16},{1,17},{2,18},{3,19},{4,20},{5,21},{6,22},{7,23},{8,24},{9,... | collective-permute-start | bytes 884744 | tf_op jit(solution)/shard_map/ppermute | solution.py:409
  36.7 12.5 %collective-permute-start.5 = (bf16[256,1024]{1,0:T(8,128)(2,1)}, bf16[256,1024]{1,0:T(8,128)(2,1)S(1)}, u32[]{:S(2)}, u32[]{:S(2)}) collective-permute-start(bf16[256,1024]{1,0:T(8,128)(2,1)} %embed.2.refs_5_), channel_id=1, source_target_pairs={{0,1},{1,0},{2,3},{3,2},{4,5},{5,4},{6,7},{7,6},{8,9},{9,8},{10,11... | collective-permute-start | bytes 1572872 | tf_op jit(solution)/shard_map/ppermute | solution.py:409
  37.0 12.3 %collective-permute-start.7 = (bf16[256,1024]{1,0:T(8,128)(2,1)S(1)}, bf16[256,1024]{1,0:T(8,128)(2,1)S(1)}, u32[]{:S(2)}, u32[]{:S(2)}) collective-permute-start(bf16[256,1024]{1,0:T(8,128)(2,1)S(1)} %copy-done.1), channel_id=1, source_target_pairs={{0,4},{1,5},{2,6},{3,7},{4,0},{5,1},{6,2},{7,3},{8,12},{9,13},{10,... | collective-permute-start | bytes 1572872 | tf_op jit(solution)/shard_map/ppermute | solution.py:409
  37.0 12.3 %collective-permute-start.8 = (bf16[256,1024]{1,0:T(8,128)(2,1)}, bf16[256,1024]{1,0:T(8,128)(2,1)}, u32[]{:S(2)}, u32[]{:S(2)}) collective-permute-start(bf16[256,1024]{1,0:T(8,128)(2,1)} %embed.2.refs_5_), channel_id=1, source_target_pairs={{0,4},{1,5},{2,6},{3,7},{4,0},{5,1},{6,2},{7,3},{8,12},{9,13},{10,... | collective-permute-start | bytes 1572872 | tf_op jit(solution)/shard_map/ppermute | solution.py:409
  37.5 11.8 %collective-permute-start.10 = (bf16[256,1024]{1,0:T(8,128)(2,1)S(1)}, bf16[256,1024]{1,0:T(8,128)(2,1)}, u32[]{:S(2)}, u32[]{:S(2)}) collective-permute-start(bf16[256,1024]{1,0:T(8,128)(2,1)S(1)} %collective-permute-done.9.refs_8_), channel_id=1, source_target_pairs={{0,4},{1,5},{2,6},{3,7},{4,0},{5,1},{6,2},{7,3},{8,12},{9,13},{10,... | collective-permute-start | bytes 1572872 | tf_op jit(solution)/shard_map/ppermute | solution.py:409
  49.3 10.2 %collective-permute-start.6 = (bf16[256,1024]{1,0:T(8,128)(2,1)S(1)}, bf16[256,1024]{1,0:T(8,128)(2,1)S(1)}, u32[]{:S(2)}, u32[]{:S(2)}) collective-permute-start(bf16[256,1024]{1,0:T(8,128)(2,1)S(1)} %collective-permute-done.5.refs_4_), channel_id=1, source_target_pairs={{0,4},{1,5},{2,6},{3,7},{4,0},{5,1},{6,2},{7,3},{8,12},{9,13},{10,... | collective-permute-start | bytes 1572872 | tf_op jit(solution)/shard_map/ppermute | solution.py:409
  66.6 10.1 %collective-permute-start.17 = (f32[16,128]{1,0:T(8,128)}, f32[16,128]{1,0:T(8,128)S(1)}, u32[]{:S(2)}, u32[]{:S(2)}) collective-permute-start(f32[16,128]{1,0:T(8,128)} %get-tuple-element.33.refs_0_), channel_id=1, source_target_pairs={{0,26},{1,27},{2,24},{3,25},{4,30},{5,31},{6,28},{7,29},{8,18},{9,... | collective-permute-start | bytes 24584 | tf_op jit(solution)/shard_map/ppermute | solution.py:409
  71.1 6.2 %collective-permute-start.16 = (f32[16,128]{1,0:T(8,128)}, f32[16,128]{1,0:T(8,128)S(1)}, u32[]{:S(2)}, u32[]{:S(2)}) collective-permute-start(f32[16,128]{1,0:T(8,128)} %get-tuple-element.33.refs_0_), channel_id=1, source_target_pairs={{0,18},{1,19},{2,16},{3,17},{4,22},{5,23},{6,20},{7,21},{8,26},{9,... | collective-permute-start | bytes 24584 | tf_op jit(solution)/shard_map/ppermute | solution.py:409
  71.4 6.4 %collective-permute-start.15 = (f32[16,128]{1,0:T(8,128)}, f32[16,128]{1,0:T(8,128)S(1)}, u32[]{:S(2)}, u32[]{:S(2)}) collective-permute-start(f32[16,128]{1,0:T(8,128)} %get-tuple-element.33.refs_0_), channel_id=1, source_target_pairs={{0,10},{1,11},{2,8},{3,9},{4,14},{5,15},{6,12},{7,13},{8,2},{9,3},... | collective-permute-start | bytes 24584 | tf_op jit(solution)/shard_map/ppermute | solution.py:409
  73.9 4.8 %collective-permute-start.14 = (f32[16,128]{1,0:T(8,128)}, f32[16,128]{1,0:T(8,128)S(1)}, u32[]{:S(2)}, u32[]{:S(2)}) collective-permute-start(f32[16,128]{1,0:T(8,128)} %get-tuple-element.33.refs_0_), channel_id=1, source_target_pairs={{0,2},{1,3},{2,0},{3,1},{4,6},{5,7},{6,4},{7,5},{8,10},{9,11},{10,... | collective-permute-start | bytes 24584 | tf_op jit(solution)/shard_map/ppermute | solution.py:409
  74.3 4.8 %collective-permute-start.13 = (f32[16,128]{1,0:T(8,128)}, f32[16,128]{1,0:T(8,128)S(1)}, u32[]{:S(2)}, u32[]{:S(2)}) collective-permute-start(f32[16,128]{1,0:T(8,128)} %get-tuple-element.33.refs_0_), channel_id=1, source_target_pairs={{0,24},{1,25},{2,26},{3,27},{4,28},{5,29},{6,30},{7,31},{8,16},{9,... | collective-permute-start | bytes 24584 | tf_op jit(solution)/shard_map/ppermute | solution.py:409
  76.7 3.9 %collective-permute-start.12 = (f32[16,128]{1,0:T(8,128)}, f32[16,128]{1,0:T(8,128)S(1)}, u32[]{:S(2)}, u32[]{:S(2)}) collective-permute-start(f32[16,128]{1,0:T(8,128)} %get-tuple-element.33.refs_0_), channel_id=1, source_target_pairs={{0,16},{1,17},{2,18},{3,19},{4,20},{5,21},{6,22},{7,23},{8,24},{9,... | collective-permute-start | bytes 24584 | tf_op jit(solution)/shard_map/ppermute | solution.py:409
  77.2 3.9 %collective-permute-start.11 = (f32[16,128]{1,0:T(8,128)}, f32[16,128]{1,0:T(8,128)S(1)}, u32[]{:S(2)}, u32[]{:S(2)}) collective-permute-start(f32[16,128]{1,0:T(8,128)} %get-tuple-element.33.refs_0_), channel_id=1, source_target_pairs={{0,8},{1,9},{2,10},{3,11},{4,12},{5,13},{6,14},{7,15},{8,0},{9,1},... | collective-permute-start | bytes 24584 | tf_op jit(solution)/shard_map/ppermute | solution.py:409
  85.1 6.6 %collective-permute-start.18 = (bf16[256,512]{1,0:T(8,128)(2,1)}, bf16[256,512]{1,0:T(8,128)(2,1)S(1)}, u32[]{:S(2)}, u32[]{:S(2)}) collective-permute-start(bf16[256,512]{1,0:T(8,128)(2,1)} %get-tuple-element.39), channel_id=1, source_target_pairs={{0,8},{1,9},{2,10},{3,11},{4,12},{5,13},{6,14},{7,15},{8,0},{9,1},... | collective-permute-start | bytes 786440 | tf_op jit(solution)/shard_map/ppermute | solution.py:409
  85.7 6.6 %collective-permute-start.19 = (bf16[256,512]{1,0:T(8,128)(2,1)}, bf16[256,512]{1,0:T(8,128)(2,1)S(1)}, u32[]{:S(2)}, u32[]{:S(2)}) collective-permute-start(bf16[256,512]{1,0:T(8,128)(2,1)} %get-tuple-element.41), channel_id=1, source_target_pairs={{0,16},{1,17},{2,18},{3,19},{4,20},{5,21},{6,22},{7,23},{8,24},{9,... | collective-permute-start | bytes 786440 | tf_op jit(solution)/shard_map/ppermute | solution.py:409
  94.9 5.2 %collective-permute-start.20 = (bf16[128,512]{1,0:T(8,128)(2,1)}, bf16[128,512]{1,0:T(8,128)(2,1)S(1)}, u32[]{:S(2)}, u32[]{:S(2)}) collective-permute-start(bf16[128,512]{1,0:T(8,128)(2,1)} %get-tuple-element.43), channel_id=1, source_target_pairs={{0,16},{1,17},{2,18},{3,19},{4,20},{5,21},{6,22},{7,23},{8,24},{9,... | collective-permute-start | bytes 393224 | tf_op jit(solution)/shard_map/ppermute | solution.py:409
  96.5 5.2 %collective-permute-start.21 = (bf16[128,512]{1,0:T(8,128)(2,1)}, bf16[128,512]{1,0:T(8,128)(2,1)S(1)}, u32[]{:S(2)}, u32[]{:S(2)}) collective-permute-start(bf16[128,512]{1,0:T(8,128)(2,1)} %get-tuple-element.45), channel_id=1, source_target_pairs={{0,8},{1,9},{2,10},{3,11},{4,12},{5,13},{6,14},{7,15},{8,0},{9,1},... | collective-permute-start | bytes 393224 | tf_op jit(solution)/shard_map/ppermute | solution.py:409
  104.1 7.4 %collective-permute-start.22 = (bf16[64,1024]{1,0:T(8,128)(2,1)}, bf16[64,1024]{1,0:T(8,128)(2,1)S(1)}, u32[]{:S(2)}, u32[]{:S(2)}) collective-permute-start(bf16[64,1024]{1,0:T(8,128)(2,1)} %get-tuple-element.47), channel_id=1, source_target_pairs={{0,2},{1,3},{2,0},{3,1},{4,6},{5,7},{6,4},{7,5},{8,10},{9,11},{10,... | collective-permute-start | bytes 393224 | tf_op jit(solution)/shard_map/ppermute | solution.py:409
  (21 other events, 129.1 us)

commit v5 on v4

--- a/solution.py
+++ b/solution.py
@@ -29,7 +29,9 @@
     per = LANES // ce
     low_tab = tab_ref[:, 0:LANES].astype(f32)
     top_tab = tab_ref[:, LANES:2 * LANES].astype(f32)
-    for at in range(0, words, LANES):
+    first = start // LANES * LANES
+    for tile in range(first, start + words, LANES):
+        low_word, high_word = max(tile, start), min(tile + LANES, start + words)
         for g in range(vec.shape[1] // LANES):
             parts = []
             for q in range(per):
@@ -37,15 +39,15 @@
                 if p >= length:
                     parts.append(jnp.zeros((ce, LANES), f32))
                     continue
-                idx = jnp.broadcast_to(ids_ref[p:p + 1, start + at:start + at + LANES], (8, LANES))
+                idx = jnp.broadcast_to(ids_ref[p:p + 1, tile:tile + LANES], (8, LANES))
                 low = jnp.bitwise_and(idx, LANES - 1)
                 top = idx >= LANES
                 for h in range(0, ce, 8):
                     one = jnp.take_along_axis(low_tab[h:h + 8], low, axis=1)
                     two = jnp.take_along_axis(top_tab[h:h + 8], low, axis=1)
                     parts.append(jnp.where(top, two, one))
-            block = jnp.concatenate(parts, axis=0)
-            vec[at:at + LANES, g * LANES:(g + 1) * LANES] = block.T.astype(bf16)
+            block = jnp.concatenate(parts, axis=0).T.astype(bf16)
+            vec[low_word - start:high_word - start, g * LANES:(g + 1) * LANES] = block[low_word - tile:high_word - tile]
 
 
 def conv_pool(vec, toep, acc, length, widths, filters):
@@ -310,10 +312,11 @@
 def combine_kernel(*refs, flips):
     nl = len(flips)
     lines = refs[:nl]
-    value, target, facts, a_keep, a_send, b_keep, b_send, loss = refs[nl:]
+    value, target, facts = refs[nl:nl + 3]
+    parts, loss = refs[nl + 3:nl + 7], refs[nl + 7]
     count, model = value.shape
     per = count // LANES
-    half, quarter = model // 2, count // 4
+    quarter = count // 4
 
     def line(j, i, kind):
         over, halves = flips[j]
@@ -338,21 +341,16 @@
         inside = facts[part, LANES:2 * LANES]
         q = i * LANES // quarter
         at = i * LANES - q * quarter
-        a, b = (a_keep, a_send)[q // 2], (b_keep, b_send)[q % 2]
-        a_at, b_at = (q % 2) * quarter + at, (q // 2) * quarter + at
         for n in range(model // LANES):
             cols = slice(n * LANES, (n + 1) * LANES)
             mix = weight * (value[part, cols].astype(f32) + shifts[n])
             mix = (mix - (target[part, cols].astype(f32) - inside * mus[n])).astype(bf16)
-            if n * LANES < half:
-                a[a_at:a_at + LANES, cols] = mix
-            else:
-                b[b_at:b_at + LANES, n * LANES - half:(n + 1) * LANES - half] = mix
+            parts[q][at:at + LANES, cols] = mix
 
 
 def combine(lines, flips, value, target, facts):
     rows, model = value.shape
-    side = jax.ShapeDtypeStruct((rows // 2, model // 2), bf16)
+    side = jax.ShapeDtypeStruct((rows // 4, model), bf16)
     return pl.pallas_call(
         functools.partial(combine_kernel, flips=flips),
         out_shape=[side] * 4 + [jax.ShapeDtypeStruct((1, LANES), f32)],
@@ -383,21 +381,21 @@
     )(*pairs)
 
 
-def add_across_kernel(a_keep, a_got, b_keep, b_got, first, second):
-    rows, half = first.shape[0], a_keep.shape[1]
-    for c, (keep, got) in enumerate(((a_keep, a_got), (b_keep, b_got))):
-        cols = slice(c * half, (c + 1) * half)
-        first[:, cols] = plus(keep[0:rows, :], got[0:rows, :])
-        second[:, cols] = plus(keep[rows:2 * rows, :], got[rows:2 * rows, :])
-
-
-def add_across(a_keep, a_got, b_keep, b_got):
-    rows, half = a_keep.shape
-    return pl.pallas_call(
-        add_across_kernel, out_shape=[jax.ShapeDtypeStruct((rows // 2, 2 * half), bf16)] * 2,
+def add_four_kernel(*refs):
+    parts, halves = refs[:4], refs[4:]
+    rows = halves[0].shape[0]
+    for i, out in enumerate(halves):
+        part = slice(i * rows, (i + 1) * rows)
+        out[...] = sum(ref[part, :].astype(f32) for ref in parts).astype(bf16)
+
+
+def add_four(*parts):
+    rows, model = parts[0].shape
+    return pl.pallas_call(
+        add_four_kernel, out_shape=[jax.ShapeDtypeStruct((rows // 2, model), bf16)] * 2,
         in_specs=[VM] * 4, out_specs=[VM] * 2,
-        compiler_params=params(), cost_estimate=cost(2 * rows * half, 12 * rows * half), name="add_across",
-    )(a_keep, a_got, b_keep, b_got)
+        compiler_params=params(), cost_estimate=cost(4 * rows * model, 10 * rows * model), name="add_four",
+    )(*parts)
 
 
 def per_device(char_ids, char_table, conv_weight, proj_weight, gate_weight, trans_weight, gate_bias, hidden, targets,
@@ -420,30 +418,36 @@
     for bit in rest:
         rows = jnp.concatenate([rows, swap(rows, bit)], axis=0)
         goal = jnp.concatenate([goal, swap(goal, bit)], axis=1)
+    weights = (char_table.T, conv_weight, proj_weight, gate_weight, trans_weight, gate_bias)
+    many = 4 * (mine << len(rest)) > local
+    size = local // 2 if many else local * 5 // 8 // 64 * 64
+    marks = (0, size)
+    ids = char_ids.T
+    e0 = embed(ids, length, 0, size, *weights)
+    e0, rows, goal = lax.optimization_barrier((e0, rows, goal))
     goal = goal.reshape(-1, 1)
     code = jnp.concatenate([goal // 256, goal % 256], axis=1).astype(bf16)
     rows = jnp.concatenate([rows, jnp.pad(code, ((0, 0), (0, LANES - 2)))], axis=1)
-
-    weights = (char_table.T, conv_weight, proj_weight, gate_weight, trans_weight, gate_bias)
-    size = local // 2
-    marks = (0, size)
-    ids = char_ids.T
-    e0 = embed(ids, length, 0, size, *weights)
     hid = [rows] + [swap(rows, b) for b in (bit_b, bit_a, bit_a | bit_b)]
-    e1 = embed(ids, length, size, size, *weights)
+    e1 = embed(ids, length, size, local - size, *weights)
     held, *hid = lax.optimization_barrier((e1, *hid))
     pieces = [e0, held]
     cores = [swap(e, core) for e in pieces]
     nears = [swap(e, near) for e in pieces]
-    fars = [swap(e, core) for e in nears]
+    held, nears[0] = lax.optimization_barrier((held, nears[0]))
+    far = swap(nears[0], core)
 
     me = me.astype(jnp.int32).reshape(1)
     meta = [tuple((bits, m) for m in marks) for bits in (0, core, near, core | near)]
-    late = 1 if 4 * hid[0].shape[0] <= local else len(nears)
-    one, target, stats = first_fold(
-        me, hid, pieces + cores + nears[:-late] + fars[:-late],
-        meta[0] + meta[1] + meta[2][:-late] + meta[3][:-late], local)
-    words, metas = nears[-late:] + fars[-late:], meta[2][-late:] + meta[3][-late:]
+    early = [(nears[0], meta[2][0]), (far, meta[3][0])]
+    late = []
+    if many:
+        early, late = [], early
+    words = pieces + cores + [w for w, _ in early]
+    one, target, stats = first_fold(me, hid, words, meta[0] + meta[1] + tuple(m for _, m in early), local)
+    held, stats = lax.optimization_barrier((nears[1], stats))
+    late += [(held, meta[2][1]), (swap(held, core), meta[3][1])]
+    words, metas = [w for w, _ in late], tuple(m for _, m in late)
     value, target, facts, line = last_fold(
         me, hid, words, metas, (0, core, near, core | near), local, e0, one, target, stats)
     bits = [bit_a, bit_b] + rest
@@ -451,9 +455,9 @@
     order = rest + [bit_b, bit_a]
     flips = tuple((sum(1 << (j - 1) for j, b in enumerate(order) if j and o & b), bool(o & rest[0])) for o in others)
     lines = [swap(line, o) for o in others]
-    a_keep, a_send, b_keep, b_send, loss = combine([line] + lines, ((0, False),) + flips, value, target, facts)
-    a_keep, a_send, b_keep, b_send = add_halves(a_keep, swap(a_send, bit_a), b_keep, swap(b_send, bit_b))
-    keep, send = add_across(a_keep, swap(a_send, bit_b), b_keep, swap(b_send, bit_a))
+    *parts, loss = combine([line] + lines, ((0, False),) + flips, value, target, facts)
+    far_part = swap(parts[3], bit_a | bit_b)
+    keep, send = add_four(parts[0], swap(parts[1], bit_b), swap(parts[2], bit_a), far_part)
     for bit in rest[:0:-1]:
         keep, send = add_halves(keep, swap(send, bit))
     grad = plus(keep, swap(send, rest[0]))

time: 113 us -> 111 us (0.982)
  waiting for transfers between devices: 27.5 us -> 20.3 us
  Pallas kernels: 49 us -> 55.6 us
    ppermute x23 -> x22, waiting for transfers between devices: 27.5 us -> 20.3 us  [swap(): return lax.ppermute(x, axes, [(i, i ^ bits) for i in range(devices)])]
    pallas_call x1, Pallas kernels: 9.32 us -> 14.1 us  [first_fold(): pl.pallas_call(functools.partial(first_kernel, nh=len(hid), metas=metas,...]
    pallas_call x1, Pallas kernels: 6.36 us -> 9.68 us  [last_fold(): pl.pallas_call(functools.partial(last_kernel, nh=len(hid), metas=metas, g...]
    pallas_call x2 -> x1, Pallas kernels: 3.82 us -> 1.97 us  [add_four(): pl.pallas_call(add_four_kernel, out_shape=[jax.ShapeDtypeStruct((rows //...]
    ppermute x23 -> x22, starting transfers between devices: 29.2 us -> 28.6 us  [swap(): return lax.ppermute(x, axes, [(i, i ^ bits) for i in range(devices)])]
  transfers between devices with their start and end apart: 23 -> 22, of which waited for: 10 -> 13; matrix products, arithmetic and copies ran while one was open for 1% -> 1% of each run, Pallas kernels for 31% -> 37%
where the time goes in v5:
time: 111 us
  Pallas kernels  55.6 us (50%)
  starting transfers between devices  28.6 us (26%)
  waiting for transfers between devices  20.3 us (18%)
  local copies, waits for them, and re-layouts  3.81 us (3%)
  other arithmetic  1.74 us (2%)
    ppermute x22, starting transfers between devices, swap(): return lax.ppermute(x, axes, [(i, i ^ bits) for i in range(devices)])  28.6 us
    pallas_call x2, Pallas kernels, embed(): pl.pallas_call(functools.partial(cnn_kernel, widths=widths, filters=filte...  26.5 us
    ppermute x22, waiting for transfers between devices, swap(): return lax.ppermute(x, axes, [(i, i ^ bits) for i in range(devices)])  20.3 us
    pallas_call x1, Pallas kernels, first_fold(): pl.pallas_call(functools.partial(first_kernel, nh=len(hid), metas=metas,...  14.1 us
    pallas_call x1, Pallas kernels, last_fold(): pl.pallas_call(functools.partial(last_kernel, nh=len(hid), metas=metas, g...  9.68 us
    pallas_call x1, Pallas kernels, combine(): pl.pallas_call(functools.partial(combine_kernel, flips=flips), out_shape=...  3.31 us
    unnamed x44, local copies, waits for them, and re-layouts  2.57 us
  transfers between devices with their start and end apart: 22, of which 13 were waited for; matrix products, arithmetic and copies ran while one was open for 1% of the time, Pallas kernels for 37%

profile of v5, /device:TPU:0, one launch (start us, length us, event | category | flops | bytes accessed | tf_op | source)
XLA Modules:
  0.0 110.9 jit_solution(7712175696647715610)
XLA Ops:
  0.6 4.1 %collective-permute-start.1 = (s32[1,64]{1,0:T(1,128)}, s32[1,64]{1,0:T(1,128)S(1)}, u32[]{:S(2)}, u32[]{:S(2)}) collective-permute-start(s32[1,64]{1,0:T(1,128)} %bitcast.27), channel_id=1, source_target_pairs={{0,2},{1,3},{2,0},{3,1},{4,6},{5,7},{6,4},{7,5},{8,10},{9,11},{10,... | collective-permute-start | bytes 776 | tf_op jit(solution)/shard_map/ppermute | solution.py:407
  4.8 15.4 %embed.3.refs_4_.refs_6_ = bf16[320,1024]{1,0:T(8,128)(2,1)} custom-call(s32[50,512]{1,0:T(8,128)} %bitcast.23, bf16[16,256]{1,0:T(8,128)(2,1)} %bitcast.25, bf16[112,896]{1,0:T(8,128)(2,1)} %conv_ref.3, f32[2,1024]{1,0:T(2,128)} %bias_ref.3, bf16[896,1024]{1,0:T(8,128)(2,1)} %proj_hbm.3, bf16[2,1024,1024]{2,1,0:T(8,128)(2,1)} %gate_hbm.3, ...), custom_call_target="tpu_custom_call" | custom-call | flops 10611589120 | bytes 12582912 | tf_op jit(solution)/shard_map/embed/pallas_call | solution.py:130
  20.5 1.9 %collective-permute-start.8 = (bf16[320,1024]{1,0:T(8,128)(2,1)}, bf16[320,1024]{1,0:T(8,128)(2,1)S(1)}, u32[]{:S(2)}, u32[]{:S(2)}) collective-permute-start(bf16[320,1024]{1,0:T(8,128)(2,1)} %embed.3.refs_4_.refs_6_), channel_id=1, source_target_pairs={{0,1},{1,0},{2,3},{3,2},{4,5},{5,4},{6,7},{7,6},{8,9},{9,8},{10,11... | collective-permute-start | bytes 1966088 | tf_op jit(solution)/shard_map/ppermute | solution.py:407
  22.5 2.5 %collective-permute-start.4 = (bf16[128,1152]{1,0:T(8,128)(2,1)S(1)}, bf16[128,1152]{1,0:T(8,128)(2,1)S(1)}, u32[]{:S(2)}, u32[]{:S(2)}) collective-permute-start(bf16[128,1152]{1,0:T(8,128)(2,1)S(1)} %fusion.1.refs_0_), channel_id=1, source_target_pairs={{0,24},{1,25},{2,26},{3,27},{4,28},{5,29},{6,30},{7,31},{8,16},{9,... | collective-permute-start | bytes 884744 | tf_op jit(solution)/shard_map/ppermute | solution.py:407
  26.0 11.1 %embed.2.refs_5_ = bf16[192,1024]{1,0:T(8,128)(2,1)} custom-call(s32[50,512]{1,0:T(8,128)} %bitcast.24, bf16[16,256]{1,0:T(8,128)(2,1)} %bitcast.26, bf16[112,896]{1,0:T(8,128)(2,1)} %conv_ref.3, f32[2,1024]{1,0:T(2,128)} %bias_ref.3, bf16[896,1024]{1,0:T(8,128)(2,1)} %proj_hbm.3, bf16[2,1024,1024]{2,1,0:T(8,128)(2,1)} %gate_hbm.3, ...), custom_call_target="tpu_custom_call" | custom-call | flops 6366953472 | bytes 12582912 | tf_op jit(solution)/shard_map/embed/pallas_call | solution.py:130
  39.3 1.3 %collective-permute-done.7.refs_7_ = bf16[192,1024]{1,0:T(8,128)(2,1)S(1)} collective-permute-done((bf16[192,1024]{1,0:T(8,128)(2,1)}, bf16[192,1024]{1,0:T(8,128)(2,1)S(1)}, u32[]{:S(2)}, u32[]{:S(2)}) %collective-permute-start.7) | collective-permute-done | bytes 393248 | tf_op jit(solution)/shard_map/ppermute | solution.py:407
  41.4 14.1 %first_fold.1 = (f32[512,1024]{1,0:T(8,128)}, bf16[512,1024]{1,0:T(8,128)(2,1)}, f32[512,256]{1,0:T(8,128)}) custom-call(s32[1]{0:T(128)} %bitcast.me_ref, bf16[128,1152]{1,0:T(8,128)(2,1)} %copy-done, bf16[128,1152]{1,0:T(8,128)(2,1)} %copy-done.6, bf16[128,1152]{1,0:T(8,128)(2,1)} %copy-done.5, bf16[128,1152]{1,0:T(8,128)(2,1)} %copy-done.4, ...), custom_call_target="tpu_custom_call" | custom-call | flops 5234491392 | bytes 4456448 | tf_op jit(solution)/shard_map/first_fold/pallas_call | solution.py:250
  56.0 1.3 %collective-permute-done.10.refs_5_ = bf16[192,1024]{1,0:T(8,128)(2,1)S(1)} collective-permute-done((bf16[192,1024]{1,0:T(8,128)(2,1)S(1)}, bf16[192,1024]{1,0:T(8,128)(2,1)S(1)}, u32[]{:S(2)}, u32[]{:S(2)}) %collective-permute-start.10) | collective-permute-done | bytes 393248 | tf_op jit(solution)/shard_map/ppermute | solution.py:407
  58.1 9.7 %last_fold.1 = (bf16[512,1024]{1,0:T(8,128)(2,1)}, bf16[512,1024]{1,0:T(8,128)(2,1)}, f32[512,256]{1,0:T(8,128)}, f32[16,128]{1,0:T(8,128)}) custom-call(s32[1]{0:T(128)} %bitcast.me_ref, bf16[128,1152]{1,0:T(8,128)(2,1)} %copy-done, bf16[128,1152]{1,0:T(8,128)(2,1)} %copy-done.6, bf16[128,1152]{1,0:T(8,128)(2,1)} %copy-done.5, bf16[128,1152]{1,0:T(8,128)(2,1)} %copy-done.4, ...), custom_call_target="tpu_custom_call" | custom-call | flops 1207959552 | bytes 1835008 | tf_op jit(solution)/shard_map/last_fold/pallas_call | solution.py:299
  67.8 4.5 %collective-permute-start.17 = (f32[16,128]{1,0:T(8,128)}, f32[16,128]{1,0:T(8,128)S(1)}, u32[]{:S(2)}, u32[]{:S(2)}) collective-permute-start(f32[16,128]{1,0:T(8,128)} %get-tuple-element.41.refs_0_), channel_id=1, source_target_pairs={{0,26},{1,27},{2,24},{3,25},{4,30},{5,31},{6,28},{7,29},{8,18},{9,... | collective-permute-start | bytes 24584 | tf_op jit(solution)/shard_map/ppermute | solution.py:407
  72.6 2.5 %collective-permute-start.15 = (f32[16,128]{1,0:T(8,128)}, f32[16,128]{1,0:T(8,128)S(1)}, u32[]{:S(2)}, u32[]{:S(2)}) collective-permute-start(f32[16,128]{1,0:T(8,128)} %get-tuple-element.41.refs_0_), channel_id=1, source_target_pairs={{0,10},{1,11},{2,8},{3,9},{4,14},{5,15},{6,12},{7,13},{8,2},{9,3},... | collective-permute-start | bytes 24584 | tf_op jit(solution)/shard_map/ppermute | solution.py:407
  75.5 2.5 %collective-permute-start.13 = (f32[16,128]{1,0:T(8,128)}, f32[16,128]{1,0:T(8,128)S(1)}, u32[]{:S(2)}, u32[]{:S(2)}) collective-permute-start(f32[16,128]{1,0:T(8,128)} %get-tuple-element.41.refs_0_), channel_id=1, source_target_pairs={{0,24},{1,25},{2,26},{3,27},{4,28},{5,29},{6,30},{7,31},{8,16},{9,... | collective-permute-start | bytes 24584 | tf_op jit(solution)/shard_map/ppermute | solution.py:407
  80.2 1.6 %collective-permute-done.12.refs_2_ = f32[16,128]{1,0:T(8,128)S(1)} collective-permute-done((f32[16,128]{1,0:T(8,128)}, f32[16,128]{1,0:T(8,128)S(1)}, u32[]{:S(2)}, u32[]{:S(2)}) %collective-permute-start.12) | collective-permute-done | bytes 8224 | tf_op jit(solution)/shard_map/ppermute | solution.py:407
  82.9 3.3 %combine.1 = (bf16[128,1024]{1,0:T(8,128)(2,1)}, bf16[128,1024]{1,0:T(8,128)(2,1)}, bf16[128,1024]{1,0:T(8,128)(2,1)}, bf16[128,1024]{1,0:T(8,128)(2,1)}, f32[1,128]{1,0:T(1,128)}) custom-call(f32[16,128]{1,0:T(8,128)} %get-tuple-element.41.refs_0_, f32[16,128]{1,0:T(8,128)} %copy-done.17, f32[16,128]{1,0:T(8,128)} %copy-done.16, f32[16,128]{1,0:T(8,128)} %copy-done.15, ...), custom_call_target="tpu_custom_call" | custom-call | flops 4194304 | bytes 4194304 | tf_op jit(solution)/shard_map/combine/pallas_call | solution.py:354
  86.2 1.5 %collective-permute-start.18 = (bf16[128,1024]{1,0:T(8,128)(2,1)}, bf16[128,1024]{1,0:T(8,128)(2,1)S(1)}, u32[]{:S(2)}, u32[]{:S(2)}) collective-permute-start(bf16[128,1024]{1,0:T(8,128)(2,1)} %get-tuple-element.47), channel_id=1, source_target_pairs={{0,16},{1,17},{2,18},{3,19},{4,20},{5,21},{6,22},{7,23},{8,24},{9,... | collective-permute-start | bytes 786440 | tf_op jit(solution)/shard_map/ppermute | solution.py:407
  88.3 1.4 %collective-permute-start.20 = (bf16[128,1024]{1,0:T(8,128)(2,1)}, bf16[128,1024]{1,0:T(8,128)(2,1)S(1)}, u32[]{:S(2)}, u32[]{:S(2)}) collective-permute-start(bf16[128,1024]{1,0:T(8,128)(2,1)} %get-tuple-element.49), channel_id=1, source_target_pairs={{0,24},{1,25},{2,26},{3,27},{4,28},{5,29},{6,30},{7,31},{8,16},{9,... | collective-permute-start | bytes 786440 | tf_op jit(solution)/shard_map/ppermute | solution.py:407
  89.7 5.7 %collective-permute-done.18.refs_1_ = bf16[128,1024]{1,0:T(8,128)(2,1)S(1)} collective-permute-done((bf16[128,1024]{1,0:T(8,128)(2,1)}, bf16[128,1024]{1,0:T(8,128)(2,1)S(1)}, u32[]{:S(2)}, u32[]{:S(2)}) %collective-permute-start.18) | collective-permute-done | bytes 262176 | tf_op jit(solution)/shard_map/ppermute | solution.py:407
  95.4 1.1 collective-permute-done.19.refs_2_
  96.5 2.8 %collective-permute-done.20.refs_3_ = bf16[128,1024]{1,0:T(8,128)(2,1)S(1)} collective-permute-done((bf16[128,1024]{1,0:T(8,128)(2,1)}, bf16[128,1024]{1,0:T(8,128)(2,1)S(1)}, u32[]{:S(2)}, u32[]{:S(2)}) %collective-permute-start.20) | collective-permute-done | bytes 262176 | tf_op jit(solution)/shard_map/ppermute | solution.py:407
  100.0 2.0 %add_four.1 = (bf16[64,1024]{1,0:T(8,128)(2,1)}, bf16[64,1024]{1,0:T(8,128)(2,1)}) custom-call(bf16[128,1024]{1,0:T(8,128)(2,1)} %get-tuple-element.46.refs_0_, bf16[128,1024]{1,0:T(8,128)(2,1)} %copy-done.7, bf16[128,1024]{1,0:T(8,128)(2,1)} %copy-done.8, bf16[128,1024]{1,0:T(8,128)(2,1)} %copy-done.9), custom_call_target="tpu_custom_call" | custom-call | flops 524288 | bytes 1310720 | tf_op jit(solution)/shard_map/add_four/pallas_call | solution.py:394
  102.0 2.6 %collective-permute-start.21 = (bf16[64,1024]{1,0:T(8,128)(2,1)}, bf16[64,1024]{1,0:T(8,128)(2,1)S(1)}, u32[]{:S(2)}, u32[]{:S(2)}) collective-permute-start(bf16[64,1024]{1,0:T(8,128)(2,1)} %get-tuple-element.51), channel_id=1, source_target_pairs={{0,2},{1,3},{2,0},{3,1},{4,6},{5,7},{6,4},{7,5},{8,10},{9,11},{10,... | collective-permute-start | bytes 393224 | tf_op jit(solution)/shard_map/ppermute | solution.py:407
  104.5 1.1 slice_bitcast_fusion
  105.6 3.7 %collective-permute-done.21 = bf16[64,1024]{1,0:T(8,128)(2,1)S(1)} collective-permute-done((bf16[64,1024]{1,0:T(8,128)(2,1)}, bf16[64,1024]{1,0:T(8,128)(2,1)S(1)}, u32[]{:S(2)}, u32[]{:S(2)}) %collective-permute-start.21) | collective-permute-done | bytes 131104 | tf_op jit(solution)/shard_map/ppermute | solution.py:407
  109.3 1.6 %add_convert_fusion = bf16[64,1024]{1,0:T(8,128)(2,1)} fusion(bf16[64,1024]{1,0:T(8,128)(2,1)S(1)} %collective-permute-done.21, bf16[64,1024]{1,0:T(8,128)(2,1)} %get-tuple-element.50), kind=kLoop, calls=%fused_computation.4 | loop fusion | flops 262144 | bytes 393216 | tf_op jit(solution)/shard_map/convert_element_type | solution.py:363
  (78 shorter events, 10.8 us)
Async XLA Ops:
  0.6 19.6 %collective-permute-start.1 = (s32[1,64]{1,0:T(1,128)}, s32[1,64]{1,0:T(1,128)S(1)}, u32[]{:S(2)}, u32[]{:S(2)}) collective-permute-start(s32[1,64]{1,0:T(1,128)} %bitcast.27), channel_id=1, source_target_pairs={{0,2},{1,3},{2,0},{3,1},{4,6},{5,7},{6,4},{7,5},{8,10},{9,11},{10,... | collective-permute-start | bytes 776 | tf_op jit(solution)/shard_map/ppermute | solution.py:407
  4.7 15.6 %collective-permute-start = (bf16[64,1024]{1,0:T(8,128)(2,1)}, bf16[64,1024]{1,0:T(8,128)(2,1)S(1)}, u32[]{:S(2)}, u32[]{:S(2)}) collective-permute-start(bf16[64,1024]{1,0:T(8,128)(2,1)} %param.16), channel_id=1, source_target_pairs={{0,2},{1,3},{2,0},{3,1},{4,6},{5,7},{6,4},{7,5},{8,10},{9,11},{10,... | collective-permute-start | bytes 393224 | tf_op jit(solution)/shard_map/ppermute | solution.py:407
  4.8 15.4 %copy-start.21 = (s32[64]{0:T(128)S(1)}, s32[64]{0:T(128)}, u32[]{:S(2)}) copy-start(s32[64]{0:T(128)} %param.17) | copy-start | bytes 772
  4.8 15.5 %copy-start.10 = (bf16[64,1024]{1,0:T(8,128)(2,1)S(1)}, bf16[64,1024]{1,0:T(8,128)(2,1)}, u32[]{:S(2)}) copy-start(bf16[64,1024]{1,0:T(8,128)(2,1)} %param.16) | copy-start | bytes 393220
  20.5 17.3 %collective-permute-start.8 = (bf16[320,1024]{1,0:T(8,128)(2,1)}, bf16[320,1024]{1,0:T(8,128)(2,1)S(1)}, u32[]{:S(2)}, u32[]{:S(2)}) collective-permute-start(bf16[320,1024]{1,0:T(8,128)(2,1)} %embed.3.refs_4_.refs_6_), channel_id=1, source_target_pairs={{0,1},{1,0},{2,3},{3,2},{4,5},{5,4},{6,7},{7,6},{8,9},{9,8},{10,11... | collective-permute-start | bytes 1966088 | tf_op jit(solution)/shard_map/ppermute | solution.py:407
  22.5 14.8 %collective-permute-start.4 = (bf16[128,1152]{1,0:T(8,128)(2,1)S(1)}, bf16[128,1152]{1,0:T(8,128)(2,1)S(1)}, u32[]{:S(2)}, u32[]{:S(2)}) collective-permute-start(bf16[128,1152]{1,0:T(8,128)(2,1)S(1)} %fusion.1.refs_0_), channel_id=1, source_target_pairs={{0,24},{1,25},{2,26},{3,27},{4,28},{5,29},{6,30},{7,31},{8,16},{9,... | collective-permute-start | bytes 884744 | tf_op jit(solution)/shard_map/ppermute | solution.py:407
  25.0 12.8 %collective-permute-start.3 = (bf16[128,1152]{1,0:T(8,128)(2,1)S(1)}, bf16[128,1152]{1,0:T(8,128)(2,1)S(1)}, u32[]{:S(2)}, u32[]{:S(2)}) collective-permute-start(bf16[128,1152]{1,0:T(8,128)(2,1)S(1)} %fusion.1.refs_0_), channel_id=1, source_target_pairs={{0,8},{1,9},{2,10},{3,11},{4,12},{5,13},{6,14},{7,15},{8,0},{9,1},... | collective-permute-start | bytes 884744 | tf_op jit(solution)/shard_map/ppermute | solution.py:407
  25.5 12.3 %collective-permute-start.2 = (bf16[128,1152]{1,0:T(8,128)(2,1)S(1)}, bf16[128,1152]{1,0:T(8,128)(2,1)S(1)}, u32[]{:S(2)}, u32[]{:S(2)}) collective-permute-start(bf16[128,1152]{1,0:T(8,128)(2,1)S(1)} %fusion.1.refs_0_), channel_id=1, source_target_pairs={{0,16},{1,17},{2,18},{3,19},{4,20},{5,21},{6,22},{7,23},{8,24},{9,... | collective-permute-start | bytes 884744 | tf_op jit(solution)/shard_map/ppermute | solution.py:407
  37.2 2.2 %collective-permute-start.6 = (bf16[320,1024]{1,0:T(8,128)(2,1)S(1)}, bf16[320,1024]{1,0:T(8,128)(2,1)S(1)}, u32[]{:S(2)}, u32[]{:S(2)}) collective-permute-start(bf16[320,1024]{1,0:T(8,128)(2,1)S(1)} %copy-done.1), channel_id=1, source_target_pairs={{0,4},{1,5},{2,6},{3,7},{4,0},{5,1},{6,2},{7,3},{8,12},{9,13},{10,... | collective-permute-start | bytes 1966088 | tf_op jit(solution)/shard_map/ppermute | solution.py:407
  37.8 3.2 %collective-permute-start.9 = (bf16[320,1024]{1,0:T(8,128)(2,1)S(1)}, bf16[320,1024]{1,0:T(8,128)(2,1)}, u32[]{:S(2)}, u32[]{:S(2)}) collective-permute-start(bf16[320,1024]{1,0:T(8,128)(2,1)S(1)} %collective-permute-done.8.refs_8_), channel_id=1, source_target_pairs={{0,4},{1,5},{2,6},{3,7},{4,0},{5,1},{6,2},{7,3},{8,12},{9,13},{10,... | collective-permute-start | bytes 1966088 | tf_op jit(solution)/shard_map/ppermute | solution.py:407
  37.9 2.8 %collective-permute-start.7 = (bf16[192,1024]{1,0:T(8,128)(2,1)}, bf16[192,1024]{1,0:T(8,128)(2,1)S(1)}, u32[]{:S(2)}, u32[]{:S(2)}) collective-permute-start(bf16[192,1024]{1,0:T(8,128)(2,1)} %embed.2.refs_5_), channel_id=1, source_target_pairs={{0,4},{1,5},{2,6},{3,7},{4,0},{5,1},{6,2},{7,3},{8,12},{9,13},{10,... | collective-permute-start | bytes 1179656 | tf_op jit(solution)/shard_map/ppermute | solution.py:407
  38.4 17.1 %collective-permute-start.5 = (bf16[192,1024]{1,0:T(8,128)(2,1)}, bf16[192,1024]{1,0:T(8,128)(2,1)S(1)}, u32[]{:S(2)}, u32[]{:S(2)}) collective-permute-start(bf16[192,1024]{1,0:T(8,128)(2,1)} %embed.2.refs_5_), channel_id=1, source_target_pairs={{0,1},{1,0},{2,3},{3,2},{4,5},{5,4},{6,7},{7,6},{8,9},{9,8},{10,11... | collective-permute-start | bytes 1179656 | tf_op jit(solution)/shard_map/ppermute | solution.py:407
  55.5 1.8 %collective-permute-start.10 = (bf16[192,1024]{1,0:T(8,128)(2,1)S(1)}, bf16[192,1024]{1,0:T(8,128)(2,1)S(1)}, u32[]{:S(2)}, u32[]{:S(2)}) collective-permute-start(bf16[192,1024]{1,0:T(8,128)(2,1)S(1)} %collective-permute-done.5.refs_4_), channel_id=1, source_target_pairs={{0,4},{1,5},{2,6},{3,7},{4,0},{5,1},{6,2},{7,3},{8,12},{9,13},{10,... | collective-permute-start | bytes 1179656 | tf_op jit(solution)/shard_map/ppermute | solution.py:407
  67.8 10.1 %collective-permute-start.17 = (f32[16,128]{1,0:T(8,128)}, f32[16,128]{1,0:T(8,128)S(1)}, u32[]{:S(2)}, u32[]{:S(2)}) collective-permute-start(f32[16,128]{1,0:T(8,128)} %get-tuple-element.41.refs_0_), channel_id=1, source_target_pairs={{0,26},{1,27},{2,24},{3,25},{4,30},{5,31},{6,28},{7,29},{8,18},{9,... | collective-permute-start | bytes 24584 | tf_op jit(solution)/shard_map/ppermute | solution.py:407
  72.3 6.1 %collective-permute-start.16 = (f32[16,128]{1,0:T(8,128)}, f32[16,128]{1,0:T(8,128)S(1)}, u32[]{:S(2)}, u32[]{:S(2)}) collective-permute-start(f32[16,128]{1,0:T(8,128)} %get-tuple-element.41.refs_0_), channel_id=1, source_target_pairs={{0,18},{1,19},{2,16},{3,17},{4,22},{5,23},{6,20},{7,21},{8,26},{9,... | collective-permute-start | bytes 24584 | tf_op jit(solution)/shard_map/ppermute | solution.py:407
  72.6 6.4 %collective-permute-start.15 = (f32[16,128]{1,0:T(8,128)}, f32[16,128]{1,0:T(8,128)S(1)}, u32[]{:S(2)}, u32[]{:S(2)}) collective-permute-start(f32[16,128]{1,0:T(8,128)} %get-tuple-element.41.refs_0_), channel_id=1, source_target_pairs={{0,10},{1,11},{2,8},{3,9},{4,14},{5,15},{6,12},{7,13},{8,2},{9,3},... | collective-permute-start | bytes 24584 | tf_op jit(solution)/shard_map/ppermute | solution.py:407
  75.1 4.8 %collective-permute-start.14 = (f32[16,128]{1,0:T(8,128)}, f32[16,128]{1,0:T(8,128)S(1)}, u32[]{:S(2)}, u32[]{:S(2)}) collective-permute-start(f32[16,128]{1,0:T(8,128)} %get-tuple-element.41.refs_0_), channel_id=1, source_target_pairs={{0,2},{1,3},{2,0},{3,1},{4,6},{5,7},{6,4},{7,5},{8,10},{9,11},{10,... | collective-permute-start | bytes 24584 | tf_op jit(solution)/shard_map/ppermute | solution.py:407
  75.5 4.8 %collective-permute-start.13 = (f32[16,128]{1,0:T(8,128)}, f32[16,128]{1,0:T(8,128)S(1)}, u32[]{:S(2)}, u32[]{:S(2)}) collective-permute-start(f32[16,128]{1,0:T(8,128)} %get-tuple-element.41.refs_0_), channel_id=1, source_target_pairs={{0,24},{1,25},{2,26},{3,27},{4,28},{5,29},{6,30},{7,31},{8,16},{9,... | collective-permute-start | bytes 24584 | tf_op jit(solution)/shard_map/ppermute | solution.py:407
  77.9 3.9 %collective-permute-start.12 = (f32[16,128]{1,0:T(8,128)}, f32[16,128]{1,0:T(8,128)S(1)}, u32[]{:S(2)}, u32[]{:S(2)}) collective-permute-start(f32[16,128]{1,0:T(8,128)} %get-tuple-element.41.refs_0_), channel_id=1, source_target_pairs={{0,16},{1,17},{2,18},{3,19},{4,20},{5,21},{6,22},{7,23},{8,24},{9,... | collective-permute-start | bytes 24584 | tf_op jit(solution)/shard_map/ppermute | solution.py:407
  78.4 3.9 %collective-permute-start.11 = (f32[16,128]{1,0:T(8,128)}, f32[16,128]{1,0:T(8,128)S(1)}, u32[]{:S(2)}, u32[]{:S(2)}) collective-permute-start(f32[16,128]{1,0:T(8,128)} %get-tuple-element.41.refs_0_), channel_id=1, source_target_pairs={{0,8},{1,9},{2,10},{3,11},{4,12},{5,13},{6,14},{7,15},{8,0},{9,1},... | collective-permute-start | bytes 24584 | tf_op jit(solution)/shard_map/ppermute | solution.py:407
  86.2 9.2 %collective-permute-start.18 = (bf16[128,1024]{1,0:T(8,128)(2,1)}, bf16[128,1024]{1,0:T(8,128)(2,1)S(1)}, u32[]{:S(2)}, u32[]{:S(2)}) collective-permute-start(bf16[128,1024]{1,0:T(8,128)(2,1)} %get-tuple-element.47), channel_id=1, source_target_pairs={{0,16},{1,17},{2,18},{3,19},{4,20},{5,21},{6,22},{7,23},{8,24},{9,... | collective-permute-start | bytes 786440 | tf_op jit(solution)/shard_map/ppermute | solution.py:407
  87.7 8.8 %collective-permute-start.19 = (bf16[128,1024]{1,0:T(8,128)(2,1)}, bf16[128,1024]{1,0:T(8,128)(2,1)S(1)}, u32[]{:S(2)}, u32[]{:S(2)}) collective-permute-start(bf16[128,1024]{1,0:T(8,128)(2,1)} %get-tuple-element.48), channel_id=1, source_target_pairs={{0,8},{1,9},{2,10},{3,11},{4,12},{5,13},{6,14},{7,15},{8,0},{9,1},... | collective-permute-start | bytes 786440 | tf_op jit(solution)/shard_map/ppermute | solution.py:407
  88.3 11.0 %collective-permute-start.20 = (bf16[128,1024]{1,0:T(8,128)(2,1)}, bf16[128,1024]{1,0:T(8,128)(2,1)S(1)}, u32[]{:S(2)}, u32[]{:S(2)}) collective-permute-start(bf16[128,1024]{1,0:T(8,128)(2,1)} %get-tuple-element.49), channel_id=1, source_target_pairs={{0,24},{1,25},{2,26},{3,27},{4,28},{5,29},{6,30},{7,31},{8,16},{9,... | collective-permute-start | bytes 786440 | tf_op jit(solution)/shard_map/ppermute | solution.py:407
  102.0 7.3 %collective-permute-start.21 = (bf16[64,1024]{1,0:T(8,128)(2,1)}, bf16[64,1024]{1,0:T(8,128)(2,1)S(1)}, u32[]{:S(2)}, u32[]{:S(2)}) collective-permute-start(bf16[64,1024]{1,0:T(8,128)(2,1)} %get-tuple-element.51), channel_id=1, source_target_pairs={{0,2},{1,3},{2,0},{3,1},{4,6},{5,7},{6,4},{7,5},{8,10},{9,11},{10,... | collective-permute-start | bytes 393224 | tf_op jit(solution)/shard_map/ppermute | solution.py:407
  (20 other events, 72.3 us)

commit v6 on v5

--- a/solution.py
+++ b/solution.py
@@ -177,14 +177,18 @@
     return jnp.where(apart == bits, place - start, -1)
 
 
-def scores_of(rows, words, score, prob):
-    at, top = 0, None
-    for ref in words:
+def scores_of(rows, words, metas, apart, place, score, prob, hot):
+    at, top, aim = 0, None, None
+    for ref, meta in zip(words, metas):
         n = ref.shape[0]
         piece = lax.dot_general(rows[...], ref[...], (((1,), (1,)), ((), ())), preferred_element_type=f32)
         score[:, at:at + n] = piece
+        hit = lax.broadcasted_iota(jnp.int32, piece.shape, 1) == spots(apart, place, meta)
+        hot[:, at:at + n] = jnp.where(hit, 1.0, 0.0).astype(bf16)
+        part = jnp.sum(jnp.where(hit, piece, 0.0), axis=1, keepdims=True)
         best = jnp.max(piece, axis=1, keepdims=True)
         top = best if top is None else jnp.maximum(top, best)
+        aim = part if aim is None else aim + part
         at += n
     at, total = 0, None
     for ref in words:
@@ -194,16 +198,7 @@
         part = jnp.sum(w.astype(f32), axis=1, keepdims=True)
         total = part if total is None else total + part
         at += n
-    return top, total
-
-
-def hot_words(words, metas, apart, place, hot):
-    at = 0
-    for ref, meta in zip(words, metas):
-        n = ref.shape[0]
-        lane = lax.broadcasted_iota(jnp.int32, (hot.shape[0], n), 1)
-        hot[:, at:at + n] = jnp.where(lane == spots(apart, place, meta), 1.0, 0.0).astype(bf16)
-        at += n
+    return top, total, aim
 
 
 def product(left, words, n, size):
@@ -227,10 +222,9 @@
     hid, words = refs[:nh], refs[nh:nh + len(metas)]
     out, target, stats, rows, score, prob, hot = refs[nh + len(metas):]
     load_rows(hid, rows)
-    top, total = scores_of(rows, words, score, prob)
-    stats[:, 0:LANES] = jnp.broadcast_to(top, (top.shape[0], LANES))
-    stats[:, LANES:2 * LANES] = jnp.broadcast_to(total, (top.shape[0], LANES))
-    hot_words(words, metas, *aims(me_ref, hid, local), hot)
+    each = scores_of(rows, words, metas, *aims(me_ref, hid, local), score, prob, hot)
+    for i, column in enumerate(each):
+        stats[:, i * LANES:(i + 1) * LANES] = jnp.broadcast_to(column, (column.shape[0], LANES))
     for n in range(0, out.shape[1], 256):
         out[:, n:n + 256] = product(prob, words, n, 256)
         target[:, n:n + 256] = product(hot, words, n, 256).astype(bf16)
@@ -250,7 +244,7 @@
     return pl.pallas_call(
         functools.partial(first_kernel, nh=len(hid), metas=metas, local=local),
         out_shape=[jax.ShapeDtypeStruct((rows, model), f32), jax.ShapeDtypeStruct((rows, model), bf16),
-                   jax.ShapeDtypeStruct((rows, 2 * LANES), f32)],
+                   jax.ShapeDtypeStruct((rows, 3 * LANES), f32)],
         in_specs=[SM] + [VM] * (len(hid) + len(words)), out_specs=[VM] * 3,
         scratch_shapes=[pltpu.VMEM((rows, model), bf16), pltpu.VMEM((rows, count), f32),
                         pltpu.VMEM((rows, count), bf16), pltpu.VMEM((rows, count), bf16)],
@@ -261,60 +255,47 @@
 
 def last_kernel(me_ref, *refs, nh, metas, group, local):
     hid, words = refs[:nh], refs[nh:nh + len(metas)]
-    own, one, before, stats, value, target, facts, lines, rows, score, prob, hot = refs[nh + len(metas):]
+    own, stats, prob, hot, facts, lines, rows, score = refs[nh + len(metas):]
     load_rows(hid, rows)
-    count, model = one.shape
+    count, model = rows.shape
     apart, place = aims(me_ref, hid, local)
-    top2, total2 = scores_of(rows, words, score, prob)
-    hot_words(words, metas, apart, place, hot)
-    top1, total1 = stats[:, 0:1], stats[:, LANES:LANES + 1]
+    top2, total2, aim2 = scores_of(rows, words, metas, apart, place, score, prob, hot)
+    top1, total1, aim1 = (stats[:, i * LANES:i * LANES + 1] for i in range(3))
     top = jnp.maximum(top1, top2)
-    s1, s2 = jnp.exp(top1 - top), jnp.exp(top2 - top)
-    total = s1 * total1 + s2 * total2
-    s1, s2 = s1 / total, s2 / total
-    whole = top + jnp.log(total)
-    centre = jnp.sum(own[0:LANES, :].astype(f32), axis=0, keepdims=True) * (1.0 / LANES)
-    aim = None
-    for n in range(0, model, 256):
-        cols = slice(n, n + 256)
-        mix = s1 * one[:, cols] + s2 * product(prob, words, n, 256)
-        value[:, cols] = (mix - centre[:, cols]).astype(bf16)
-        goal = product(hot, words, n, 256) + before[:, cols].astype(f32)
-        target[:, cols] = goal.astype(bf16)
-        part = jnp.sum(goal * rows[:, cols].astype(f32), axis=1, keepdims=True)
-        aim = part if aim is None else aim + part
+    total = jnp.exp(top1 - top) * total1 + jnp.exp(top2 - top) * total2
     inside = sum(jnp.where(apart == bits, 1.0, 0.0) for bits in group)
-    facts[:, 0:LANES] = jnp.broadcast_to(whole, (count, LANES))
+    facts[:, 0:LANES] = jnp.broadcast_to(top2, (count, LANES))
     facts[:, LANES:2 * LANES] = jnp.broadcast_to(inside, (count, LANES))
     per = count // LANES
-    to_lines(whole, lines, 0)
-    to_lines(aim, lines, per)
+    to_lines(top + jnp.log(total), lines, 0)
+    to_lines(aim1 + aim2, lines, per)
+    centre = jnp.sum(own[0:LANES, :].astype(f32), axis=0, keepdims=True) * (1.0 / LANES)
     for n in range(model // LANES):
         lines[2 * per + n:2 * per + n + 1, :] = centre[:, n * LANES:(n + 1) * LANES]
 
 
-def last_fold(me, hid, words, metas, group, local, own, one, before, stats):
-    rows, model = one.shape
+def last_scores(me, hid, words, metas, group, local, own, stats):
+    model = own.shape[1]
+    rows = stats.shape[0]
     count = sum(w.shape[0] for w in words)
     return pl.pallas_call(
         functools.partial(last_kernel, nh=len(hid), metas=metas, group=group, local=local),
-        out_shape=[jax.ShapeDtypeStruct((rows, model), bf16)] * 2 + [
+        out_shape=[jax.ShapeDtypeStruct((rows, count), bf16)] * 2 + [
             jax.ShapeDtypeStruct((rows, 2 * LANES), f32),
             jax.ShapeDtypeStruct((2 * rows // LANES + model // LANES, LANES), f32)],
-        in_specs=[SM] + [VM] * (len(hid) + len(words) + 4), out_specs=[VM] * 4,
-        scratch_shapes=[pltpu.VMEM((rows, model), bf16), pltpu.VMEM((rows, count), f32),
-                        pltpu.VMEM((rows, count), bf16), pltpu.VMEM((rows, count), bf16)],
-        compiler_params=params(), cost_estimate=cost(6 * rows * count * model, 2 * (rows + count) * model),
-        name="last_fold",
-    )(me, *hid, *words, own, one, before, stats)
-
-
-def combine_kernel(*refs, flips):
+        in_specs=[SM] + [VM] * (len(hid) + len(words) + 2), out_specs=[VM] * 4,
+        scratch_shapes=[pltpu.VMEM((rows, model), bf16), pltpu.VMEM((rows, count), f32)],
+        compiler_params=params(), cost_estimate=cost(2 * rows * count * model, 2 * (rows + count) * model),
+        name="last_scores",
+    )(me, *hid, *words, own, stats)
+
+
+def close_kernel(*refs, flips, nw):
     nl = len(flips)
-    lines = refs[:nl]
-    value, target, facts = refs[nl:nl + 3]
-    parts, loss = refs[nl + 3:nl + 7], refs[nl + 7]
-    count, model = value.shape
+    lines, words = refs[:nl], refs[nl:nl + nw]
+    prob, hot, one, before, stats, facts = refs[nl + nw:nl + nw + 6]
+    parts, loss = refs[nl + nw + 6:nl + nw + 10], refs[nl + nw + 10]
+    count, model = one.shape
     per = count // LANES
     quarter = count // 4
 
@@ -323,40 +304,39 @@
         v = lines[j][kind * per + (i ^ over):kind * per + (i ^ over) + 1, :]
         return pltpu.roll(v, LANES // 2, axis=1) if halves else v
 
-    mus, shifts = [], []
-    for n in range(model // LANES):
-        row = slice(2 * per + n, 2 * per + n + 1)
-        mu = sum(ref[row, :] for ref in lines) * (1.0 / nl)
-        mus.append(jnp.broadcast_to(mu, (LANES, LANES)))
-        shifts.append(jnp.broadcast_to(lines[0][row, :] - mu, (LANES, LANES)))
+    scales = []
     for i in range(per):
         each = [line(j, i, 0) for j in range(nl)]
         top = functools.reduce(jnp.maximum, each)
         whole = top + jnp.log(sum(jnp.exp(v - top) for v in each))
         if i == 0:
             loss[...] = whole - sum(line(j, i, 1) for j in range(nl))
+        weight = jnp.broadcast_to(jnp.exp(each[0] - whole), (LANES, LANES)).T
         whole = jnp.broadcast_to(whole, (LANES, LANES)).T
         part = slice(i * LANES, (i + 1) * LANES)
-        weight = jnp.exp(facts[part, 0:LANES] - whole)
-        inside = facts[part, LANES:2 * LANES]
-        q = i * LANES // quarter
-        at = i * LANES - q * quarter
-        for n in range(model // LANES):
-            cols = slice(n * LANES, (n + 1) * LANES)
-            mix = weight * (value[part, cols].astype(f32) + shifts[n])
-            mix = (mix - (target[part, cols].astype(f32) - inside * mus[n])).astype(bf16)
-            parts[q][at:at + LANES, cols] = mix
-
-
-def combine(lines, flips, value, target, facts):
-    rows, model = value.shape
+        scales.append((jnp.exp(stats[part, 0:LANES] - whole)[:, 0:1], jnp.exp(facts[part, 0:LANES] - whole)[:, 0:1],
+                       (facts[part, LANES:2 * LANES] - weight)[:, 0:1]))
+    c1, c2, c3 = (jnp.concatenate(c, axis=0) for c in zip(*scales))
+    for n in range(0, model, 256):
+        cols = slice(n, n + 256)
+        mu = jnp.concatenate([
+            sum(ref[2 * per + m // LANES:2 * per + m // LANES + 1, :] for ref in lines) * (1.0 / nl)
+            for m in range(n, n + 256, LANES)], axis=1)
+        goal = product(hot, words, n, 256) + before[:, cols].astype(f32)
+        mix = (c1 * one[:, cols] + c2 * product(prob, words, n, 256) + (c3 * mu - goal)).astype(bf16)
+        for q in range(4):
+            parts[q][:, cols] = mix[q * quarter:(q + 1) * quarter]
+
+
+def close(lines, flips, words, prob, hot, one, before, stats, facts):
+    rows, model = one.shape
     side = jax.ShapeDtypeStruct((rows // 4, model), bf16)
     return pl.pallas_call(
-        functools.partial(combine_kernel, flips=flips),
+        functools.partial(close_kernel, flips=flips, nw=len(words)),
         out_shape=[side] * 4 + [jax.ShapeDtypeStruct((1, LANES), f32)],
-        in_specs=[VM] * (len(lines) + 3), out_specs=[VM] * 5,
-        compiler_params=params(), cost_estimate=cost(8 * rows * model, 8 * rows * model), name="combine",
-    )(*lines, value, target, facts)
+        in_specs=[VM] * (len(lines) + len(words) + 6), out_specs=[VM] * 5, compiler_params=params(),
+        cost_estimate=cost(4 * rows * prob.shape[1] * model, 8 * rows * model), name="close",
+    )(*lines, *words, prob, hot, one, before, stats, facts)
 
 
 def plus(a, b):
@@ -420,7 +400,7 @@
         goal = jnp.concatenate([goal, swap(goal, bit)], axis=1)
     weights = (char_table.T, conv_weight, proj_weight, gate_weight, trans_weight, gate_bias)
     many = 4 * (mine << len(rest)) > local
-    size = local // 2 if many else local * 5 // 8 // 64 * 64
+    size = local // 2
     marks = (0, size)
     ids = char_ids.T
     e0 = embed(ids, length, 0, size, *weights)
@@ -448,14 +428,14 @@
     held, stats = lax.optimization_barrier((nears[1], stats))
     late += [(held, meta[2][1]), (swap(held, core), meta[3][1])]
     words, metas = [w for w, _ in late], tuple(m for _, m in late)
-    value, target, facts, line = last_fold(
-        me, hid, words, metas, (0, core, near, core | near), local, e0, one, target, stats)
+    prob, hot, facts, line = last_scores(
+        me, hid, words, metas, (0, core, near, core | near), local, e0, stats)
     bits = [bit_a, bit_b] + rest
     others = [sum(b for j, b in enumerate(bits) if k >> j & 1) for k in range(1, 1 << len(bits))]
     order = rest + [bit_b, bit_a]
     flips = tuple((sum(1 << (j - 1) for j, b in enumerate(order) if j and o & b), bool(o & rest[0])) for o in others)
     lines = [swap(line, o) for o in others]
-    *parts, loss = combine([line] + lines, ((0, False),) + flips, value, target, facts)
+    *parts, loss = close([line] + lines, ((0, False),) + flips, words, prob, hot, one, target, stats, facts)
     far_part = swap(parts[3], bit_a | bit_b)
     keep, send = add_four(parts[0], swap(parts[1], bit_b), swap(parts[2], bit_a), far_part)
     for bit in rest[:0:-1]:

time: 111 us -> 107 us (0.964)
  Pallas kernels: 55.6 us -> 47.4 us
  waiting for transfers between devices: 20.3 us -> 27.8 us
  starting transfers between devices: 28.6 us -> 25.4 us
    ppermute x22, waiting for transfers between devices: 20.3 us -> 27.8 us  [swap(): return lax.ppermute(x, axes, [(i, i ^ bits) for i in range(devices)])]
    pallas_call x1, Pallas kernels: 14.1 us -> 9.6 us  [first_fold(): pl.pallas_call(functools.partial(first_kernel, nh=len(hid), metas=metas,...]
    ppermute x22, starting transfers between devices: 28.6 us -> 25.4 us  [swap(): return lax.ppermute(x, axes, [(i, i ^ bits) for i in range(devices)])]
    pallas_call x2, Pallas kernels: 13 us -> 9.82 us  [the longest x1 5.24 us: close(): pl.pallas_call(functools.partial(close_kernel, flips=flips, nw=len(words)...]
    unnamed x44 -> x42, local copies, waits for them, and re-layouts: 2.57 us -> 2.14 us
  transfers between devices with their start and end apart: 22 -> 22, of which waited for: 13 -> 10; matrix products, arithmetic and copies ran while one was open for 1% -> 1% of each run, Pallas kernels for 37% -> 33%
where the time goes in v6:
time: 107 us
  Pallas kernels  47.4 us (44%)
  waiting for transfers between devices  27.8 us (26%)
  starting transfers between devices  25.4 us (24%)
  local copies, waits for them, and re-layouts  3.41 us (3%)
  other arithmetic  1.74 us (2%)
    ppermute x22, waiting for transfers between devices, swap(): return lax.ppermute(x, axes, [(i, i ^ bits) for i in range(devices)])  27.8 us
    pallas_call x2, Pallas kernels, embed(): pl.pallas_call(functools.partial(cnn_kernel, widths=widths, filters=filte...  26 us
    ppermute x22, starting transfers between devices, swap(): return lax.ppermute(x, axes, [(i, i ^ bits) for i in range(devices)])  25.4 us
    pallas_call x1, Pallas kernels, first_fold(): pl.pallas_call(functools.partial(first_kernel, nh=len(hid), metas=metas,...  9.6 us
    pallas_call x1, Pallas kernels, close(): pl.pallas_call(functools.partial(close_kernel, flips=flips, nw=len(words)...  5.24 us
    pallas_call x1, Pallas kernels, last_scores(): pl.pallas_call(functools.partial(last_kernel, nh=len(hid), metas=metas, g...  4.58 us
    unnamed x42, local copies, waits for them, and re-layouts  2.14 us
  transfers between devices with their start and end apart: 22, of which 10 were waited for; matrix products, arithmetic and copies ran while one was open for 1% of the time, Pallas kernels for 33%

profile of v6, /device:TPU:0, one launch (start us, length us, event | category | flops | bytes accessed | tf_op | source)
XLA Modules:
  0.0 106.7 jit_solution(14129240793951595355)
XLA Ops:
  0.6 4.1 %collective-permute-start.1 = (s32[1,64]{1,0:T(1,128)}, s32[1,64]{1,0:T(1,128)S(1)}, u32[]{:S(2)}, u32[]{:S(2)}) collective-permute-start(s32[1,64]{1,0:T(1,128)} %bitcast.27), channel_id=1, source_target_pairs={{0,2},{1,3},{2,0},{3,1},{4,6},{5,7},{6,4},{7,5},{8,10},{9,11},{10,... | collective-permute-start | bytes 776 | tf_op jit(solution)/shard_map/ppermute | solution.py:387
  4.8 12.9 %embed.3.refs_4_.refs_6_ = bf16[256,1024]{1,0:T(8,128)(2,1)} custom-call(s32[50,512]{1,0:T(8,128)} %bitcast.23, bf16[16,256]{1,0:T(8,128)(2,1)} %bitcast.25, bf16[112,896]{1,0:T(8,128)(2,1)} %conv_ref.3, f32[2,1024]{1,0:T(2,128)} %bias_ref.3, bf16[896,1024]{1,0:T(8,128)(2,1)} %proj_hbm.3, bf16[2,1024,1024]{2,1,0:T(8,128)(2,1)} %gate_hbm.3, ...), custom_call_target="tpu_custom_call" | custom-call | flops 8489271296 | bytes 12582912 | tf_op jit(solution)/shard_map/embed/pallas_call | solution.py:130
  18.1 1.8 %collective-permute-start.2 = (bf16[128,1152]{1,0:T(8,128)(2,1)S(1)}, bf16[128,1152]{1,0:T(8,128)(2,1)S(1)}, u32[]{:S(2)}, u32[]{:S(2)}) collective-permute-start(bf16[128,1152]{1,0:T(8,128)(2,1)S(1)} %fusion.1.refs_0_), channel_id=1, source_target_pairs={{0,16},{1,17},{2,18},{3,19},{4,20},{5,21},{6,22},{7,23},{8,24},{9,... | collective-permute-start | bytes 884744 | tf_op jit(solution)/shard_map/ppermute | solution.py:387
  19.9 1.5 %collective-permute-start.3 = (bf16[128,1152]{1,0:T(8,128)(2,1)S(1)}, bf16[128,1152]{1,0:T(8,128)(2,1)S(1)}, u32[]{:S(2)}, u32[]{:S(2)}) collective-permute-start(bf16[128,1152]{1,0:T(8,128)(2,1)S(1)} %fusion.1.refs_0_), channel_id=1, source_target_pairs={{0,8},{1,9},{2,10},{3,11},{4,12},{5,13},{6,14},{7,15},{8,0},{9,1},... | collective-permute-start | bytes 884744 | tf_op jit(solution)/shard_map/ppermute | solution.py:387
  21.7 1.8 %collective-permute-start.8 = (bf16[256,1024]{1,0:T(8,128)(2,1)}, bf16[256,1024]{1,0:T(8,128)(2,1)S(1)}, u32[]{:S(2)}, u32[]{:S(2)}) collective-permute-start(bf16[256,1024]{1,0:T(8,128)(2,1)} %embed.3.refs_4_.refs_6_), channel_id=1, source_target_pairs={{0,1},{1,0},{2,3},{3,2},{4,5},{5,4},{6,7},{7,6},{8,9},{9,8},{10,11... | collective-permute-start | bytes 1572872 | tf_op jit(solution)/shard_map/ppermute | solution.py:387
  23.5 13.1 %embed.2.refs_5_ = bf16[256,1024]{1,0:T(8,128)(2,1)} custom-call(s32[50,512]{1,0:T(8,128)} %bitcast.24, bf16[16,256]{1,0:T(8,128)(2,1)} %bitcast.26, bf16[112,896]{1,0:T(8,128)(2,1)} %conv_ref.3, f32[2,1024]{1,0:T(2,128)} %bias_ref.3, bf16[896,1024]{1,0:T(8,128)(2,1)} %proj_hbm.3, bf16[2,1024,1024]{2,1,0:T(8,128)(2,1)} %gate_hbm.3, ...), custom_call_target="tpu_custom_call" | custom-call | flops 8489271296 | bytes 12582912 | tf_op jit(solution)/shard_map/embed/pallas_call | solution.py:130
  38.6 1.8 %collective-permute-done.7.refs_7_ = bf16[256,1024]{1,0:T(8,128)(2,1)} collective-permute-done((bf16[256,1024]{1,0:T(8,128)(2,1)}, bf16[256,1024]{1,0:T(8,128)(2,1)}, u32[]{:S(2)}, u32[]{:S(2)}) %collective-permute-start.7) | collective-permute-done | bytes 524320 | tf_op jit(solution)/shard_map/ppermute | solution.py:387
  40.5 9.6 %first_fold.1 = (f32[512,1024]{1,0:T(8,128)}, bf16[512,1024]{1,0:T(8,128)(2,1)}, f32[512,384]{1,0:T(8,128)}) custom-call(s32[1]{0:T(128)} %bitcast.me_ref, bf16[128,1152]{1,0:T(8,128)(2,1)} %copy-done.2, bf16[128,1152]{1,0:T(8,128)(2,1)} %copy-done.4, bf16[128,1152]{1,0:T(8,128)(2,1)} %copy-done.5, bf16[128,1152]{1,0:T(8,128)(2,1)} %copy-done.6, ...), custom_call_target="tpu_custom_call" | custom-call | flops 4831838208 | bytes 4194304 | tf_op jit(solution)/shard_map/first_fold/pallas_call | solution.py:244
  50.1 1.8 %collective-permute-done.5.refs_4_.refs_8_ = bf16[256,1024]{1,0:T(8,128)(2,1)S(1)} collective-permute-done((bf16[256,1024]{1,0:T(8,128)(2,1)}, bf16[256,1024]{1,0:T(8,128)(2,1)S(1)}, u32[]{:S(2)}, u32[]{:S(2)}) %collective-permute-start.5) | collective-permute-done | bytes 524320 | tf_op jit(solution)/shard_map/ppermute | solution.py:387
  51.9 1.9 %collective-permute-done.10.refs_5_.refs_9_ = bf16[256,1024]{1,0:T(8,128)(2,1)S(1)} collective-permute-done((bf16[256,1024]{1,0:T(8,128)(2,1)S(1)}, bf16[256,1024]{1,0:T(8,128)(2,1)S(1)}, u32[]{:S(2)}, u32[]{:S(2)}) %collective-permute-start.10) | collective-permute-done | bytes 524320 | tf_op jit(solution)/shard_map/ppermute | solution.py:387
  54.6 4.6 %last_scores.1 = (bf16[512,512]{1,0:T(8,128)(2,1)}, bf16[512,512]{1,0:T(8,128)(2,1)}, f32[512,256]{1,0:T(8,128)}, f32[16,128]{1,0:T(8,128)}) custom-call(s32[1]{0:T(128)} %bitcast.me_ref, bf16[128,1152]{1,0:T(8,128)(2,1)} %copy-done.2, bf16[128,1152]{1,0:T(8,128)(2,1)} %copy-done.4, bf16[128,1152]{1,0:T(8,128)(2,1)} %copy-done.5, ...), custom_call_target="tpu_custom_call" | custom-call | flops 536870912 | bytes 2097152 | tf_op jit(solution)/shard_map/last_scores/pallas_call | solution.py:281
  59.2 1.5 %collective-permute-start.11 = (f32[16,128]{1,0:T(8,128)}, f32[16,128]{1,0:T(8,128)S(1)}, u32[]{:S(2)}, u32[]{:S(2)}) collective-permute-start(f32[16,128]{1,0:T(8,128)} %get-tuple-element.39.refs_0_), channel_id=1, source_target_pairs={{0,8},{1,9},{2,10},{3,11},{4,12},{5,13},{6,14},{7,15},{8,0},{9,1},... | collective-permute-start | bytes 24584 | tf_op jit(solution)/shard_map/ppermute | solution.py:387
  60.7 1.5 %collective-permute-start.12 = (f32[16,128]{1,0:T(8,128)}, f32[16,128]{1,0:T(8,128)S(1)}, u32[]{:S(2)}, u32[]{:S(2)}) collective-permute-start(f32[16,128]{1,0:T(8,128)} %get-tuple-element.39.refs_0_), channel_id=1, source_target_pairs={{0,16},{1,17},{2,18},{3,19},{4,20},{5,21},{6,22},{7,23},{8,24},{9,... | collective-permute-start | bytes 24584 | tf_op jit(solution)/shard_map/ppermute | solution.py:387
  62.7 2.6 %collective-permute-start.14 = (f32[16,128]{1,0:T(8,128)}, f32[16,128]{1,0:T(8,128)S(1)}, u32[]{:S(2)}, u32[]{:S(2)}) collective-permute-start(f32[16,128]{1,0:T(8,128)} %get-tuple-element.39.refs_0_), channel_id=1, source_target_pairs={{0,2},{1,3},{2,0},{3,1},{4,6},{5,7},{6,4},{7,5},{8,10},{9,11},{10,... | collective-permute-start | bytes 24584 | tf_op jit(solution)/shard_map/ppermute | solution.py:387
  66.5 3.5 %collective-permute-start.16 = (f32[16,128]{1,0:T(8,128)}, f32[16,128]{1,0:T(8,128)S(1)}, u32[]{:S(2)}, u32[]{:S(2)}) collective-permute-start(f32[16,128]{1,0:T(8,128)} %get-tuple-element.39.refs_0_), channel_id=1, source_target_pairs={{0,18},{1,19},{2,16},{3,17},{4,22},{5,23},{6,20},{7,21},{8,26},{9,... | collective-permute-start | bytes 24584 | tf_op jit(solution)/shard_map/ppermute | solution.py:387
  70.9 1.3 %collective-permute-done.16.refs_6_ = f32[16,128]{1,0:T(8,128)S(1)} collective-permute-done((f32[16,128]{1,0:T(8,128)}, f32[16,128]{1,0:T(8,128)S(1)}, u32[]{:S(2)}, u32[]{:S(2)}) %collective-permute-start.16) | collective-permute-done | bytes 8224 | tf_op jit(solution)/shard_map/ppermute | solution.py:387
  72.2 4.4 %collective-permute-done.17.refs_7_ = f32[16,128]{1,0:T(8,128)S(1)} collective-permute-done((f32[16,128]{1,0:T(8,128)}, f32[16,128]{1,0:T(8,128)S(1)}, u32[]{:S(2)}, u32[]{:S(2)}) %collective-permute-start.17) | collective-permute-done | bytes 8224 | tf_op jit(solution)/shard_map/ppermute | solution.py:387
  77.2 5.2 %close.1 = (bf16[128,1024]{1,0:T(8,128)(2,1)}, bf16[128,1024]{1,0:T(8,128)(2,1)}, bf16[128,1024]{1,0:T(8,128)(2,1)}, bf16[128,1024]{1,0:T(8,128)(2,1)}, f32[1,128]{1,0:T(1,128)}) custom-call(f32[16,128]{1,0:T(8,128)} %get-tuple-element.39.refs_0_, f32[16,128]{1,0:T(8,128)} %copy-done.11, f32[16,128]{1,0:T(8,128)} %copy-done.12, f32[16,128]{1,0:T(8,128)} %copy-done.13, ...), custom_call_target="tpu_custom_call" | custom-call | flops 1073741824 | bytes 4194304 | tf_op jit(solution)/shard_map/close/pallas_call | solution.py:334
  83.5 2.4 %collective-permute-start.20 = (bf16[128,1024]{1,0:T(8,128)(2,1)}, bf16[128,1024]{1,0:T(8,128)(2,1)S(1)}, u32[]{:S(2)}, u32[]{:S(2)}) collective-permute-start(bf16[128,1024]{1,0:T(8,128)(2,1)} %get-tuple-element.49), channel_id=1, source_target_pairs={{0,24},{1,25},{2,26},{3,27},{4,28},{5,29},{6,30},{7,31},{8,16},{9,... | collective-permute-start | bytes 786440 | tf_op jit(solution)/shard_map/ppermute | solution.py:387
  86.0 5.9 %collective-permute-done.18.refs_1_ = bf16[128,1024]{1,0:T(8,128)(2,1)S(1)} collective-permute-done((bf16[128,1024]{1,0:T(8,128)(2,1)}, bf16[128,1024]{1,0:T(8,128)(2,1)S(1)}, u32[]{:S(2)}, u32[]{:S(2)}) %collective-permute-start.18) | collective-permute-done | bytes 262176 | tf_op jit(solution)/shard_map/ppermute | solution.py:387
  91.9 3.2 %collective-permute-done.20.refs_3_ = bf16[128,1024]{1,0:T(8,128)(2,1)S(1)} collective-permute-done((bf16[128,1024]{1,0:T(8,128)(2,1)}, bf16[128,1024]{1,0:T(8,128)(2,1)S(1)}, u32[]{:S(2)}, u32[]{:S(2)}) %collective-permute-start.20) | collective-permute-done | bytes 262176 | tf_op jit(solution)/shard_map/ppermute | solution.py:387
  95.8 2.0 %add_four.1 = (bf16[64,1024]{1,0:T(8,128)(2,1)}, bf16[64,1024]{1,0:T(8,128)(2,1)}) custom-call(bf16[128,1024]{1,0:T(8,128)(2,1)} %get-tuple-element.46.refs_0_, bf16[128,1024]{1,0:T(8,128)(2,1)} %copy-done.7, bf16[128,1024]{1,0:T(8,128)(2,1)} %copy-done.8, bf16[128,1024]{1,0:T(8,128)(2,1)} %copy-done.9), custom_call_target="tpu_custom_call" | custom-call | flops 524288 | bytes 1310720 | tf_op jit(solution)/shard_map/add_four/pallas_call | solution.py:374
  99.2 5.9 %collective-permute-done.21 = bf16[64,1024]{1,0:T(8,128)(2,1)S(1)} collective-permute-done((bf16[64,1024]{1,0:T(8,128)(2,1)}, bf16[64,1024]{1,0:T(8,128)(2,1)S(1)}, u32[]{:S(2)}, u32[]{:S(2)}) %collective-permute-start.21) | collective-permute-done | bytes 131104 | tf_op jit(solution)/shard_map/ppermute | solution.py:387
  105.1 1.6 %add_convert_fusion = bf16[64,1024]{1,0:T(8,128)(2,1)} fusion(bf16[64,1024]{1,0:T(8,128)(2,1)S(1)} %collective-permute-done.21, bf16[64,1024]{1,0:T(8,128)(2,1)} %get-tuple-element.50), kind=kLoop, calls=%fused_computation.4 | loop fusion | flops 262144 | bytes 393216 | tf_op jit(solution)/shard_map/convert_element_type | solution.py:343
  (76 shorter events, 9.7 us)
Async XLA Ops:
  0.6 17.1 %collective-permute-start.1 = (s32[1,64]{1,0:T(1,128)}, s32[1,64]{1,0:T(1,128)S(1)}, u32[]{:S(2)}, u32[]{:S(2)}) collective-permute-start(s32[1,64]{1,0:T(1,128)} %bitcast.27), channel_id=1, source_target_pairs={{0,2},{1,3},{2,0},{3,1},{4,6},{5,7},{6,4},{7,5},{8,10},{9,11},{10,... | collective-permute-start | bytes 776 | tf_op jit(solution)/shard_map/ppermute | solution.py:387
  4.7 13.1 %collective-permute-start = (bf16[64,1024]{1,0:T(8,128)(2,1)}, bf16[64,1024]{1,0:T(8,128)(2,1)S(1)}, u32[]{:S(2)}, u32[]{:S(2)}) collective-permute-start(bf16[64,1024]{1,0:T(8,128)(2,1)} %param.16), channel_id=1, source_target_pairs={{0,2},{1,3},{2,0},{3,1},{4,6},{5,7},{6,4},{7,5},{8,10},{9,11},{10,... | collective-permute-start | bytes 393224 | tf_op jit(solution)/shard_map/ppermute | solution.py:387
  18.1 18.5 %copy-start.2 = (bf16[128,1152]{1,0:T(8,128)(2,1)}, bf16[128,1152]{1,0:T(8,128)(2,1)S(1)}, u32[]{:S(2)}) copy-start(bf16[128,1152]{1,0:T(8,128)(2,1)S(1)} %fusion.1.refs_0_) | copy-start | bytes 884740
  18.1 18.5 %copy-start.3 = (bf16[256,1024]{1,0:T(8,128)(2,1)S(1)}, bf16[256,1024]{1,0:T(8,128)(2,1)}, u32[]{:S(2)}) copy-start(bf16[256,1024]{1,0:T(8,128)(2,1)} %embed.3.refs_4_.refs_6_) | copy-start | bytes 1572868
  18.1 18.6 %collective-permute-start.2 = (bf16[128,1152]{1,0:T(8,128)(2,1)S(1)}, bf16[128,1152]{1,0:T(8,128)(2,1)S(1)}, u32[]{:S(2)}, u32[]{:S(2)}) collective-permute-start(bf16[128,1152]{1,0:T(8,128)(2,1)S(1)} %fusion.1.refs_0_), channel_id=1, source_target_pairs={{0,16},{1,17},{2,18},{3,19},{4,20},{5,21},{6,22},{7,23},{8,24},{9,... | collective-permute-start | bytes 884744 | tf_op jit(solution)/shard_map/ppermute | solution.py:387
  19.9 16.8 %collective-permute-start.3 = (bf16[128,1152]{1,0:T(8,128)(2,1)S(1)}, bf16[128,1152]{1,0:T(8,128)(2,1)S(1)}, u32[]{:S(2)}, u32[]{:S(2)}) collective-permute-start(bf16[128,1152]{1,0:T(8,128)(2,1)S(1)} %fusion.1.refs_0_), channel_id=1, source_target_pairs={{0,8},{1,9},{2,10},{3,11},{4,12},{5,13},{6,14},{7,15},{8,0},{9,1},... | collective-permute-start | bytes 884744 | tf_op jit(solution)/shard_map/ppermute | solution.py:387
  21.4 15.3 %collective-permute-start.4 = (bf16[128,1152]{1,0:T(8,128)(2,1)S(1)}, bf16[128,1152]{1,0:T(8,128)(2,1)S(1)}, u32[]{:S(2)}, u32[]{:S(2)}) collective-permute-start(bf16[128,1152]{1,0:T(8,128)(2,1)S(1)} %fusion.1.refs_0_), channel_id=1, source_target_pairs={{0,24},{1,25},{2,26},{3,27},{4,28},{5,29},{6,30},{7,31},{8,16},{9,... | collective-permute-start | bytes 884744 | tf_op jit(solution)/shard_map/ppermute | solution.py:387
  21.7 15.7 %collective-permute-start.8 = (bf16[256,1024]{1,0:T(8,128)(2,1)}, bf16[256,1024]{1,0:T(8,128)(2,1)S(1)}, u32[]{:S(2)}, u32[]{:S(2)}) collective-permute-start(bf16[256,1024]{1,0:T(8,128)(2,1)} %embed.3.refs_4_.refs_6_), channel_id=1, source_target_pairs={{0,1},{1,0},{2,3},{3,2},{4,5},{5,4},{6,7},{7,6},{8,9},{9,8},{10,11... | collective-permute-start | bytes 1572872 | tf_op jit(solution)/shard_map/ppermute | solution.py:387
  36.6 2.0 %collective-permute-start.6 = (bf16[256,1024]{1,0:T(8,128)(2,1)S(1)}, bf16[256,1024]{1,0:T(8,128)(2,1)S(1)}, u32[]{:S(2)}, u32[]{:S(2)}) collective-permute-start(bf16[256,1024]{1,0:T(8,128)(2,1)S(1)} %copy-done.3), channel_id=1, source_target_pairs={{0,4},{1,5},{2,6},{3,7},{4,0},{5,1},{6,2},{7,3},{8,12},{9,13},{10,... | collective-permute-start | bytes 1572872 | tf_op jit(solution)/shard_map/ppermute | solution.py:387
  36.8 3.7 %collective-permute-start.7 = (bf16[256,1024]{1,0:T(8,128)(2,1)}, bf16[256,1024]{1,0:T(8,128)(2,1)}, u32[]{:S(2)}, u32[]{:S(2)}) collective-permute-start(bf16[256,1024]{1,0:T(8,128)(2,1)} %embed.2.refs_5_), channel_id=1, source_target_pairs={{0,4},{1,5},{2,6},{3,7},{4,0},{5,1},{6,2},{7,3},{8,12},{9,13},{10,... | collective-permute-start | bytes 1572872 | tf_op jit(solution)/shard_map/ppermute | solution.py:387
  37.3 3.1 %collective-permute-start.9 = (bf16[256,1024]{1,0:T(8,128)(2,1)S(1)}, bf16[256,1024]{1,0:T(8,128)(2,1)}, u32[]{:S(2)}, u32[]{:S(2)}) collective-permute-start(bf16[256,1024]{1,0:T(8,128)(2,1)S(1)} %collective-permute-done.8.refs_8_), channel_id=1, source_target_pairs={{0,4},{1,5},{2,6},{3,7},{4,0},{5,1},{6,2},{7,3},{8,12},{9,13},{10,... | collective-permute-start | bytes 1572872 | tf_op jit(solution)/shard_map/ppermute | solution.py:387
  37.4 14.5 %collective-permute-start.5 = (bf16[256,1024]{1,0:T(8,128)(2,1)}, bf16[256,1024]{1,0:T(8,128)(2,1)S(1)}, u32[]{:S(2)}, u32[]{:S(2)}) collective-permute-start(bf16[256,1024]{1,0:T(8,128)(2,1)} %embed.2.refs_5_), channel_id=1, source_target_pairs={{0,1},{1,0},{2,3},{3,2},{4,5},{5,4},{6,7},{7,6},{8,9},{9,8},{10,11... | collective-permute-start | bytes 1572872 | tf_op jit(solution)/shard_map/ppermute | solution.py:387
  51.9 1.9 %collective-permute-start.10 = (bf16[256,1024]{1,0:T(8,128)(2,1)S(1)}, bf16[256,1024]{1,0:T(8,128)(2,1)S(1)}, u32[]{:S(2)}, u32[]{:S(2)}) collective-permute-start(bf16[256,1024]{1,0:T(8,128)(2,1)S(1)} %collective-permute-done.5.refs_4_.refs_8_), channel_id=1, source_target_pairs={{0,4},{1,5},{2,6},{3,7},{4,0},{5,1},{6,2},{7,3},{8,12},{9,13},{10,... | collective-permute-start | bytes 1572872 | tf_op jit(solution)/shard_map/ppermute | solution.py:387
  59.2 7.3 %collective-permute-start.11 = (f32[16,128]{1,0:T(8,128)}, f32[16,128]{1,0:T(8,128)S(1)}, u32[]{:S(2)}, u32[]{:S(2)}) collective-permute-start(f32[16,128]{1,0:T(8,128)} %get-tuple-element.39.refs_0_), channel_id=1, source_target_pairs={{0,8},{1,9},{2,10},{3,11},{4,12},{5,13},{6,14},{7,15},{8,0},{9,1},... | collective-permute-start | bytes 24584 | tf_op jit(solution)/shard_map/ppermute | solution.py:387
  60.7 9.4 %collective-permute-start.12 = (f32[16,128]{1,0:T(8,128)}, f32[16,128]{1,0:T(8,128)S(1)}, u32[]{:S(2)}, u32[]{:S(2)}) collective-permute-start(f32[16,128]{1,0:T(8,128)} %get-tuple-element.39.refs_0_), channel_id=1, source_target_pairs={{0,16},{1,17},{2,18},{3,19},{4,20},{5,21},{6,22},{7,23},{8,24},{9,... | collective-permute-start | bytes 24584 | tf_op jit(solution)/shard_map/ppermute | solution.py:387
  62.2 8.1 %collective-permute-start.13 = (f32[16,128]{1,0:T(8,128)}, f32[16,128]{1,0:T(8,128)S(1)}, u32[]{:S(2)}, u32[]{:S(2)}) collective-permute-start(f32[16,128]{1,0:T(8,128)} %get-tuple-element.39.refs_0_), channel_id=1, source_target_pairs={{0,24},{1,25},{2,26},{3,27},{4,28},{5,29},{6,30},{7,31},{8,16},{9,... | collective-permute-start | bytes 24584 | tf_op jit(solution)/shard_map/ppermute | solution.py:387
  62.7 7.7 %collective-permute-start.14 = (f32[16,128]{1,0:T(8,128)}, f32[16,128]{1,0:T(8,128)S(1)}, u32[]{:S(2)}, u32[]{:S(2)}) collective-permute-start(f32[16,128]{1,0:T(8,128)} %get-tuple-element.39.refs_0_), channel_id=1, source_target_pairs={{0,2},{1,3},{2,0},{3,1},{4,6},{5,7},{6,4},{7,5},{8,10},{9,11},{10,... | collective-permute-start | bytes 24584 | tf_op jit(solution)/shard_map/ppermute | solution.py:387
  65.3 5.7 %collective-permute-start.15 = (f32[16,128]{1,0:T(8,128)}, f32[16,128]{1,0:T(8,128)S(1)}, u32[]{:S(2)}, u32[]{:S(2)}) collective-permute-start(f32[16,128]{1,0:T(8,128)} %get-tuple-element.39.refs_0_), channel_id=1, source_target_pairs={{0,10},{1,11},{2,8},{3,9},{4,14},{5,15},{6,12},{7,13},{8,2},{9,3},... | collective-permute-start | bytes 24584 | tf_op jit(solution)/shard_map/ppermute | solution.py:387
  66.5 5.7 %collective-permute-start.16 = (f32[16,128]{1,0:T(8,128)}, f32[16,128]{1,0:T(8,128)S(1)}, u32[]{:S(2)}, u32[]{:S(2)}) collective-permute-start(f32[16,128]{1,0:T(8,128)} %get-tuple-element.39.refs_0_), channel_id=1, source_target_pairs={{0,18},{1,19},{2,16},{3,17},{4,22},{5,23},{6,20},{7,21},{8,26},{9,... | collective-permute-start | bytes 24584 | tf_op jit(solution)/shard_map/ppermute | solution.py:387
  70.1 6.6 %collective-permute-start.17 = (f32[16,128]{1,0:T(8,128)}, f32[16,128]{1,0:T(8,128)S(1)}, u32[]{:S(2)}, u32[]{:S(2)}) collective-permute-start(f32[16,128]{1,0:T(8,128)} %get-tuple-element.39.refs_0_), channel_id=1, source_target_pairs={{0,26},{1,27},{2,24},{3,25},{4,30},{5,31},{6,28},{7,29},{8,18},{9,... | collective-permute-start | bytes 24584 | tf_op jit(solution)/shard_map/ppermute | solution.py:387
  82.5 9.4 %collective-permute-start.18 = (bf16[128,1024]{1,0:T(8,128)(2,1)}, bf16[128,1024]{1,0:T(8,128)(2,1)S(1)}, u32[]{:S(2)}, u32[]{:S(2)}) collective-permute-start(bf16[128,1024]{1,0:T(8,128)(2,1)} %get-tuple-element.47), channel_id=1, source_target_pairs={{0,16},{1,17},{2,18},{3,19},{4,20},{5,21},{6,22},{7,23},{8,24},{9,... | collective-permute-start | bytes 786440 | tf_op jit(solution)/shard_map/ppermute | solution.py:387
  83.0 8.9 %collective-permute-start.19 = (bf16[128,1024]{1,0:T(8,128)(2,1)}, bf16[128,1024]{1,0:T(8,128)(2,1)S(1)}, u32[]{:S(2)}, u32[]{:S(2)}) collective-permute-start(bf16[128,1024]{1,0:T(8,128)(2,1)} %get-tuple-element.48), channel_id=1, source_target_pairs={{0,8},{1,9},{2,10},{3,11},{4,12},{5,13},{6,14},{7,15},{8,0},{9,1},... | collective-permute-start | bytes 786440 | tf_op jit(solution)/shard_map/ppermute | solution.py:387
  83.5 11.5 %collective-permute-start.20 = (bf16[128,1024]{1,0:T(8,128)(2,1)}, bf16[128,1024]{1,0:T(8,128)(2,1)S(1)}, u32[]{:S(2)}, u32[]{:S(2)}) collective-permute-start(bf16[128,1024]{1,0:T(8,128)(2,1)} %get-tuple-element.49), channel_id=1, source_target_pairs={{0,24},{1,25},{2,26},{3,27},{4,28},{5,29},{6,30},{7,31},{8,16},{9,... | collective-permute-start | bytes 786440 | tf_op jit(solution)/shard_map/ppermute | solution.py:387
  97.7 7.4 %collective-permute-start.21 = (bf16[64,1024]{1,0:T(8,128)(2,1)}, bf16[64,1024]{1,0:T(8,128)(2,1)S(1)}, u32[]{:S(2)}, u32[]{:S(2)}) collective-permute-start(bf16[64,1024]{1,0:T(8,128)(2,1)} %get-tuple-element.51), channel_id=1, source_target_pairs={{0,2},{1,3},{2,0},{3,1},{4,6},{5,7},{6,4},{7,5},{8,10},{9,11},{10,... | collective-permute-start | bytes 393224 | tf_op jit(solution)/shard_map/ppermute | solution.py:387
  (19 other events, 92.1 us)

commit v7 on v6

--- a/solution.py
+++ b/solution.py
@@ -51,34 +51,24 @@
 
 
 def conv_pool(vec, toep, acc, length, widths, filters):
-    words = vec.shape[0]
-    def tile(b, k, o, lhs):
+    def tile(k, o, lhs):
         cols = slice((k * SPAN + o) * filters, (k * SPAN + o + 2) * filters)
         return jnp.dot(lhs, toep[:, cols], preferred_element_type=f32)
     acc[...] = jnp.full(acc.shape, -jnp.inf, f32)
-    least = (length - widths + 1) // SPAN
-    def body(b, _):
-        lhs = vec[:, pl.ds(pl.multiple_of(b * LANES, LANES), 2 * LANES)]
-        for k in range(widths):
-            best = acc[:, k * filters:(k + 1) * filters]
-            for o in range(0, SPAN, 2):
-                r = tile(b, k, o, lhs)
-                best = jnp.maximum(best, jnp.maximum(r[:, :filters], r[:, filters:]))
-            acc[:, k * filters:(k + 1) * filters] = best
-        return 0
-    lax.fori_loop(0, least, body, 0)
-    for b in range(least, -(-length // SPAN)):
+    for b in range(-(-length // SPAN)):
         lhs = vec[:, b * LANES:(b + 2) * LANES]
         for k in range(widths):
             usable = min(SPAN, length - k - b * SPAN)
-            if usable <= 0: continue
+            if usable <= 0:
+                continue
             best = acc[:, k * filters:(k + 1) * filters]
             for o in range(0, usable, 2):
-                r = tile(b, k, o, lhs)
+                r = tile(k, o, lhs)
                 best = jnp.maximum(best, r[:, :filters])
                 if o + 1 < usable:
                     best = jnp.maximum(best, r[:, filters:])
             acc[:, k * filters:(k + 1) * filters] = best
+
 
 def cnn_kernel(ids_ref, tab_ref, conv_ref, bias_ref, proj_hbm, gate_hbm, trans_hbm, *rest,
                widths, filters, ce, length, layers, nt, start):
@@ -292,16 +282,18 @@
 
 def close_kernel(*refs, flips, nw):
     nl = len(flips)
-    lines, words = refs[:nl], refs[nl:nl + nw]
-    prob, hot, one, before, stats, facts = refs[nl + nw:nl + nw + 6]
-    parts, loss = refs[nl + nw + 6:nl + nw + 10], refs[nl + nw + 10]
+    lines, words, rest = refs[:4], refs[4:4 + nw], refs[4 + nw:]
+    prob, hot, one, before, stats, facts = rest[:6]
+    parts, loss = rest[6:10], rest[10]
+    size = lines[0].shape[0] * 4 // nl
     count, model = one.shape
     per = count // LANES
     quarter = count // 4
 
     def line(j, i, kind):
         over, halves = flips[j]
-        v = lines[j][kind * per + (i ^ over):kind * per + (i ^ over) + 1, :]
+        at = j % (nl // 4) * size + kind * per + (i ^ over)
+        v = lines[j // (nl // 4)][at:at + 1, :]
         return pltpu.roll(v, LANES // 2, axis=1) if halves else v
 
     scales = []
@@ -320,7 +312,8 @@
     for n in range(0, model, 256):
         cols = slice(n, n + 256)
         mu = jnp.concatenate([
-            sum(ref[2 * per + m // LANES:2 * per + m // LANES + 1, :] for ref in lines) * (1.0 / nl)
+            sum(ref[at + 2 * per + m // LANES:at + 2 * per + m // LANES + 1, :]
+                for ref in lines for at in range(0, ref.shape[0], size)) * (1.0 / nl)
             for m in range(n, n + 256, LANES)], axis=1)
         goal = product(hot, words, n, 256) + before[:, cols].astype(f32)
         mix = (c1 * one[:, cols] + c2 * product(prob, words, n, 256) + (c3 * mu - goal)).astype(bf16)
@@ -430,12 +423,16 @@
     words, metas = [w for w, _ in late], tuple(m for _, m in late)
     prob, hot, facts, line = last_scores(
         me, hid, words, metas, (0, core, near, core | near), local, e0, stats)
-    bits = [bit_a, bit_b] + rest
-    others = [sum(b for j, b in enumerate(bits) if k >> j & 1) for k in range(1, 1 << len(bits))]
+    lines, others = line, [0]
+    for bit in rest:
+        lines = jnp.concatenate([lines, swap(lines, bit)], axis=0)
+        others += [o | bit for o in others]
+    plane = (bit_b, bit_a, bit_a | bit_b)
+    lines = [lines] + [swap(lines, o) for o in plane]
+    others = [o | p for p in (0,) + plane for o in others]
     order = rest + [bit_b, bit_a]
     flips = tuple((sum(1 << (j - 1) for j, b in enumerate(order) if j and o & b), bool(o & rest[0])) for o in others)
-    lines = [swap(line, o) for o in others]
-    *parts, loss = close([line] + lines, ((0, False),) + flips, words, prob, hot, one, target, stats, facts)
+    *parts, loss = close(lines, flips, words, prob, hot, one, target, stats, facts)
     far_part = swap(parts[3], bit_a | bit_b)
     keep, send = add_four(parts[0], swap(parts[1], bit_b), swap(parts[2], bit_a), far_part)
     for bit in rest[:0:-1]:

time: 107 us -> 99.4 us (0.929)
  waiting for transfers between devices: 27.8 us -> 24.9 us
  starting transfers between devices: 25.4 us -> 22.7 us
  Pallas kernels: 47.4 us -> 44.8 us
    ppermute x22 -> x19, waiting for transfers between devices: 27.8 us -> 24.9 us  [swap(): return lax.ppermute(x, axes, [(i, i ^ bits) for i in range(devices)])]
    pallas_call x2, Pallas kernels: 26 us -> 23.2 us  [embed(): pl.pallas_call(functools.partial(cnn_kernel, widths=widths, filters=filte...]
    ppermute x22 -> x19, starting transfers between devices: 25.4 us -> 22.7 us  [swap(): return lax.ppermute(x, axes, [(i, i ^ bits) for i in range(devices)])]
    unnamed x42 -> x37, local copies, waits for them, and re-layouts: 2.14 us -> 2.88 us
  transfers between devices with their start and end apart: 22 -> 19, of which waited for: 10 -> 11; matrix products, arithmetic and copies ran while one was open for 1% -> 2% of each run, Pallas kernels for 33% -> 33%
where the time goes in v7:
time: 99.4 us; the launch traced here: 99.1 us
  Pallas kernels  44.8 us (45%)
  waiting for transfers between devices  24.9 us (25%)
  starting transfers between devices  22.7 us (23%)
  local copies, waits for them, and re-layouts  4.16 us (4%)
  other arithmetic  1.74 us (2%)
    ppermute x19, waiting for transfers between devices, swap(): return lax.ppermute(x, axes, [(i, i ^ bits) for i in range(devices)])  24.9 us
    pallas_call x2, Pallas kernels, embed(): pl.pallas_call(functools.partial(cnn_kernel, widths=widths, filters=filte...  23.2 us
    ppermute x19, starting transfers between devices, swap(): return lax.ppermute(x, axes, [(i, i ^ bits) for i in range(devices)])  22.7 us
    pallas_call x1, Pallas kernels, first_fold(): pl.pallas_call(functools.partial(first_kernel, nh=len(hid), metas=metas,...  9.59 us
    pallas_call x1, Pallas kernels, close(): pl.pallas_call(functools.partial(close_kernel, flips=flips, nw=len(words)...  5.24 us
    pallas_call x1, Pallas kernels, last_scores(): pl.pallas_call(functools.partial(last_kernel, nh=len(hid), metas=metas, g...  4.81 us
    unnamed x37, local copies, waits for them, and re-layouts  2.88 us
  transfers between devices with their start and end apart: 19, of which 11 were waited for; matrix products, arithmetic and copies ran while one was open for 2% of the time, Pallas kernels for 33%

profile of v7, /device:TPU:0, one launch (start us, length us, event | category | flops | bytes accessed | tf_op | source)
XLA Modules:
  0.0 99.1 jit_solution(9501494829653577966)
XLA Ops:
  0.6 4.1 %collective-permute-start.1 = (s32[1,64]{1,0:T(1,128)}, s32[1,64]{1,0:T(1,128)S(1)}, u32[]{:S(2)}, u32[]{:S(2)}) collective-permute-start(s32[1,64]{1,0:T(1,128)} %bitcast.27), channel_id=1, source_target_pairs={{0,2},{1,3},{2,0},{3,1},{4,6},{5,7},{6,4},{7,5},{8,10},{9,11},{10,... | collective-permute-start | bytes 776 | tf_op jit(solution)/shard_map/ppermute | solution.py:380
  4.8 11.5 %embed.3.refs_4_.refs_6_ = bf16[256,1024]{1,0:T(8,128)(2,1)} custom-call(s32[50,512]{1,0:T(8,128)} %bitcast.23, bf16[16,256]{1,0:T(8,128)(2,1)} %bitcast.25, bf16[112,896]{1,0:T(8,128)(2,1)} %conv_ref.3, f32[2,1024]{1,0:T(2,128)} %bias_ref.3, bf16[896,1024]{1,0:T(8,128)(2,1)} %proj_hbm.3, bf16[2,1024,1024]{2,1,0:T(8,128)(2,1)} %gate_hbm.3, ...), custom_call_target="tpu_custom_call" | custom-call | flops 8489271296 | bytes 12582912 | tf_op jit(solution)/shard_map/embed/pallas_call | solution.py:120
  16.7 1.8 %collective-permute-start.2 = (bf16[128,1152]{1,0:T(8,128)(2,1)S(1)}, bf16[128,1152]{1,0:T(8,128)(2,1)S(1)}, u32[]{:S(2)}, u32[]{:S(2)}) collective-permute-start(bf16[128,1152]{1,0:T(8,128)(2,1)S(1)} %fusion.1.refs_0_), channel_id=1, source_target_pairs={{0,16},{1,17},{2,18},{3,19},{4,20},{5,21},{6,22},{7,23},{8,24},{9,... | collective-permute-start | bytes 884744 | tf_op jit(solution)/shard_map/ppermute | solution.py:380
  18.5 1.5 %collective-permute-start.3 = (bf16[128,1152]{1,0:T(8,128)(2,1)S(1)}, bf16[128,1152]{1,0:T(8,128)(2,1)S(1)}, u32[]{:S(2)}, u32[]{:S(2)}) collective-permute-start(bf16[128,1152]{1,0:T(8,128)(2,1)S(1)} %fusion.1.refs_0_), channel_id=1, source_target_pairs={{0,8},{1,9},{2,10},{3,11},{4,12},{5,13},{6,14},{7,15},{8,0},{9,1},... | collective-permute-start | bytes 884744 | tf_op jit(solution)/shard_map/ppermute | solution.py:380
  20.2 1.8 %collective-permute-start.8 = (bf16[256,1024]{1,0:T(8,128)(2,1)}, bf16[256,1024]{1,0:T(8,128)(2,1)S(1)}, u32[]{:S(2)}, u32[]{:S(2)}) collective-permute-start(bf16[256,1024]{1,0:T(8,128)(2,1)} %embed.3.refs_4_.refs_6_), channel_id=1, source_target_pairs={{0,1},{1,0},{2,3},{3,2},{4,5},{5,4},{6,7},{7,6},{8,9},{9,8},{10,11... | collective-permute-start | bytes 1572872 | tf_op jit(solution)/shard_map/ppermute | solution.py:380
  22.1 11.7 %embed.2.refs_5_ = bf16[256,1024]{1,0:T(8,128)(2,1)} custom-call(s32[50,512]{1,0:T(8,128)} %bitcast.24, bf16[16,256]{1,0:T(8,128)(2,1)} %bitcast.26, bf16[112,896]{1,0:T(8,128)(2,1)} %conv_ref.3, f32[2,1024]{1,0:T(2,128)} %bias_ref.3, bf16[896,1024]{1,0:T(8,128)(2,1)} %proj_hbm.3, bf16[2,1024,1024]{2,1,0:T(8,128)(2,1)} %gate_hbm.3, ...), custom_call_target="tpu_custom_call" | custom-call | flops 8489271296 | bytes 12582912 | tf_op jit(solution)/shard_map/embed/pallas_call | solution.py:120
  35.8 1.8 %collective-permute-done.7.refs_7_ = bf16[256,1024]{1,0:T(8,128)(2,1)} collective-permute-done((bf16[256,1024]{1,0:T(8,128)(2,1)}, bf16[256,1024]{1,0:T(8,128)(2,1)}, u32[]{:S(2)}, u32[]{:S(2)}) %collective-permute-start.7) | collective-permute-done | bytes 524320 | tf_op jit(solution)/shard_map/ppermute | solution.py:380
  37.7 9.6 %first_fold.1 = (f32[512,1024]{1,0:T(8,128)}, bf16[512,1024]{1,0:T(8,128)(2,1)}, f32[512,384]{1,0:T(8,128)}) custom-call(s32[1]{0:T(128)} %bitcast.me_ref, bf16[128,1152]{1,0:T(8,128)(2,1)} %copy-done.2, bf16[128,1152]{1,0:T(8,128)(2,1)} %copy-done.4, bf16[128,1152]{1,0:T(8,128)(2,1)} %copy-done.5, bf16[128,1152]{1,0:T(8,128)(2,1)} %copy-done.6, ...), custom_call_target="tpu_custom_call" | custom-call | flops 4831838208 | bytes 4194304 | tf_op jit(solution)/shard_map/first_fold/pallas_call | solution.py:234
  47.2 1.8 %collective-permute-done.5.refs_4_ = bf16[256,1024]{1,0:T(8,128)(2,1)S(1)} collective-permute-done((bf16[256,1024]{1,0:T(8,128)(2,1)}, bf16[256,1024]{1,0:T(8,128)(2,1)S(1)}, u32[]{:S(2)}, u32[]{:S(2)}) %collective-permute-start.5) | collective-permute-done | bytes 524320 | tf_op jit(solution)/shard_map/ppermute | solution.py:380
  49.1 1.9 %collective-permute-done.10.refs_5_ = bf16[256,1024]{1,0:T(8,128)(2,1)S(1)} collective-permute-done((bf16[256,1024]{1,0:T(8,128)(2,1)S(1)}, bf16[256,1024]{1,0:T(8,128)(2,1)S(1)}, u32[]{:S(2)}, u32[]{:S(2)}) %collective-permute-start.10) | collective-permute-done | bytes 524320 | tf_op jit(solution)/shard_map/ppermute | solution.py:380
  51.8 4.8 %last_scores.1 = (bf16[512,512]{1,0:T(8,128)(2,1)}, bf16[512,512]{1,0:T(8,128)(2,1)}, f32[512,256]{1,0:T(8,128)}, f32[16,128]{1,0:T(8,128)}) custom-call(s32[1]{0:T(128)} %bitcast.me_ref, bf16[128,1152]{1,0:T(8,128)(2,1)} %copy-done.2, bf16[128,1152]{1,0:T(8,128)(2,1)} %copy-done.4, bf16[128,1152]{1,0:T(8,128)(2,1)} %copy-done.5, ...), custom_call_target="tpu_custom_call" | custom-call | flops 536870912 | bytes 2097152 | tf_op jit(solution)/shard_map/last_scores/pallas_call | solution.py:271
  56.6 2.6 %collective-permute-start.11 = (f32[16,128]{1,0:T(8,128)}, f32[16,128]{1,0:T(8,128)S(1)}, u32[]{:S(2)}, u32[]{:S(2)}) collective-permute-start(f32[16,128]{1,0:T(8,128)} %get-tuple-element.39), channel_id=1, source_target_pairs={{0,2},{1,3},{2,0},{3,1},{4,6},{5,7},{6,4},{7,5},{8,10},{9,11},{10,... | collective-permute-start | bytes 24584 | tf_op jit(solution)/shard_map/ppermute | solution.py:380
  61.3 1.5 %collective-permute-start.12 = (f32[32,128]{1,0:T(8,128)S(1)}, f32[32,128]{1,0:T(8,128)S(1)}, u32[]{:S(2)}, u32[]{:S(2)}) collective-permute-start(f32[32,128]{1,0:T(8,128)S(1)} %constant_dynamic-update-slice_fusion.refs_0_), channel_id=1, source_target_pairs={{0,16},{1,17},{2,18},{3,19},{4,20},{5,21},{6,22},{7,23},{8,24},{9,... | collective-permute-start | bytes 49160 | tf_op jit(solution)/shard_map/ppermute | solution.py:380
  62.9 1.5 %collective-permute-start.13 = (f32[32,128]{1,0:T(8,128)S(1)}, f32[32,128]{1,0:T(8,128)S(1)}, u32[]{:S(2)}, u32[]{:S(2)}) collective-permute-start(f32[32,128]{1,0:T(8,128)S(1)} %constant_dynamic-update-slice_fusion.refs_0_), channel_id=1, source_target_pairs={{0,8},{1,9},{2,10},{3,11},{4,12},{5,13},{6,14},{7,15},{8,0},{9,1},... | collective-permute-start | bytes 49160 | tf_op jit(solution)/shard_map/ppermute | solution.py:380
  65.1 1.5 %collective-permute-done.13.refs_2_ = f32[32,128]{1,0:T(8,128)S(1)} collective-permute-done((f32[32,128]{1,0:T(8,128)S(1)}, f32[32,128]{1,0:T(8,128)S(1)}, u32[]{:S(2)}, u32[]{:S(2)}) %collective-permute-start.13) | collective-permute-done | bytes 16416 | tf_op jit(solution)/shard_map/ppermute | solution.py:380
  66.6 2.4 %collective-permute-done.14.refs_3_ = f32[32,128]{1,0:T(8,128)S(1)} collective-permute-done((f32[32,128]{1,0:T(8,128)S(1)}, f32[32,128]{1,0:T(8,128)S(1)}, u32[]{:S(2)}, u32[]{:S(2)}) %collective-permute-start.14) | collective-permute-done | bytes 16416 | tf_op jit(solution)/shard_map/ppermute | solution.py:380
  69.6 5.2 %close.1 = (bf16[128,1024]{1,0:T(8,128)(2,1)}, bf16[128,1024]{1,0:T(8,128)(2,1)}, bf16[128,1024]{1,0:T(8,128)(2,1)}, bf16[128,1024]{1,0:T(8,128)(2,1)}, f32[1,128]{1,0:T(1,128)}) custom-call(f32[32,128]{1,0:T(8,128)} %copy-done.11, f32[32,128]{1,0:T(8,128)} %copy-done.12, f32[32,128]{1,0:T(8,128)} %copy-done.13, f32[32,128]{1,0:T(8,128)} %copy-done.14, ...), custom_call_target="tpu_custom_call" | custom-call | flops 1073741824 | bytes 4194304 | tf_op jit(solution)/shard_map/close/pallas_call | solution.py:327
  75.9 2.4 %collective-permute-start.17 = (bf16[128,1024]{1,0:T(8,128)(2,1)}, bf16[128,1024]{1,0:T(8,128)(2,1)S(1)}, u32[]{:S(2)}, u32[]{:S(2)}) collective-permute-start(bf16[128,1024]{1,0:T(8,128)(2,1)} %get-tuple-element.49), channel_id=1, source_target_pairs={{0,24},{1,25},{2,26},{3,27},{4,28},{5,29},{6,30},{7,31},{8,16},{9,... | collective-permute-start | bytes 786440 | tf_op jit(solution)/shard_map/ppermute | solution.py:380
  78.3 5.9 %collective-permute-done.15.refs_1_ = bf16[128,1024]{1,0:T(8,128)(2,1)S(1)} collective-permute-done((bf16[128,1024]{1,0:T(8,128)(2,1)}, bf16[128,1024]{1,0:T(8,128)(2,1)S(1)}, u32[]{:S(2)}, u32[]{:S(2)}) %collective-permute-start.15) | collective-permute-done | bytes 262176 | tf_op jit(solution)/shard_map/ppermute | solution.py:380
  84.2 3.2 %collective-permute-done.17.refs_3_ = bf16[128,1024]{1,0:T(8,128)(2,1)S(1)} collective-permute-done((bf16[128,1024]{1,0:T(8,128)(2,1)}, bf16[128,1024]{1,0:T(8,128)(2,1)S(1)}, u32[]{:S(2)}, u32[]{:S(2)}) %collective-permute-start.17) | collective-permute-done | bytes 262176 | tf_op jit(solution)/shard_map/ppermute | solution.py:380
  88.2 2.0 %add_four.1 = (bf16[64,1024]{1,0:T(8,128)(2,1)}, bf16[64,1024]{1,0:T(8,128)(2,1)}) custom-call(bf16[128,1024]{1,0:T(8,128)(2,1)} %get-tuple-element.46.refs_0_, bf16[128,1024]{1,0:T(8,128)(2,1)} %copy-done.7, bf16[128,1024]{1,0:T(8,128)(2,1)} %copy-done.8, bf16[128,1024]{1,0:T(8,128)(2,1)} %copy-done.9), custom_call_target="tpu_custom_call" | custom-call | flops 524288 | bytes 1310720 | tf_op jit(solution)/shard_map/add_four/pallas_call | solution.py:367
  90.1 2.6 %collective-permute-start.18 = (bf16[64,1024]{1,0:T(8,128)(2,1)}, bf16[64,1024]{1,0:T(8,128)(2,1)S(1)}, u32[]{:S(2)}, u32[]{:S(2)}) collective-permute-start(bf16[64,1024]{1,0:T(8,128)(2,1)} %get-tuple-element.51), channel_id=1, source_target_pairs={{0,2},{1,3},{2,0},{3,1},{4,6},{5,7},{6,4},{7,5},{8,10},{9,11},{10,... | collective-permute-start | bytes 393224 | tf_op jit(solution)/shard_map/ppermute | solution.py:380
  93.9 3.7 %collective-permute-done.18 = bf16[64,1024]{1,0:T(8,128)(2,1)S(1)} collective-permute-done((bf16[64,1024]{1,0:T(8,128)(2,1)}, bf16[64,1024]{1,0:T(8,128)(2,1)S(1)}, u32[]{:S(2)}, u32[]{:S(2)}) %collective-permute-start.18) | collective-permute-done | bytes 131104 | tf_op jit(solution)/shard_map/ppermute | solution.py:380
  97.5 1.6 %add_convert_fusion = bf16[64,1024]{1,0:T(8,128)(2,1)} fusion(bf16[64,1024]{1,0:T(8,128)(2,1)S(1)} %collective-permute-done.18, bf16[64,1024]{1,0:T(8,128)(2,1)} %get-tuple-element.50), kind=kLoop, calls=%fused_computation.4 | loop fusion | flops 262144 | bytes 393216 | tf_op jit(solution)/shard_map/convert_element_type | solution.py:336
  (66 shorter events, 9.7 us)
Async XLA Ops:
  0.6 15.7 %collective-permute-start.1 = (s32[1,64]{1,0:T(1,128)}, s32[1,64]{1,0:T(1,128)S(1)}, u32[]{:S(2)}, u32[]{:S(2)}) collective-permute-start(s32[1,64]{1,0:T(1,128)} %bitcast.27), channel_id=1, source_target_pairs={{0,2},{1,3},{2,0},{3,1},{4,6},{5,7},{6,4},{7,5},{8,10},{9,11},{10,... | collective-permute-start | bytes 776 | tf_op jit(solution)/shard_map/ppermute | solution.py:380
  4.7 11.7 %collective-permute-start = (bf16[64,1024]{1,0:T(8,128)(2,1)}, bf16[64,1024]{1,0:T(8,128)(2,1)S(1)}, u32[]{:S(2)}, u32[]{:S(2)}) collective-permute-start(bf16[64,1024]{1,0:T(8,128)(2,1)} %param.16), channel_id=1, source_target_pairs={{0,2},{1,3},{2,0},{3,1},{4,6},{5,7},{6,4},{7,5},{8,10},{9,11},{10,... | collective-permute-start | bytes 393224 | tf_op jit(solution)/shard_map/ppermute | solution.py:380
  4.8 11.5 %copy-start.17 = (s32[64]{0:T(128)S(1)}, s32[64]{0:T(128)}, u32[]{:S(2)}) copy-start(s32[64]{0:T(128)} %param.17) | copy-start | bytes 772
  4.8 11.6 %copy-start.10 = (bf16[64,1024]{1,0:T(8,128)(2,1)S(1)}, bf16[64,1024]{1,0:T(8,128)(2,1)}, u32[]{:S(2)}) copy-start(bf16[64,1024]{1,0:T(8,128)(2,1)} %param.16) | copy-start | bytes 393220
  16.7 17.1 %copy-start.2 = (bf16[128,1152]{1,0:T(8,128)(2,1)}, bf16[128,1152]{1,0:T(8,128)(2,1)S(1)}, u32[]{:S(2)}) copy-start(bf16[128,1152]{1,0:T(8,128)(2,1)S(1)} %fusion.1.refs_0_) | copy-start | bytes 884740
  16.7 17.1 %copy-start.3 = (bf16[256,1024]{1,0:T(8,128)(2,1)S(1)}, bf16[256,1024]{1,0:T(8,128)(2,1)}, u32[]{:S(2)}) copy-start(bf16[256,1024]{1,0:T(8,128)(2,1)} %embed.3.refs_4_.refs_6_) | copy-start | bytes 1572868
  16.7 17.2 %collective-permute-start.2 = (bf16[128,1152]{1,0:T(8,128)(2,1)S(1)}, bf16[128,1152]{1,0:T(8,128)(2,1)S(1)}, u32[]{:S(2)}, u32[]{:S(2)}) collective-permute-start(bf16[128,1152]{1,0:T(8,128)(2,1)S(1)} %fusion.1.refs_0_), channel_id=1, source_target_pairs={{0,16},{1,17},{2,18},{3,19},{4,20},{5,21},{6,22},{7,23},{8,24},{9,... | collective-permute-start | bytes 884744 | tf_op jit(solution)/shard_map/ppermute | solution.py:380
  18.5 15.4 %collective-permute-start.3 = (bf16[128,1152]{1,0:T(8,128)(2,1)S(1)}, bf16[128,1152]{1,0:T(8,128)(2,1)S(1)}, u32[]{:S(2)}, u32[]{:S(2)}) collective-permute-start(bf16[128,1152]{1,0:T(8,128)(2,1)S(1)} %fusion.1.refs_0_), channel_id=1, source_target_pairs={{0,8},{1,9},{2,10},{3,11},{4,12},{5,13},{6,14},{7,15},{8,0},{9,1},... | collective-permute-start | bytes 884744 | tf_op jit(solution)/shard_map/ppermute | solution.py:380
  20.0 13.9 %collective-permute-start.4 = (bf16[128,1152]{1,0:T(8,128)(2,1)S(1)}, bf16[128,1152]{1,0:T(8,128)(2,1)S(1)}, u32[]{:S(2)}, u32[]{:S(2)}) collective-permute-start(bf16[128,1152]{1,0:T(8,128)(2,1)S(1)} %fusion.1.refs_0_), channel_id=1, source_target_pairs={{0,24},{1,25},{2,26},{3,27},{4,28},{5,29},{6,30},{7,31},{8,16},{9,... | collective-permute-start | bytes 884744 | tf_op jit(solution)/shard_map/ppermute | solution.py:380
  20.2 14.2 %collective-permute-start.8 = (bf16[256,1024]{1,0:T(8,128)(2,1)}, bf16[256,1024]{1,0:T(8,128)(2,1)S(1)}, u32[]{:S(2)}, u32[]{:S(2)}) collective-permute-start(bf16[256,1024]{1,0:T(8,128)(2,1)} %embed.3.refs_4_.refs_6_), channel_id=1, source_target_pairs={{0,1},{1,0},{2,3},{3,2},{4,5},{5,4},{6,7},{7,6},{8,9},{9,8},{10,11... | collective-permute-start | bytes 1572872 | tf_op jit(solution)/shard_map/ppermute | solution.py:380
  33.8 2.0 %collective-permute-start.6 = (bf16[256,1024]{1,0:T(8,128)(2,1)S(1)}, bf16[256,1024]{1,0:T(8,128)(2,1)S(1)}, u32[]{:S(2)}, u32[]{:S(2)}) collective-permute-start(bf16[256,1024]{1,0:T(8,128)(2,1)S(1)} %copy-done.3), channel_id=1, source_target_pairs={{0,4},{1,5},{2,6},{3,7},{4,0},{5,1},{6,2},{7,3},{8,12},{9,13},{10,... | collective-permute-start | bytes 1572872 | tf_op jit(solution)/shard_map/ppermute | solution.py:380
  33.9 3.7 %collective-permute-start.7 = (bf16[256,1024]{1,0:T(8,128)(2,1)}, bf16[256,1024]{1,0:T(8,128)(2,1)}, u32[]{:S(2)}, u32[]{:S(2)}) collective-permute-start(bf16[256,1024]{1,0:T(8,128)(2,1)} %embed.2.refs_5_), channel_id=1, source_target_pairs={{0,4},{1,5},{2,6},{3,7},{4,0},{5,1},{6,2},{7,3},{8,12},{9,13},{10,... | collective-permute-start | bytes 1572872 | tf_op jit(solution)/shard_map/ppermute | solution.py:380
  34.5 3.1 %collective-permute-start.9 = (bf16[256,1024]{1,0:T(8,128)(2,1)S(1)}, bf16[256,1024]{1,0:T(8,128)(2,1)}, u32[]{:S(2)}, u32[]{:S(2)}) collective-permute-start(bf16[256,1024]{1,0:T(8,128)(2,1)S(1)} %collective-permute-done.8.refs_8_), channel_id=1, source_target_pairs={{0,4},{1,5},{2,6},{3,7},{4,0},{5,1},{6,2},{7,3},{8,12},{9,13},{10,... | collective-permute-start | bytes 1572872 | tf_op jit(solution)/shard_map/ppermute | solution.py:380
  34.6 14.5 %collective-permute-start.5 = (bf16[256,1024]{1,0:T(8,128)(2,1)}, bf16[256,1024]{1,0:T(8,128)(2,1)S(1)}, u32[]{:S(2)}, u32[]{:S(2)}) collective-permute-start(bf16[256,1024]{1,0:T(8,128)(2,1)} %embed.2.refs_5_), channel_id=1, source_target_pairs={{0,1},{1,0},{2,3},{3,2},{4,5},{5,4},{6,7},{7,6},{8,9},{9,8},{10,11... | collective-permute-start | bytes 1572872 | tf_op jit(solution)/shard_map/ppermute | solution.py:380
  49.0 1.9 %collective-permute-start.10 = (bf16[256,1024]{1,0:T(8,128)(2,1)S(1)}, bf16[256,1024]{1,0:T(8,128)(2,1)S(1)}, u32[]{:S(2)}, u32[]{:S(2)}) collective-permute-start(bf16[256,1024]{1,0:T(8,128)(2,1)S(1)} %collective-permute-done.5.refs_4_), channel_id=1, source_target_pairs={{0,4},{1,5},{2,6},{3,7},{4,0},{5,1},{6,2},{7,3},{8,12},{9,13},{10,... | collective-permute-start | bytes 1572872 | tf_op jit(solution)/shard_map/ppermute | solution.py:380
  56.6 4.8 %collective-permute-start.11 = (f32[16,128]{1,0:T(8,128)}, f32[16,128]{1,0:T(8,128)S(1)}, u32[]{:S(2)}, u32[]{:S(2)}) collective-permute-start(f32[16,128]{1,0:T(8,128)} %get-tuple-element.39), channel_id=1, source_target_pairs={{0,2},{1,3},{2,0},{3,1},{4,6},{5,7},{6,4},{7,5},{8,10},{9,11},{10,... | collective-permute-start | bytes 24584 | tf_op jit(solution)/shard_map/ppermute | solution.py:380
  61.3 7.7 %copy-start.11 = (f32[32,128]{1,0:T(8,128)}, f32[32,128]{1,0:T(8,128)S(1)}, u32[]{:S(2)}) copy-start(f32[32,128]{1,0:T(8,128)S(1)} %constant_dynamic-update-slice_fusion.refs_0_) | copy-start | bytes 49156
  61.3 3.7 %collective-permute-start.12 = (f32[32,128]{1,0:T(8,128)S(1)}, f32[32,128]{1,0:T(8,128)S(1)}, u32[]{:S(2)}, u32[]{:S(2)}) collective-permute-start(f32[32,128]{1,0:T(8,128)S(1)} %constant_dynamic-update-slice_fusion.refs_0_), channel_id=1, source_target_pairs={{0,16},{1,17},{2,18},{3,19},{4,20},{5,21},{6,22},{7,23},{8,24},{9,... | collective-permute-start | bytes 49160 | tf_op jit(solution)/shard_map/ppermute | solution.py:380
  62.9 3.7 %collective-permute-start.13 = (f32[32,128]{1,0:T(8,128)S(1)}, f32[32,128]{1,0:T(8,128)S(1)}, u32[]{:S(2)}, u32[]{:S(2)}) collective-permute-start(f32[32,128]{1,0:T(8,128)S(1)} %constant_dynamic-update-slice_fusion.refs_0_), channel_id=1, source_target_pairs={{0,8},{1,9},{2,10},{3,11},{4,12},{5,13},{6,14},{7,15},{8,0},{9,1},... | collective-permute-start | bytes 49160 | tf_op jit(solution)/shard_map/ppermute | solution.py:380
  64.4 4.6 %collective-permute-start.14 = (f32[32,128]{1,0:T(8,128)S(1)}, f32[32,128]{1,0:T(8,128)S(1)}, u32[]{:S(2)}, u32[]{:S(2)}) collective-permute-start(f32[32,128]{1,0:T(8,128)S(1)} %constant_dynamic-update-slice_fusion.refs_0_), channel_id=1, source_target_pairs={{0,24},{1,25},{2,26},{3,27},{4,28},{5,29},{6,30},{7,31},{8,16},{9,... | collective-permute-start | bytes 49160 | tf_op jit(solution)/shard_map/ppermute | solution.py:380
  74.8 9.4 %collective-permute-start.15 = (bf16[128,1024]{1,0:T(8,128)(2,1)}, bf16[128,1024]{1,0:T(8,128)(2,1)S(1)}, u32[]{:S(2)}, u32[]{:S(2)}) collective-permute-start(bf16[128,1024]{1,0:T(8,128)(2,1)} %get-tuple-element.47), channel_id=1, source_target_pairs={{0,16},{1,17},{2,18},{3,19},{4,20},{5,21},{6,22},{7,23},{8,24},{9,... | collective-permute-start | bytes 786440 | tf_op jit(solution)/shard_map/ppermute | solution.py:380
  75.3 8.9 %collective-permute-start.16 = (bf16[128,1024]{1,0:T(8,128)(2,1)}, bf16[128,1024]{1,0:T(8,128)(2,1)S(1)}, u32[]{:S(2)}, u32[]{:S(2)}) collective-permute-start(bf16[128,1024]{1,0:T(8,128)(2,1)} %get-tuple-element.48), channel_id=1, source_target_pairs={{0,8},{1,9},{2,10},{3,11},{4,12},{5,13},{6,14},{7,15},{8,0},{9,1},... | collective-permute-start | bytes 786440 | tf_op jit(solution)/shard_map/ppermute | solution.py:380
  75.9 11.6 %collective-permute-start.17 = (bf16[128,1024]{1,0:T(8,128)(2,1)}, bf16[128,1024]{1,0:T(8,128)(2,1)S(1)}, u32[]{:S(2)}, u32[]{:S(2)}) collective-permute-start(bf16[128,1024]{1,0:T(8,128)(2,1)} %get-tuple-element.49), channel_id=1, source_target_pairs={{0,24},{1,25},{2,26},{3,27},{4,28},{5,29},{6,30},{7,31},{8,16},{9,... | collective-permute-start | bytes 786440 | tf_op jit(solution)/shard_map/ppermute | solution.py:380
  90.1 7.4 %collective-permute-start.18 = (bf16[64,1024]{1,0:T(8,128)(2,1)}, bf16[64,1024]{1,0:T(8,128)(2,1)S(1)}, u32[]{:S(2)}, u32[]{:S(2)}) collective-permute-start(bf16[64,1024]{1,0:T(8,128)(2,1)} %get-tuple-element.51), channel_id=1, source_target_pairs={{0,2},{1,3},{2,0},{3,1},{4,6},{5,7},{6,4},{7,5},{8,10},{9,11},{10,... | collective-permute-start | bytes 393224 | tf_op jit(solution)/shard_map/ppermute | solution.py:380
  (13 other events, 33.0 us)

commit v8 on v7

--- a/solution.py
+++ b/solution.py
@@ -11,56 +11,58 @@
 SPAN = 8
 
 
-def prep_toeplitz(conv_ref, toep, ce, widths, filters):
+def prep_toeplitz(conv_ref, toep, ce, k, filters):
     depth = toep.shape[0]
-    for k in range(widths):
-        rows = (k + 1) * ce
-        piece = conv_ref[0:rows, k * filters:(k + 1) * filters]
-        for o in range(SPAN):
-            cols = slice((k * SPAN + o) * filters, (k * SPAN + o + 1) * filters)
-            if o:
-                toep[0:o * ce, cols] = jnp.zeros((o * ce, filters), bf16)
-            toep[o * ce:o * ce + rows, cols] = piece
-            rest = depth - o * ce - rows
-            if rest:
-                toep[o * ce + rows:depth, cols] = jnp.zeros((rest, filters), bf16)
-
-def lookup(ids_ref, start, words, tab_ref, vec, length, ce):
+    rows = (k + 1) * ce
+    piece = conv_ref[0:rows, k * filters:(k + 1) * filters]
+    for o in range(SPAN):
+        cols = slice((k * SPAN + o) * filters, (k * SPAN + o + 1) * filters)
+        if o:
+            toep[0:o * ce, cols] = jnp.zeros((o * ce, filters), bf16)
+        toep[o * ce:o * ce + rows, cols] = piece
+        rest = depth - o * ce - rows
+        if rest:
+            toep[o * ce + rows:depth, cols] = jnp.zeros((rest, filters), bf16)
+
+
+def lookup(ids_ref, start, words, tab_ref, vec, length, ce, g):
     per = LANES // ce
     low_tab = tab_ref[:, 0:LANES].astype(f32)
     top_tab = tab_ref[:, LANES:2 * LANES].astype(f32)
     first = start // LANES * LANES
     for tile in range(first, start + words, LANES):
         low_word, high_word = max(tile, start), min(tile + LANES, start + words)
-        for g in range(vec.shape[1] // LANES):
-            parts = []
-            for q in range(per):
-                p = g * per + q
-                if p >= length:
-                    parts.append(jnp.zeros((ce, LANES), f32))
-                    continue
-                idx = jnp.broadcast_to(ids_ref[p:p + 1, tile:tile + LANES], (8, LANES))
-                low = jnp.bitwise_and(idx, LANES - 1)
-                top = idx >= LANES
-                for h in range(0, ce, 8):
-                    one = jnp.take_along_axis(low_tab[h:h + 8], low, axis=1)
-                    two = jnp.take_along_axis(top_tab[h:h + 8], low, axis=1)
-                    parts.append(jnp.where(top, two, one))
-            block = jnp.concatenate(parts, axis=0).T.astype(bf16)
-            vec[low_word - start:high_word - start, g * LANES:(g + 1) * LANES] = block[low_word - tile:high_word - tile]
-
-
-def conv_pool(vec, toep, acc, length, widths, filters):
+        parts = []
+        for p in range(g * per, (g + 1) * per):
+            if p >= length:
+                parts.append(jnp.zeros((ce, LANES), f32))
+                continue
+            idx = jnp.broadcast_to(ids_ref[p:p + 1, tile:tile + LANES], (8, LANES))
+            low = jnp.bitwise_and(idx, LANES - 1)
+            top = idx >= LANES
+            for h in range(0, ce, 8):
+                one = jnp.take_along_axis(low_tab[h:h + 8], low, axis=1)
+                two = jnp.take_along_axis(top_tab[h:h + 8], low, axis=1)
+                parts.append(jnp.where(top, two, one))
+        block = jnp.concatenate(parts, axis=0).T.astype(bf16)
+        vec[low_word - start:high_word - start, g * LANES:(g + 1) * LANES] = block[low_word - tile:high_word - tile]
+
+
+def conv_pool(vec, toep, acc, length, widths, filters, look, build):
     def tile(k, o, lhs):
         cols = slice((k * SPAN + o) * filters, (k * SPAN + o + 2) * filters)
         return jnp.dot(lhs, toep[:, cols], preferred_element_type=f32)
     acc[...] = jnp.full(acc.shape, -jnp.inf, f32)
+    look(0)
     for b in range(-(-length // SPAN)):
+        look(b + 1)
         lhs = vec[:, b * LANES:(b + 2) * LANES]
         for k in range(widths):
             usable = min(SPAN, length - k - b * SPAN)
             if usable <= 0:
                 continue
+            if b == 0:
+                build(k)
             best = acc[:, k * filters:(k + 1) * filters]
             for o in range(0, usable, 2):
                 r = tile(k, o, lhs)
@@ -78,9 +80,10 @@
     for c in copies:
         c.start()
     words = out_ref.shape[0]
-    prep_toeplitz(conv_ref, toep, ce, widths, filters)
-    lookup(ids_ref, start, words, tab_ref, vec, length, ce)
-    conv_pool(vec, toep, acc, length, widths, filters)
+    conv_pool(
+        vec, toep, acc, length, widths, filters,
+        lambda g: lookup(ids_ref, start, words, tab_ref, vec, length, ce, g),
+        lambda k: prep_toeplitz(conv_ref, toep, ce, k, filters))
     for c in copies:
         c.wait()
     feat[...] = jnp.tanh(acc[...]).astype(bf16)
@@ -201,6 +204,14 @@
     return res
 
 
+def pack(columns, out):
+    lane = lax.broadcasted_iota(jnp.int32, out.shape, 1)
+    res = jnp.zeros(out.shape, f32)
+    for i, column in enumerate(columns):
+        res = jnp.where(lane == i, column, res)
+    out[...] = res
+
+
 def load_rows(hid, rows):
     at = 0
     for h in hid:
@@ -213,8 +224,7 @@
     out, target, stats, rows, score, prob, hot = refs[nh + len(metas):]
     load_rows(hid, rows)
     each = scores_of(rows, words, metas, *aims(me_ref, hid, local), score, prob, hot)
-    for i, column in enumerate(each):
-        stats[:, i * LANES:(i + 1) * LANES] = jnp.broadcast_to(column, (column.shape[0], LANES))
+    pack(each, stats)
     for n in range(0, out.shape[1], 256):
         out[:, n:n + 256] = product(prob, words, n, 256)
         target[:, n:n + 256] = product(hot, words, n, 256).astype(bf16)
@@ -234,7 +244,7 @@
     return pl.pallas_call(
         functools.partial(first_kernel, nh=len(hid), metas=metas, local=local),
         out_shape=[jax.ShapeDtypeStruct((rows, model), f32), jax.ShapeDtypeStruct((rows, model), bf16),
-                   jax.ShapeDtypeStruct((rows, 3 * LANES), f32)],
+                   jax.ShapeDtypeStruct((rows, LANES), f32)],
         in_specs=[SM] + [VM] * (len(hid) + len(words)), out_specs=[VM] * 3,
         scratch_shapes=[pltpu.VMEM((rows, model), bf16), pltpu.VMEM((rows, count), f32),
                         pltpu.VMEM((rows, count), bf16), pltpu.VMEM((rows, count), bf16)],
@@ -245,39 +255,38 @@
 
 def last_kernel(me_ref, *refs, nh, metas, group, local):
     hid, words = refs[:nh], refs[nh:nh + len(metas)]
-    own, stats, prob, hot, facts, lines, rows, score = refs[nh + len(metas):]
+    stats, prob, hot, facts, lines, rows, score = refs[nh + len(metas):]
     load_rows(hid, rows)
     count, model = rows.shape
     apart, place = aims(me_ref, hid, local)
     top2, total2, aim2 = scores_of(rows, words, metas, apart, place, score, prob, hot)
-    top1, total1, aim1 = (stats[:, i * LANES:i * LANES + 1] for i in range(3))
+    top1, total1, aim1 = (stats[:, i:i + 1] for i in range(3))
     top = jnp.maximum(top1, top2)
     total = jnp.exp(top1 - top) * total1 + jnp.exp(top2 - top) * total2
     inside = sum(jnp.where(apart == bits, 1.0, 0.0) for bits in group)
-    facts[:, 0:LANES] = jnp.broadcast_to(top2, (count, LANES))
-    facts[:, LANES:2 * LANES] = jnp.broadcast_to(inside, (count, LANES))
+    pack((top2, inside), facts)
     per = count // LANES
     to_lines(top + jnp.log(total), lines, 0)
     to_lines(aim1 + aim2, lines, per)
-    centre = jnp.sum(own[0:LANES, :].astype(f32), axis=0, keepdims=True) * (1.0 / LANES)
+    centre = jnp.sum(words[0][0:LANES, :].astype(f32), axis=0, keepdims=True) * (1.0 / LANES)
     for n in range(model // LANES):
         lines[2 * per + n:2 * per + n + 1, :] = centre[:, n * LANES:(n + 1) * LANES]
 
 
-def last_scores(me, hid, words, metas, group, local, own, stats):
-    model = own.shape[1]
+def last_scores(me, hid, words, metas, group, local, stats):
+    model = words[0].shape[1]
     rows = stats.shape[0]
     count = sum(w.shape[0] for w in words)
     return pl.pallas_call(
         functools.partial(last_kernel, nh=len(hid), metas=metas, group=group, local=local),
         out_shape=[jax.ShapeDtypeStruct((rows, count), bf16)] * 2 + [
-            jax.ShapeDtypeStruct((rows, 2 * LANES), f32),
+            jax.ShapeDtypeStruct((rows, LANES), f32),
             jax.ShapeDtypeStruct((2 * rows // LANES + model // LANES, LANES), f32)],
-        in_specs=[SM] + [VM] * (len(hid) + len(words) + 2), out_specs=[VM] * 4,
+        in_specs=[SM] + [VM] * (len(hid) + len(words) + 1), out_specs=[VM] * 4,
         scratch_shapes=[pltpu.VMEM((rows, model), bf16), pltpu.VMEM((rows, count), f32)],
         compiler_params=params(), cost_estimate=cost(2 * rows * count * model, 2 * (rows + count) * model),
         name="last_scores",
-    )(me, *hid, *words, own, stats)
+    )(me, *hid, *words, stats)
 
 
 def close_kernel(*refs, flips, nw):
@@ -306,8 +315,8 @@
         weight = jnp.broadcast_to(jnp.exp(each[0] - whole), (LANES, LANES)).T
         whole = jnp.broadcast_to(whole, (LANES, LANES)).T
         part = slice(i * LANES, (i + 1) * LANES)
-        scales.append((jnp.exp(stats[part, 0:LANES] - whole)[:, 0:1], jnp.exp(facts[part, 0:LANES] - whole)[:, 0:1],
-                       (facts[part, LANES:2 * LANES] - weight)[:, 0:1]))
+        scales.append((jnp.exp(stats[part, 0:1] - whole[:, 0:1]), jnp.exp(facts[part, 0:1] - whole[:, 0:1]),
+                       facts[part, 1:2] - weight[:, 0:1]))
     c1, c2, c3 = (jnp.concatenate(c, axis=0) for c in zip(*scales))
     for n in range(0, model, 256):
         cols = slice(n, n + 256)
@@ -422,7 +431,7 @@
     late += [(held, meta[2][1]), (swap(held, core), meta[3][1])]
     words, metas = [w for w, _ in late], tuple(m for _, m in late)
     prob, hot, facts, line = last_scores(
-        me, hid, words, metas, (0, core, near, core | near), local, e0, stats)
+        me, hid, words, metas, (0, core, near, core | near), local, stats)
     lines, others = line, [0]
     for bit in rest:
         lines = jnp.concatenate([lines, swap(lines, bit)], axis=0)

time: 99.4 us -> 98.8 us (level)
  no operation moved by 1% of the time
where the time goes in v8:
time: 98.8 us; the launch traced here: 98.5 us
  Pallas kernels  44.1 us (45%)
  waiting for transfers between devices  24.9 us (25%)
  starting transfers between devices  22.7 us (23%)
  local copies, waits for them, and re-layouts  4.21 us (4%)
  other arithmetic  1.74 us (2%)
    ppermute x19, waiting for transfers between devices, swap(): return lax.ppermute(x, axes, [(i, i ^ bits) for i in range(devices)])  24.9 us
    pallas_call x2, Pallas kernels, embed(): pl.pallas_call(functools.partial(cnn_kernel, widths=widths, filters=filte...  23.2 us
    ppermute x19, starting transfers between devices, swap(): return lax.ppermute(x, axes, [(i, i ^ bits) for i in range(devices)])  22.7 us
    pallas_call x1, Pallas kernels, first_fold(): pl.pallas_call(functools.partial(first_kernel, nh=len(hid), metas=metas,...  9.5 us
    pallas_call x1, Pallas kernels, close(): pl.pallas_call(functools.partial(close_kernel, flips=flips, nw=len(words)...  5.19 us
    pallas_call x1, Pallas kernels, last_scores(): pl.pallas_call(functools.partial(last_kernel, nh=len(hid), metas=metas, g...  4.26 us
    unnamed x37, local copies, waits for them, and re-layouts  2.88 us
  transfers between devices with their start and end apart: 19, of which 11 were waited for; matrix products, arithmetic and copies ran while one was open for 2% of the time, Pallas kernels for 33%

profile of v8, /device:TPU:0, one launch (start us, length us, event | category | flops | bytes accessed | tf_op | source)
XLA Modules:
  0.0 98.5 jit_solution(4689009918541409072)
XLA Ops:
  0.6 4.1 %collective-permute-start.1 = (s32[1,64]{1,0:T(1,128)}, s32[1,64]{1,0:T(1,128)S(1)}, u32[]{:S(2)}, u32[]{:S(2)}) collective-permute-start(s32[1,64]{1,0:T(1,128)} %bitcast.27), channel_id=1, source_target_pairs={{0,2},{1,3},{2,0},{3,1},{4,6},{5,7},{6,4},{7,5},{8,10},{9,11},{10,... | collective-permute-start | bytes 776 | tf_op jit(solution)/shard_map/ppermute | solution.py:389
  4.8 11.5 %embed.3.refs_4_ = bf16[256,1024]{1,0:T(8,128)(2,1)} custom-call(s32[50,512]{1,0:T(8,128)} %bitcast.23, bf16[16,256]{1,0:T(8,128)(2,1)} %bitcast.25, bf16[112,896]{1,0:T(8,128)(2,1)} %conv_ref.3, f32[2,1024]{1,0:T(2,128)} %bias_ref.3, bf16[896,1024]{1,0:T(8,128)(2,1)} %proj_hbm.3, bf16[2,1024,1024]{2,1,0:T(8,128)(2,1)} %gate_hbm.3, ...), custom_call_target="tpu_custom_call" | custom-call | flops 8489271296 | bytes 12582912 | tf_op jit(solution)/shard_map/embed/pallas_call | solution.py:123
  16.7 1.8 %collective-permute-start.2 = (bf16[128,1152]{1,0:T(8,128)(2,1)S(1)}, bf16[128,1152]{1,0:T(8,128)(2,1)S(1)}, u32[]{:S(2)}, u32[]{:S(2)}) collective-permute-start(bf16[128,1152]{1,0:T(8,128)(2,1)S(1)} %fusion.1.refs_0_), channel_id=1, source_target_pairs={{0,16},{1,17},{2,18},{3,19},{4,20},{5,21},{6,22},{7,23},{8,24},{9,... | collective-permute-start | bytes 884744 | tf_op jit(solution)/shard_map/ppermute | solution.py:389
  18.6 1.5 %collective-permute-start.3 = (bf16[128,1152]{1,0:T(8,128)(2,1)S(1)}, bf16[128,1152]{1,0:T(8,128)(2,1)S(1)}, u32[]{:S(2)}, u32[]{:S(2)}) collective-permute-start(bf16[128,1152]{1,0:T(8,128)(2,1)S(1)} %fusion.1.refs_0_), channel_id=1, source_target_pairs={{0,8},{1,9},{2,10},{3,11},{4,12},{5,13},{6,14},{7,15},{8,0},{9,1},... | collective-permute-start | bytes 884744 | tf_op jit(solution)/shard_map/ppermute | solution.py:389
  20.3 1.8 %collective-permute-start.8 = (bf16[256,1024]{1,0:T(8,128)(2,1)}, bf16[256,1024]{1,0:T(8,128)(2,1)S(1)}, u32[]{:S(2)}, u32[]{:S(2)}) collective-permute-start(bf16[256,1024]{1,0:T(8,128)(2,1)} %embed.3.refs_4_), channel_id=1, source_target_pairs={{0,1},{1,0},{2,3},{3,2},{4,5},{5,4},{6,7},{7,6},{8,9},{9,8},{10,11... | collective-permute-start | bytes 1572872 | tf_op jit(solution)/shard_map/ppermute | solution.py:389
  22.1 11.7 %embed.2.refs_5_ = bf16[256,1024]{1,0:T(8,128)(2,1)} custom-call(s32[50,512]{1,0:T(8,128)} %bitcast.24, bf16[16,256]{1,0:T(8,128)(2,1)} %bitcast.26, bf16[112,896]{1,0:T(8,128)(2,1)} %conv_ref.3, f32[2,1024]{1,0:T(2,128)} %bias_ref.3, bf16[896,1024]{1,0:T(8,128)(2,1)} %proj_hbm.3, bf16[2,1024,1024]{2,1,0:T(8,128)(2,1)} %gate_hbm.3, ...), custom_call_target="tpu_custom_call" | custom-call | flops 8489271296 | bytes 12582912 | tf_op jit(solution)/shard_map/embed/pallas_call | solution.py:123
  35.8 1.8 %collective-permute-done.7.refs_7_ = bf16[256,1024]{1,0:T(8,128)(2,1)} collective-permute-done((bf16[256,1024]{1,0:T(8,128)(2,1)}, bf16[256,1024]{1,0:T(8,128)(2,1)}, u32[]{:S(2)}, u32[]{:S(2)}) %collective-permute-start.7) | collective-permute-done | bytes 524320 | tf_op jit(solution)/shard_map/ppermute | solution.py:389
  37.7 9.5 %first_fold.1 = (f32[512,1024]{1,0:T(8,128)}, bf16[512,1024]{1,0:T(8,128)(2,1)}, f32[512,128]{1,0:T(8,128)}) custom-call(s32[1]{0:T(128)} %bitcast.me_ref, bf16[128,1152]{1,0:T(8,128)(2,1)} %copy-done.2, bf16[128,1152]{1,0:T(8,128)(2,1)} %copy-done.3, bf16[128,1152]{1,0:T(8,128)(2,1)} %copy-done.4, bf16[128,1152]{1,0:T(8,128)(2,1)} %copy-done.5, ...), custom_call_target="tpu_custom_call" | custom-call | flops 4831838208 | bytes 4194304 | tf_op jit(solution)/shard_map/first_fold/pallas_call | solution.py:244
  47.2 1.9 %collective-permute-done.5.refs_4_ = bf16[256,1024]{1,0:T(8,128)(2,1)S(1)} collective-permute-done((bf16[256,1024]{1,0:T(8,128)(2,1)}, bf16[256,1024]{1,0:T(8,128)(2,1)S(1)}, u32[]{:S(2)}, u32[]{:S(2)}) %collective-permute-start.5) | collective-permute-done | bytes 524320 | tf_op jit(solution)/shard_map/ppermute | solution.py:389
  49.1 1.9 %collective-permute-done.10.refs_5_ = bf16[256,1024]{1,0:T(8,128)(2,1)S(1)} collective-permute-done((bf16[256,1024]{1,0:T(8,128)(2,1)S(1)}, bf16[256,1024]{1,0:T(8,128)(2,1)S(1)}, u32[]{:S(2)}, u32[]{:S(2)}) %collective-permute-start.10) | collective-permute-done | bytes 524320 | tf_op jit(solution)/shard_map/ppermute | solution.py:389
  51.8 4.3 %last_scores.1 = (bf16[512,512]{1,0:T(8,128)(2,1)}, bf16[512,512]{1,0:T(8,128)(2,1)}, f32[512,128]{1,0:T(8,128)}, f32[16,128]{1,0:T(8,128)}) custom-call(s32[1]{0:T(128)} %bitcast.me_ref, bf16[128,1152]{1,0:T(8,128)(2,1)} %copy-done.2, bf16[128,1152]{1,0:T(8,128)(2,1)} %copy-done.3, bf16[128,1152]{1,0:T(8,128)(2,1)} %copy-done.4, ...), custom_call_target="tpu_custom_call" | custom-call | flops 536870912 | bytes 2097152 | tf_op jit(solution)/shard_map/last_scores/pallas_call | solution.py:280
  56.0 2.6 %collective-permute-start.11 = (f32[16,128]{1,0:T(8,128)}, f32[16,128]{1,0:T(8,128)S(1)}, u32[]{:S(2)}, u32[]{:S(2)}) collective-permute-start(f32[16,128]{1,0:T(8,128)} %get-tuple-element.39), channel_id=1, source_target_pairs={{0,2},{1,3},{2,0},{3,1},{4,6},{5,7},{6,4},{7,5},{8,10},{9,11},{10,... | collective-permute-start | bytes 24584 | tf_op jit(solution)/shard_map/ppermute | solution.py:389
  60.8 1.5 %collective-permute-start.12 = (f32[32,128]{1,0:T(8,128)S(1)}, f32[32,128]{1,0:T(8,128)S(1)}, u32[]{:S(2)}, u32[]{:S(2)}) collective-permute-start(f32[32,128]{1,0:T(8,128)S(1)} %constant_dynamic-update-slice_fusion.refs_0_), channel_id=1, source_target_pairs={{0,16},{1,17},{2,18},{3,19},{4,20},{5,21},{6,22},{7,23},{8,24},{9,... | collective-permute-start | bytes 49160 | tf_op jit(solution)/shard_map/ppermute | solution.py:389
  62.3 1.5 %collective-permute-start.13 = (f32[32,128]{1,0:T(8,128)S(1)}, f32[32,128]{1,0:T(8,128)S(1)}, u32[]{:S(2)}, u32[]{:S(2)}) collective-permute-start(f32[32,128]{1,0:T(8,128)S(1)} %constant_dynamic-update-slice_fusion.refs_0_), channel_id=1, source_target_pairs={{0,8},{1,9},{2,10},{3,11},{4,12},{5,13},{6,14},{7,15},{8,0},{9,1},... | collective-permute-start | bytes 49160 | tf_op jit(solution)/shard_map/ppermute | solution.py:389
  64.5 1.5 %collective-permute-done.13.refs_2_ = f32[32,128]{1,0:T(8,128)S(1)} collective-permute-done((f32[32,128]{1,0:T(8,128)S(1)}, f32[32,128]{1,0:T(8,128)S(1)}, u32[]{:S(2)}, u32[]{:S(2)}) %collective-permute-start.13) | collective-permute-done | bytes 16416 | tf_op jit(solution)/shard_map/ppermute | solution.py:389
  66.1 2.4 %collective-permute-done.14.refs_3_ = f32[32,128]{1,0:T(8,128)S(1)} collective-permute-done((f32[32,128]{1,0:T(8,128)S(1)}, f32[32,128]{1,0:T(8,128)S(1)}, u32[]{:S(2)}, u32[]{:S(2)}) %collective-permute-start.14) | collective-permute-done | bytes 16416 | tf_op jit(solution)/shard_map/ppermute | solution.py:389
  69.1 5.2 %close.1 = (bf16[128,1024]{1,0:T(8,128)(2,1)}, bf16[128,1024]{1,0:T(8,128)(2,1)}, bf16[128,1024]{1,0:T(8,128)(2,1)}, bf16[128,1024]{1,0:T(8,128)(2,1)}, f32[1,128]{1,0:T(1,128)}) custom-call(f32[32,128]{1,0:T(8,128)} %copy-done.10, f32[32,128]{1,0:T(8,128)} %copy-done.11, f32[32,128]{1,0:T(8,128)} %copy-done.12, f32[32,128]{1,0:T(8,128)} %copy-done.13, ...), custom_call_target="tpu_custom_call" | custom-call | flops 1073741824 | bytes 4194304 | tf_op jit(solution)/shard_map/close/pallas_call | solution.py:336
  75.3 2.5 %collective-permute-start.17 = (bf16[128,1024]{1,0:T(8,128)(2,1)}, bf16[128,1024]{1,0:T(8,128)(2,1)S(1)}, u32[]{:S(2)}, u32[]{:S(2)}) collective-permute-start(bf16[128,1024]{1,0:T(8,128)(2,1)} %get-tuple-element.49), channel_id=1, source_target_pairs={{0,24},{1,25},{2,26},{3,27},{4,28},{5,29},{6,30},{7,31},{8,16},{9,... | collective-permute-start | bytes 786440 | tf_op jit(solution)/shard_map/ppermute | solution.py:389
  77.7 5.9 %collective-permute-done.15.refs_1_ = bf16[128,1024]{1,0:T(8,128)(2,1)S(1)} collective-permute-done((bf16[128,1024]{1,0:T(8,128)(2,1)}, bf16[128,1024]{1,0:T(8,128)(2,1)S(1)}, u32[]{:S(2)}, u32[]{:S(2)}) %collective-permute-start.15) | collective-permute-done | bytes 262176 | tf_op jit(solution)/shard_map/ppermute | solution.py:389
  83.6 3.2 %collective-permute-done.17.refs_3_ = bf16[128,1024]{1,0:T(8,128)(2,1)S(1)} collective-permute-done((bf16[128,1024]{1,0:T(8,128)(2,1)}, bf16[128,1024]{1,0:T(8,128)(2,1)S(1)}, u32[]{:S(2)}, u32[]{:S(2)}) %collective-permute-start.17) | collective-permute-done | bytes 262176 | tf_op jit(solution)/shard_map/ppermute | solution.py:389
  87.6 2.0 %add_four.1 = (bf16[64,1024]{1,0:T(8,128)(2,1)}, bf16[64,1024]{1,0:T(8,128)(2,1)}) custom-call(bf16[128,1024]{1,0:T(8,128)(2,1)} %get-tuple-element.46.refs_0_, bf16[128,1024]{1,0:T(8,128)(2,1)} %copy-done.6, bf16[128,1024]{1,0:T(8,128)(2,1)} %copy-done.7, bf16[128,1024]{1,0:T(8,128)(2,1)} %copy-done.8), custom_call_target="tpu_custom_call" | custom-call | flops 524288 | bytes 1310720 | tf_op jit(solution)/shard_map/add_four/pallas_call | solution.py:376
  89.5 2.6 %collective-permute-start.18 = (bf16[64,1024]{1,0:T(8,128)(2,1)}, bf16[64,1024]{1,0:T(8,128)(2,1)S(1)}, u32[]{:S(2)}, u32[]{:S(2)}) collective-permute-start(bf16[64,1024]{1,0:T(8,128)(2,1)} %get-tuple-element.51), channel_id=1, source_target_pairs={{0,2},{1,3},{2,0},{3,1},{4,6},{5,7},{6,4},{7,5},{8,10},{9,11},{10,... | collective-permute-start | bytes 393224 | tf_op jit(solution)/shard_map/ppermute | solution.py:389
  93.3 3.6 %collective-permute-done.18 = bf16[64,1024]{1,0:T(8,128)(2,1)S(1)} collective-permute-done((bf16[64,1024]{1,0:T(8,128)(2,1)}, bf16[64,1024]{1,0:T(8,128)(2,1)S(1)}, u32[]{:S(2)}, u32[]{:S(2)}) %collective-permute-start.18) | collective-permute-done | bytes 131104 | tf_op jit(solution)/shard_map/ppermute | solution.py:389
  96.9 1.6 %add_convert_fusion = bf16[64,1024]{1,0:T(8,128)(2,1)} fusion(bf16[64,1024]{1,0:T(8,128)(2,1)S(1)} %collective-permute-done.18, bf16[64,1024]{1,0:T(8,128)(2,1)} %get-tuple-element.50), kind=kLoop, calls=%fused_computation.4 | loop fusion | flops 262144 | bytes 393216 | tf_op jit(solution)/shard_map/convert_element_type | solution.py:345
  (66 shorter events, 9.8 us)
Async XLA Ops:
  0.6 15.7 %collective-permute-start.1 = (s32[1,64]{1,0:T(1,128)}, s32[1,64]{1,0:T(1,128)S(1)}, u32[]{:S(2)}, u32[]{:S(2)}) collective-permute-start(s32[1,64]{1,0:T(1,128)} %bitcast.27), channel_id=1, source_target_pairs={{0,2},{1,3},{2,0},{3,1},{4,6},{5,7},{6,4},{7,5},{8,10},{9,11},{10,... | collective-permute-start | bytes 776 | tf_op jit(solution)/shard_map/ppermute | solution.py:389
  4.7 11.7 %collective-permute-start = (bf16[64,1024]{1,0:T(8,128)(2,1)}, bf16[64,1024]{1,0:T(8,128)(2,1)S(1)}, u32[]{:S(2)}, u32[]{:S(2)}) collective-permute-start(bf16[64,1024]{1,0:T(8,128)(2,1)} %param.16), channel_id=1, source_target_pairs={{0,2},{1,3},{2,0},{3,1},{4,6},{5,7},{6,4},{7,5},{8,10},{9,11},{10,... | collective-permute-start | bytes 393224 | tf_op jit(solution)/shard_map/ppermute | solution.py:389
  4.8 11.6 %copy-start.17 = (s32[64]{0:T(128)S(1)}, s32[64]{0:T(128)}, u32[]{:S(2)}) copy-start(s32[64]{0:T(128)} %param.17) | copy-start | bytes 772
  4.8 11.6 %copy-start.9 = (bf16[64,1024]{1,0:T(8,128)(2,1)S(1)}, bf16[64,1024]{1,0:T(8,128)(2,1)}, u32[]{:S(2)}) copy-start(bf16[64,1024]{1,0:T(8,128)(2,1)} %param.16) | copy-start | bytes 393220
  16.7 17.1 %copy-start.2 = (bf16[128,1152]{1,0:T(8,128)(2,1)}, bf16[128,1152]{1,0:T(8,128)(2,1)S(1)}, u32[]{:S(2)}) copy-start(bf16[128,1152]{1,0:T(8,128)(2,1)S(1)} %fusion.1.refs_0_) | copy-start | bytes 884740
  16.7 17.1 %copy-start.14 = (bf16[256,1024]{1,0:T(8,128)(2,1)S(1)}, bf16[256,1024]{1,0:T(8,128)(2,1)}, u32[]{:S(2)}) copy-start(bf16[256,1024]{1,0:T(8,128)(2,1)} %embed.3.refs_4_) | copy-start | bytes 1572868
  16.7 17.2 %collective-permute-start.2 = (bf16[128,1152]{1,0:T(8,128)(2,1)S(1)}, bf16[128,1152]{1,0:T(8,128)(2,1)S(1)}, u32[]{:S(2)}, u32[]{:S(2)}) collective-permute-start(bf16[128,1152]{1,0:T(8,128)(2,1)S(1)} %fusion.1.refs_0_), channel_id=1, source_target_pairs={{0,16},{1,17},{2,18},{3,19},{4,20},{5,21},{6,22},{7,23},{8,24},{9,... | collective-permute-start | bytes 884744 | tf_op jit(solution)/shard_map/ppermute | solution.py:389
  18.6 15.4 %collective-permute-start.3 = (bf16[128,1152]{1,0:T(8,128)(2,1)S(1)}, bf16[128,1152]{1,0:T(8,128)(2,1)S(1)}, u32[]{:S(2)}, u32[]{:S(2)}) collective-permute-start(bf16[128,1152]{1,0:T(8,128)(2,1)S(1)} %fusion.1.refs_0_), channel_id=1, source_target_pairs={{0,8},{1,9},{2,10},{3,11},{4,12},{5,13},{6,14},{7,15},{8,0},{9,1},... | collective-permute-start | bytes 884744 | tf_op jit(solution)/shard_map/ppermute | solution.py:389
  20.0 13.9 %collective-permute-start.4 = (bf16[128,1152]{1,0:T(8,128)(2,1)S(1)}, bf16[128,1152]{1,0:T(8,128)(2,1)S(1)}, u32[]{:S(2)}, u32[]{:S(2)}) collective-permute-start(bf16[128,1152]{1,0:T(8,128)(2,1)S(1)} %fusion.1.refs_0_), channel_id=1, source_target_pairs={{0,24},{1,25},{2,26},{3,27},{4,28},{5,29},{6,30},{7,31},{8,16},{9,... | collective-permute-start | bytes 884744 | tf_op jit(solution)/shard_map/ppermute | solution.py:389
  20.3 14.2 %collective-permute-start.8 = (bf16[256,1024]{1,0:T(8,128)(2,1)}, bf16[256,1024]{1,0:T(8,128)(2,1)S(1)}, u32[]{:S(2)}, u32[]{:S(2)}) collective-permute-start(bf16[256,1024]{1,0:T(8,128)(2,1)} %embed.3.refs_4_), channel_id=1, source_target_pairs={{0,1},{1,0},{2,3},{3,2},{4,5},{5,4},{6,7},{7,6},{8,9},{9,8},{10,11... | collective-permute-start | bytes 1572872 | tf_op jit(solution)/shard_map/ppermute | solution.py:389
  33.8 2.0 %collective-permute-start.6 = (bf16[256,1024]{1,0:T(8,128)(2,1)S(1)}, bf16[256,1024]{1,0:T(8,128)(2,1)S(1)}, u32[]{:S(2)}, u32[]{:S(2)}) collective-permute-start(bf16[256,1024]{1,0:T(8,128)(2,1)S(1)} %copy-done.14), channel_id=1, source_target_pairs={{0,4},{1,5},{2,6},{3,7},{4,0},{5,1},{6,2},{7,3},{8,12},{9,13},{10,... | collective-permute-start | bytes 1572872 | tf_op jit(solution)/shard_map/ppermute | solution.py:389
  33.9 3.7 %collective-permute-start.7 = (bf16[256,1024]{1,0:T(8,128)(2,1)}, bf16[256,1024]{1,0:T(8,128)(2,1)}, u32[]{:S(2)}, u32[]{:S(2)}) collective-permute-start(bf16[256,1024]{1,0:T(8,128)(2,1)} %embed.2.refs_5_), channel_id=1, source_target_pairs={{0,4},{1,5},{2,6},{3,7},{4,0},{5,1},{6,2},{7,3},{8,12},{9,13},{10,... | collective-permute-start | bytes 1572872 | tf_op jit(solution)/shard_map/ppermute | solution.py:389
  34.5 3.1 %collective-permute-start.9 = (bf16[256,1024]{1,0:T(8,128)(2,1)S(1)}, bf16[256,1024]{1,0:T(8,128)(2,1)}, u32[]{:S(2)}, u32[]{:S(2)}) collective-permute-start(bf16[256,1024]{1,0:T(8,128)(2,1)S(1)} %collective-permute-done.8.refs_8_), channel_id=1, source_target_pairs={{0,4},{1,5},{2,6},{3,7},{4,0},{5,1},{6,2},{7,3},{8,12},{9,13},{10,... | collective-permute-start | bytes 1572872 | tf_op jit(solution)/shard_map/ppermute | solution.py:389
  34.6 14.5 %collective-permute-start.5 = (bf16[256,1024]{1,0:T(8,128)(2,1)}, bf16[256,1024]{1,0:T(8,128)(2,1)S(1)}, u32[]{:S(2)}, u32[]{:S(2)}) collective-permute-start(bf16[256,1024]{1,0:T(8,128)(2,1)} %embed.2.refs_5_), channel_id=1, source_target_pairs={{0,1},{1,0},{2,3},{3,2},{4,5},{5,4},{6,7},{7,6},{8,9},{9,8},{10,11... | collective-permute-start | bytes 1572872 | tf_op jit(solution)/shard_map/ppermute | solution.py:389
  49.1 1.9 %collective-permute-start.10 = (bf16[256,1024]{1,0:T(8,128)(2,1)S(1)}, bf16[256,1024]{1,0:T(8,128)(2,1)S(1)}, u32[]{:S(2)}, u32[]{:S(2)}) collective-permute-start(bf16[256,1024]{1,0:T(8,128)(2,1)S(1)} %collective-permute-done.5.refs_4_), channel_id=1, source_target_pairs={{0,4},{1,5},{2,6},{3,7},{4,0},{5,1},{6,2},{7,3},{8,12},{9,13},{10,... | collective-permute-start | bytes 1572872 | tf_op jit(solution)/shard_map/ppermute | solution.py:389
  56.0 4.8 %collective-permute-start.11 = (f32[16,128]{1,0:T(8,128)}, f32[16,128]{1,0:T(8,128)S(1)}, u32[]{:S(2)}, u32[]{:S(2)}) collective-permute-start(f32[16,128]{1,0:T(8,128)} %get-tuple-element.39), channel_id=1, source_target_pairs={{0,2},{1,3},{2,0},{3,1},{4,6},{5,7},{6,4},{7,5},{8,10},{9,11},{10,... | collective-permute-start | bytes 24584 | tf_op jit(solution)/shard_map/ppermute | solution.py:389
  60.8 7.7 %copy-start.10 = (f32[32,128]{1,0:T(8,128)}, f32[32,128]{1,0:T(8,128)S(1)}, u32[]{:S(2)}) copy-start(f32[32,128]{1,0:T(8,128)S(1)} %constant_dynamic-update-slice_fusion.refs_0_) | copy-start | bytes 49156
  60.8 3.7 %collective-permute-start.12 = (f32[32,128]{1,0:T(8,128)S(1)}, f32[32,128]{1,0:T(8,128)S(1)}, u32[]{:S(2)}, u32[]{:S(2)}) collective-permute-start(f32[32,128]{1,0:T(8,128)S(1)} %constant_dynamic-update-slice_fusion.refs_0_), channel_id=1, source_target_pairs={{0,16},{1,17},{2,18},{3,19},{4,20},{5,21},{6,22},{7,23},{8,24},{9,... | collective-permute-start | bytes 49160 | tf_op jit(solution)/shard_map/ppermute | solution.py:389
  62.3 3.7 %collective-permute-start.13 = (f32[32,128]{1,0:T(8,128)S(1)}, f32[32,128]{1,0:T(8,128)S(1)}, u32[]{:S(2)}, u32[]{:S(2)}) collective-permute-start(f32[32,128]{1,0:T(8,128)S(1)} %constant_dynamic-update-slice_fusion.refs_0_), channel_id=1, source_target_pairs={{0,8},{1,9},{2,10},{3,11},{4,12},{5,13},{6,14},{7,15},{8,0},{9,1},... | collective-permute-start | bytes 49160 | tf_op jit(solution)/shard_map/ppermute | solution.py:389
  63.8 4.6 %collective-permute-start.14 = (f32[32,128]{1,0:T(8,128)S(1)}, f32[32,128]{1,0:T(8,128)S(1)}, u32[]{:S(2)}, u32[]{:S(2)}) collective-permute-start(f32[32,128]{1,0:T(8,128)S(1)} %constant_dynamic-update-slice_fusion.refs_0_), channel_id=1, source_target_pairs={{0,24},{1,25},{2,26},{3,27},{4,28},{5,29},{6,30},{7,31},{8,16},{9,... | collective-permute-start | bytes 49160 | tf_op jit(solution)/shard_map/ppermute | solution.py:389
  74.2 9.4 %collective-permute-start.15 = (bf16[128,1024]{1,0:T(8,128)(2,1)}, bf16[128,1024]{1,0:T(8,128)(2,1)S(1)}, u32[]{:S(2)}, u32[]{:S(2)}) collective-permute-start(bf16[128,1024]{1,0:T(8,128)(2,1)} %get-tuple-element.47), channel_id=1, source_target_pairs={{0,16},{1,17},{2,18},{3,19},{4,20},{5,21},{6,22},{7,23},{8,24},{9,... | collective-permute-start | bytes 786440 | tf_op jit(solution)/shard_map/ppermute | solution.py:389
  74.8 8.9 %collective-permute-start.16 = (bf16[128,1024]{1,0:T(8,128)(2,1)}, bf16[128,1024]{1,0:T(8,128)(2,1)S(1)}, u32[]{:S(2)}, u32[]{:S(2)}) collective-permute-start(bf16[128,1024]{1,0:T(8,128)(2,1)} %get-tuple-element.48), channel_id=1, source_target_pairs={{0,8},{1,9},{2,10},{3,11},{4,12},{5,13},{6,14},{7,15},{8,0},{9,1},... | collective-permute-start | bytes 786440 | tf_op jit(solution)/shard_map/ppermute | solution.py:389
  75.3 11.6 %collective-permute-start.17 = (bf16[128,1024]{1,0:T(8,128)(2,1)}, bf16[128,1024]{1,0:T(8,128)(2,1)S(1)}, u32[]{:S(2)}, u32[]{:S(2)}) collective-permute-start(bf16[128,1024]{1,0:T(8,128)(2,1)} %get-tuple-element.49), channel_id=1, source_target_pairs={{0,24},{1,25},{2,26},{3,27},{4,28},{5,29},{6,30},{7,31},{8,16},{9,... | collective-permute-start | bytes 786440 | tf_op jit(solution)/shard_map/ppermute | solution.py:389
  89.5 7.4 %collective-permute-start.18 = (bf16[64,1024]{1,0:T(8,128)(2,1)}, bf16[64,1024]{1,0:T(8,128)(2,1)S(1)}, u32[]{:S(2)}, u32[]{:S(2)}) collective-permute-start(bf16[64,1024]{1,0:T(8,128)(2,1)} %get-tuple-element.51), channel_id=1, source_target_pairs={{0,2},{1,3},{2,0},{3,1},{4,6},{5,7},{6,4},{7,5},{8,10},{9,11},{10,... | collective-permute-start | bytes 393224 | tf_op jit(solution)/shard_map/ppermute | solution.py:389
  (13 other events, 33.0 us)

commit v9 on v8

--- a/solution.py
+++ b/solution.py
@@ -49,9 +49,12 @@
 
 
 def conv_pool(vec, toep, acc, length, widths, filters, look, build):
+    ce = toep.shape[0] // (2 * SPAN)
+
     def tile(k, o, lhs):
         cols = slice((k * SPAN + o) * filters, (k * SPAN + o + 2) * filters)
-        return jnp.dot(lhs, toep[:, cols], preferred_element_type=f32)
+        depth = LANES if (o + k + 2) * ce <= LANES else 2 * LANES
+        return jnp.dot(lhs[:, 0:depth], toep[0:depth, cols], preferred_element_type=f32)
     acc[...] = jnp.full(acc.shape, -jnp.inf, f32)
     look(0)
     for b in range(-(-length // SPAN)):

time: 98.8 us -> 98.3 us (level)
  no operation moved by 1% of the time
where the time goes in v9:
time: 98.3 us; the launch traced here: 98 us
  Pallas kernels  43.6 us (44%)
  waiting for transfers between devices  24.7 us (25%)
  starting transfers between devices  22.9 us (23%)
  local copies, waits for them, and re-layouts  4.21 us (4%)
  other arithmetic  1.74 us (2%)
    ppermute x19, waiting for transfers between devices, swap(): return lax.ppermute(x, axes, [(i, i ^ bits) for i in range(devices)])  24.7 us
    ppermute x19, starting transfers between devices, swap(): return lax.ppermute(x, axes, [(i, i ^ bits) for i in range(devices)])  22.9 us
    pallas_call x2, Pallas kernels, embed(): pl.pallas_call(functools.partial(cnn_kernel, widths=widths, filters=filte...  22.7 us
    pallas_call x1, Pallas kernels, first_fold(): pl.pallas_call(functools.partial(first_kernel, nh=len(hid), metas=metas,...  9.5 us
    pallas_call x1, Pallas kernels, close(): pl.pallas_call(functools.partial(close_kernel, flips=flips, nw=len(words)...  5.18 us
    pallas_call x1, Pallas kernels, last_scores(): pl.pallas_call(functools.partial(last_kernel, nh=len(hid), metas=metas, g...  4.26 us
    unnamed x37, local copies, waits for them, and re-layouts  2.88 us
  transfers between devices with their start and end apart: 19, of which 11 were waited for; matrix products, arithmetic and copies ran while one was open for 2% of the time, Pallas kernels for 33%

profile of v9, /device:TPU:0, one launch (start us, length us, event | category | flops | bytes accessed | tf_op | source)
XLA Modules:
  0.0 98.0 jit_solution(4215918183566518385)
XLA Ops:
  0.6 4.1 %collective-permute-start.1 = (s32[1,64]{1,0:T(1,128)}, s32[1,64]{1,0:T(1,128)S(1)}, u32[]{:S(2)}, u32[]{:S(2)}) collective-permute-start(s32[1,64]{1,0:T(1,128)} %bitcast.27), channel_id=1, source_target_pairs={{0,2},{1,3},{2,0},{3,1},{4,6},{5,7},{6,4},{7,5},{8,10},{9,11},{10,... | collective-permute-start | bytes 776 | tf_op jit(solution)/shard_map/ppermute | solution.py:392
  4.8 11.3 %embed.3.refs_4_ = bf16[256,1024]{1,0:T(8,128)(2,1)} custom-call(s32[50,512]{1,0:T(8,128)} %bitcast.23, bf16[16,256]{1,0:T(8,128)(2,1)} %bitcast.25, bf16[112,896]{1,0:T(8,128)(2,1)} %conv_ref.3, f32[2,1024]{1,0:T(2,128)} %bias_ref.3, bf16[896,1024]{1,0:T(8,128)(2,1)} %proj_hbm.3, bf16[2,1024,1024]{2,1,0:T(8,128)(2,1)} %gate_hbm.3, ...), custom_call_target="tpu_custom_call" | custom-call | flops 8489271296 | bytes 12582912 | tf_op jit(solution)/shard_map/embed/pallas_call | solution.py:126
  16.4 1.8 %collective-permute-start.2 = (bf16[128,1152]{1,0:T(8,128)(2,1)S(1)}, bf16[128,1152]{1,0:T(8,128)(2,1)S(1)}, u32[]{:S(2)}, u32[]{:S(2)}) collective-permute-start(bf16[128,1152]{1,0:T(8,128)(2,1)S(1)} %fusion.1.refs_0_), channel_id=1, source_target_pairs={{0,16},{1,17},{2,18},{3,19},{4,20},{5,21},{6,22},{7,23},{8,24},{9,... | collective-permute-start | bytes 884744 | tf_op jit(solution)/shard_map/ppermute | solution.py:392
  18.3 1.5 %collective-permute-start.3 = (bf16[128,1152]{1,0:T(8,128)(2,1)S(1)}, bf16[128,1152]{1,0:T(8,128)(2,1)S(1)}, u32[]{:S(2)}, u32[]{:S(2)}) collective-permute-start(bf16[128,1152]{1,0:T(8,128)(2,1)S(1)} %fusion.1.refs_0_), channel_id=1, source_target_pairs={{0,8},{1,9},{2,10},{3,11},{4,12},{5,13},{6,14},{7,15},{8,0},{9,1},... | collective-permute-start | bytes 884744 | tf_op jit(solution)/shard_map/ppermute | solution.py:392
  20.0 1.8 %collective-permute-start.8 = (bf16[256,1024]{1,0:T(8,128)(2,1)}, bf16[256,1024]{1,0:T(8,128)(2,1)S(1)}, u32[]{:S(2)}, u32[]{:S(2)}) collective-permute-start(bf16[256,1024]{1,0:T(8,128)(2,1)} %embed.3.refs_4_), channel_id=1, source_target_pairs={{0,1},{1,0},{2,3},{3,2},{4,5},{5,4},{6,7},{7,6},{8,9},{9,8},{10,11... | collective-permute-start | bytes 1572872 | tf_op jit(solution)/shard_map/ppermute | solution.py:392
  21.8 11.4 %embed.2.refs_5_ = bf16[256,1024]{1,0:T(8,128)(2,1)} custom-call(s32[50,512]{1,0:T(8,128)} %bitcast.24, bf16[16,256]{1,0:T(8,128)(2,1)} %bitcast.26, bf16[112,896]{1,0:T(8,128)(2,1)} %conv_ref.3, f32[2,1024]{1,0:T(2,128)} %bias_ref.3, bf16[896,1024]{1,0:T(8,128)(2,1)} %proj_hbm.3, bf16[2,1024,1024]{2,1,0:T(8,128)(2,1)} %gate_hbm.3, ...), custom_call_target="tpu_custom_call" | custom-call | flops 8489271296 | bytes 12582912 | tf_op jit(solution)/shard_map/embed/pallas_call | solution.py:126
  35.2 1.8 %collective-permute-done.7.refs_7_ = bf16[256,1024]{1,0:T(8,128)(2,1)} collective-permute-done((bf16[256,1024]{1,0:T(8,128)(2,1)}, bf16[256,1024]{1,0:T(8,128)(2,1)}, u32[]{:S(2)}, u32[]{:S(2)}) %collective-permute-start.7) | collective-permute-done | bytes 524320 | tf_op jit(solution)/shard_map/ppermute | solution.py:392
  37.1 9.5 %first_fold.1 = (f32[512,1024]{1,0:T(8,128)}, bf16[512,1024]{1,0:T(8,128)(2,1)}, f32[512,128]{1,0:T(8,128)}) custom-call(s32[1]{0:T(128)} %bitcast.me_ref, bf16[128,1152]{1,0:T(8,128)(2,1)} %copy-done.2, bf16[128,1152]{1,0:T(8,128)(2,1)} %copy-done.3, bf16[128,1152]{1,0:T(8,128)(2,1)} %copy-done.4, bf16[128,1152]{1,0:T(8,128)(2,1)} %copy-done.5, ...), custom_call_target="tpu_custom_call" | custom-call | flops 4831838208 | bytes 4194304 | tf_op jit(solution)/shard_map/first_fold/pallas_call | solution.py:247
  46.6 1.9 %collective-permute-done.5.refs_4_ = bf16[256,1024]{1,0:T(8,128)(2,1)S(1)} collective-permute-done((bf16[256,1024]{1,0:T(8,128)(2,1)}, bf16[256,1024]{1,0:T(8,128)(2,1)S(1)}, u32[]{:S(2)}, u32[]{:S(2)}) %collective-permute-start.5) | collective-permute-done | bytes 524320 | tf_op jit(solution)/shard_map/ppermute | solution.py:392
  48.5 1.9 %collective-permute-done.10.refs_5_ = bf16[256,1024]{1,0:T(8,128)(2,1)S(1)} collective-permute-done((bf16[256,1024]{1,0:T(8,128)(2,1)S(1)}, bf16[256,1024]{1,0:T(8,128)(2,1)S(1)}, u32[]{:S(2)}, u32[]{:S(2)}) %collective-permute-start.10) | collective-permute-done | bytes 524320 | tf_op jit(solution)/shard_map/ppermute | solution.py:392
  51.2 4.3 %last_scores.1 = (bf16[512,512]{1,0:T(8,128)(2,1)}, bf16[512,512]{1,0:T(8,128)(2,1)}, f32[512,128]{1,0:T(8,128)}, f32[16,128]{1,0:T(8,128)}) custom-call(s32[1]{0:T(128)} %bitcast.me_ref, bf16[128,1152]{1,0:T(8,128)(2,1)} %copy-done.2, bf16[128,1152]{1,0:T(8,128)(2,1)} %copy-done.3, bf16[128,1152]{1,0:T(8,128)(2,1)} %copy-done.4, ...), custom_call_target="tpu_custom_call" | custom-call | flops 536870912 | bytes 2097152 | tf_op jit(solution)/shard_map/last_scores/pallas_call | solution.py:283
  55.5 2.6 %collective-permute-start.11 = (f32[16,128]{1,0:T(8,128)}, f32[16,128]{1,0:T(8,128)S(1)}, u32[]{:S(2)}, u32[]{:S(2)}) collective-permute-start(f32[16,128]{1,0:T(8,128)} %get-tuple-element.39), channel_id=1, source_target_pairs={{0,2},{1,3},{2,0},{3,1},{4,6},{5,7},{6,4},{7,5},{8,10},{9,11},{10,... | collective-permute-start | bytes 24584 | tf_op jit(solution)/shard_map/ppermute | solution.py:392
  60.3 1.5 %collective-permute-start.12 = (f32[32,128]{1,0:T(8,128)S(1)}, f32[32,128]{1,0:T(8,128)S(1)}, u32[]{:S(2)}, u32[]{:S(2)}) collective-permute-start(f32[32,128]{1,0:T(8,128)S(1)} %constant_dynamic-update-slice_fusion.refs_0_), channel_id=1, source_target_pairs={{0,16},{1,17},{2,18},{3,19},{4,20},{5,21},{6,22},{7,23},{8,24},{9,... | collective-permute-start | bytes 49160 | tf_op jit(solution)/shard_map/ppermute | solution.py:392
  61.8 1.5 %collective-permute-start.13 = (f32[32,128]{1,0:T(8,128)S(1)}, f32[32,128]{1,0:T(8,128)S(1)}, u32[]{:S(2)}, u32[]{:S(2)}) collective-permute-start(f32[32,128]{1,0:T(8,128)S(1)} %constant_dynamic-update-slice_fusion.refs_0_), channel_id=1, source_target_pairs={{0,8},{1,9},{2,10},{3,11},{4,12},{5,13},{6,14},{7,15},{8,0},{9,1},... | collective-permute-start | bytes 49160 | tf_op jit(solution)/shard_map/ppermute | solution.py:392
  64.0 1.5 %collective-permute-done.13.refs_2_ = f32[32,128]{1,0:T(8,128)S(1)} collective-permute-done((f32[32,128]{1,0:T(8,128)S(1)}, f32[32,128]{1,0:T(8,128)S(1)}, u32[]{:S(2)}, u32[]{:S(2)}) %collective-permute-start.13) | collective-permute-done | bytes 16416 | tf_op jit(solution)/shard_map/ppermute | solution.py:392
  65.5 2.4 %collective-permute-done.14.refs_3_ = f32[32,128]{1,0:T(8,128)S(1)} collective-permute-done((f32[32,128]{1,0:T(8,128)S(1)}, f32[32,128]{1,0:T(8,128)S(1)}, u32[]{:S(2)}, u32[]{:S(2)}) %collective-permute-start.14) | collective-permute-done | bytes 16416 | tf_op jit(solution)/shard_map/ppermute | solution.py:392
  68.5 5.2 %close.1 = (bf16[128,1024]{1,0:T(8,128)(2,1)}, bf16[128,1024]{1,0:T(8,128)(2,1)}, bf16[128,1024]{1,0:T(8,128)(2,1)}, bf16[128,1024]{1,0:T(8,128)(2,1)}, f32[1,128]{1,0:T(1,128)}) custom-call(f32[32,128]{1,0:T(8,128)} %copy-done.10, f32[32,128]{1,0:T(8,128)} %copy-done.11, f32[32,128]{1,0:T(8,128)} %copy-done.12, f32[32,128]{1,0:T(8,128)} %copy-done.13, ...), custom_call_target="tpu_custom_call" | custom-call | flops 1073741824 | bytes 4194304 | tf_op jit(solution)/shard_map/close/pallas_call | solution.py:339
  74.7 2.5 %collective-permute-start.17 = (bf16[128,1024]{1,0:T(8,128)(2,1)}, bf16[128,1024]{1,0:T(8,128)(2,1)S(1)}, u32[]{:S(2)}, u32[]{:S(2)}) collective-permute-start(bf16[128,1024]{1,0:T(8,128)(2,1)} %get-tuple-element.49), channel_id=1, source_target_pairs={{0,24},{1,25},{2,26},{3,27},{4,28},{5,29},{6,30},{7,31},{8,16},{9,... | collective-permute-start | bytes 786440 | tf_op jit(solution)/shard_map/ppermute | solution.py:392
  77.2 5.9 %collective-permute-done.15.refs_1_ = bf16[128,1024]{1,0:T(8,128)(2,1)S(1)} collective-permute-done((bf16[128,1024]{1,0:T(8,128)(2,1)}, bf16[128,1024]{1,0:T(8,128)(2,1)S(1)}, u32[]{:S(2)}, u32[]{:S(2)}) %collective-permute-start.15) | collective-permute-done | bytes 262176 | tf_op jit(solution)/shard_map/ppermute | solution.py:392
  83.1 3.2 %collective-permute-done.17.refs_3_ = bf16[128,1024]{1,0:T(8,128)(2,1)S(1)} collective-permute-done((bf16[128,1024]{1,0:T(8,128)(2,1)}, bf16[128,1024]{1,0:T(8,128)(2,1)S(1)}, u32[]{:S(2)}, u32[]{:S(2)}) %collective-permute-start.17) | collective-permute-done | bytes 262176 | tf_op jit(solution)/shard_map/ppermute | solution.py:392
  87.0 2.0 %add_four.1 = (bf16[64,1024]{1,0:T(8,128)(2,1)}, bf16[64,1024]{1,0:T(8,128)(2,1)}) custom-call(bf16[128,1024]{1,0:T(8,128)(2,1)} %get-tuple-element.46.refs_0_, bf16[128,1024]{1,0:T(8,128)(2,1)} %copy-done.6, bf16[128,1024]{1,0:T(8,128)(2,1)} %copy-done.7, bf16[128,1024]{1,0:T(8,128)(2,1)} %copy-done.8), custom_call_target="tpu_custom_call" | custom-call | flops 524288 | bytes 1310720 | tf_op jit(solution)/shard_map/add_four/pallas_call | solution.py:379
  89.0 2.6 %collective-permute-start.18 = (bf16[64,1024]{1,0:T(8,128)(2,1)}, bf16[64,1024]{1,0:T(8,128)(2,1)S(1)}, u32[]{:S(2)}, u32[]{:S(2)}) collective-permute-start(bf16[64,1024]{1,0:T(8,128)(2,1)} %get-tuple-element.51), channel_id=1, source_target_pairs={{0,2},{1,3},{2,0},{3,1},{4,6},{5,7},{6,4},{7,5},{8,10},{9,11},{10,... | collective-permute-start | bytes 393224 | tf_op jit(solution)/shard_map/ppermute | solution.py:392
  92.8 3.7 %collective-permute-done.18 = bf16[64,1024]{1,0:T(8,128)(2,1)S(1)} collective-permute-done((bf16[64,1024]{1,0:T(8,128)(2,1)}, bf16[64,1024]{1,0:T(8,128)(2,1)S(1)}, u32[]{:S(2)}, u32[]{:S(2)}) %collective-permute-start.18) | collective-permute-done | bytes 131104 | tf_op jit(solution)/shard_map/ppermute | solution.py:392
  96.4 1.6 %add_convert_fusion = bf16[64,1024]{1,0:T(8,128)(2,1)} fusion(bf16[64,1024]{1,0:T(8,128)(2,1)S(1)} %collective-permute-done.18, bf16[64,1024]{1,0:T(8,128)(2,1)} %get-tuple-element.50), kind=kLoop, calls=%fused_computation.4 | loop fusion | flops 262144 | bytes 393216 | tf_op jit(solution)/shard_map/convert_element_type | solution.py:348
  (66 shorter events, 9.8 us)
Async XLA Ops:
  0.6 15.5 %collective-permute-start.1 = (s32[1,64]{1,0:T(1,128)}, s32[1,64]{1,0:T(1,128)S(1)}, u32[]{:S(2)}, u32[]{:S(2)}) collective-permute-start(s32[1,64]{1,0:T(1,128)} %bitcast.27), channel_id=1, source_target_pairs={{0,2},{1,3},{2,0},{3,1},{4,6},{5,7},{6,4},{7,5},{8,10},{9,11},{10,... | collective-permute-start | bytes 776 | tf_op jit(solution)/shard_map/ppermute | solution.py:392
  4.7 11.5 %collective-permute-start = (bf16[64,1024]{1,0:T(8,128)(2,1)}, bf16[64,1024]{1,0:T(8,128)(2,1)S(1)}, u32[]{:S(2)}, u32[]{:S(2)}) collective-permute-start(bf16[64,1024]{1,0:T(8,128)(2,1)} %param.16), channel_id=1, source_target_pairs={{0,2},{1,3},{2,0},{3,1},{4,6},{5,7},{6,4},{7,5},{8,10},{9,11},{10,... | collective-permute-start | bytes 393224 | tf_op jit(solution)/shard_map/ppermute | solution.py:392
  4.8 11.3 %copy-start.17 = (s32[64]{0:T(128)S(1)}, s32[64]{0:T(128)}, u32[]{:S(2)}) copy-start(s32[64]{0:T(128)} %param.17) | copy-start | bytes 772
  4.8 11.4 %copy-start.9 = (bf16[64,1024]{1,0:T(8,128)(2,1)S(1)}, bf16[64,1024]{1,0:T(8,128)(2,1)}, u32[]{:S(2)}) copy-start(bf16[64,1024]{1,0:T(8,128)(2,1)} %param.16) | copy-start | bytes 393220
  16.4 16.8 %copy-start.2 = (bf16[128,1152]{1,0:T(8,128)(2,1)}, bf16[128,1152]{1,0:T(8,128)(2,1)S(1)}, u32[]{:S(2)}) copy-start(bf16[128,1152]{1,0:T(8,128)(2,1)S(1)} %fusion.1.refs_0_) | copy-start | bytes 884740
  16.4 16.8 %copy-start.14 = (bf16[256,1024]{1,0:T(8,128)(2,1)S(1)}, bf16[256,1024]{1,0:T(8,128)(2,1)}, u32[]{:S(2)}) copy-start(bf16[256,1024]{1,0:T(8,128)(2,1)} %embed.3.refs_4_) | copy-start | bytes 1572868
  16.4 16.9 %collective-permute-start.2 = (bf16[128,1152]{1,0:T(8,128)(2,1)S(1)}, bf16[128,1152]{1,0:T(8,128)(2,1)S(1)}, u32[]{:S(2)}, u32[]{:S(2)}) collective-permute-start(bf16[128,1152]{1,0:T(8,128)(2,1)S(1)} %fusion.1.refs_0_), channel_id=1, source_target_pairs={{0,16},{1,17},{2,18},{3,19},{4,20},{5,21},{6,22},{7,23},{8,24},{9,... | collective-permute-start | bytes 884744 | tf_op jit(solution)/shard_map/ppermute | solution.py:392
  18.3 15.1 %collective-permute-start.3 = (bf16[128,1152]{1,0:T(8,128)(2,1)S(1)}, bf16[128,1152]{1,0:T(8,128)(2,1)S(1)}, u32[]{:S(2)}, u32[]{:S(2)}) collective-permute-start(bf16[128,1152]{1,0:T(8,128)(2,1)S(1)} %fusion.1.refs_0_), channel_id=1, source_target_pairs={{0,8},{1,9},{2,10},{3,11},{4,12},{5,13},{6,14},{7,15},{8,0},{9,1},... | collective-permute-start | bytes 884744 | tf_op jit(solution)/shard_map/ppermute | solution.py:392
  19.8 13.6 %collective-permute-start.4 = (bf16[128,1152]{1,0:T(8,128)(2,1)S(1)}, bf16[128,1152]{1,0:T(8,128)(2,1)S(1)}, u32[]{:S(2)}, u32[]{:S(2)}) collective-permute-start(bf16[128,1152]{1,0:T(8,128)(2,1)S(1)} %fusion.1.refs_0_), channel_id=1, source_target_pairs={{0,24},{1,25},{2,26},{3,27},{4,28},{5,29},{6,30},{7,31},{8,16},{9,... | collective-permute-start | bytes 884744 | tf_op jit(solution)/shard_map/ppermute | solution.py:392
  20.0 14.0 %collective-permute-start.8 = (bf16[256,1024]{1,0:T(8,128)(2,1)}, bf16[256,1024]{1,0:T(8,128)(2,1)S(1)}, u32[]{:S(2)}, u32[]{:S(2)}) collective-permute-start(bf16[256,1024]{1,0:T(8,128)(2,1)} %embed.3.refs_4_), channel_id=1, source_target_pairs={{0,1},{1,0},{2,3},{3,2},{4,5},{5,4},{6,7},{7,6},{8,9},{9,8},{10,11... | collective-permute-start | bytes 1572872 | tf_op jit(solution)/shard_map/ppermute | solution.py:392
  33.3 2.0 %collective-permute-start.6 = (bf16[256,1024]{1,0:T(8,128)(2,1)S(1)}, bf16[256,1024]{1,0:T(8,128)(2,1)S(1)}, u32[]{:S(2)}, u32[]{:S(2)}) collective-permute-start(bf16[256,1024]{1,0:T(8,128)(2,1)S(1)} %copy-done.14), channel_id=1, source_target_pairs={{0,4},{1,5},{2,6},{3,7},{4,0},{5,1},{6,2},{7,3},{8,12},{9,13},{10,... | collective-permute-start | bytes 1572872 | tf_op jit(solution)/shard_map/ppermute | solution.py:392
  33.4 3.7 %collective-permute-start.7 = (bf16[256,1024]{1,0:T(8,128)(2,1)}, bf16[256,1024]{1,0:T(8,128)(2,1)}, u32[]{:S(2)}, u32[]{:S(2)}) collective-permute-start(bf16[256,1024]{1,0:T(8,128)(2,1)} %embed.2.refs_5_), channel_id=1, source_target_pairs={{0,4},{1,5},{2,6},{3,7},{4,0},{5,1},{6,2},{7,3},{8,12},{9,13},{10,... | collective-permute-start | bytes 1572872 | tf_op jit(solution)/shard_map/ppermute | solution.py:392
  33.9 3.1 %collective-permute-start.9 = (bf16[256,1024]{1,0:T(8,128)(2,1)S(1)}, bf16[256,1024]{1,0:T(8,128)(2,1)}, u32[]{:S(2)}, u32[]{:S(2)}) collective-permute-start(bf16[256,1024]{1,0:T(8,128)(2,1)S(1)} %collective-permute-done.8.refs_8_), channel_id=1, source_target_pairs={{0,4},{1,5},{2,6},{3,7},{4,0},{5,1},{6,2},{7,3},{8,12},{9,13},{10,... | collective-permute-start | bytes 1572872 | tf_op jit(solution)/shard_map/ppermute | solution.py:392
  34.0 14.5 %collective-permute-start.5 = (bf16[256,1024]{1,0:T(8,128)(2,1)}, bf16[256,1024]{1,0:T(8,128)(2,1)S(1)}, u32[]{:S(2)}, u32[]{:S(2)}) collective-permute-start(bf16[256,1024]{1,0:T(8,128)(2,1)} %embed.2.refs_5_), channel_id=1, source_target_pairs={{0,1},{1,0},{2,3},{3,2},{4,5},{5,4},{6,7},{7,6},{8,9},{9,8},{10,11... | collective-permute-start | bytes 1572872 | tf_op jit(solution)/shard_map/ppermute | solution.py:392
  48.5 1.9 %collective-permute-start.10 = (bf16[256,1024]{1,0:T(8,128)(2,1)S(1)}, bf16[256,1024]{1,0:T(8,128)(2,1)S(1)}, u32[]{:S(2)}, u32[]{:S(2)}) collective-permute-start(bf16[256,1024]{1,0:T(8,128)(2,1)S(1)} %collective-permute-done.5.refs_4_), channel_id=1, source_target_pairs={{0,4},{1,5},{2,6},{3,7},{4,0},{5,1},{6,2},{7,3},{8,12},{9,13},{10,... | collective-permute-start | bytes 1572872 | tf_op jit(solution)/shard_map/ppermute | solution.py:392
  55.5 4.8 %collective-permute-start.11 = (f32[16,128]{1,0:T(8,128)}, f32[16,128]{1,0:T(8,128)S(1)}, u32[]{:S(2)}, u32[]{:S(2)}) collective-permute-start(f32[16,128]{1,0:T(8,128)} %get-tuple-element.39), channel_id=1, source_target_pairs={{0,2},{1,3},{2,0},{3,1},{4,6},{5,7},{6,4},{7,5},{8,10},{9,11},{10,... | collective-permute-start | bytes 24584 | tf_op jit(solution)/shard_map/ppermute | solution.py:392
  60.3 7.7 %copy-start.10 = (f32[32,128]{1,0:T(8,128)}, f32[32,128]{1,0:T(8,128)S(1)}, u32[]{:S(2)}) copy-start(f32[32,128]{1,0:T(8,128)S(1)} %constant_dynamic-update-slice_fusion.refs_0_) | copy-start | bytes 49156
  60.3 3.7 %collective-permute-start.12 = (f32[32,128]{1,0:T(8,128)S(1)}, f32[32,128]{1,0:T(8,128)S(1)}, u32[]{:S(2)}, u32[]{:S(2)}) collective-permute-start(f32[32,128]{1,0:T(8,128)S(1)} %constant_dynamic-update-slice_fusion.refs_0_), channel_id=1, source_target_pairs={{0,16},{1,17},{2,18},{3,19},{4,20},{5,21},{6,22},{7,23},{8,24},{9,... | collective-permute-start | bytes 49160 | tf_op jit(solution)/shard_map/ppermute | solution.py:392
  61.8 3.7 %collective-permute-start.13 = (f32[32,128]{1,0:T(8,128)S(1)}, f32[32,128]{1,0:T(8,128)S(1)}, u32[]{:S(2)}, u32[]{:S(2)}) collective-permute-start(f32[32,128]{1,0:T(8,128)S(1)} %constant_dynamic-update-slice_fusion.refs_0_), channel_id=1, source_target_pairs={{0,8},{1,9},{2,10},{3,11},{4,12},{5,13},{6,14},{7,15},{8,0},{9,1},... | collective-permute-start | bytes 49160 | tf_op jit(solution)/shard_map/ppermute | solution.py:392
  63.3 4.6 %collective-permute-start.14 = (f32[32,128]{1,0:T(8,128)S(1)}, f32[32,128]{1,0:T(8,128)S(1)}, u32[]{:S(2)}, u32[]{:S(2)}) collective-permute-start(f32[32,128]{1,0:T(8,128)S(1)} %constant_dynamic-update-slice_fusion.refs_0_), channel_id=1, source_target_pairs={{0,24},{1,25},{2,26},{3,27},{4,28},{5,29},{6,30},{7,31},{8,16},{9,... | collective-permute-start | bytes 49160 | tf_op jit(solution)/shard_map/ppermute | solution.py:392
  73.7 9.4 %collective-permute-start.15 = (bf16[128,1024]{1,0:T(8,128)(2,1)}, bf16[128,1024]{1,0:T(8,128)(2,1)S(1)}, u32[]{:S(2)}, u32[]{:S(2)}) collective-permute-start(bf16[128,1024]{1,0:T(8,128)(2,1)} %get-tuple-element.47), channel_id=1, source_target_pairs={{0,16},{1,17},{2,18},{3,19},{4,20},{5,21},{6,22},{7,23},{8,24},{9,... | collective-permute-start | bytes 786440 | tf_op jit(solution)/shard_map/ppermute | solution.py:392
  74.2 8.9 %collective-permute-start.16 = (bf16[128,1024]{1,0:T(8,128)(2,1)}, bf16[128,1024]{1,0:T(8,128)(2,1)S(1)}, u32[]{:S(2)}, u32[]{:S(2)}) collective-permute-start(bf16[128,1024]{1,0:T(8,128)(2,1)} %get-tuple-element.48), channel_id=1, source_target_pairs={{0,8},{1,9},{2,10},{3,11},{4,12},{5,13},{6,14},{7,15},{8,0},{9,1},... | collective-permute-start | bytes 786440 | tf_op jit(solution)/shard_map/ppermute | solution.py:392
  74.7 11.6 %collective-permute-start.17 = (bf16[128,1024]{1,0:T(8,128)(2,1)}, bf16[128,1024]{1,0:T(8,128)(2,1)S(1)}, u32[]{:S(2)}, u32[]{:S(2)}) collective-permute-start(bf16[128,1024]{1,0:T(8,128)(2,1)} %get-tuple-element.49), channel_id=1, source_target_pairs={{0,24},{1,25},{2,26},{3,27},{4,28},{5,29},{6,30},{7,31},{8,16},{9,... | collective-permute-start | bytes 786440 | tf_op jit(solution)/shard_map/ppermute | solution.py:392
  89.0 7.4 %collective-permute-start.18 = (bf16[64,1024]{1,0:T(8,128)(2,1)}, bf16[64,1024]{1,0:T(8,128)(2,1)S(1)}, u32[]{:S(2)}, u32[]{:S(2)}) collective-permute-start(bf16[64,1024]{1,0:T(8,128)(2,1)} %get-tuple-element.51), channel_id=1, source_target_pairs={{0,2},{1,3},{2,0},{3,1},{4,6},{5,7},{6,4},{7,5},{8,10},{9,11},{10,... | collective-permute-start | bytes 393224 | tf_op jit(solution)/shard_map/ppermute | solution.py:392
  (13 other events, 33.0 us)

commit v10 on v9

--- a/solution.py
+++ b/solution.py
@@ -294,18 +294,17 @@
 
 def close_kernel(*refs, flips, nw):
     nl = len(flips)
-    lines, words, rest = refs[:4], refs[4:4 + nw], refs[4 + nw:]
+    lines, words, rest = refs[:nl], refs[nl:nl + nw], refs[nl + nw:]
     prob, hot, one, before, stats, facts = rest[:6]
     parts, loss = rest[6:10], rest[10]
-    size = lines[0].shape[0] * 4 // nl
     count, model = one.shape
     per = count // LANES
     quarter = count // 4
 
     def line(j, i, kind):
         over, halves = flips[j]
-        at = j % (nl // 4) * size + kind * per + (i ^ over)
-        v = lines[j // (nl // 4)][at:at + 1, :]
+        at = kind * per + (i ^ over)
+        v = lines[j][at:at + 1, :]
         return pltpu.roll(v, LANES // 2, axis=1) if halves else v
 
     scales = []
@@ -324,8 +323,7 @@
     for n in range(0, model, 256):
         cols = slice(n, n + 256)
         mu = jnp.concatenate([
-            sum(ref[at + 2 * per + m // LANES:at + 2 * per + m // LANES + 1, :]
-                for ref in lines for at in range(0, ref.shape[0], size)) * (1.0 / nl)
+            sum(ref[2 * per + m // LANES:2 * per + m // LANES + 1, :] for ref in lines) * (1.0 / nl)
             for m in range(n, n + 256, LANES)], axis=1)
         goal = product(hot, words, n, 256) + before[:, cols].astype(f32)
         mix = (c1 * one[:, cols] + c2 * product(prob, words, n, 256) + (c3 * mu - goal)).astype(bf16)
@@ -435,12 +433,12 @@
     words, metas = [w for w, _ in late], tuple(m for _, m in late)
     prob, hot, facts, line = last_scores(
         me, hid, words, metas, (0, core, near, core | near), local, stats)
-    lines, others = line, [0]
+    lines, others = [line], [0]
     for bit in rest:
-        lines = jnp.concatenate([lines, swap(lines, bit)], axis=0)
+        lines += [swap(v, bit) for v in lines]
         others += [o | bit for o in others]
     plane = (bit_b, bit_a, bit_a | bit_b)
-    lines = [lines] + [swap(lines, o) for o in plane]
+    lines += [swap(v, o) for o in plane for v in lines]
     others = [o | p for p in (0,) + plane for o in others]
     order = rest + [bit_b, bit_a]
     flips = tuple((sum(1 << (j - 1) for j, b in enumerate(order) if j and o & b), bool(o & rest[0])) for o in others)

time: 98.3 us -> 99.4 us (1.011)
  starting transfers between devices: 22.9 us -> 25 us
    ppermute x19 -> x22, starting transfers between devices: 22.9 us -> 25 us  [swap(): return lax.ppermute(x, axes, [(i, i ^ bits) for i in range(devices)])]
    unnamed x37 -> x42, local copies, waits for them, and re-layouts: 2.88 us -> 2.14 us
    ppermute x19 -> x22, waiting for transfers between devices: 24.7 us -> 24.5 us  [swap(): return lax.ppermute(x, axes, [(i, i ^ bits) for i in range(devices)])]
  transfers between devices with their start and end apart: 19 -> 22, of which waited for: 11 -> 10; matrix products, arithmetic and copies ran while one was open for 2% -> 1% of each run, Pallas kernels for 33% -> 32%
where the time goes in v10:
time: 99.4 us; the launch traced here: 99.2 us
  Pallas kernels  43.6 us (44%)
  starting transfers between devices  25 us (25%)
  waiting for transfers between devices  24.5 us (25%)
  local copies, waits for them, and re-layouts  3.44 us (3%)
  other arithmetic  1.74 us (2%)
    ppermute x22, starting transfers between devices, swap(): return lax.ppermute(x, axes, [(i, i ^ bits) for i in range(devices)])  25 us
    ppermute x22, waiting for transfers between devices, swap(): return lax.ppermute(x, axes, [(i, i ^ bits) for i in range(devices)])  24.5 us
    pallas_call x2, Pallas kernels, embed(): pl.pallas_call(functools.partial(cnn_kernel, widths=widths, filters=filte...  22.7 us
    pallas_call x1, Pallas kernels, first_fold(): pl.pallas_call(functools.partial(first_kernel, nh=len(hid), metas=metas,...  9.53 us
    pallas_call x1, Pallas kernels, close(): pl.pallas_call(functools.partial(close_kernel, flips=flips, nw=len(words)...  5.23 us
    pallas_call x1, Pallas kernels, last_scores(): pl.pallas_call(functools.partial(last_kernel, nh=len(hid), metas=metas, g...  4.25 us
    unnamed x42, local copies, waits for them, and re-layouts  2.14 us
  transfers between devices with their start and end apart: 22, of which 10 were waited for; matrix products, arithmetic and copies ran while one was open for 1% of the time, Pallas kernels for 32%

profile of v10, /device:TPU:0, one launch (start us, length us, event | category | flops | bytes accessed | tf_op | source)
XLA Modules:
  0.0 99.2 jit_solution(3379713891048107027)
XLA Ops:
  0.6 4.1 %collective-permute-start.1 = (s32[1,64]{1,0:T(1,128)}, s32[1,64]{1,0:T(1,128)S(1)}, u32[]{:S(2)}, u32[]{:S(2)}) collective-permute-start(s32[1,64]{1,0:T(1,128)} %bitcast.27), channel_id=1, source_target_pairs={{0,2},{1,3},{2,0},{3,1},{4,6},{5,7},{6,4},{7,5},{8,10},{9,11},{10,... | collective-permute-start | bytes 776 | tf_op jit(solution)/shard_map/ppermute | solution.py:390
  4.8 11.3 %embed.3.refs_4_ = bf16[256,1024]{1,0:T(8,128)(2,1)} custom-call(s32[50,512]{1,0:T(8,128)} %bitcast.23, bf16[16,256]{1,0:T(8,128)(2,1)} %bitcast.25, bf16[112,896]{1,0:T(8,128)(2,1)} %conv_ref.3, f32[2,1024]{1,0:T(2,128)} %bias_ref.3, bf16[896,1024]{1,0:T(8,128)(2,1)} %proj_hbm.3, bf16[2,1024,1024]{2,1,0:T(8,128)(2,1)} %gate_hbm.3, ...), custom_call_target="tpu_custom_call" | custom-call | flops 8489271296 | bytes 12582912 | tf_op jit(solution)/shard_map/embed/pallas_call | solution.py:126
  16.4 1.8 %collective-permute-start.2 = (bf16[128,1152]{1,0:T(8,128)(2,1)S(1)}, bf16[128,1152]{1,0:T(8,128)(2,1)S(1)}, u32[]{:S(2)}, u32[]{:S(2)}) collective-permute-start(bf16[128,1152]{1,0:T(8,128)(2,1)S(1)} %fusion.1.refs_0_), channel_id=1, source_target_pairs={{0,16},{1,17},{2,18},{3,19},{4,20},{5,21},{6,22},{7,23},{8,24},{9,... | collective-permute-start | bytes 884744 | tf_op jit(solution)/shard_map/ppermute | solution.py:390
  18.3 1.5 %collective-permute-start.3 = (bf16[128,1152]{1,0:T(8,128)(2,1)S(1)}, bf16[128,1152]{1,0:T(8,128)(2,1)S(1)}, u32[]{:S(2)}, u32[]{:S(2)}) collective-permute-start(bf16[128,1152]{1,0:T(8,128)(2,1)S(1)} %fusion.1.refs_0_), channel_id=1, source_target_pairs={{0,8},{1,9},{2,10},{3,11},{4,12},{5,13},{6,14},{7,15},{8,0},{9,1},... | collective-permute-start | bytes 884744 | tf_op jit(solution)/shard_map/ppermute | solution.py:390
  20.0 1.8 %collective-permute-start.8 = (bf16[256,1024]{1,0:T(8,128)(2,1)}, bf16[256,1024]{1,0:T(8,128)(2,1)S(1)}, u32[]{:S(2)}, u32[]{:S(2)}) collective-permute-start(bf16[256,1024]{1,0:T(8,128)(2,1)} %embed.3.refs_4_), channel_id=1, source_target_pairs={{0,1},{1,0},{2,3},{3,2},{4,5},{5,4},{6,7},{7,6},{8,9},{9,8},{10,11... | collective-permute-start | bytes 1572872 | tf_op jit(solution)/shard_map/ppermute | solution.py:390
  21.8 11.4 %embed.2.refs_5_ = bf16[256,1024]{1,0:T(8,128)(2,1)} custom-call(s32[50,512]{1,0:T(8,128)} %bitcast.24, bf16[16,256]{1,0:T(8,128)(2,1)} %bitcast.26, bf16[112,896]{1,0:T(8,128)(2,1)} %conv_ref.3, f32[2,1024]{1,0:T(2,128)} %bias_ref.3, bf16[896,1024]{1,0:T(8,128)(2,1)} %proj_hbm.3, bf16[2,1024,1024]{2,1,0:T(8,128)(2,1)} %gate_hbm.3, ...), custom_call_target="tpu_custom_call" | custom-call | flops 8489271296 | bytes 12582912 | tf_op jit(solution)/shard_map/embed/pallas_call | solution.py:126
  35.2 1.8 %collective-permute-done.7.refs_7_ = bf16[256,1024]{1,0:T(8,128)(2,1)} collective-permute-done((bf16[256,1024]{1,0:T(8,128)(2,1)}, bf16[256,1024]{1,0:T(8,128)(2,1)}, u32[]{:S(2)}, u32[]{:S(2)}) %collective-permute-start.7) | collective-permute-done | bytes 524320 | tf_op jit(solution)/shard_map/ppermute | solution.py:390
  37.1 9.5 %first_fold.1 = (f32[512,1024]{1,0:T(8,128)}, bf16[512,1024]{1,0:T(8,128)(2,1)}, f32[512,128]{1,0:T(8,128)}) custom-call(s32[1]{0:T(128)} %bitcast.me_ref, bf16[128,1152]{1,0:T(8,128)(2,1)} %copy-done.2, bf16[128,1152]{1,0:T(8,128)(2,1)} %copy-done.3, bf16[128,1152]{1,0:T(8,128)(2,1)} %copy-done.4, bf16[128,1152]{1,0:T(8,128)(2,1)} %copy-done.5, ...), custom_call_target="tpu_custom_call" | custom-call | flops 4831838208 | bytes 4194304 | tf_op jit(solution)/shard_map/first_fold/pallas_call | solution.py:247
  46.6 1.9 %collective-permute-done.5.refs_4_.refs_8_ = bf16[256,1024]{1,0:T(8,128)(2,1)S(1)} collective-permute-done((bf16[256,1024]{1,0:T(8,128)(2,1)}, bf16[256,1024]{1,0:T(8,128)(2,1)S(1)}, u32[]{:S(2)}, u32[]{:S(2)}) %collective-permute-start.5) | collective-permute-done | bytes 524320 | tf_op jit(solution)/shard_map/ppermute | solution.py:390
  48.5 1.9 %collective-permute-done.10.refs_5_.refs_9_ = bf16[256,1024]{1,0:T(8,128)(2,1)S(1)} collective-permute-done((bf16[256,1024]{1,0:T(8,128)(2,1)S(1)}, bf16[256,1024]{1,0:T(8,128)(2,1)S(1)}, u32[]{:S(2)}, u32[]{:S(2)}) %collective-permute-start.10) | collective-permute-done | bytes 524320 | tf_op jit(solution)/shard_map/ppermute | solution.py:390
  51.2 4.3 %last_scores.1 = (bf16[512,512]{1,0:T(8,128)(2,1)}, bf16[512,512]{1,0:T(8,128)(2,1)}, f32[512,128]{1,0:T(8,128)}, f32[16,128]{1,0:T(8,128)}) custom-call(s32[1]{0:T(128)} %bitcast.me_ref, bf16[128,1152]{1,0:T(8,128)(2,1)} %copy-done.2, bf16[128,1152]{1,0:T(8,128)(2,1)} %copy-done.3, bf16[128,1152]{1,0:T(8,128)(2,1)} %copy-done.4, ...), custom_call_target="tpu_custom_call" | custom-call | flops 536870912 | bytes 2097152 | tf_op jit(solution)/shard_map/last_scores/pallas_call | solution.py:283
  55.5 2.6 %collective-permute-start.11 = (f32[16,128]{1,0:T(8,128)}, f32[16,128]{1,0:T(8,128)S(1)}, u32[]{:S(2)}, u32[]{:S(2)}) collective-permute-start(f32[16,128]{1,0:T(8,128)} %get-tuple-element.39.refs_0_), channel_id=1, source_target_pairs={{0,2},{1,3},{2,0},{3,1},{4,6},{5,7},{6,4},{7,5},{8,10},{9,11},{10,... | collective-permute-start | bytes 24584 | tf_op jit(solution)/shard_map/ppermute | solution.py:390
  58.1 1.5 %collective-permute-start.12 = (f32[16,128]{1,0:T(8,128)}, f32[16,128]{1,0:T(8,128)S(1)}, u32[]{:S(2)}, u32[]{:S(2)}) collective-permute-start(f32[16,128]{1,0:T(8,128)} %get-tuple-element.39.refs_0_), channel_id=1, source_target_pairs={{0,16},{1,17},{2,18},{3,19},{4,20},{5,21},{6,22},{7,23},{8,24},{9,... | collective-permute-start | bytes 24584 | tf_op jit(solution)/shard_map/ppermute | solution.py:390
  59.6 1.5 %collective-permute-start.14 = (f32[16,128]{1,0:T(8,128)}, f32[16,128]{1,0:T(8,128)S(1)}, u32[]{:S(2)}, u32[]{:S(2)}) collective-permute-start(f32[16,128]{1,0:T(8,128)} %get-tuple-element.39.refs_0_), channel_id=1, source_target_pairs={{0,8},{1,9},{2,10},{3,11},{4,12},{5,13},{6,14},{7,15},{8,0},{9,1},... | collective-permute-start | bytes 24584 | tf_op jit(solution)/shard_map/ppermute | solution.py:390
  61.6 1.5 %collective-permute-start.13 = (f32[16,128]{1,0:T(8,128)S(1)}, f32[16,128]{1,0:T(8,128)S(1)}, u32[]{:S(2)}, u32[]{:S(2)}) collective-permute-start(f32[16,128]{1,0:T(8,128)S(1)} %collective-permute-done.11.refs_1_), channel_id=1, source_target_pairs={{0,16},{1,17},{2,18},{3,19},{4,20},{5,21},{6,22},{7,23},{8,24},{9,... | collective-permute-start | bytes 24584 | tf_op jit(solution)/shard_map/ppermute | solution.py:390
  63.1 1.5 %collective-permute-start.15 = (f32[16,128]{1,0:T(8,128)S(1)}, f32[16,128]{1,0:T(8,128)S(1)}, u32[]{:S(2)}, u32[]{:S(2)}) collective-permute-start(f32[16,128]{1,0:T(8,128)S(1)} %collective-permute-done.11.refs_1_), channel_id=1, source_target_pairs={{0,8},{1,9},{2,10},{3,11},{4,12},{5,13},{6,14},{7,15},{8,0},{9,1},... | collective-permute-start | bytes 24584 | tf_op jit(solution)/shard_map/ppermute | solution.py:390
  66.7 2.4 %collective-permute-done.17.refs_7_ = f32[16,128]{1,0:T(8,128)S(1)} collective-permute-done((f32[16,128]{1,0:T(8,128)S(1)}, f32[16,128]{1,0:T(8,128)S(1)}, u32[]{:S(2)}, u32[]{:S(2)}) %collective-permute-start.17) | collective-permute-done | bytes 8224 | tf_op jit(solution)/shard_map/ppermute | solution.py:390
  69.8 5.2 %close.1 = (bf16[128,1024]{1,0:T(8,128)(2,1)}, bf16[128,1024]{1,0:T(8,128)(2,1)}, bf16[128,1024]{1,0:T(8,128)(2,1)}, bf16[128,1024]{1,0:T(8,128)(2,1)}, f32[1,128]{1,0:T(1,128)}) custom-call(f32[16,128]{1,0:T(8,128)} %get-tuple-element.39.refs_0_, f32[16,128]{1,0:T(8,128)} %copy-done.10, f32[16,128]{1,0:T(8,128)} %copy-done.11, f32[16,128]{1,0:T(8,128)} %copy-done.14, ...), custom_call_target="tpu_custom_call" | custom-call | flops 1073741824 | bytes 4194304 | tf_op jit(solution)/shard_map/close/pallas_call | solution.py:337
  76.0 2.5 %collective-permute-start.20 = (bf16[128,1024]{1,0:T(8,128)(2,1)}, bf16[128,1024]{1,0:T(8,128)(2,1)S(1)}, u32[]{:S(2)}, u32[]{:S(2)}) collective-permute-start(bf16[128,1024]{1,0:T(8,128)(2,1)} %get-tuple-element.49), channel_id=1, source_target_pairs={{0,24},{1,25},{2,26},{3,27},{4,28},{5,29},{6,30},{7,31},{8,16},{9,... | collective-permute-start | bytes 786440 | tf_op jit(solution)/shard_map/ppermute | solution.py:390
  78.5 5.9 %collective-permute-done.18.refs_1_ = bf16[128,1024]{1,0:T(8,128)(2,1)S(1)} collective-permute-done((bf16[128,1024]{1,0:T(8,128)(2,1)}, bf16[128,1024]{1,0:T(8,128)(2,1)S(1)}, u32[]{:S(2)}, u32[]{:S(2)}) %collective-permute-start.18) | collective-permute-done | bytes 262176 | tf_op jit(solution)/shard_map/ppermute | solution.py:390
  84.4 3.2 %collective-permute-done.20.refs_3_ = bf16[128,1024]{1,0:T(8,128)(2,1)S(1)} collective-permute-done((bf16[128,1024]{1,0:T(8,128)(2,1)}, bf16[128,1024]{1,0:T(8,128)(2,1)S(1)}, u32[]{:S(2)}, u32[]{:S(2)}) %collective-permute-start.20) | collective-permute-done | bytes 262176 | tf_op jit(solution)/shard_map/ppermute | solution.py:390
  88.3 2.0 %add_four.1 = (bf16[64,1024]{1,0:T(8,128)(2,1)}, bf16[64,1024]{1,0:T(8,128)(2,1)}) custom-call(bf16[128,1024]{1,0:T(8,128)(2,1)} %get-tuple-element.46.refs_0_, bf16[128,1024]{1,0:T(8,128)(2,1)} %copy-done.6, bf16[128,1024]{1,0:T(8,128)(2,1)} %copy-done.7, bf16[128,1024]{1,0:T(8,128)(2,1)} %copy-done.8), custom_call_target="tpu_custom_call" | custom-call | flops 524288 | bytes 1310720 | tf_op jit(solution)/shard_map/add_four/pallas_call | solution.py:377
  92.7 4.9 %collective-permute-done.21 = bf16[64,1024]{1,0:T(8,128)(2,1)S(1)} collective-permute-done((bf16[64,1024]{1,0:T(8,128)(2,1)}, bf16[64,1024]{1,0:T(8,128)(2,1)S(1)}, u32[]{:S(2)}, u32[]{:S(2)}) %collective-permute-start.21) | collective-permute-done | bytes 131104 | tf_op jit(solution)/shard_map/ppermute | solution.py:390
  97.6 1.6 %add_convert_fusion = bf16[64,1024]{1,0:T(8,128)(2,1)} fusion(bf16[64,1024]{1,0:T(8,128)(2,1)S(1)} %collective-permute-done.21, bf16[64,1024]{1,0:T(8,128)(2,1)} %get-tuple-element.50), kind=kLoop, calls=%fused_computation.4 | loop fusion | flops 262144 | bytes 393216 | tf_op jit(solution)/shard_map/convert_element_type | solution.py:346
  (76 shorter events, 10.6 us)
Async XLA Ops:
  0.6 15.4 %collective-permute-start.1 = (s32[1,64]{1,0:T(1,128)}, s32[1,64]{1,0:T(1,128)S(1)}, u32[]{:S(2)}, u32[]{:S(2)}) collective-permute-start(s32[1,64]{1,0:T(1,128)} %bitcast.27), channel_id=1, source_target_pairs={{0,2},{1,3},{2,0},{3,1},{4,6},{5,7},{6,4},{7,5},{8,10},{9,11},{10,... | collective-permute-start | bytes 776 | tf_op jit(solution)/shard_map/ppermute | solution.py:390
  4.7 11.4 %collective-permute-start = (bf16[64,1024]{1,0:T(8,128)(2,1)}, bf16[64,1024]{1,0:T(8,128)(2,1)S(1)}, u32[]{:S(2)}, u32[]{:S(2)}) collective-permute-start(bf16[64,1024]{1,0:T(8,128)(2,1)} %param.16), channel_id=1, source_target_pairs={{0,2},{1,3},{2,0},{3,1},{4,6},{5,7},{6,4},{7,5},{8,10},{9,11},{10,... | collective-permute-start | bytes 393224 | tf_op jit(solution)/shard_map/ppermute | solution.py:390
  16.4 16.8 %copy-start.2 = (bf16[128,1152]{1,0:T(8,128)(2,1)}, bf16[128,1152]{1,0:T(8,128)(2,1)S(1)}, u32[]{:S(2)}) copy-start(bf16[128,1152]{1,0:T(8,128)(2,1)S(1)} %fusion.1.refs_0_) | copy-start | bytes 884740
  16.4 16.8 %copy-start.17 = (bf16[256,1024]{1,0:T(8,128)(2,1)S(1)}, bf16[256,1024]{1,0:T(8,128)(2,1)}, u32[]{:S(2)}) copy-start(bf16[256,1024]{1,0:T(8,128)(2,1)} %embed.3.refs_4_) | copy-start | bytes 1572868
  16.4 16.9 %collective-permute-start.2 = (bf16[128,1152]{1,0:T(8,128)(2,1)S(1)}, bf16[128,1152]{1,0:T(8,128)(2,1)S(1)}, u32[]{:S(2)}, u32[]{:S(2)}) collective-permute-start(bf16[128,1152]{1,0:T(8,128)(2,1)S(1)} %fusion.1.refs_0_), channel_id=1, source_target_pairs={{0,16},{1,17},{2,18},{3,19},{4,20},{5,21},{6,22},{7,23},{8,24},{9,... | collective-permute-start | bytes 884744 | tf_op jit(solution)/shard_map/ppermute | solution.py:390
  18.3 15.1 %collective-permute-start.3 = (bf16[128,1152]{1,0:T(8,128)(2,1)S(1)}, bf16[128,1152]{1,0:T(8,128)(2,1)S(1)}, u32[]{:S(2)}, u32[]{:S(2)}) collective-permute-start(bf16[128,1152]{1,0:T(8,128)(2,1)S(1)} %fusion.1.refs_0_), channel_id=1, source_target_pairs={{0,8},{1,9},{2,10},{3,11},{4,12},{5,13},{6,14},{7,15},{8,0},{9,1},... | collective-permute-start | bytes 884744 | tf_op jit(solution)/shard_map/ppermute | solution.py:390
  19.8 13.6 %collective-permute-start.4 = (bf16[128,1152]{1,0:T(8,128)(2,1)S(1)}, bf16[128,1152]{1,0:T(8,128)(2,1)S(1)}, u32[]{:S(2)}, u32[]{:S(2)}) collective-permute-start(bf16[128,1152]{1,0:T(8,128)(2,1)S(1)} %fusion.1.refs_0_), channel_id=1, source_target_pairs={{0,24},{1,25},{2,26},{3,27},{4,28},{5,29},{6,30},{7,31},{8,16},{9,... | collective-permute-start | bytes 884744 | tf_op jit(solution)/shard_map/ppermute | solution.py:390
  20.0 14.0 %collective-permute-start.8 = (bf16[256,1024]{1,0:T(8,128)(2,1)}, bf16[256,1024]{1,0:T(8,128)(2,1)S(1)}, u32[]{:S(2)}, u32[]{:S(2)}) collective-permute-start(bf16[256,1024]{1,0:T(8,128)(2,1)} %embed.3.refs_4_), channel_id=1, source_target_pairs={{0,1},{1,0},{2,3},{3,2},{4,5},{5,4},{6,7},{7,6},{8,9},{9,8},{10,11... | collective-permute-start | bytes 1572872 | tf_op jit(solution)/shard_map/ppermute | solution.py:390
  33.3 2.0 %collective-permute-start.6 = (bf16[256,1024]{1,0:T(8,128)(2,1)S(1)}, bf16[256,1024]{1,0:T(8,128)(2,1)S(1)}, u32[]{:S(2)}, u32[]{:S(2)}) collective-permute-start(bf16[256,1024]{1,0:T(8,128)(2,1)S(1)} %copy-done.17), channel_id=1, source_target_pairs={{0,4},{1,5},{2,6},{3,7},{4,0},{5,1},{6,2},{7,3},{8,12},{9,13},{10,... | collective-permute-start | bytes 1572872 | tf_op jit(solution)/shard_map/ppermute | solution.py:390
  33.4 3.7 %collective-permute-start.7 = (bf16[256,1024]{1,0:T(8,128)(2,1)}, bf16[256,1024]{1,0:T(8,128)(2,1)}, u32[]{:S(2)}, u32[]{:S(2)}) collective-permute-start(bf16[256,1024]{1,0:T(8,128)(2,1)} %embed.2.refs_5_), channel_id=1, source_target_pairs={{0,4},{1,5},{2,6},{3,7},{4,0},{5,1},{6,2},{7,3},{8,12},{9,13},{10,... | collective-permute-start | bytes 1572872 | tf_op jit(solution)/shard_map/ppermute | solution.py:390
  33.9 3.1 %collective-permute-start.9 = (bf16[256,1024]{1,0:T(8,128)(2,1)S(1)}, bf16[256,1024]{1,0:T(8,128)(2,1)}, u32[]{:S(2)}, u32[]{:S(2)}) collective-permute-start(bf16[256,1024]{1,0:T(8,128)(2,1)S(1)} %collective-permute-done.8.refs_8_), channel_id=1, source_target_pairs={{0,4},{1,5},{2,6},{3,7},{4,0},{5,1},{6,2},{7,3},{8,12},{9,13},{10,... | collective-permute-start | bytes 1572872 | tf_op jit(solution)/shard_map/ppermute | solution.py:390
  34.0 14.5 %collective-permute-start.5 = (bf16[256,1024]{1,0:T(8,128)(2,1)}, bf16[256,1024]{1,0:T(8,128)(2,1)S(1)}, u32[]{:S(2)}, u32[]{:S(2)}) collective-permute-start(bf16[256,1024]{1,0:T(8,128)(2,1)} %embed.2.refs_5_), channel_id=1, source_target_pairs={{0,1},{1,0},{2,3},{3,2},{4,5},{5,4},{6,7},{7,6},{8,9},{9,8},{10,11... | collective-permute-start | bytes 1572872 | tf_op jit(solution)/shard_map/ppermute | solution.py:390
  48.5 1.9 %collective-permute-start.10 = (bf16[256,1024]{1,0:T(8,128)(2,1)S(1)}, bf16[256,1024]{1,0:T(8,128)(2,1)S(1)}, u32[]{:S(2)}, u32[]{:S(2)}) collective-permute-start(bf16[256,1024]{1,0:T(8,128)(2,1)S(1)} %collective-permute-done.5.refs_4_.refs_8_), channel_id=1, source_target_pairs={{0,4},{1,5},{2,6},{3,7},{4,0},{5,1},{6,2},{7,3},{8,12},{9,13},{10,... | collective-permute-start | bytes 1572872 | tf_op jit(solution)/shard_map/ppermute | solution.py:390
  55.5 6.1 %collective-permute-start.11 = (f32[16,128]{1,0:T(8,128)}, f32[16,128]{1,0:T(8,128)S(1)}, u32[]{:S(2)}, u32[]{:S(2)}) collective-permute-start(f32[16,128]{1,0:T(8,128)} %get-tuple-element.39.refs_0_), channel_id=1, source_target_pairs={{0,2},{1,3},{2,0},{3,1},{4,6},{5,7},{6,4},{7,5},{8,10},{9,11},{10,... | collective-permute-start | bytes 24584 | tf_op jit(solution)/shard_map/ppermute | solution.py:390
  58.1 6.5 %collective-permute-start.12 = (f32[16,128]{1,0:T(8,128)}, f32[16,128]{1,0:T(8,128)S(1)}, u32[]{:S(2)}, u32[]{:S(2)}) collective-permute-start(f32[16,128]{1,0:T(8,128)} %get-tuple-element.39.refs_0_), channel_id=1, source_target_pairs={{0,16},{1,17},{2,18},{3,19},{4,20},{5,21},{6,22},{7,23},{8,24},{9,... | collective-permute-start | bytes 24584 | tf_op jit(solution)/shard_map/ppermute | solution.py:390
  59.6 5.5 %collective-permute-start.14 = (f32[16,128]{1,0:T(8,128)}, f32[16,128]{1,0:T(8,128)S(1)}, u32[]{:S(2)}, u32[]{:S(2)}) collective-permute-start(f32[16,128]{1,0:T(8,128)} %get-tuple-element.39.refs_0_), channel_id=1, source_target_pairs={{0,8},{1,9},{2,10},{3,11},{4,12},{5,13},{6,14},{7,15},{8,0},{9,1},... | collective-permute-start | bytes 24584 | tf_op jit(solution)/shard_map/ppermute | solution.py:390
  61.1 4.8 %collective-permute-start.16 = (f32[16,128]{1,0:T(8,128)}, f32[16,128]{1,0:T(8,128)S(1)}, u32[]{:S(2)}, u32[]{:S(2)}) collective-permute-start(f32[16,128]{1,0:T(8,128)} %get-tuple-element.39.refs_0_), channel_id=1, source_target_pairs={{0,24},{1,25},{2,26},{3,27},{4,28},{5,29},{6,30},{7,31},{8,16},{9,... | collective-permute-start | bytes 24584 | tf_op jit(solution)/shard_map/ppermute | solution.py:390
  61.6 4.3 %collective-permute-start.13 = (f32[16,128]{1,0:T(8,128)S(1)}, f32[16,128]{1,0:T(8,128)S(1)}, u32[]{:S(2)}, u32[]{:S(2)}) collective-permute-start(f32[16,128]{1,0:T(8,128)S(1)} %collective-permute-done.11.refs_1_), channel_id=1, source_target_pairs={{0,16},{1,17},{2,18},{3,19},{4,20},{5,21},{6,22},{7,23},{8,24},{9,... | collective-permute-start | bytes 24584 | tf_op jit(solution)/shard_map/ppermute | solution.py:390
  63.1 3.7 %collective-permute-start.15 = (f32[16,128]{1,0:T(8,128)S(1)}, f32[16,128]{1,0:T(8,128)S(1)}, u32[]{:S(2)}, u32[]{:S(2)}) collective-permute-start(f32[16,128]{1,0:T(8,128)S(1)} %collective-permute-done.11.refs_1_), channel_id=1, source_target_pairs={{0,8},{1,9},{2,10},{3,11},{4,12},{5,13},{6,14},{7,15},{8,0},{9,1},... | collective-permute-start | bytes 24584 | tf_op jit(solution)/shard_map/ppermute | solution.py:390
  64.6 4.6 %collective-permute-start.17 = (f32[16,128]{1,0:T(8,128)S(1)}, f32[16,128]{1,0:T(8,128)S(1)}, u32[]{:S(2)}, u32[]{:S(2)}) collective-permute-start(f32[16,128]{1,0:T(8,128)S(1)} %collective-permute-done.11.refs_1_), channel_id=1, source_target_pairs={{0,24},{1,25},{2,26},{3,27},{4,28},{5,29},{6,30},{7,31},{8,16},{9,... | collective-permute-start | bytes 24584 | tf_op jit(solution)/shard_map/ppermute | solution.py:390
  75.0 9.4 %collective-permute-start.18 = (bf16[128,1024]{1,0:T(8,128)(2,1)}, bf16[128,1024]{1,0:T(8,128)(2,1)S(1)}, u32[]{:S(2)}, u32[]{:S(2)}) collective-permute-start(bf16[128,1024]{1,0:T(8,128)(2,1)} %get-tuple-element.47), channel_id=1, source_target_pairs={{0,16},{1,17},{2,18},{3,19},{4,20},{5,21},{6,22},{7,23},{8,24},{9,... | collective-permute-start | bytes 786440 | tf_op jit(solution)/shard_map/ppermute | solution.py:390
  75.5 8.9 %collective-permute-start.19 = (bf16[128,1024]{1,0:T(8,128)(2,1)}, bf16[128,1024]{1,0:T(8,128)(2,1)S(1)}, u32[]{:S(2)}, u32[]{:S(2)}) collective-permute-start(bf16[128,1024]{1,0:T(8,128)(2,1)} %get-tuple-element.48), channel_id=1, source_target_pairs={{0,8},{1,9},{2,10},{3,11},{4,12},{5,13},{6,14},{7,15},{8,0},{9,1},... | collective-permute-start | bytes 786440 | tf_op jit(solution)/shard_map/ppermute | solution.py:390
  76.0 11.6 %collective-permute-start.20 = (bf16[128,1024]{1,0:T(8,128)(2,1)}, bf16[128,1024]{1,0:T(8,128)(2,1)S(1)}, u32[]{:S(2)}, u32[]{:S(2)}) collective-permute-start(bf16[128,1024]{1,0:T(8,128)(2,1)} %get-tuple-element.49), channel_id=1, source_target_pairs={{0,24},{1,25},{2,26},{3,27},{4,28},{5,29},{6,30},{7,31},{8,16},{9,... | collective-permute-start | bytes 786440 | tf_op jit(solution)/shard_map/ppermute | solution.py:390
  90.3 7.3 %collective-permute-start.21 = (bf16[64,1024]{1,0:T(8,128)(2,1)}, bf16[64,1024]{1,0:T(8,128)(2,1)S(1)}, u32[]{:S(2)}, u32[]{:S(2)}) collective-permute-start(bf16[64,1024]{1,0:T(8,128)(2,1)} %get-tuple-element.51), channel_id=1, source_target_pairs={{0,2},{1,3},{2,0},{3,1},{4,6},{5,7},{6,4},{7,5},{8,10},{9,11},{10,... | collective-permute-start | bytes 393224 | tf_op jit(solution)/shard_map/ppermute | solution.py:390
  (19 other events, 74.6 us)
